TPU v7x, 512 devices: a whole 4x8x8 slice. The times are simulated.
512 devices in a mesh: section: 16 (over x_hi, y), fsdp: 32 (over x_lo, z, core).
Axes of the slice: x: 4 (x_hi: 2, x_lo: 2; x = x_hi * 2 + x_lo), y: 8, z: 8, core: 2. Of those that a mesh axis runs over, the one named last changes fastest.
Arguments:
- inputs: bfloat16 [16, 8, 1024, 4096], P('section', None, 'fsdp'), may hold values from -6 to 6
- upstream: bfloat16 [8, 1024, 4096], P(None, 'fsdp'), may hold values from -6 to 6
- weights: bfloat16 [16, 4096, 512], P('section', 'fsdp')
- gain: bfloat16 [16, 4096], P('section', 'fsdp'), may hold values from 0.5 to 1.5
Outputs:
- weight_grad: float32 [16, 4096, 512], P('section', 'fsdp')
- gain_grad: float32 [16, 4096], P('section')
All inputs are finite; a program needn't handle non-finite values.
Results may differ from a plain program's by a relative error of at most 0.035.
Values may be sent and summed in bfloat16 or wider, within the bound.
No kernel may reach another device: no remote copies, remote signals or barrier semaphores. Data moves between devices by JAX's collectives and lax.ppermute only.
A program may use at most 128 MiB of HBM per device.

v0:
```python
import jax
import jax.numpy as jnp
from jax import lax
from jax.sharding import PartitionSpec as P


def passed_along(value, axis, steps):
    count = lax.axis_size(axis)
    leading, last = (max(0, -steps), min(count, count - steps))
    return lax.ppermute(value, axis, [(source, source + steps) for source in range(leading, last)])


def rope_tables(length, head):
    half_head = head // 2
    position = lax.iota(jnp.float32, length)
    freq = jnp.power(500000.0, -2.0 * lax.iota(jnp.float32, half_head) / head)
    angle = position[:, None] * freq[None, :]
    return (jnp.cos(angle), jnp.sin(angle))


def rotate(value_rows, cosine, sine_table):
    half_head = value_rows.shape[-1] // 2
    first = value_rows[..., :half_head]
    second = value_rows[..., half_head:]
    return jnp.concatenate(
        [first * cosine - second * sine_table, second * cosine + first * sine_table], axis=-1
    )


def unrotate(value_rows, cosine, sine_table):
    half_head = value_rows.shape[-1] // 2
    first = value_rows[..., :half_head]
    second = value_rows[..., half_head:]
    return jnp.concatenate(
        [first * cosine + second * sine_table, second * cosine - first * sine_table], axis=-1
    )


def contract_rows(left, right):
    return lax.dot_general(
        left, right, (((0,), (0,)), ((), ())), preferred_element_type=jnp.float32
    )


def contract_cols(left, right):
    return lax.dot_general(
        left, right, (((1,), (1,)), ((), ())), preferred_element_type=jnp.float32
    )


def on_device(inputs, upstream, weights, gain):
    sections = lax.axis_size("section")
    here = lax.axis_index("section")
    micro_count = inputs.shape[1]
    length = inputs.shape[2]
    width = inputs.shape[3]
    head = weights.shape[2] // 4
    tokens_all = micro_count * length
    xfloat = inputs[0].reshape(tokens_all, width).astype(jnp.float32)
    inv_rms = lax.rsqrt(jnp.mean(xfloat * xfloat, axis=1, keepdims=True) + 1e-05)
    normed = xfloat * inv_rms
    w_full, gain_full = (
        lax.all_gather(weights[0], "fsdp", axis=0, tiled=True),
        lax.all_gather(gain[0], "fsdp", axis=0, tiled=True),
    )
    hidden = (normed * gain_full.astype(jnp.float32)).astype(jnp.bfloat16)
    proj = jnp.dot(hidden, w_full[:, : 3 * head], preferred_element_type=jnp.float32)
    wide_gain = gain_full.astype(jnp.float32)
    w_proj = w_full[:, : 3 * head]
    w_back = w_full[:, 3 * head :]
    cosine, sine_table = rope_tables(length, head)
    proj_seq = proj.reshape(micro_count, length, 3 * head)
    query_rows = rotate(proj_seq[..., :head], cosine, sine_table).astype(jnp.bfloat16)
    key_rows = rotate(proj_seq[..., head : 2 * head], cosine, sine_table).astype(jnp.bfloat16)
    value_rows = proj_seq[..., 2 * head :].astype(jnp.bfloat16)
    score_scale = head ** (-0.5)
    causal = lax.broadcasted_iota(jnp.int32, (length, length), 0) >= lax.broadcasted_iota(
        jnp.int32, (length, length), 1
    )

    def work(micro, grad_in, state):
        grad_store, proj_store, att_store, gain_acc, extra = state
        query_m = lax.dynamic_index_in_dim(query_rows, micro, 0, keepdims=False)
        keys_m = lax.dynamic_index_in_dim(key_rows, micro, 0, keepdims=False)
        values_m = lax.dynamic_index_in_dim(value_rows, micro, 0, keepdims=False)
        normed_m = lax.dynamic_slice_in_dim(normed, micro * length, length, 0)
        inv_m = lax.dynamic_slice_in_dim(inv_rms, micro * length, length, 0)
        score_matrix = contract_cols(query_m, keys_m) * score_scale
        probs = jax.nn.softmax(jnp.where(causal, score_matrix, -1e30), axis=-1)
        probability_matrix = probs.astype(jnp.bfloat16)
        attended_output = jnp.dot(
            probability_matrix, values_m, preferred_element_type=jnp.float32
        ).astype(jnp.bfloat16)
        attention_gradient = jnp.dot(grad_in, w_back, preferred_element_type=jnp.float32).astype(
            jnp.bfloat16
        )
        probability_gradient = contract_cols(attention_gradient, values_m)
        score_gradient = (
            probs
            * (probability_gradient - jnp.sum(probability_gradient * probs, axis=-1, keepdims=True))
            * score_scale
        ).astype(jnp.bfloat16)
        query_gradient = jnp.dot(score_gradient, keys_m, preferred_element_type=jnp.float32)
        key_gradient = contract_rows(score_gradient, query_m)
        value_gradient = contract_rows(probability_matrix, attention_gradient)
        grad_proj = jnp.concatenate(
            [
                unrotate(query_gradient, cosine, sine_table),
                unrotate(key_gradient, cosine, sine_table),
                value_gradient,
            ],
            axis=-1,
        ).astype(jnp.bfloat16)
        grad_hidden = contract_cols(grad_proj, w_proj)
        gain_term = jnp.sum(grad_hidden * normed_m, axis=0)
        grad_normed = grad_hidden * wide_gain
        grad_x = inv_m * (
            grad_normed - normed_m * jnp.mean(grad_normed * normed_m, axis=-1, keepdims=True)
        )
        grad_out = (grad_in.astype(jnp.float32) + grad_x).astype(jnp.bfloat16)
        grad_store = lax.dynamic_update_index_in_dim(grad_store, grad_in, micro, 0)
        proj_store = lax.dynamic_update_index_in_dim(proj_store, grad_proj, micro, 0)
        att_store = lax.dynamic_update_index_in_dim(att_store, attended_output, micro, 0)
        return (grad_out, (grad_store, proj_store, att_store, gain_acc + gain_term, extra))

    def spare(micro, grad_in, state):
        return (jnp.zeros_like(grad_in), state)

    def tick(tick_no, received, state):
        micro = tick_no - (sections - 1 - here)
        active = jnp.logical_and(micro >= 0, micro < micro_count)
        clipped = jnp.clip(micro, 0, micro_count - 1)
        top_grad = lax.dynamic_index_in_dim(upstream, clipped, 0, keepdims=False)
        grad_in = jnp.where(here == sections - 1, top_grad, received)
        return lax.cond(active, work, spare, clipped, grad_in, state)

    def step_loop(tick_no, carry):
        received, state = carry
        sent, state = tick(tick_no, received, state)
        received = passed_along(sent, "section", -1)
        return (received, state)

    extra_start = jnp.zeros((1,), jnp.float32)
    state_start = (
        jnp.zeros((micro_count, length, width), jnp.bfloat16),
        jnp.zeros((micro_count, length, 3 * head), jnp.bfloat16),
        jnp.zeros((micro_count, length, head), jnp.bfloat16),
        jnp.zeros((width,), jnp.float32),
        extra_start,
    )
    total_ticks = sections + micro_count - 1
    received, state = lax.fori_loop(
        0, total_ticks - 1, step_loop, (jnp.zeros((length, width), jnp.bfloat16), state_start)
    )
    leftover, state = tick(total_ticks - 1, received, state)
    grad_store, proj_store, att_store, gain_acc, extra = state
    gain_sum = lax.psum(gain_acc, "fsdp")
    grad_flat = grad_store.reshape(tokens_all, width)
    proj_flat = proj_store.reshape(tokens_all, 3 * head)
    att_flat = att_store.reshape(tokens_all, head)
    shard = lax.psum_scatter(
        jnp.concatenate(
            [contract_rows(hidden, proj_flat), contract_rows(grad_flat, att_flat)], axis=1
        ).astype(jnp.bfloat16),
        "fsdp",
        scatter_dimension=0,
        tiled=True,
    ).astype(jnp.float32)
    return (shard[None], gain_sum[None])


def solution(mesh):
    return jax.shard_map(
        on_device,
        mesh=mesh,
        in_specs=(
            P("section", None, "fsdp", None),
            P(None, "fsdp", None),
            P("section", "fsdp", None),
            P("section", "fsdp"),
        ),
        out_specs=(P("section", "fsdp", None), P("section", None)),
        check_vma=False,
    )
```

profile of v0, /device:TPU:1, one launch (start us, length us, event | category | flops | bytes accessed | tf_op | source)
XLA Modules:
  0.0 767.1 jit_solution(6606745490900244712)
XLA Ops:
  10.7 41.6 %all-gather = bf16[1,4096]{1,0:T(2,128)(2,1)S(1)} all-gather(bf16[1,128]{1,0:T(2,128)(2,1)} %param.13), channel_id=2, replica_groups=mesh['section'=16,'fsdp'=32] {'fsdp'}, dimensions={1}, use_global_device_ids=true | all-gather | bytes 8448 | tf_op jit(solution)/shard_map/all_gather | solution.py:64
  57.0 29.4 %all-gather.4.cloned.1.call-done = bf16[1,4096,512]{2,1,0:T(8,128)(2,1)} async-done(((bf16[1,128,512]{2,1,0:T(8,128)(2,1)}), bf16[1,4096,512]{2,1,0:T(8,128)(2,1)}) %all-gather.4.cloned.1.call-update) | async-done | bytes 4194320 | tf_op jit(solution)/shard_map/all_gather | solution.py:63
  96.4 502.5 %while.26 = (s32[]{:T(128)}, bf16[32,4096]{1,0:T(8,128)(2,1)}, bf16[8,32,4096]{2,1,0:T(8,128)(2,1)}, bf16[8,32,384]{2,1,0:T(8,128)(2,1)}, bf16[8,32,128]{2,1,0:T...) while((s32[]{:T(128)}, bf16[32,4096]{1,0:T(8,128)(2,1)}, ...), condition=%wide.region_9.10_spmd.clone.clone.clone, body=%wide.region_1.9_spmd.clone.clone.clone.sunk | while | flops 137564064 | bytes 10755985 | solution.py:152
  210.8 9.6 %collective-permute-done = bf16[32,4096]{1,0:T(8,128)(2,1)S(1)} collective-permute-done((bf16[32,4096]{1,0:T(8,128)(2,1)}, bf16[32,4096]{1,0:T(8,128)(2,1)S(1)}, u32[]{:S(2)}, u32[]{:S(2)}) %collective-permute-start) | collective-permute-done | bytes 262176 | tf_op jit(solution)/shard_map/while/body/eval_jaxpr/ppermute | solution.py:10
  223.2 10.7 %collective-permute-done = bf16[32,4096]{1,0:T(8,128)(2,1)S(1)} collective-permute-done((bf16[32,4096]{1,0:T(8,128)(2,1)}, bf16[32,4096]{1,0:T(8,128)(2,1)S(1)}, u32[]{:S(2)}, u32[]{:S(2)}) %collective-permute-start) | collective-permute-done | bytes 262176 | tf_op jit(solution)/shard_map/while/body/eval_jaxpr/ppermute | solution.py:10
  236.7 12.2 %collective-permute-done = bf16[32,4096]{1,0:T(8,128)(2,1)S(1)} collective-permute-done((bf16[32,4096]{1,0:T(8,128)(2,1)}, bf16[32,4096]{1,0:T(8,128)(2,1)S(1)}, u32[]{:S(2)}, u32[]{:S(2)}) %collective-permute-start) | collective-permute-done | bytes 262176 | tf_op jit(solution)/shard_map/while/body/eval_jaxpr/ppermute | solution.py:10
  251.8 169.2 %collective-permute-done = bf16[32,4096]{1,0:T(8,128)(2,1)S(1)} collective-permute-done((bf16[32,4096]{1,0:T(8,128)(2,1)}, bf16[32,4096]{1,0:T(8,128)(2,1)S(1)}, u32[]{:S(2)}, u32[]{:S(2)}) %collective-permute-start) | collective-permute-done | bytes 262176 | tf_op jit(solution)/shard_map/while/body/eval_jaxpr/ppermute | solution.py:10
  421.7 13.6 %conditional.7 = (bf16[32,4096]{1,0:T(8,128)(2,1)}, bf16[8,32,4096]{2,1,0:T(8,128)(2,1)}, bf16[8,32,384]{2,1,0:T(8,128)(2,1)}, bf16[8,32,128]{2,1,0:T(8,128)(2,1)}, f32[4096]{0:T(1024)S(1)}) conditional(s32[]{:T(128)} %convert_element_type.189, (bf16[8,32,4096]{2,1,0:T(8,128)(2,1)}, bf16[8,32,384]{2,1,0:T(8,128)(2,1)}, ...), branch_computations={%region_2.2_spmd, %region_3.8_spmd.clone} | conditional | flops 137562016 | bytes 8641706 | solution.py:135
  436.6 9.8 %collective-permute-done = bf16[32,4096]{1,0:T(8,128)(2,1)S(1)} collective-permute-done((bf16[32,4096]{1,0:T(8,128)(2,1)}, bf16[32,4096]{1,0:T(8,128)(2,1)S(1)}, u32[]{:S(2)}, u32[]{:S(2)}) %collective-permute-start) | collective-permute-done | bytes 262176 | tf_op jit(solution)/shard_map/while/body/eval_jaxpr/ppermute | solution.py:10
  447.1 13.6 %conditional.7 = (bf16[32,4096]{1,0:T(8,128)(2,1)}, bf16[8,32,4096]{2,1,0:T(8,128)(2,1)}, bf16[8,32,384]{2,1,0:T(8,128)(2,1)}, bf16[8,32,128]{2,1,0:T(8,128)(2,1)}, f32[4096]{0:T(1024)S(1)}) conditional(s32[]{:T(128)} %convert_element_type.189, (bf16[8,32,4096]{2,1,0:T(8,128)(2,1)}, bf16[8,32,384]{2,1,0:T(8,128)(2,1)}, ...), branch_computations={%region_2.2_spmd, %region_3.8_spmd.clone} | conditional | flops 137562016 | bytes 8641706 | solution.py:135
  462.0 9.7 %collective-permute-done = bf16[32,4096]{1,0:T(8,128)(2,1)S(1)} collective-permute-done((bf16[32,4096]{1,0:T(8,128)(2,1)}, bf16[32,4096]{1,0:T(8,128)(2,1)S(1)}, u32[]{:S(2)}, u32[]{:S(2)}) %collective-permute-start) | collective-permute-done | bytes 262176 | tf_op jit(solution)/shard_map/while/body/eval_jaxpr/ppermute | solution.py:10
  472.4 13.6 %conditional.7 = (bf16[32,4096]{1,0:T(8,128)(2,1)}, bf16[8,32,4096]{2,1,0:T(8,128)(2,1)}, bf16[8,32,384]{2,1,0:T(8,128)(2,1)}, bf16[8,32,128]{2,1,0:T(8,128)(2,1)}, f32[4096]{0:T(1024)S(1)}) conditional(s32[]{:T(128)} %convert_element_type.189, (bf16[8,32,4096]{2,1,0:T(8,128)(2,1)}, bf16[8,32,384]{2,1,0:T(8,128)(2,1)}, ...), branch_computations={%region_2.2_spmd, %region_3.8_spmd.clone} | conditional | flops 137562016 | bytes 8641706 | solution.py:135
  487.3 9.9 %collective-permute-done = bf16[32,4096]{1,0:T(8,128)(2,1)S(1)} collective-permute-done((bf16[32,4096]{1,0:T(8,128)(2,1)}, bf16[32,4096]{1,0:T(8,128)(2,1)S(1)}, u32[]{:S(2)}, u32[]{:S(2)}) %collective-permute-start) | collective-permute-done | bytes 262176 | tf_op jit(solution)/shard_map/while/body/eval_jaxpr/ppermute | solution.py:10
  497.9 13.6 %conditional.7 = (bf16[32,4096]{1,0:T(8,128)(2,1)}, bf16[8,32,4096]{2,1,0:T(8,128)(2,1)}, bf16[8,32,384]{2,1,0:T(8,128)(2,1)}, bf16[8,32,128]{2,1,0:T(8,128)(2,1)}, f32[4096]{0:T(1024)S(1)}) conditional(s32[]{:T(128)} %convert_element_type.189, (bf16[8,32,4096]{2,1,0:T(8,128)(2,1)}, bf16[8,32,384]{2,1,0:T(8,128)(2,1)}, ...), branch_computations={%region_2.2_spmd, %region_3.8_spmd.clone} | conditional | flops 137562016 | bytes 8641706 | solution.py:135
  512.8 9.4 %collective-permute-done = bf16[32,4096]{1,0:T(8,128)(2,1)S(1)} collective-permute-done((bf16[32,4096]{1,0:T(8,128)(2,1)}, bf16[32,4096]{1,0:T(8,128)(2,1)S(1)}, u32[]{:S(2)}, u32[]{:S(2)}) %collective-permute-start) | collective-permute-done | bytes 262176 | tf_op jit(solution)/shard_map/while/body/eval_jaxpr/ppermute | solution.py:10
  523.0 13.6 %conditional.7 = (bf16[32,4096]{1,0:T(8,128)(2,1)}, bf16[8,32,4096]{2,1,0:T(8,128)(2,1)}, bf16[8,32,384]{2,1,0:T(8,128)(2,1)}, bf16[8,32,128]{2,1,0:T(8,128)(2,1)}, f32[4096]{0:T(1024)S(1)}) conditional(s32[]{:T(128)} %convert_element_type.189, (bf16[8,32,4096]{2,1,0:T(8,128)(2,1)}, bf16[8,32,384]{2,1,0:T(8,128)(2,1)}, ...), branch_computations={%region_2.2_spmd, %region_3.8_spmd.clone} | conditional | flops 137562016 | bytes 8641706 | solution.py:135
  537.9 9.7 %collective-permute-done = bf16[32,4096]{1,0:T(8,128)(2,1)S(1)} collective-permute-done((bf16[32,4096]{1,0:T(8,128)(2,1)}, bf16[32,4096]{1,0:T(8,128)(2,1)S(1)}, u32[]{:S(2)}, u32[]{:S(2)}) %collective-permute-start) | collective-permute-done | bytes 262176 | tf_op jit(solution)/shard_map/while/body/eval_jaxpr/ppermute | solution.py:10
  548.4 13.6 %conditional.7 = (bf16[32,4096]{1,0:T(8,128)(2,1)}, bf16[8,32,4096]{2,1,0:T(8,128)(2,1)}, bf16[8,32,384]{2,1,0:T(8,128)(2,1)}, bf16[8,32,128]{2,1,0:T(8,128)(2,1)}, f32[4096]{0:T(1024)S(1)}) conditional(s32[]{:T(128)} %convert_element_type.189, (bf16[8,32,4096]{2,1,0:T(8,128)(2,1)}, bf16[8,32,384]{2,1,0:T(8,128)(2,1)}, ...), branch_computations={%region_2.2_spmd, %region_3.8_spmd.clone} | conditional | flops 137562016 | bytes 8641706 | solution.py:135
  563.3 9.5 %collective-permute-done = bf16[32,4096]{1,0:T(8,128)(2,1)S(1)} collective-permute-done((bf16[32,4096]{1,0:T(8,128)(2,1)}, bf16[32,4096]{1,0:T(8,128)(2,1)S(1)}, u32[]{:S(2)}, u32[]{:S(2)}) %collective-permute-start) | collective-permute-done | bytes 262176 | tf_op jit(solution)/shard_map/while/body/eval_jaxpr/ppermute | solution.py:10
  573.6 13.6 %conditional.7 = (bf16[32,4096]{1,0:T(8,128)(2,1)}, bf16[8,32,4096]{2,1,0:T(8,128)(2,1)}, bf16[8,32,384]{2,1,0:T(8,128)(2,1)}, bf16[8,32,128]{2,1,0:T(8,128)(2,1)}, f32[4096]{0:T(1024)S(1)}) conditional(s32[]{:T(128)} %convert_element_type.189, (bf16[8,32,4096]{2,1,0:T(8,128)(2,1)}, bf16[8,32,384]{2,1,0:T(8,128)(2,1)}, ...), branch_computations={%region_2.2_spmd, %region_3.8_spmd.clone} | conditional | flops 137562016 | bytes 8641706 | solution.py:135
  588.5 9.7 %collective-permute-done = bf16[32,4096]{1,0:T(8,128)(2,1)S(1)} collective-permute-done((bf16[32,4096]{1,0:T(8,128)(2,1)}, bf16[32,4096]{1,0:T(8,128)(2,1)S(1)}, u32[]{:S(2)}, u32[]{:S(2)}) %collective-permute-start) | collective-permute-done | bytes 262176 | tf_op jit(solution)/shard_map/while/body/eval_jaxpr/ppermute | solution.py:10
  598.9 12.5 %conditional.2 = (bf16[8,32,4096]{2,1,0:T(8,128)(2,1)}, bf16[8,32,128]{2,1,0:T(8,128)(2,1)}, f32[4096]{0:T(1024)S(1)}, bf16[256,384]{1,0:T(8,128)(2,1)}) conditional(s32[]{:T(128)} %convert_element_type.138, (bf16[8,32,4096]{2,1,0:T(8,128)(2,1)}, bf16[8,32,128]{2,1,0:T(8,128)(2,1)}, f32[4096]{0:T(1024)S(1)}, ...), branch_computations={%region_10.11_spmd, %region_11.16_spmd} | conditional | flops 136382368 | bytes 7605022 | solution.py:135
  624.3 120.4 %psum.7 = f32[1,4096]{1,0:T(1,128)} all-reduce(f32[1,4096]{1,0:T(1,128)S(1)} %bitcast.142), channel_id=1, replica_groups=mesh['section'=16,'fsdp'=32] {'fsdp'}, use_global_device_ids=true, to_apply=%region_17.18 | all-reduce | flops 4096 | bytes 32768 | tf_op jit(solution)/shard_map/psum | solution.py:157
  744.7 13.7 %reduce-scatter.4.cloned.1.call-done = bf16[128,512]{1,0:T(8,128)(2,1)} async-done(((bf16[4096,512]{1,0:T(8,128)(2,1)}), bf16[128,512]{1,0:T(8,128)(2,1)}) %reduce-scatter.4.cloned.1.call-update) | async-done | bytes 131088
  (381 shorter events, 287.6 us)
Async XLA Ops:
  7.2 79.2 %all-gather.4.cloned.1.call-start = ((), (), s32[]{:S(2)}) async-start(), calls=%async_computation.1 | async-start | bytes 4325376 | tf_op jit(solution)/shard_map/all_gather | solution.py:63
  7.9 750.5 %reduce-scatter.4.cloned.1.call-start = ((), (), s32[]{:S(2)}) async-start(), calls=%async_computation.2 | async-start | bytes 4325376
  97.2 9.7 %collective-permute-start = (bf16[32,4096]{1,0:T(8,128)(2,1)}, bf16[32,4096]{1,0:T(8,128)(2,1)S(1)}, u32[]{:S(2)}, u32[]{:S(2)}) collective-permute-start(bf16[32,4096]{1,0:T(8,128)(2,1)} %get-tuple-element.1282), channel_id=1, source_target_pairs={{32,0},{64,32},{96,64},{128,96},{160,128},{192,160},{224,192},{256... | collective-permute-start | bytes 786440 | tf_op jit(solution)/shard_map/while/body/eval_jaxpr/ppermute | solution.py:10
  108.4 8.8 %collective-permute-start = (bf16[32,4096]{1,0:T(8,128)(2,1)}, bf16[32,4096]{1,0:T(8,128)(2,1)S(1)}, u32[]{:S(2)}, u32[]{:S(2)}) collective-permute-start(bf16[32,4096]{1,0:T(8,128)(2,1)} %get-tuple-element.1282), channel_id=1, source_target_pairs={{32,0},{64,32},{96,64},{128,96},{160,128},{192,160},{224,192},{256... | collective-permute-start | bytes 786440 | tf_op jit(solution)/shard_map/while/body/eval_jaxpr/ppermute | solution.py:10
  118.6 7.9 %collective-permute-start = (bf16[32,4096]{1,0:T(8,128)(2,1)}, bf16[32,4096]{1,0:T(8,128)(2,1)S(1)}, u32[]{:S(2)}, u32[]{:S(2)}) collective-permute-start(bf16[32,4096]{1,0:T(8,128)(2,1)} %get-tuple-element.1282), channel_id=1, source_target_pairs={{32,0},{64,32},{96,64},{128,96},{160,128},{192,160},{224,192},{256... | collective-permute-start | bytes 786440 | tf_op jit(solution)/shard_map/while/body/eval_jaxpr/ppermute | solution.py:10
  128.0 9.1 %collective-permute-start = (bf16[32,4096]{1,0:T(8,128)(2,1)}, bf16[32,4096]{1,0:T(8,128)(2,1)S(1)}, u32[]{:S(2)}, u32[]{:S(2)}) collective-permute-start(bf16[32,4096]{1,0:T(8,128)(2,1)} %get-tuple-element.1282), channel_id=1, source_target_pairs={{32,0},{64,32},{96,64},{128,96},{160,128},{192,160},{224,192},{256... | collective-permute-start | bytes 786440 | tf_op jit(solution)/shard_map/while/body/eval_jaxpr/ppermute | solution.py:10
  138.5 7.4 collective-permute-start
  147.4 8.2 %collective-permute-start = (bf16[32,4096]{1,0:T(8,128)(2,1)}, bf16[32,4096]{1,0:T(8,128)(2,1)S(1)}, u32[]{:S(2)}, u32[]{:S(2)}) collective-permute-start(bf16[32,4096]{1,0:T(8,128)(2,1)} %get-tuple-element.1282), channel_id=1, source_target_pairs={{32,0},{64,32},{96,64},{128,96},{160,128},{192,160},{224,192},{256... | collective-permute-start | bytes 786440 | tf_op jit(solution)/shard_map/while/body/eval_jaxpr/ppermute | solution.py:10
  157.2 8.5 %collective-permute-start = (bf16[32,4096]{1,0:T(8,128)(2,1)}, bf16[32,4096]{1,0:T(8,128)(2,1)S(1)}, u32[]{:S(2)}, u32[]{:S(2)}) collective-permute-start(bf16[32,4096]{1,0:T(8,128)(2,1)} %get-tuple-element.1282), channel_id=1, source_target_pairs={{32,0},{64,32},{96,64},{128,96},{160,128},{192,160},{224,192},{256... | collective-permute-start | bytes 786440 | tf_op jit(solution)/shard_map/while/body/eval_jaxpr/ppermute | solution.py:10
  167.2 8.5 %collective-permute-start = (bf16[32,4096]{1,0:T(8,128)(2,1)}, bf16[32,4096]{1,0:T(8,128)(2,1)S(1)}, u32[]{:S(2)}, u32[]{:S(2)}) collective-permute-start(bf16[32,4096]{1,0:T(8,128)(2,1)} %get-tuple-element.1282), channel_id=1, source_target_pairs={{32,0},{64,32},{96,64},{128,96},{160,128},{192,160},{224,192},{256... | collective-permute-start | bytes 786440 | tf_op jit(solution)/shard_map/while/body/eval_jaxpr/ppermute | solution.py:10
  177.2 8.5 %collective-permute-start = (bf16[32,4096]{1,0:T(8,128)(2,1)}, bf16[32,4096]{1,0:T(8,128)(2,1)S(1)}, u32[]{:S(2)}, u32[]{:S(2)}) collective-permute-start(bf16[32,4096]{1,0:T(8,128)(2,1)} %get-tuple-element.1282), channel_id=1, source_target_pairs={{32,0},{64,32},{96,64},{128,96},{160,128},{192,160},{224,192},{256... | collective-permute-start | bytes 786440 | tf_op jit(solution)/shard_map/while/body/eval_jaxpr/ppermute | solution.py:10
  187.2 9.8 %collective-permute-start = (bf16[32,4096]{1,0:T(8,128)(2,1)}, bf16[32,4096]{1,0:T(8,128)(2,1)S(1)}, u32[]{:S(2)}, u32[]{:S(2)}) collective-permute-start(bf16[32,4096]{1,0:T(8,128)(2,1)} %get-tuple-element.1282), channel_id=1, source_target_pairs={{32,0},{64,32},{96,64},{128,96},{160,128},{192,160},{224,192},{256... | collective-permute-start | bytes 786440 | tf_op jit(solution)/shard_map/while/body/eval_jaxpr/ppermute | solution.py:10
  198.5 9.6 %collective-permute-start = (bf16[32,4096]{1,0:T(8,128)(2,1)}, bf16[32,4096]{1,0:T(8,128)(2,1)S(1)}, u32[]{:S(2)}, u32[]{:S(2)}) collective-permute-start(bf16[32,4096]{1,0:T(8,128)(2,1)} %get-tuple-element.1282), channel_id=1, source_target_pairs={{32,0},{64,32},{96,64},{128,96},{160,128},{192,160},{224,192},{256... | collective-permute-start | bytes 786440 | tf_op jit(solution)/shard_map/while/body/eval_jaxpr/ppermute | solution.py:10
  209.5 10.9 %collective-permute-start = (bf16[32,4096]{1,0:T(8,128)(2,1)}, bf16[32,4096]{1,0:T(8,128)(2,1)S(1)}, u32[]{:S(2)}, u32[]{:S(2)}) collective-permute-start(bf16[32,4096]{1,0:T(8,128)(2,1)} %get-tuple-element.1282), channel_id=1, source_target_pairs={{32,0},{64,32},{96,64},{128,96},{160,128},{192,160},{224,192},{256... | collective-permute-start | bytes 786440 | tf_op jit(solution)/shard_map/while/body/eval_jaxpr/ppermute | solution.py:10
  221.9 12.0 %collective-permute-start = (bf16[32,4096]{1,0:T(8,128)(2,1)}, bf16[32,4096]{1,0:T(8,128)(2,1)S(1)}, u32[]{:S(2)}, u32[]{:S(2)}) collective-permute-start(bf16[32,4096]{1,0:T(8,128)(2,1)} %get-tuple-element.1282), channel_id=1, source_target_pairs={{32,0},{64,32},{96,64},{128,96},{160,128},{192,160},{224,192},{256... | collective-permute-start | bytes 786440 | tf_op jit(solution)/shard_map/while/body/eval_jaxpr/ppermute | solution.py:10
  235.5 13.5 %collective-permute-start = (bf16[32,4096]{1,0:T(8,128)(2,1)}, bf16[32,4096]{1,0:T(8,128)(2,1)S(1)}, u32[]{:S(2)}, u32[]{:S(2)}) collective-permute-start(bf16[32,4096]{1,0:T(8,128)(2,1)} %get-tuple-element.1282), channel_id=1, source_target_pairs={{32,0},{64,32},{96,64},{128,96},{160,128},{192,160},{224,192},{256... | collective-permute-start | bytes 786440 | tf_op jit(solution)/shard_map/while/body/eval_jaxpr/ppermute | solution.py:10
  250.5 170.5 %collective-permute-start = (bf16[32,4096]{1,0:T(8,128)(2,1)}, bf16[32,4096]{1,0:T(8,128)(2,1)S(1)}, u32[]{:S(2)}, u32[]{:S(2)}) collective-permute-start(bf16[32,4096]{1,0:T(8,128)(2,1)} %get-tuple-element.1282), channel_id=1, source_target_pairs={{32,0},{64,32},{96,64},{128,96},{160,128},{192,160},{224,192},{256... | collective-permute-start | bytes 786440 | tf_op jit(solution)/shard_map/while/body/eval_jaxpr/ppermute | solution.py:10
  435.3 11.1 %collective-permute-start = (bf16[32,4096]{1,0:T(8,128)(2,1)}, bf16[32,4096]{1,0:T(8,128)(2,1)S(1)}, u32[]{:S(2)}, u32[]{:S(2)}) collective-permute-start(bf16[32,4096]{1,0:T(8,128)(2,1)} %get-tuple-element.1282), channel_id=1, source_target_pairs={{32,0},{64,32},{96,64},{128,96},{160,128},{192,160},{224,192},{256... | collective-permute-start | bytes 786440 | tf_op jit(solution)/shard_map/while/body/eval_jaxpr/ppermute | solution.py:10
  460.7 11.0 %collective-permute-start = (bf16[32,4096]{1,0:T(8,128)(2,1)}, bf16[32,4096]{1,0:T(8,128)(2,1)S(1)}, u32[]{:S(2)}, u32[]{:S(2)}) collective-permute-start(bf16[32,4096]{1,0:T(8,128)(2,1)} %get-tuple-element.1282), channel_id=1, source_target_pairs={{32,0},{64,32},{96,64},{128,96},{160,128},{192,160},{224,192},{256... | collective-permute-start | bytes 786440 | tf_op jit(solution)/shard_map/while/body/eval_jaxpr/ppermute | solution.py:10
  486.0 11.2 %collective-permute-start = (bf16[32,4096]{1,0:T(8,128)(2,1)}, bf16[32,4096]{1,0:T(8,128)(2,1)S(1)}, u32[]{:S(2)}, u32[]{:S(2)}) collective-permute-start(bf16[32,4096]{1,0:T(8,128)(2,1)} %get-tuple-element.1282), channel_id=1, source_target_pairs={{32,0},{64,32},{96,64},{128,96},{160,128},{192,160},{224,192},{256... | collective-permute-start | bytes 786440 | tf_op jit(solution)/shard_map/while/body/eval_jaxpr/ppermute | solution.py:10
  511.6 10.7 %collective-permute-start = (bf16[32,4096]{1,0:T(8,128)(2,1)}, bf16[32,4096]{1,0:T(8,128)(2,1)S(1)}, u32[]{:S(2)}, u32[]{:S(2)}) collective-permute-start(bf16[32,4096]{1,0:T(8,128)(2,1)} %get-tuple-element.1282), channel_id=1, source_target_pairs={{32,0},{64,32},{96,64},{128,96},{160,128},{192,160},{224,192},{256... | collective-permute-start | bytes 786440 | tf_op jit(solution)/shard_map/while/body/eval_jaxpr/ppermute | solution.py:10
  536.6 11.0 %collective-permute-start = (bf16[32,4096]{1,0:T(8,128)(2,1)}, bf16[32,4096]{1,0:T(8,128)(2,1)S(1)}, u32[]{:S(2)}, u32[]{:S(2)}) collective-permute-start(bf16[32,4096]{1,0:T(8,128)(2,1)} %get-tuple-element.1282), channel_id=1, source_target_pairs={{32,0},{64,32},{96,64},{128,96},{160,128},{192,160},{224,192},{256... | collective-permute-start | bytes 786440 | tf_op jit(solution)/shard_map/while/body/eval_jaxpr/ppermute | solution.py:10
  562.0 10.8 %collective-permute-start = (bf16[32,4096]{1,0:T(8,128)(2,1)}, bf16[32,4096]{1,0:T(8,128)(2,1)S(1)}, u32[]{:S(2)}, u32[]{:S(2)}) collective-permute-start(bf16[32,4096]{1,0:T(8,128)(2,1)} %get-tuple-element.1282), channel_id=1, source_target_pairs={{32,0},{64,32},{96,64},{128,96},{160,128},{192,160},{224,192},{256... | collective-permute-start | bytes 786440 | tf_op jit(solution)/shard_map/while/body/eval_jaxpr/ppermute | solution.py:10
  587.2 11.0 %collective-permute-start = (bf16[32,4096]{1,0:T(8,128)(2,1)}, bf16[32,4096]{1,0:T(8,128)(2,1)S(1)}, u32[]{:S(2)}, u32[]{:S(2)}) collective-permute-start(bf16[32,4096]{1,0:T(8,128)(2,1)} %get-tuple-element.1282), channel_id=1, source_target_pairs={{32,0},{64,32},{96,64},{128,96},{160,128},{192,160},{224,192},{256... | collective-permute-start | bytes 786440 | tf_op jit(solution)/shard_map/while/body/eval_jaxpr/ppermute | solution.py:10
  (35 other events, 208.2 us)
Sparse Core Ops, SparseCore 0:
  10.2 76.1 all-gather.3
  624.4 133.9 reduce-scatter.3
where the time goes:
time: 774 us; the launch traced here: 767 us
  waiting for transfers between devices  395 us (51%)
  blocking collectives  162 us (21%)
  matrix products  77.4 us (10%)
  local copies, waits for them, and re-layouts  48.2 us (6%)
  other arithmetic  40.2 us (5%)
  starting transfers between devices  28.2 us (4%)
  between operations  14.2 us (2%)
    ppermute x22, waiting for transfers between devices, passed_along(): lax.ppermute(value, axis, [(source, source + steps) for source in range(l...  351 us
    psum x1, blocking collectives, on_device(): gain_sum = lax.psum(gain_acc, 'fsdp')  120 us
    all_gather x1, blocking collectives, on_device(): lax.all_gather(gain[0], 'fsdp', axis=0, tiled=True)  41.6 us
    dot_general x24, matrix products, contract_cols(): lax.dot_general(left, right, (((1,), (1,)), ((), ())), preferred_element_...  31.5 us
    all_gather x1, waiting for transfers between devices, on_device(): lax.all_gather(weights[0], 'fsdp', axis=0, tiled=True)  29.4 us
    ppermute x22, starting transfers between devices, passed_along(): lax.ppermute(value, axis, [(source, source + steps) for source in range(l...  28.2 us
  transfers between devices with their start and end apart: 24, of which 24 were waited for; matrix products, arithmetic and copies ran while one was open for 1% of the time, Pallas kernels for 0%

commit v1 on v0

v1 whole, which is shorter than its diff:
```python
import jax
import jax.numpy as jnp
from jax import lax
from jax.sharding import PartitionSpec as P


def passed_along(value, axis, steps):
    count = lax.axis_size(axis)
    leading, last = (max(0, -steps), min(count, count - steps))
    return lax.ppermute(value, axis, [(source, source + steps) for source in range(leading, last)])


def rope_tables(length, head):
    half_head = head // 2
    position = lax.iota(jnp.float32, length)
    freq = jnp.power(500000.0, -2.0 * lax.iota(jnp.float32, half_head) / head)
    angle = position[:, None] * freq[None, :]
    return (jnp.cos(angle), jnp.sin(angle))


def rotate(value_rows, cosine, sine_table):
    half_head = value_rows.shape[-1] // 2
    first = value_rows[..., :half_head]
    second = value_rows[..., half_head:]
    return jnp.concatenate(
        [first * cosine - second * sine_table, second * cosine + first * sine_table], axis=-1
    )


def unrotate(value_rows, cosine, sine_table):
    half_head = value_rows.shape[-1] // 2
    first = value_rows[..., :half_head]
    second = value_rows[..., half_head:]
    return jnp.concatenate(
        [first * cosine + second * sine_table, second * cosine - first * sine_table], axis=-1
    )


def contract_rows(left, right):
    return lax.dot_general(
        left, right, (((0,), (0,)), ((), ())), preferred_element_type=jnp.float32
    )


def contract_cols(left, right):
    return lax.dot_general(
        left, right, (((1,), (1,)), ((), ())), preferred_element_type=jnp.float32
    )


def on_device(inputs, upstream, weights, gain):
    sections = lax.axis_size("section")
    here = lax.axis_index("section")
    micro_count = inputs.shape[1]
    length = inputs.shape[2]
    width = inputs.shape[3]
    head = weights.shape[2] // 4
    rows_here = weights.shape[1]
    groups = lax.axis_size("fsdp")

    gain_rows = jnp.zeros((16, weights.shape[2]), jnp.bfloat16)
    gain_rows = lax.dynamic_update_slice(gain_rows, gain[0][None, :], (0, 0))
    packed = jnp.concatenate([weights[0], gain_rows], axis=0)
    gathered = lax.all_gather(packed, "fsdp", axis=0, tiled=True).reshape(
        groups, rows_here + 16, weights.shape[2]
    )
    w_full = gathered[:, :rows_here, :].reshape(groups * rows_here, weights.shape[2])
    gain_full = gathered[:, rows_here, :rows_here].reshape(groups * rows_here)
    wide_gain = gain_full.astype(jnp.float32)
    w_proj = w_full[:, : 3 * head]
    w_back = w_full[:, 3 * head :]

    xfloat = inputs[0].astype(jnp.float32)
    inv_rms = lax.rsqrt(jnp.mean(xfloat * xfloat, axis=-1, keepdims=True) + 1e-05)
    normed = xfloat * inv_rms
    hidden = (normed * wide_gain).astype(jnp.bfloat16)
    proj = jnp.dot(
        hidden.reshape(micro_count * length, width), w_proj, preferred_element_type=jnp.float32
    ).reshape(micro_count, length, 3 * head)
    cosine, sine_table = rope_tables(length, head)
    query_rows = rotate(proj[..., :head], cosine, sine_table).astype(jnp.bfloat16)
    key_rows = rotate(proj[..., head : 2 * head], cosine, sine_table).astype(jnp.bfloat16)
    value_rows = proj[..., 2 * head :].astype(jnp.bfloat16)
    score_scale = head ** (-0.5)
    causal = lax.broadcasted_iota(jnp.int32, (length, length), 0) >= lax.broadcasted_iota(
        jnp.int32, (length, length), 1
    )
    scores = jnp.einsum(
        "mqh,mkh->mqk", query_rows, key_rows, preferred_element_type=jnp.float32
    ) * score_scale
    probs = jax.nn.softmax(jnp.where(causal[None], scores, -1e30), axis=-1)
    probs_b = probs.astype(jnp.bfloat16)
    attended = jnp.einsum(
        "mqk,mkh->mqh", probs_b, value_rows, preferred_element_type=jnp.float32
    ).astype(jnp.bfloat16)

    def tick(tick_no, received, state):
        grad_store, proj_store, gain_acc = state
        micro = tick_no - (sections - 1 - here)
        active = jnp.logical_and(micro >= 0, micro < micro_count)
        clipped = jnp.clip(micro, 0, micro_count - 1)
        slot = jnp.clip(micro, -1, micro_count) + 1
        top_grad = lax.dynamic_index_in_dim(upstream, clipped, 0, keepdims=False)
        grad_in = jnp.where(here == sections - 1, top_grad, received)
        query_m = lax.dynamic_index_in_dim(query_rows, clipped, 0, keepdims=False)
        keys_m = lax.dynamic_index_in_dim(key_rows, clipped, 0, keepdims=False)
        values_m = lax.dynamic_index_in_dim(value_rows, clipped, 0, keepdims=False)
        probs_m = lax.dynamic_index_in_dim(probs, clipped, 0, keepdims=False)
        probs_bm = lax.dynamic_index_in_dim(probs_b, clipped, 0, keepdims=False)
        normed_m = lax.dynamic_index_in_dim(normed, clipped, 0, keepdims=False)
        inv_m = lax.dynamic_index_in_dim(inv_rms, clipped, 0, keepdims=False)
        attention_gradient = jnp.dot(
            grad_in, w_back, preferred_element_type=jnp.float32
        ).astype(jnp.bfloat16)
        probability_gradient = contract_cols(attention_gradient, values_m)
        score_gradient = (
            probs_m
            * (probability_gradient - jnp.sum(probability_gradient * probs_m, axis=-1, keepdims=True))
            * score_scale
        ).astype(jnp.bfloat16)
        query_gradient = jnp.dot(score_gradient, keys_m, preferred_element_type=jnp.float32)
        key_gradient = contract_rows(score_gradient, query_m)
        value_gradient = contract_rows(probs_bm, attention_gradient)
        grad_proj = jnp.concatenate(
            [
                unrotate(query_gradient, cosine, sine_table),
                unrotate(key_gradient, cosine, sine_table),
                value_gradient,
            ],
            axis=-1,
        ).astype(jnp.bfloat16)
        grad_hidden = contract_cols(grad_proj, w_proj)
        gain_term = jnp.sum(grad_hidden * normed_m, axis=0)
        grad_normed = grad_hidden * wide_gain
        grad_x = inv_m * (
            grad_normed - normed_m * jnp.mean(grad_normed * normed_m, axis=-1, keepdims=True)
        )
        grad_out = (grad_in.astype(jnp.float32) + grad_x).astype(jnp.bfloat16)
        grad_store = lax.dynamic_update_index_in_dim(grad_store, grad_in, slot, 0)
        proj_store = lax.dynamic_update_index_in_dim(proj_store, grad_proj, slot, 0)
        gain_acc = gain_acc + jnp.where(active, gain_term, 0.0)
        return grad_out, (grad_store, proj_store, gain_acc)

    def step_loop(tick_no, carry):
        received, state = carry
        sent, state = tick(tick_no, received, state)
        received = passed_along(sent, "section", -1)
        return (received, state)

    state_start = (
        jnp.zeros((micro_count + 2, length, width), jnp.bfloat16),
        jnp.zeros((micro_count + 2, length, 3 * head), jnp.bfloat16),
        jnp.zeros((width,), jnp.float32),
    )
    total_ticks = sections + micro_count - 1
    received, state = lax.fori_loop(
        0, total_ticks - 1, step_loop, (jnp.zeros((length, width), jnp.bfloat16), state_start)
    )
    leftover, state = tick(total_ticks - 1, received, state)
    grad_store, proj_store, gain_acc = state
    tokens_all = micro_count * length
    grad_flat = grad_store[1 : micro_count + 1].reshape(tokens_all, width)
    proj_flat = proj_store[1 : micro_count + 1].reshape(tokens_all, 3 * head)
    att_flat = attended.reshape(tokens_all, head)
    shard = lax.psum_scatter(
        jnp.concatenate(
            [
                contract_rows(hidden.reshape(tokens_all, width), proj_flat),
                contract_rows(grad_flat, att_flat),
            ],
            axis=1,
        ).astype(jnp.bfloat16),
        "fsdp",
        scatter_dimension=0,
        tiled=True,
    ).astype(jnp.float32)
    gain_sum = jnp.sum(lax.all_gather(gain_acc, "fsdp", axis=0), axis=0)
    return (shard[None], gain_sum[None])


def solution(mesh):
    return jax.shard_map(
        on_device,
        mesh=mesh,
        in_specs=(
            P("section", None, "fsdp", None),
            P(None, "fsdp", None),
            P("section", "fsdp", None),
            P("section", "fsdp"),
        ),
        out_specs=(P("section", "fsdp", None), P("section", None)),
        check_vma=False,
    )
```

time: 774 us -> 816 us (1.054)
  blocking collectives: 162 us -> 56.8 us
  matrix products: 77.4 us -> 175 us
  other arithmetic: 40.2 us -> 118 us
  waiting for transfers between devices: 395 us -> 358 us
    ppermute x22, waiting for transfers between devices: 351 us -> 173 us  [passed_along(): lax.ppermute(value, axis, [(source, source + steps) for source in range(l...]
    psum x1 -> x0, blocking collectives: 120 us -> none  [on_device(): gain_sum = lax.psum(gain_acc, 'fsdp')]
    unnamed x3, waiting for transfers between devices: 14.4 us -> 112 us
    convert_element_type x17 -> x47, other arithmetic: 15.6 us -> 61.6 us  [the longest x22 42.2 us: tick(): grad_out = (grad_in.astype(jnp.float32) + grad_x).astype(jnp.bfloat16)]
    all_gather x1, waiting for transfers between devices: 29.4 us -> 73.4 us  [on_device(): lax.all_gather(packed, 'fsdp', axis=0, tiled=True)]
    dot_general x24 -> x46, matrix products: 31.5 us -> 72.5 us  [contract_cols(): lax.dot_general(left, right, (((1,), (1,)), ((), ())), preferred_element_...]
    dot_general x18 -> x48, matrix products: 11.6 us -> 44.7 us  [contract_rows(): lax.dot_general(left, right, (((0,), (0,)), ((), ())), preferred_element_...]
    dynamic_update_slice x8 -> x23, other arithmetic: 14.4 us -> 40.9 us  [tick(): grad_store = lax.dynamic_update_index_in_dim(grad_store, grad_in, slot, 0)]
  transfers between devices with their start and end apart: 24 -> 24, of which waited for: 24 -> 24; matrix products, arithmetic and copies ran while one was open for 1% -> 3% of each run, Pallas kernels for 0% -> 0%
where the time goes in v1:
time: 816 us; the launch traced here: 802 us
  waiting for transfers between devices  358 us (44%)
  matrix products  175 us (21%)
  other arithmetic  118 us (14%)
  blocking collectives  56.8 us (7%)
  local copies, waits for them, and re-layouts  51.6 us (6%)
  starting transfers between devices  28.2 us (3%)
  between operations  14.3 us (2%)
    ppermute x22, waiting for transfers between devices, passed_along(): lax.ppermute(value, axis, [(source, source + steps) for source in range(l...  173 us
    unnamed x3, waiting for transfers between devices  112 us
    all_gather x1, waiting for transfers between devices, on_device(): lax.all_gather(packed, 'fsdp', axis=0, tiled=True)  73.4 us
    dot_general x46, matrix products, contract_cols(): lax.dot_general(left, right, (((1,), (1,)), ((), ())), preferred_element_...  72.5 us
    all_gather x1, blocking collectives, on_device(): gain_sum = jnp.sum(lax.all_gather(gain_acc, 'fsdp', axis=0), axis=0)  56.8 us
    dot_general x48, matrix products, contract_rows(): lax.dot_general(left, right, (((0,), (0,)), ((), ())), preferred_element_...  44.7 us
    convert_element_type x22, other arithmetic, tick(): grad_out = (grad_in.astype(jnp.float32) + grad_x).astype(jnp.bfloat16)  42.2 us
    dynamic_update_slice x23, other arithmetic, tick(): grad_store = lax.dynamic_update_index_in_dim(grad_store, grad_in, slot, 0)  40.9 us
  transfers between devices with their start and end apart: 24, of which 24 were waited for; matrix products, arithmetic and copies ran while one was open for 3% of the time, Pallas kernels for 0%

profile of v1, /device:TPU:1, one launch (start us, length us, event | category | flops | bytes accessed | tf_op | source)
XLA Modules:
  0.0 802.2 jit_solution(6295574927163842685)
XLA Ops:
  13.8 73.4 %all-gather.3.cloned.1.call-done = bf16[4608,512]{1,0:T(8,128)(2,1)} async-done(((bf16[144,512]{1,0:T(8,128)(2,1)}), bf16[4608,512]{1,0:T(8,128)(2,1)}) %all-gather.3.cloned.1.call-update) | async-done | bytes 4718608 | tf_op jit(solution)/shard_map/all_gather | solution.py:64
  102.9 492.0 %while.25 = (s32[]{:T(128)}, bf16[32,4096]{1,0:T(8,128)(2,1)}, bf16[10,32,4096]{2,1,0:T(8,128)(2,1)}, bf16[10,32,384]{2,1,0:T(8,128)(2,1)}, f32[4096]{0:T(1024)S...) while((s32[]{:T(128)}, bf16[32,4096]{1,0:T(8,128)(2,1)}, ...), condition=%wide.region_7.8_spmd.clone.clone.clone.clone, body=%wide.region_3.7_spmd.clone.clone.clone.clone.sunk | while | flops 137027552 | bytes 10679635 | solution.py:156
  116.8 7.7 collective-permute-done
  139.0 6.8 collective-permute-done
  180.7 7.2 collective-permute-done
  243.1 6.5 collective-permute-done
  264.1 6.5 collective-permute-done
  285.2 6.5 collective-permute-done
  306.2 6.5 collective-permute-done
  327.3 8.8 %collective-permute-done = bf16[32,4096]{1,0:T(8,128)(2,1)S(1)} collective-permute-done((bf16[32,4096]{1,0:T(8,128)(2,1)}, bf16[32,4096]{1,0:T(8,128)(2,1)S(1)}, u32[]{:S(2)}, u32[]{:S(2)}) %collective-permute-start) | collective-permute-done | bytes 262176 | tf_op jit(solution)/shard_map/while/body/eval_jaxpr/ppermute | solution.py:10
  350.6 8.9 %collective-permute-done = bf16[32,4096]{1,0:T(8,128)(2,1)S(1)} collective-permute-done((bf16[32,4096]{1,0:T(8,128)(2,1)}, bf16[32,4096]{1,0:T(8,128)(2,1)S(1)}, u32[]{:S(2)}, u32[]{:S(2)}) %collective-permute-start) | collective-permute-done | bytes 262176 | tf_op jit(solution)/shard_map/while/body/eval_jaxpr/ppermute | solution.py:10
  374.0 8.9 %collective-permute-done = bf16[32,4096]{1,0:T(8,128)(2,1)S(1)} collective-permute-done((bf16[32,4096]{1,0:T(8,128)(2,1)}, bf16[32,4096]{1,0:T(8,128)(2,1)S(1)}, u32[]{:S(2)}, u32[]{:S(2)}) %collective-permute-start) | collective-permute-done | bytes 262176 | tf_op jit(solution)/shard_map/while/body/eval_jaxpr/ppermute | solution.py:10
  397.5 8.9 %collective-permute-done = bf16[32,4096]{1,0:T(8,128)(2,1)S(1)} collective-permute-done((bf16[32,4096]{1,0:T(8,128)(2,1)}, bf16[32,4096]{1,0:T(8,128)(2,1)S(1)}, u32[]{:S(2)}, u32[]{:S(2)}) %collective-permute-start) | collective-permute-done | bytes 262176 | tf_op jit(solution)/shard_map/while/body/eval_jaxpr/ppermute | solution.py:10
  420.9 8.8 %collective-permute-done = bf16[32,4096]{1,0:T(8,128)(2,1)S(1)} collective-permute-done((bf16[32,4096]{1,0:T(8,128)(2,1)}, bf16[32,4096]{1,0:T(8,128)(2,1)S(1)}, u32[]{:S(2)}, u32[]{:S(2)}) %collective-permute-start) | collective-permute-done | bytes 262176 | tf_op jit(solution)/shard_map/while/body/eval_jaxpr/ppermute | solution.py:10
  444.3 8.9 %collective-permute-done = bf16[32,4096]{1,0:T(8,128)(2,1)S(1)} collective-permute-done((bf16[32,4096]{1,0:T(8,128)(2,1)}, bf16[32,4096]{1,0:T(8,128)(2,1)S(1)}, u32[]{:S(2)}, u32[]{:S(2)}) %collective-permute-start) | collective-permute-done | bytes 262176 | tf_op jit(solution)/shard_map/while/body/eval_jaxpr/ppermute | solution.py:10
  467.7 8.9 %collective-permute-done = bf16[32,4096]{1,0:T(8,128)(2,1)S(1)} collective-permute-done((bf16[32,4096]{1,0:T(8,128)(2,1)}, bf16[32,4096]{1,0:T(8,128)(2,1)S(1)}, u32[]{:S(2)}, u32[]{:S(2)}) %collective-permute-start) | collective-permute-done | bytes 262176 | tf_op jit(solution)/shard_map/while/body/eval_jaxpr/ppermute | solution.py:10
  491.0 9.0 %collective-permute-done = bf16[32,4096]{1,0:T(8,128)(2,1)S(1)} collective-permute-done((bf16[32,4096]{1,0:T(8,128)(2,1)}, bf16[32,4096]{1,0:T(8,128)(2,1)S(1)}, u32[]{:S(2)}, u32[]{:S(2)}) %collective-permute-start) | collective-permute-done | bytes 262176 | tf_op jit(solution)/shard_map/while/body/eval_jaxpr/ppermute | solution.py:10
  514.5 9.0 %collective-permute-done = bf16[32,4096]{1,0:T(8,128)(2,1)S(1)} collective-permute-done((bf16[32,4096]{1,0:T(8,128)(2,1)}, bf16[32,4096]{1,0:T(8,128)(2,1)S(1)}, u32[]{:S(2)}, u32[]{:S(2)}) %collective-permute-start) | collective-permute-done | bytes 262176 | tf_op jit(solution)/shard_map/while/body/eval_jaxpr/ppermute | solution.py:10
  537.9 9.0 %collective-permute-done = bf16[32,4096]{1,0:T(8,128)(2,1)S(1)} collective-permute-done((bf16[32,4096]{1,0:T(8,128)(2,1)}, bf16[32,4096]{1,0:T(8,128)(2,1)S(1)}, u32[]{:S(2)}, u32[]{:S(2)}) %collective-permute-start) | collective-permute-done | bytes 262176 | tf_op jit(solution)/shard_map/while/body/eval_jaxpr/ppermute | solution.py:10
  561.5 8.9 %collective-permute-done = bf16[32,4096]{1,0:T(8,128)(2,1)S(1)} collective-permute-done((bf16[32,4096]{1,0:T(8,128)(2,1)}, bf16[32,4096]{1,0:T(8,128)(2,1)S(1)}, u32[]{:S(2)}, u32[]{:S(2)}) %collective-permute-start) | collective-permute-done | bytes 262176 | tf_op jit(solution)/shard_map/while/body/eval_jaxpr/ppermute | solution.py:10
  584.9 9.3 %collective-permute-done = bf16[32,4096]{1,0:T(8,128)(2,1)S(1)} collective-permute-done((bf16[32,4096]{1,0:T(8,128)(2,1)}, bf16[32,4096]{1,0:T(8,128)(2,1)S(1)}, u32[]{:S(2)}, u32[]{:S(2)}) %collective-permute-start) | collective-permute-done | bytes 262176 | tf_op jit(solution)/shard_map/while/body/eval_jaxpr/ppermute | solution.py:10
  614.5 6.5 copy.14
  624.1 56.8 %all-gather = f32[131072]{0:T(1024)S(1)} all-gather(f32[4096]{0:T(1024)S(1)} %select_add_fusion.1), channel_id=2, replica_groups=mesh['section'=16,'fsdp'=32] {'fsdp'}, dimensions={0}, use_global_device_ids=true | all-gather | bytes 540672 | tf_op jit(solution)/shard_map/all_gather | solution.py:177
  681.7 111.7 %reduce-scatter.4.cloned.1.call-done = bf16[128,512]{1,0:T(8,128)(2,1)} async-done(((bf16[4096,512]{1,0:T(8,128)(2,1)}), bf16[128,512]{1,0:T(8,128)(2,1)}) %reduce-scatter.4.cloned.1.call-update) | async-done | bytes 131088
  (489 shorter events, 383.3 us)
Async XLA Ops:
  7.2 80.1 %all-gather.3.cloned.1.call-start = ((), (), s32[]{:S(2)}) async-start(), calls=%async_computation.1 | async-start | bytes 4866048 | tf_op jit(solution)/shard_map/all_gather | solution.py:64
  9.0 784.5 %reduce-scatter.4.cloned.1.call-start = ((), (), s32[]{:S(2)}) async-start(), calls=%async_computation.2 | async-start | bytes 4325376
  114.8 9.7 %collective-permute-start = (bf16[32,4096]{1,0:T(8,128)(2,1)}, bf16[32,4096]{1,0:T(8,128)(2,1)S(1)}, u32[]{:S(2)}, u32[]{:S(2)}) collective-permute-start(bf16[32,4096]{1,0:T(8,128)(2,1)} %fusion.145), channel_id=1, source_target_pairs={{32,0},{64,32},{96,64},{128,96},{160,128},{192,160},{224,192},{256... | collective-permute-start | bytes 786440 | tf_op jit(solution)/shard_map/while/body/eval_jaxpr/ppermute | solution.py:10
  137.0 8.8 %collective-permute-start = (bf16[32,4096]{1,0:T(8,128)(2,1)}, bf16[32,4096]{1,0:T(8,128)(2,1)S(1)}, u32[]{:S(2)}, u32[]{:S(2)}) collective-permute-start(bf16[32,4096]{1,0:T(8,128)(2,1)} %fusion.145), channel_id=1, source_target_pairs={{32,0},{64,32},{96,64},{128,96},{160,128},{192,160},{224,192},{256... | collective-permute-start | bytes 786440 | tf_op jit(solution)/shard_map/while/body/eval_jaxpr/ppermute | solution.py:10
  158.3 7.9 collective-permute-start
  178.7 9.2 %collective-permute-start = (bf16[32,4096]{1,0:T(8,128)(2,1)}, bf16[32,4096]{1,0:T(8,128)(2,1)S(1)}, u32[]{:S(2)}, u32[]{:S(2)}) collective-permute-start(bf16[32,4096]{1,0:T(8,128)(2,1)} %fusion.145), channel_id=1, source_target_pairs={{32,0},{64,32},{96,64},{128,96},{160,128},{192,160},{224,192},{256... | collective-permute-start | bytes 786440 | tf_op jit(solution)/shard_map/while/body/eval_jaxpr/ppermute | solution.py:10
  200.4 7.4 collective-permute-start
  220.3 8.2 %collective-permute-start = (bf16[32,4096]{1,0:T(8,128)(2,1)}, bf16[32,4096]{1,0:T(8,128)(2,1)S(1)}, u32[]{:S(2)}, u32[]{:S(2)}) collective-permute-start(bf16[32,4096]{1,0:T(8,128)(2,1)} %fusion.145), channel_id=1, source_target_pairs={{32,0},{64,32},{96,64},{128,96},{160,128},{192,160},{224,192},{256... | collective-permute-start | bytes 786440 | tf_op jit(solution)/shard_map/while/body/eval_jaxpr/ppermute | solution.py:10
  241.1 8.5 %collective-permute-start = (bf16[32,4096]{1,0:T(8,128)(2,1)}, bf16[32,4096]{1,0:T(8,128)(2,1)S(1)}, u32[]{:S(2)}, u32[]{:S(2)}) collective-permute-start(bf16[32,4096]{1,0:T(8,128)(2,1)} %fusion.145), channel_id=1, source_target_pairs={{32,0},{64,32},{96,64},{128,96},{160,128},{192,160},{224,192},{256... | collective-permute-start | bytes 786440 | tf_op jit(solution)/shard_map/while/body/eval_jaxpr/ppermute | solution.py:10
  262.1 8.5 %collective-permute-start = (bf16[32,4096]{1,0:T(8,128)(2,1)}, bf16[32,4096]{1,0:T(8,128)(2,1)S(1)}, u32[]{:S(2)}, u32[]{:S(2)}) collective-permute-start(bf16[32,4096]{1,0:T(8,128)(2,1)} %fusion.145), channel_id=1, source_target_pairs={{32,0},{64,32},{96,64},{128,96},{160,128},{192,160},{224,192},{256... | collective-permute-start | bytes 786440 | tf_op jit(solution)/shard_map/while/body/eval_jaxpr/ppermute | solution.py:10
  283.2 8.5 %collective-permute-start = (bf16[32,4096]{1,0:T(8,128)(2,1)}, bf16[32,4096]{1,0:T(8,128)(2,1)S(1)}, u32[]{:S(2)}, u32[]{:S(2)}) collective-permute-start(bf16[32,4096]{1,0:T(8,128)(2,1)} %fusion.145), channel_id=1, source_target_pairs={{32,0},{64,32},{96,64},{128,96},{160,128},{192,160},{224,192},{256... | collective-permute-start | bytes 786440 | tf_op jit(solution)/shard_map/while/body/eval_jaxpr/ppermute | solution.py:10
  304.2 8.5 %collective-permute-start = (bf16[32,4096]{1,0:T(8,128)(2,1)}, bf16[32,4096]{1,0:T(8,128)(2,1)S(1)}, u32[]{:S(2)}, u32[]{:S(2)}) collective-permute-start(bf16[32,4096]{1,0:T(8,128)(2,1)} %fusion.145), channel_id=1, source_target_pairs={{32,0},{64,32},{96,64},{128,96},{160,128},{192,160},{224,192},{256... | collective-permute-start | bytes 786440 | tf_op jit(solution)/shard_map/while/body/eval_jaxpr/ppermute | solution.py:10
  325.3 10.8 %collective-permute-start = (bf16[32,4096]{1,0:T(8,128)(2,1)}, bf16[32,4096]{1,0:T(8,128)(2,1)S(1)}, u32[]{:S(2)}, u32[]{:S(2)}) collective-permute-start(bf16[32,4096]{1,0:T(8,128)(2,1)} %fusion.145), channel_id=1, source_target_pairs={{32,0},{64,32},{96,64},{128,96},{160,128},{192,160},{224,192},{256... | collective-permute-start | bytes 786440 | tf_op jit(solution)/shard_map/while/body/eval_jaxpr/ppermute | solution.py:10
  348.6 10.9 %collective-permute-start = (bf16[32,4096]{1,0:T(8,128)(2,1)}, bf16[32,4096]{1,0:T(8,128)(2,1)S(1)}, u32[]{:S(2)}, u32[]{:S(2)}) collective-permute-start(bf16[32,4096]{1,0:T(8,128)(2,1)} %fusion.145), channel_id=1, source_target_pairs={{32,0},{64,32},{96,64},{128,96},{160,128},{192,160},{224,192},{256... | collective-permute-start | bytes 786440 | tf_op jit(solution)/shard_map/while/body/eval_jaxpr/ppermute | solution.py:10
  372.0 10.9 %collective-permute-start = (bf16[32,4096]{1,0:T(8,128)(2,1)}, bf16[32,4096]{1,0:T(8,128)(2,1)S(1)}, u32[]{:S(2)}, u32[]{:S(2)}) collective-permute-start(bf16[32,4096]{1,0:T(8,128)(2,1)} %fusion.145), channel_id=1, source_target_pairs={{32,0},{64,32},{96,64},{128,96},{160,128},{192,160},{224,192},{256... | collective-permute-start | bytes 786440 | tf_op jit(solution)/shard_map/while/body/eval_jaxpr/ppermute | solution.py:10
  395.5 10.9 %collective-permute-start = (bf16[32,4096]{1,0:T(8,128)(2,1)}, bf16[32,4096]{1,0:T(8,128)(2,1)S(1)}, u32[]{:S(2)}, u32[]{:S(2)}) collective-permute-start(bf16[32,4096]{1,0:T(8,128)(2,1)} %fusion.145), channel_id=1, source_target_pairs={{32,0},{64,32},{96,64},{128,96},{160,128},{192,160},{224,192},{256... | collective-permute-start | bytes 786440 | tf_op jit(solution)/shard_map/while/body/eval_jaxpr/ppermute | solution.py:10
  418.9 10.8 %collective-permute-start = (bf16[32,4096]{1,0:T(8,128)(2,1)}, bf16[32,4096]{1,0:T(8,128)(2,1)S(1)}, u32[]{:S(2)}, u32[]{:S(2)}) collective-permute-start(bf16[32,4096]{1,0:T(8,128)(2,1)} %fusion.145), channel_id=1, source_target_pairs={{32,0},{64,32},{96,64},{128,96},{160,128},{192,160},{224,192},{256... | collective-permute-start | bytes 786440 | tf_op jit(solution)/shard_map/while/body/eval_jaxpr/ppermute | solution.py:10
  442.3 10.9 %collective-permute-start = (bf16[32,4096]{1,0:T(8,128)(2,1)}, bf16[32,4096]{1,0:T(8,128)(2,1)S(1)}, u32[]{:S(2)}, u32[]{:S(2)}) collective-permute-start(bf16[32,4096]{1,0:T(8,128)(2,1)} %fusion.145), channel_id=1, source_target_pairs={{32,0},{64,32},{96,64},{128,96},{160,128},{192,160},{224,192},{256... | collective-permute-start | bytes 786440 | tf_op jit(solution)/shard_map/while/body/eval_jaxpr/ppermute | solution.py:10
  465.6 10.9 %collective-permute-start = (bf16[32,4096]{1,0:T(8,128)(2,1)}, bf16[32,4096]{1,0:T(8,128)(2,1)S(1)}, u32[]{:S(2)}, u32[]{:S(2)}) collective-permute-start(bf16[32,4096]{1,0:T(8,128)(2,1)} %fusion.145), channel_id=1, source_target_pairs={{32,0},{64,32},{96,64},{128,96},{160,128},{192,160},{224,192},{256... | collective-permute-start | bytes 786440 | tf_op jit(solution)/shard_map/while/body/eval_jaxpr/ppermute | solution.py:10
  489.0 11.0 %collective-permute-start = (bf16[32,4096]{1,0:T(8,128)(2,1)}, bf16[32,4096]{1,0:T(8,128)(2,1)S(1)}, u32[]{:S(2)}, u32[]{:S(2)}) collective-permute-start(bf16[32,4096]{1,0:T(8,128)(2,1)} %fusion.145), channel_id=1, source_target_pairs={{32,0},{64,32},{96,64},{128,96},{160,128},{192,160},{224,192},{256... | collective-permute-start | bytes 786440 | tf_op jit(solution)/shard_map/while/body/eval_jaxpr/ppermute | solution.py:10
  512.5 10.9 %collective-permute-start = (bf16[32,4096]{1,0:T(8,128)(2,1)}, bf16[32,4096]{1,0:T(8,128)(2,1)S(1)}, u32[]{:S(2)}, u32[]{:S(2)}) collective-permute-start(bf16[32,4096]{1,0:T(8,128)(2,1)} %fusion.145), channel_id=1, source_target_pairs={{32,0},{64,32},{96,64},{128,96},{160,128},{192,160},{224,192},{256... | collective-permute-start | bytes 786440 | tf_op jit(solution)/shard_map/while/body/eval_jaxpr/ppermute | solution.py:10
  535.9 11.0 %collective-permute-start = (bf16[32,4096]{1,0:T(8,128)(2,1)}, bf16[32,4096]{1,0:T(8,128)(2,1)S(1)}, u32[]{:S(2)}, u32[]{:S(2)}) collective-permute-start(bf16[32,4096]{1,0:T(8,128)(2,1)} %fusion.145), channel_id=1, source_target_pairs={{32,0},{64,32},{96,64},{128,96},{160,128},{192,160},{224,192},{256... | collective-permute-start | bytes 786440 | tf_op jit(solution)/shard_map/while/body/eval_jaxpr/ppermute | solution.py:10
  559.5 10.9 %collective-permute-start = (bf16[32,4096]{1,0:T(8,128)(2,1)}, bf16[32,4096]{1,0:T(8,128)(2,1)S(1)}, u32[]{:S(2)}, u32[]{:S(2)}) collective-permute-start(bf16[32,4096]{1,0:T(8,128)(2,1)} %fusion.145), channel_id=1, source_target_pairs={{32,0},{64,32},{96,64},{128,96},{160,128},{192,160},{224,192},{256... | collective-permute-start | bytes 786440 | tf_op jit(solution)/shard_map/while/body/eval_jaxpr/ppermute | solution.py:10
  582.9 11.3 %collective-permute-start = (bf16[32,4096]{1,0:T(8,128)(2,1)}, bf16[32,4096]{1,0:T(8,128)(2,1)S(1)}, u32[]{:S(2)}, u32[]{:S(2)}) collective-permute-start(bf16[32,4096]{1,0:T(8,128)(2,1)} %fusion.145), channel_id=1, source_target_pairs={{32,0},{64,32},{96,64},{128,96},{160,128},{192,160},{224,192},{256... | collective-permute-start | bytes 786440 | tf_op jit(solution)/shard_map/while/body/eval_jaxpr/ppermute | solution.py:10
  (33 other events, 69.1 us)
Sparse Core Ops, SparseCore 0:
  10.7 76.5 all-gather.2
  621.1 172.3 reduce-scatter.3

commit v2 on v1

--- a/solution.py
+++ b/solution.py
@@ -1,11 +1,15 @@
 import jax
 import jax.numpy as jnp
 from jax import lax
-from jax.sharding import PartitionSpec as P
+from jax.sharding import Mesh, PartitionSpec as P
+
+SECTION = ("sh", "sy")
+FSDP = ("fx", "fz", "fc")
+SH, SY, FX, FZ, FC = 2, 8, 2, 8, 2
 
 
 def passed_along(value, axis, steps):
-    count = lax.axis_size(axis)
+    count = SH * SY
     leading, last = (max(0, -steps), min(count, count - steps))
     return lax.ppermute(value, axis, [(source, source + steps) for source in range(leading, last)])
 
@@ -49,20 +53,25 @@
 
 
 def on_device(inputs, upstream, weights, gain):
-    sections = lax.axis_size("section")
-    here = lax.axis_index("section")
+    sections = SH * SY
+    here = lax.axis_index("sh") * SY + lax.axis_index("sy")
     micro_count = inputs.shape[1]
     length = inputs.shape[2]
     width = inputs.shape[3]
     head = weights.shape[2] // 4
     rows_here = weights.shape[1]
-    groups = lax.axis_size("fsdp")
+    groups = FX * FZ * FC
 
     gain_rows = jnp.zeros((16, weights.shape[2]), jnp.bfloat16)
     gain_rows = lax.dynamic_update_slice(gain_rows, gain[0][None, :], (0, 0))
     packed = jnp.concatenate([weights[0], gain_rows], axis=0)
-    gathered = lax.all_gather(packed, "fsdp", axis=0, tiled=True).reshape(
-        groups, rows_here + 16, weights.shape[2]
+    staged = lax.all_gather(packed, "fx", axis=0, tiled=True)
+    staged = lax.all_gather(staged, "fz", axis=0, tiled=True)
+    staged = lax.all_gather(staged, "fc", axis=0, tiled=True)
+    gathered = (
+        staged.reshape(FC, FZ, FX, rows_here + 16, weights.shape[2])
+        .transpose(2, 1, 0, 3, 4)
+        .reshape(groups, rows_here + 16, weights.shape[2])
     )
     w_full = gathered[:, :rows_here, :].reshape(groups * rows_here, weights.shape[2])
     gain_full = gathered[:, rows_here, :rows_here].reshape(groups * rows_here)
@@ -144,7 +153,7 @@
     def step_loop(tick_no, carry):
         received, state = carry
         sent, state = tick(tick_no, received, state)
-        received = passed_along(sent, "section", -1)
+        received = passed_along(sent, SECTION, -1)
         return (received, state)
 
     state_start = (
@@ -162,32 +171,47 @@
     grad_flat = grad_store[1 : micro_count + 1].reshape(tokens_all, width)
     proj_flat = proj_store[1 : micro_count + 1].reshape(tokens_all, 3 * head)
     att_flat = attended.reshape(tokens_all, head)
-    shard = lax.psum_scatter(
-        jnp.concatenate(
-            [
-                contract_rows(hidden.reshape(tokens_all, width), proj_flat),
-                contract_rows(grad_flat, att_flat),
-            ],
-            axis=1,
-        ).astype(jnp.bfloat16),
-        "fsdp",
-        scatter_dimension=0,
-        tiled=True,
-    ).astype(jnp.float32)
-    gain_sum = jnp.sum(lax.all_gather(gain_acc, "fsdp", axis=0), axis=0)
+    def stage_order(rows):
+        return (
+            rows.reshape(tokens_all, FX, FZ, FC, rows_here)
+            .transpose(0, 3, 2, 1, 4)
+            .reshape(tokens_all, width)
+        )
+
+    terms = jnp.concatenate(
+        [
+            contract_rows(stage_order(hidden.reshape(tokens_all, width)), proj_flat),
+            contract_rows(stage_order(grad_flat), att_flat),
+        ],
+        axis=1,
+    ).astype(jnp.bfloat16)
+    cols = terms.shape[1]
+    terms = lax.psum_scatter(terms.reshape(FC, -1, cols), "fc", scatter_dimension=0, tiled=True)
+    terms = lax.psum_scatter(terms.reshape(FZ, -1, cols), "fz", scatter_dimension=0, tiled=True)
+    terms = lax.psum_scatter(terms.reshape(FX, -1, cols), "fx", scatter_dimension=0, tiled=True)
+    shard = terms.reshape(rows_here, cols).astype(jnp.float32)
+    gain_sum = jnp.sum(lax.all_gather(gain_acc, FSDP, axis=0), axis=0)
     return (shard[None], gain_sum[None])
 
 
 def solution(mesh):
+    global SH, SY, FX, FZ, FC
+    sections = mesh.shape["section"]
+    groups = mesh.shape["fsdp"]
+    SH, SY = 2, sections // 2
+    FX, FZ, FC = 2, groups // 4, 2
+    sub_mesh = Mesh(
+        mesh.devices.reshape(SH, SY, FX, FZ, FC), ("sh", "sy", "fx", "fz", "fc")
+    )
     return jax.shard_map(
         on_device,
-        mesh=mesh,
+        mesh=sub_mesh,
         in_specs=(
-            P("section", None, "fsdp", None),
-            P(None, "fsdp", None),
-            P("section", "fsdp", None),
-            P("section", "fsdp"),
+            P(SECTION, None, FSDP, None),
+            P(None, FSDP, None),
+            P(SECTION, FSDP, None),
+            P(SECTION, FSDP),
         ),
-        out_specs=(P("section", "fsdp", None), P("section", None)),
+        out_specs=(P(SECTION, FSDP, None), P(SECTION, None)),
         check_vma=False,
     )

time: 816 us -> 815 us (level)
  local copies, waits for them, and re-layouts: 51.6 us -> 69.2 us
  blocking collectives: 56.8 us -> 43.8 us
    reduce_scatter x0 -> x3, waiting for transfers between devices: none -> 116 us  [the longest x1 74.3 us: on_device(): lax.psum_scatter(terms.reshape(FC, -1, cols), 'fc', scatter_dimension=0,...]
    unnamed x3 -> x5, waiting for transfers between devices: 112 us -> 0.08 us
    transpose x0 -> x3, local copies, waits for them, and re-layouts: none -> 13.6 us  [the longest x2 10.9 us: stage_order(): return rows.reshape(tokens_all, FX, FZ, FC, rows_here).transpose(0, 3, 2,...]
    all_gather x1 -> x2, blocking collectives: 56.8 us -> 43.8 us  [the longest x1 38.5 us: on_device(): gain_sum = jnp.sum(lax.all_gather(gain_acc, FSDP, axis=0), axis=0)]
    all_gather x1 -> x2, waiting for transfers between devices: 73.4 us -> 67.6 us  [the longest x1 48.5 us: on_device(): staged = lax.all_gather(staged, 'fz', axis=0, tiled=True)]
  transfers between devices with their start and end apart: 24 -> 27, of which waited for: 24 -> 26; matrix products, arithmetic and copies ran while one was open for 3% -> 3% of each run, Pallas kernels for 0% -> 0%
where the time goes in v2:
time: 815 us; the launch traced here: 804 us
  waiting for transfers between devices  355 us (44%)
  matrix products  173 us (21%)
  other arithmetic  120 us (15%)
  local copies, waits for them, and re-layouts  69.2 us (8%)
  blocking collectives  43.8 us (5%)
  starting transfers between devices  28.4 us (3%)
  between operations  14 us (2%)
    ppermute x22, waiting for transfers between devices, passed_along(): lax.ppermute(value, axis, [(source, source + steps) for source in range(l...  172 us
    reduce_scatter x1, waiting for transfers between devices, on_device(): lax.psum_scatter(terms.reshape(FC, -1, cols), 'fc', scatter_dimension=0,...  74.3 us
    dot_general x46, matrix products, contract_cols(): lax.dot_general(left, right, (((1,), (1,)), ((), ())), preferred_element_...  72.3 us
    all_gather x1, waiting for transfers between devices, on_device(): staged = lax.all_gather(staged, 'fz', axis=0, tiled=True)  48.5 us
    convert_element_type x22, other arithmetic, tick(): grad_out = (grad_in.astype(jnp.float32) + grad_x).astype(jnp.bfloat16)  42.3 us
    dynamic_update_slice x23, other arithmetic, tick(): grad_store = lax.dynamic_update_index_in_dim(grad_store, grad_in, slot, 0)  41.8 us
    reduce_scatter x1, waiting for transfers between devices, on_device(): lax.psum_scatter(terms.reshape(FZ, -1, cols), 'fz', scatter_dimension=0,...  41.4 us
    dot_general x48, matrix products, contract_rows(): lax.dot_general(left, right, (((0,), (0,)), ((), ())), preferred_element_...  41.2 us
  transfers between devices with their start and end apart: 27, of which 26 were waited for; matrix products, arithmetic and copies ran while one was open for 3% of the time, Pallas kernels for 0%

profile of v2, /device:TPU:1, one launch (start us, length us, event | category | flops | bytes accessed | tf_op | source)
XLA Modules:
  0.0 804.2 jit_solution(14835930300608285806)
XLA Ops:
  13.7 48.5 %all-gather.4.cloned.1.call-done = bf16[2304,512]{1,0:T(8,128)(2,1)} async-done(((bf16[288,512]{1,0:T(8,128)(2,1)}), bf16[2304,512]{1,0:T(8,128)(2,1)}) %all-gather.4.cloned.1.call-update) | async-done | bytes 2359312 | tf_op jit(solution)/shard_map/all_gather | solution.py:69
  70.8 19.1 %all-gather.6.cloned.1.call-done = bf16[4608,512]{1,0:T(8,128)(2,1)} async-done(((bf16[2304,512]{1,0:T(8,128)(2,1)}), bf16[4608,512]{1,0:T(8,128)(2,1)}) %all-gather.6.cloned.1.call-update) | async-done | bytes 4718608 | tf_op jit(solution)/shard_map/all_gather | solution.py:70
  108.4 490.8 %while.25 = (s32[]{:T(128)}, bf16[32,4096]{1,0:T(8,128)(2,1)}, bf16[10,32,4096]{2,1,0:T(8,128)(2,1)}, bf16[10,32,384]{2,1,0:T(8,128)(2,1)}, f32[4096]{0:T(1024)S...) while((s32[]{:T(128)}, bf16[32,4096]{1,0:T(8,128)(2,1)}, ...), condition=%wide.region_7.8_spmd.clone.clone.clone.clone, body=%wide.region_3.7_spmd.clone.clone.clone.clone.sunk | while | flops 137027552 | bytes 10679643 | solution.py:165
  122.3 7.8 collective-permute-done
  144.6 6.9 collective-permute-done
  247.7 6.5 collective-permute-done
  268.8 6.5 collective-permute-done
  289.8 6.5 collective-permute-done
  310.8 6.5 collective-permute-done
  331.9 8.8 %collective-permute-done = bf16[32,4096]{1,0:T(8,128)(2,1)S(1)} collective-permute-done((bf16[32,4096]{1,0:T(8,128)(2,1)}, bf16[32,4096]{1,0:T(8,128)(2,1)S(1)}, u32[]{:S(2)}, u32[]{:S(2)}) %collective-permute-start) | collective-permute-done | bytes 262176 | tf_op jit(solution)/shard_map/while/body/eval_jaxpr/ppermute | solution.py:14
  355.2 8.9 %collective-permute-done = bf16[32,4096]{1,0:T(8,128)(2,1)S(1)} collective-permute-done((bf16[32,4096]{1,0:T(8,128)(2,1)}, bf16[32,4096]{1,0:T(8,128)(2,1)S(1)}, u32[]{:S(2)}, u32[]{:S(2)}) %collective-permute-start) | collective-permute-done | bytes 262176 | tf_op jit(solution)/shard_map/while/body/eval_jaxpr/ppermute | solution.py:14
  378.6 8.9 %collective-permute-done = bf16[32,4096]{1,0:T(8,128)(2,1)S(1)} collective-permute-done((bf16[32,4096]{1,0:T(8,128)(2,1)}, bf16[32,4096]{1,0:T(8,128)(2,1)S(1)}, u32[]{:S(2)}, u32[]{:S(2)}) %collective-permute-start) | collective-permute-done | bytes 262176 | tf_op jit(solution)/shard_map/while/body/eval_jaxpr/ppermute | solution.py:14
  402.1 8.9 %collective-permute-done = bf16[32,4096]{1,0:T(8,128)(2,1)S(1)} collective-permute-done((bf16[32,4096]{1,0:T(8,128)(2,1)}, bf16[32,4096]{1,0:T(8,128)(2,1)S(1)}, u32[]{:S(2)}, u32[]{:S(2)}) %collective-permute-start) | collective-permute-done | bytes 262176 | tf_op jit(solution)/shard_map/while/body/eval_jaxpr/ppermute | solution.py:14
  425.5 9.0 %collective-permute-done = bf16[32,4096]{1,0:T(8,128)(2,1)S(1)} collective-permute-done((bf16[32,4096]{1,0:T(8,128)(2,1)}, bf16[32,4096]{1,0:T(8,128)(2,1)S(1)}, u32[]{:S(2)}, u32[]{:S(2)}) %collective-permute-start) | collective-permute-done | bytes 262176 | tf_op jit(solution)/shard_map/while/body/eval_jaxpr/ppermute | solution.py:14
  449.0 8.7 %collective-permute-done = bf16[32,4096]{1,0:T(8,128)(2,1)S(1)} collective-permute-done((bf16[32,4096]{1,0:T(8,128)(2,1)}, bf16[32,4096]{1,0:T(8,128)(2,1)S(1)}, u32[]{:S(2)}, u32[]{:S(2)}) %collective-permute-start) | collective-permute-done | bytes 262176 | tf_op jit(solution)/shard_map/while/body/eval_jaxpr/ppermute | solution.py:14
  472.1 8.9 %collective-permute-done = bf16[32,4096]{1,0:T(8,128)(2,1)S(1)} collective-permute-done((bf16[32,4096]{1,0:T(8,128)(2,1)}, bf16[32,4096]{1,0:T(8,128)(2,1)S(1)}, u32[]{:S(2)}, u32[]{:S(2)}) %collective-permute-start) | collective-permute-done | bytes 262176 | tf_op jit(solution)/shard_map/while/body/eval_jaxpr/ppermute | solution.py:14
  495.6 8.9 %collective-permute-done = bf16[32,4096]{1,0:T(8,128)(2,1)S(1)} collective-permute-done((bf16[32,4096]{1,0:T(8,128)(2,1)}, bf16[32,4096]{1,0:T(8,128)(2,1)S(1)}, u32[]{:S(2)}, u32[]{:S(2)}) %collective-permute-start) | collective-permute-done | bytes 262176 | tf_op jit(solution)/shard_map/while/body/eval_jaxpr/ppermute | solution.py:14
  518.9 9.0 %collective-permute-done = bf16[32,4096]{1,0:T(8,128)(2,1)S(1)} collective-permute-done((bf16[32,4096]{1,0:T(8,128)(2,1)}, bf16[32,4096]{1,0:T(8,128)(2,1)S(1)}, u32[]{:S(2)}, u32[]{:S(2)}) %collective-permute-start) | collective-permute-done | bytes 262176 | tf_op jit(solution)/shard_map/while/body/eval_jaxpr/ppermute | solution.py:14
  542.4 9.1 %collective-permute-done = bf16[32,4096]{1,0:T(8,128)(2,1)S(1)} collective-permute-done((bf16[32,4096]{1,0:T(8,128)(2,1)}, bf16[32,4096]{1,0:T(8,128)(2,1)S(1)}, u32[]{:S(2)}, u32[]{:S(2)}) %collective-permute-start) | collective-permute-done | bytes 262176 | tf_op jit(solution)/shard_map/while/body/eval_jaxpr/ppermute | solution.py:14
  566.1 8.7 %collective-permute-done = bf16[32,4096]{1,0:T(8,128)(2,1)S(1)} collective-permute-done((bf16[32,4096]{1,0:T(8,128)(2,1)}, bf16[32,4096]{1,0:T(8,128)(2,1)S(1)}, u32[]{:S(2)}, u32[]{:S(2)}) %collective-permute-start) | collective-permute-done | bytes 262176 | tf_op jit(solution)/shard_map/while/body/eval_jaxpr/ppermute | solution.py:14
  589.3 9.2 %collective-permute-done = bf16[32,4096]{1,0:T(8,128)(2,1)S(1)} collective-permute-done((bf16[32,4096]{1,0:T(8,128)(2,1)}, bf16[32,4096]{1,0:T(8,128)(2,1)S(1)}, u32[]{:S(2)}, u32[]{:S(2)}) %collective-permute-start) | collective-permute-done | bytes 262176 | tf_op jit(solution)/shard_map/while/body/eval_jaxpr/ppermute | solution.py:14
  633.8 74.3 %reduce-scatter.4.cloned.1.call-done = bf16[1,2048,512]{1,2,0:T(8,128)(2,1)} async-done(((bf16[2,2048,512]{1,2,0:T(8,128)(2,1)}), bf16[1,2048,512]{1,2,0:T(8,128)(2,1)}) %reduce-scatter.4.cloned.1.call-update) | async-done | bytes 2097168 | tf_op jit(solution)/shard_map/reduce_scatter | solution.py:189
  712.3 41.4 %reduce-scatter.6.cloned.1.call-done = bf16[1,256,512]{2,1,0:T(8,128)(2,1)} async-done(((bf16[8,256,512]{2,1,0:T(8,128)(2,1)}), bf16[1,256,512]{2,1,0:T(8,128)(2,1)}) %reduce-scatter.6.cloned.1.call-update) | async-done | bytes 262160 | tf_op jit(solution)/shard_map/reduce_scatter | solution.py:190
  756.8 38.5 %all-gather = f32[131072]{0:T(1024)S(1)} all-gather(f32[4096]{0:T(1024)S(1)} %select_add_fusion.1), channel_id=2, replica_groups=mesh['sh'=2,'sy'=8,'fx'=2,'fz'=8,'fc'=2] {'fx','fz','fc'}, dimensions={0}, use_global_device_ids=true | all-gather | bytes 540672 | tf_op jit(solution)/shard_map/all_gather | solution.py:193
  (507 shorter events, 419.6 us)
Async XLA Ops:
  7.2 55.1 %all-gather.4.cloned.1.call-start = ((), (), s32[]{:S(2)}) async-start(), calls=%async_computation.3 | async-start | bytes 2654208 | tf_op jit(solution)/shard_map/all_gather | solution.py:69
  13.7 76.2 %all-gather.6.cloned.1.call-start = ((), (), s32[]{:S(2)}) async-start(), calls=%async_computation.4 | async-start | bytes 7077888 | tf_op jit(solution)/shard_map/all_gather | solution.py:70
  62.3 645.9 %reduce-scatter.4.cloned.1.call-start = ((), (), s32[]{:S(2)}) async-start(), calls=%async_computation.5 | async-start | bytes 6291456 | tf_op jit(solution)/shard_map/reduce_scatter | solution.py:189
  120.3 9.8 %collective-permute-start = (bf16[32,4096]{1,0:T(8,128)(2,1)}, bf16[32,4096]{1,0:T(8,128)(2,1)S(1)}, u32[]{:S(2)}, u32[]{:S(2)}) collective-permute-start(bf16[32,4096]{1,0:T(8,128)(2,1)} %fusion.147), channel_id=1, source_target_pairs={{32,0},{64,32},{96,64},{128,96},{160,128},{192,160},{224,192},{256... | collective-permute-start | bytes 786440 | tf_op jit(solution)/shard_map/while/body/eval_jaxpr/ppermute | solution.py:14
  142.6 8.9 %collective-permute-start = (bf16[32,4096]{1,0:T(8,128)(2,1)}, bf16[32,4096]{1,0:T(8,128)(2,1)S(1)}, u32[]{:S(2)}, u32[]{:S(2)}) collective-permute-start(bf16[32,4096]{1,0:T(8,128)(2,1)} %fusion.147), channel_id=1, source_target_pairs={{32,0},{64,32},{96,64},{128,96},{160,128},{192,160},{224,192},{256... | collective-permute-start | bytes 786440 | tf_op jit(solution)/shard_map/while/body/eval_jaxpr/ppermute | solution.py:14
  225.0 8.2 %collective-permute-start = (bf16[32,4096]{1,0:T(8,128)(2,1)}, bf16[32,4096]{1,0:T(8,128)(2,1)S(1)}, u32[]{:S(2)}, u32[]{:S(2)}) collective-permute-start(bf16[32,4096]{1,0:T(8,128)(2,1)} %fusion.147), channel_id=1, source_target_pairs={{32,0},{64,32},{96,64},{128,96},{160,128},{192,160},{224,192},{256... | collective-permute-start | bytes 786440 | tf_op jit(solution)/shard_map/while/body/eval_jaxpr/ppermute | solution.py:14
  245.7 8.5 %collective-permute-start = (bf16[32,4096]{1,0:T(8,128)(2,1)}, bf16[32,4096]{1,0:T(8,128)(2,1)S(1)}, u32[]{:S(2)}, u32[]{:S(2)}) collective-permute-start(bf16[32,4096]{1,0:T(8,128)(2,1)} %fusion.147), channel_id=1, source_target_pairs={{32,0},{64,32},{96,64},{128,96},{160,128},{192,160},{224,192},{256... | collective-permute-start | bytes 786440 | tf_op jit(solution)/shard_map/while/body/eval_jaxpr/ppermute | solution.py:14
  266.8 8.5 %collective-permute-start = (bf16[32,4096]{1,0:T(8,128)(2,1)}, bf16[32,4096]{1,0:T(8,128)(2,1)S(1)}, u32[]{:S(2)}, u32[]{:S(2)}) collective-permute-start(bf16[32,4096]{1,0:T(8,128)(2,1)} %fusion.147), channel_id=1, source_target_pairs={{32,0},{64,32},{96,64},{128,96},{160,128},{192,160},{224,192},{256... | collective-permute-start | bytes 786440 | tf_op jit(solution)/shard_map/while/body/eval_jaxpr/ppermute | solution.py:14
  287.8 8.5 %collective-permute-start = (bf16[32,4096]{1,0:T(8,128)(2,1)}, bf16[32,4096]{1,0:T(8,128)(2,1)S(1)}, u32[]{:S(2)}, u32[]{:S(2)}) collective-permute-start(bf16[32,4096]{1,0:T(8,128)(2,1)} %fusion.147), channel_id=1, source_target_pairs={{32,0},{64,32},{96,64},{128,96},{160,128},{192,160},{224,192},{256... | collective-permute-start | bytes 786440 | tf_op jit(solution)/shard_map/while/body/eval_jaxpr/ppermute | solution.py:14
  308.8 8.5 %collective-permute-start = (bf16[32,4096]{1,0:T(8,128)(2,1)}, bf16[32,4096]{1,0:T(8,128)(2,1)S(1)}, u32[]{:S(2)}, u32[]{:S(2)}) collective-permute-start(bf16[32,4096]{1,0:T(8,128)(2,1)} %fusion.147), channel_id=1, source_target_pairs={{32,0},{64,32},{96,64},{128,96},{160,128},{192,160},{224,192},{256... | collective-permute-start | bytes 786440 | tf_op jit(solution)/shard_map/while/body/eval_jaxpr/ppermute | solution.py:14
  329.9 10.8 %collective-permute-start = (bf16[32,4096]{1,0:T(8,128)(2,1)}, bf16[32,4096]{1,0:T(8,128)(2,1)S(1)}, u32[]{:S(2)}, u32[]{:S(2)}) collective-permute-start(bf16[32,4096]{1,0:T(8,128)(2,1)} %fusion.147), channel_id=1, source_target_pairs={{32,0},{64,32},{96,64},{128,96},{160,128},{192,160},{224,192},{256... | collective-permute-start | bytes 786440 | tf_op jit(solution)/shard_map/while/body/eval_jaxpr/ppermute | solution.py:14
  353.2 10.9 %collective-permute-start = (bf16[32,4096]{1,0:T(8,128)(2,1)}, bf16[32,4096]{1,0:T(8,128)(2,1)S(1)}, u32[]{:S(2)}, u32[]{:S(2)}) collective-permute-start(bf16[32,4096]{1,0:T(8,128)(2,1)} %fusion.147), channel_id=1, source_target_pairs={{32,0},{64,32},{96,64},{128,96},{160,128},{192,160},{224,192},{256... | collective-permute-start | bytes 786440 | tf_op jit(solution)/shard_map/while/body/eval_jaxpr/ppermute | solution.py:14
  376.6 10.9 %collective-permute-start = (bf16[32,4096]{1,0:T(8,128)(2,1)}, bf16[32,4096]{1,0:T(8,128)(2,1)S(1)}, u32[]{:S(2)}, u32[]{:S(2)}) collective-permute-start(bf16[32,4096]{1,0:T(8,128)(2,1)} %fusion.147), channel_id=1, source_target_pairs={{32,0},{64,32},{96,64},{128,96},{160,128},{192,160},{224,192},{256... | collective-permute-start | bytes 786440 | tf_op jit(solution)/shard_map/while/body/eval_jaxpr/ppermute | solution.py:14
  400.0 10.9 %collective-permute-start = (bf16[32,4096]{1,0:T(8,128)(2,1)}, bf16[32,4096]{1,0:T(8,128)(2,1)S(1)}, u32[]{:S(2)}, u32[]{:S(2)}) collective-permute-start(bf16[32,4096]{1,0:T(8,128)(2,1)} %fusion.147), channel_id=1, source_target_pairs={{32,0},{64,32},{96,64},{128,96},{160,128},{192,160},{224,192},{256... | collective-permute-start | bytes 786440 | tf_op jit(solution)/shard_map/while/body/eval_jaxpr/ppermute | solution.py:14
  423.5 11.0 %collective-permute-start = (bf16[32,4096]{1,0:T(8,128)(2,1)}, bf16[32,4096]{1,0:T(8,128)(2,1)S(1)}, u32[]{:S(2)}, u32[]{:S(2)}) collective-permute-start(bf16[32,4096]{1,0:T(8,128)(2,1)} %fusion.147), channel_id=1, source_target_pairs={{32,0},{64,32},{96,64},{128,96},{160,128},{192,160},{224,192},{256... | collective-permute-start | bytes 786440 | tf_op jit(solution)/shard_map/while/body/eval_jaxpr/ppermute | solution.py:14
  447.0 10.7 %collective-permute-start = (bf16[32,4096]{1,0:T(8,128)(2,1)}, bf16[32,4096]{1,0:T(8,128)(2,1)S(1)}, u32[]{:S(2)}, u32[]{:S(2)}) collective-permute-start(bf16[32,4096]{1,0:T(8,128)(2,1)} %fusion.147), channel_id=1, source_target_pairs={{32,0},{64,32},{96,64},{128,96},{160,128},{192,160},{224,192},{256... | collective-permute-start | bytes 786440 | tf_op jit(solution)/shard_map/while/body/eval_jaxpr/ppermute | solution.py:14
  470.2 10.9 %collective-permute-start = (bf16[32,4096]{1,0:T(8,128)(2,1)}, bf16[32,4096]{1,0:T(8,128)(2,1)S(1)}, u32[]{:S(2)}, u32[]{:S(2)}) collective-permute-start(bf16[32,4096]{1,0:T(8,128)(2,1)} %fusion.147), channel_id=1, source_target_pairs={{32,0},{64,32},{96,64},{128,96},{160,128},{192,160},{224,192},{256... | collective-permute-start | bytes 786440 | tf_op jit(solution)/shard_map/while/body/eval_jaxpr/ppermute | solution.py:14
  493.6 10.9 %collective-permute-start = (bf16[32,4096]{1,0:T(8,128)(2,1)}, bf16[32,4096]{1,0:T(8,128)(2,1)S(1)}, u32[]{:S(2)}, u32[]{:S(2)}) collective-permute-start(bf16[32,4096]{1,0:T(8,128)(2,1)} %fusion.147), channel_id=1, source_target_pairs={{32,0},{64,32},{96,64},{128,96},{160,128},{192,160},{224,192},{256... | collective-permute-start | bytes 786440 | tf_op jit(solution)/shard_map/while/body/eval_jaxpr/ppermute | solution.py:14
  516.9 11.0 %collective-permute-start = (bf16[32,4096]{1,0:T(8,128)(2,1)}, bf16[32,4096]{1,0:T(8,128)(2,1)S(1)}, u32[]{:S(2)}, u32[]{:S(2)}) collective-permute-start(bf16[32,4096]{1,0:T(8,128)(2,1)} %fusion.147), channel_id=1, source_target_pairs={{32,0},{64,32},{96,64},{128,96},{160,128},{192,160},{224,192},{256... | collective-permute-start | bytes 786440 | tf_op jit(solution)/shard_map/while/body/eval_jaxpr/ppermute | solution.py:14
  540.4 11.1 %collective-permute-start = (bf16[32,4096]{1,0:T(8,128)(2,1)}, bf16[32,4096]{1,0:T(8,128)(2,1)S(1)}, u32[]{:S(2)}, u32[]{:S(2)}) collective-permute-start(bf16[32,4096]{1,0:T(8,128)(2,1)} %fusion.147), channel_id=1, source_target_pairs={{32,0},{64,32},{96,64},{128,96},{160,128},{192,160},{224,192},{256... | collective-permute-start | bytes 786440 | tf_op jit(solution)/shard_map/while/body/eval_jaxpr/ppermute | solution.py:14
  564.1 10.7 %collective-permute-start = (bf16[32,4096]{1,0:T(8,128)(2,1)}, bf16[32,4096]{1,0:T(8,128)(2,1)S(1)}, u32[]{:S(2)}, u32[]{:S(2)}) collective-permute-start(bf16[32,4096]{1,0:T(8,128)(2,1)} %fusion.147), channel_id=1, source_target_pairs={{32,0},{64,32},{96,64},{128,96},{160,128},{192,160},{224,192},{256... | collective-permute-start | bytes 786440 | tf_op jit(solution)/shard_map/while/body/eval_jaxpr/ppermute | solution.py:14
  587.3 11.2 %collective-permute-start = (bf16[32,4096]{1,0:T(8,128)(2,1)}, bf16[32,4096]{1,0:T(8,128)(2,1)S(1)}, u32[]{:S(2)}, u32[]{:S(2)}) collective-permute-start(bf16[32,4096]{1,0:T(8,128)(2,1)} %fusion.147), channel_id=1, source_target_pairs={{32,0},{64,32},{96,64},{128,96},{160,128},{192,160},{224,192},{256... | collective-permute-start | bytes 786440 | tf_op jit(solution)/shard_map/while/body/eval_jaxpr/ppermute | solution.py:14
  633.8 119.9 %reduce-scatter.6.cloned.1.call-start = ((), (), s32[]{:S(2)}) async-start(), calls=%async_computation.6 | async-start | bytes 2359296 | tf_op jit(solution)/shard_map/reduce_scatter | solution.py:190
  712.1 83.9 %reduce-scatter.8.cloned.1.call-start = ((), (), s32[]{:S(2)}) async-start(), calls=%async_computation.7 | async-start | bytes 393216 | tf_op jit(solution)/shard_map/reduce_scatter | solution.py:191
  (36 other events, 149.8 us)
Sparse Core Ops, SparseCore 0:
  13.8 48.4 all-gather.3
  64.3 25.5 all-gather.5
  633.9 74.1 reduce-scatter.3
  712.2 41.3 reduce-scatter.5
  756.5 22.2 reduce-scatter.7

commit v3 on v2

--- a/solution.py
+++ b/solution.py
@@ -1,6 +1,8 @@
 import jax
 import jax.numpy as jnp
 from jax import lax
+from jax.experimental import pallas as pl
+from jax.experimental.pallas import tpu as pltpu
 from jax.sharding import Mesh, PartitionSpec as P
 
 SECTION = ("sh", "sy")
@@ -50,6 +52,98 @@
     return lax.dot_general(
         left, right, (((1,), (1,)), ((), ())), preferred_element_type=jnp.float32
     )
+
+
+def tick_kernel(
+    scal, recv_ref, up_ref, wb_ref, wp_ref, gain_ref, normed_ref, inv_ref, probs_ref, probs_b_ref,
+    q_ref, k_ref, v_ref, cos_ref, sin_ref, gstore_in, pstore_in, gacc_ref,
+    out_ref, gstore_ref, pstore_ref, gacc_out,
+):
+    head = q_ref.shape[-1]
+    score_scale = head ** (-0.5)
+    grad_in = jnp.where(scal[3] == 1, up_ref[...], recv_ref[...])
+    ga = jnp.dot(grad_in, wb_ref[...], preferred_element_type=jnp.float32).astype(jnp.bfloat16)
+    probs = probs_ref[...]
+    gprob = lax.dot_general(
+        ga, v_ref[...], (((1,), (1,)), ((), ())), preferred_element_type=jnp.float32
+    )
+    gs = (probs * (gprob - jnp.sum(gprob * probs, axis=-1, keepdims=True)) * score_scale).astype(
+        jnp.bfloat16
+    )
+    gq = jnp.dot(gs, k_ref[...], preferred_element_type=jnp.float32)
+    gk = lax.dot_general(gs, q_ref[...], (((0,), (0,)), ((), ())), preferred_element_type=jnp.float32)
+    gv = lax.dot_general(
+        probs_b_ref[...], ga, (((0,), (0,)), ((), ())), preferred_element_type=jnp.float32
+    )
+    cosine = cos_ref[...]
+    sine = sin_ref[...]
+    gq = gq * cosine + pltpu.roll(gq, head // 2, 1) * sine
+    gk = gk * cosine + pltpu.roll(gk, head // 2, 1) * sine
+    gp = jnp.concatenate([gq, gk, gv], axis=-1).astype(jnp.bfloat16)
+    gh = lax.dot_general(gp, wp_ref[...], (((1,), (1,)), ((), ())), preferred_element_type=jnp.float32)
+    normed = normed_ref[...]
+    gain_term = jnp.sum(gh * normed, axis=0, keepdims=True)
+    gn = gh * gain_ref[...]
+    mean = jnp.sum(gn * normed, axis=-1, keepdims=True) * (1.0 / gn.shape[-1])
+    gx = inv_ref[...] * (gn - normed * mean)
+    out_ref[...] = (grad_in.astype(jnp.float32) + gx).astype(out_ref.dtype)
+    gstore_ref[...] = grad_in
+    pstore_ref[...] = gp
+    gacc_out[...] = gacc_ref[...] + jnp.where(scal[2] == 1, gain_term, 0.0)
+
+
+def tick_call(scal, recv, upstream, w_back, w_proj, gain_row, normed, inv_rms, probs, probs_b,
+              query_rows, key_rows, value_rows, cos2, sin2, grad_store, proj_store, gain_acc):
+    micro_count, length, width = normed.shape
+    head = query_rows.shape[-1]
+    full = lambda shape: pl.BlockSpec(shape, lambda i, s: (0,) * len(shape))
+    per_micro = lambda shape: pl.BlockSpec((None,) + shape, lambda i, s: (s[0],) + (0,) * len(shape))
+    per_slot = lambda shape: pl.BlockSpec((None,) + shape, lambda i, s: (s[1],) + (0,) * len(shape))
+    flops = 2 * length * width * 4 * head * 2
+    return pl.pallas_call(
+        tick_kernel,
+        out_shape=(
+            jax.ShapeDtypeStruct((length, width), jnp.bfloat16),
+            jax.ShapeDtypeStruct(grad_store.shape, grad_store.dtype),
+            jax.ShapeDtypeStruct(proj_store.shape, proj_store.dtype),
+            jax.ShapeDtypeStruct(gain_acc.shape, gain_acc.dtype),
+        ),
+        grid_spec=pltpu.PrefetchScalarGridSpec(
+            num_scalar_prefetch=1,
+            grid=(1,),
+            in_specs=[
+                full((length, width)),
+                per_micro((length, width)),
+                full((width, head)),
+                full((width, 3 * head)),
+                full((1, width)),
+                per_micro((length, width)),
+                per_micro((length, 1)),
+                per_micro((length, length)),
+                per_micro((length, length)),
+                per_micro((length, head)),
+                per_micro((length, head)),
+                per_micro((length, head)),
+                full((length, head)),
+                full((length, head)),
+                pl.BlockSpec(memory_space=pl.ANY),
+                pl.BlockSpec(memory_space=pl.ANY),
+                full((1, width)),
+            ],
+            out_specs=[
+                full((length, width)),
+                per_slot((length, width)),
+                per_slot((length, 3 * head)),
+                full((1, width)),
+            ],
+        ),
+        input_output_aliases={15: 1, 16: 2, 17: 3},
+        cost_estimate=pl.CostEstimate(
+            flops=flops, transcendentals=0, bytes_accessed=2 * width * 4 * head + 8 * length * width
+        ),
+        compiler_params=pltpu.CompilerParams(vmem_limit_bytes=48 * 1024 * 1024),
+    )(scal, recv, upstream, w_back, w_proj, gain_row, normed, inv_rms, probs, probs_b,
+      query_rows, key_rows, value_rows, cos2, sin2, grad_store, proj_store, gain_acc)
 
 
 def on_device(inputs, upstream, weights, gain):
@@ -103,52 +197,24 @@
         "mqk,mkh->mqh", probs_b, value_rows, preferred_element_type=jnp.float32
     ).astype(jnp.bfloat16)
 
+    cos2 = jnp.concatenate([cosine, cosine], axis=-1)
+    sin2 = jnp.concatenate([sine_table, -sine_table], axis=-1)
+    gain_row = wide_gain.reshape(1, width)
+
     def tick(tick_no, received, state):
         grad_store, proj_store, gain_acc = state
         micro = tick_no - (sections - 1 - here)
         active = jnp.logical_and(micro >= 0, micro < micro_count)
         clipped = jnp.clip(micro, 0, micro_count - 1)
         slot = jnp.clip(micro, -1, micro_count) + 1
-        top_grad = lax.dynamic_index_in_dim(upstream, clipped, 0, keepdims=False)
-        grad_in = jnp.where(here == sections - 1, top_grad, received)
-        query_m = lax.dynamic_index_in_dim(query_rows, clipped, 0, keepdims=False)
-        keys_m = lax.dynamic_index_in_dim(key_rows, clipped, 0, keepdims=False)
-        values_m = lax.dynamic_index_in_dim(value_rows, clipped, 0, keepdims=False)
-        probs_m = lax.dynamic_index_in_dim(probs, clipped, 0, keepdims=False)
-        probs_bm = lax.dynamic_index_in_dim(probs_b, clipped, 0, keepdims=False)
-        normed_m = lax.dynamic_index_in_dim(normed, clipped, 0, keepdims=False)
-        inv_m = lax.dynamic_index_in_dim(inv_rms, clipped, 0, keepdims=False)
-        attention_gradient = jnp.dot(
-            grad_in, w_back, preferred_element_type=jnp.float32
-        ).astype(jnp.bfloat16)
-        probability_gradient = contract_cols(attention_gradient, values_m)
-        score_gradient = (
-            probs_m
-            * (probability_gradient - jnp.sum(probability_gradient * probs_m, axis=-1, keepdims=True))
-            * score_scale
-        ).astype(jnp.bfloat16)
-        query_gradient = jnp.dot(score_gradient, keys_m, preferred_element_type=jnp.float32)
-        key_gradient = contract_rows(score_gradient, query_m)
-        value_gradient = contract_rows(probs_bm, attention_gradient)
-        grad_proj = jnp.concatenate(
-            [
-                unrotate(query_gradient, cosine, sine_table),
-                unrotate(key_gradient, cosine, sine_table),
-                value_gradient,
-            ],
-            axis=-1,
-        ).astype(jnp.bfloat16)
-        grad_hidden = contract_cols(grad_proj, w_proj)
-        gain_term = jnp.sum(grad_hidden * normed_m, axis=0)
-        grad_normed = grad_hidden * wide_gain
-        grad_x = inv_m * (
-            grad_normed - normed_m * jnp.mean(grad_normed * normed_m, axis=-1, keepdims=True)
+        scal = jnp.stack(
+            [clipped, slot, active.astype(jnp.int32), (here == sections - 1).astype(jnp.int32)]
+        ).astype(jnp.int32)
+        grad_out, grad_store, proj_store, gain_acc = tick_call(
+            scal, received, upstream, w_back, w_proj, gain_row, normed, inv_rms, probs, probs_b,
+            query_rows, key_rows, value_rows, cos2, sin2, grad_store, proj_store, gain_acc.reshape(1, width),
         )
-        grad_out = (grad_in.astype(jnp.float32) + grad_x).astype(jnp.bfloat16)
-        grad_store = lax.dynamic_update_index_in_dim(grad_store, grad_in, slot, 0)
-        proj_store = lax.dynamic_update_index_in_dim(proj_store, grad_proj, slot, 0)
-        gain_acc = gain_acc + jnp.where(active, gain_term, 0.0)
-        return grad_out, (grad_store, proj_store, gain_acc)
+        return grad_out, (grad_store, proj_store, gain_acc.reshape(width))
 
     def step_loop(tick_no, carry):
         received, state = carry

time: 815 us -> 651 us (0.80); the launches traced: 804 us -> 650 us
  matrix products: 173 us -> 4.31 us
  Pallas kernels: 0 us -> 125 us
  other arithmetic: 120 us -> 15.9 us
  local copies, waits for them, and re-layouts: 69.2 us -> 55 us
    dot_general x92 -> x0, matrix products: 127 us -> none  [the longest x46 72.3 us: contract_cols(): lax.dot_general(left, right, (((1,), (1,)), ((), ())), preferred_element_...]
    pallas_call x0 -> x23, Pallas kernels: none -> 125 us  [tick_call(): pl.pallas_call(tick_kernel, out_shape=(jax.ShapeDtypeStruct((length, widt...]
    convert_element_type x45 -> x1, other arithmetic: 59.1 us -> 2.6 us  [on_device(): hidden = (normed * wide_gain).astype(jnp.bfloat16)]
    dynamic_update_slice x23 -> x0, other arithmetic: 41.8 us -> none  [tick(): grad_store = lax.dynamic_update_index_in_dim(grad_store, grad_in, slot, 0)]
    dot_general x48 -> x2, matrix products: 41.2 us -> 1.84 us  [contract_rows(): lax.dot_general(left, right, (((0,), (0,)), ((), ())), preferred_element_...]
    ppermute x22, waiting for transfers between devices: 172 us -> 195 us  [passed_along(): lax.ppermute(value, axis, [(source, source + steps) for source in range(l...]
    while x44 -> x1, local copies, waits for them, and re-layouts: 15.4 us -> 0.13 us  [on_device(): lax.fori_loop(0, total_ticks - 1, step_loop, (jnp.zeros((length, width),...]
    dynamic_update_slice x23 -> x0, local copies, waits for them, and re-layouts: 13.5 us -> none  [tick(): proj_store = lax.dynamic_update_index_in_dim(proj_store, grad_proj, slot, 0)]
where the time goes in v3:
time: 651 us; the launch traced here: 650 us
  waiting for transfers between devices  362 us (56%)
  Pallas kernels  125 us (19%)
  local copies, waits for them, and re-layouts  55 us (8%)
  blocking collectives  44.2 us (7%)
  starting transfers between devices  28.4 us (4%)
  other arithmetic  15.9 us (2%)
  between operations  14 us (2%)
    ppermute x22, waiting for transfers between devices, passed_along(): lax.ppermute(value, axis, [(source, source + steps) for source in range(l...  195 us
    pallas_call x23, Pallas kernels, tick_call(): pl.pallas_call(tick_kernel, out_shape=(jax.ShapeDtypeStruct((length, widt...  125 us
    reduce_scatter x1, waiting for transfers between devices, on_device(): lax.psum_scatter(terms.reshape(FC, -1, cols), 'fc', scatter_dimension=0,...  66.6 us
    all_gather x1, waiting for transfers between devices, on_device(): staged = lax.all_gather(staged, 'fz', axis=0, tiled=True)  48.5 us
    reduce_scatter x1, waiting for transfers between devices, on_device(): lax.psum_scatter(terms.reshape(FZ, -1, cols), 'fz', scatter_dimension=0,...  41.4 us
    all_gather x1, blocking collectives, on_device(): gain_sum = jnp.sum(lax.all_gather(gain_acc, FSDP, axis=0), axis=0)  38.9 us
    ppermute x22, starting transfers between devices, passed_along(): lax.ppermute(value, axis, [(source, source + steps) for source in range(l...  28.2 us
  transfers between devices with their start and end apart: 27, of which 26 were waited for; matrix products, arithmetic and copies ran while one was open for 3% of the time, Pallas kernels for 0%

profile of v3, /device:TPU:1, one launch (start us, length us, event | category | flops | bytes accessed | tf_op | source)
XLA Modules:
  0.0 649.6 jit_solution(1847006412224026132)
XLA Ops:
  13.7 48.5 %all-gather.4.cloned.1.call-done = bf16[2304,512]{1,0:T(8,128)(2,1)} async-done(((bf16[288,512]{1,0:T(8,128)(2,1)}), bf16[2304,512]{1,0:T(8,128)(2,1)}) %all-gather.4.cloned.1.call-update) | async-done | bytes 2359312 | tf_op jit(solution)/shard_map/all_gather | solution.py:163
  68.3 7.2 %copy.29 = f32[256,2,8,2,128]{0,4,1,2,3:T(8,128)} copy(f32[256,2,8,2,128]{4,3,2,1,0:T(2,128)} %reshape.194) | data formatting | bytes 8388608 | tf_op jit(solution)/shard_map/convert_element_type | solution.py:176
  78.9 11.0 %all-gather.6.cloned.1.call-done = bf16[4608,512]{1,0:T(8,128)(2,1)} async-done(((bf16[2304,512]{1,0:T(8,128)(2,1)}), bf16[4608,512]{1,0:T(8,128)(2,1)}) %all-gather.6.cloned.1.call-update) | async-done | bytes 4718608 | tf_op jit(solution)/shard_map/all_gather | solution.py:164
  89.9 9.4 %copy.30 = bf16[2,8,2,144,512]{4,2,1,0,3:T(2,128)(2,1)} copy(bf16[2,8,2,144,512]{4,3,0,1,2:T(8,128)(2,1)} %bitcast.86) | data formatting | bytes 9437184 | tf_op jit(solution)/shard_map/transpose | solution.py:167
  99.3 8.1 %reshape.183 = bf16[32,144,512]{2,0,1:T(8,128)(2,1)} reshape(bf16[2,8,2,144,512]{4,2,1,0,3:T(2,128)(2,1)} %copy.30) | data formatting | bytes 9437184 | tf_op jit(solution)/shard_map/reshape | solution.py:168
  121.8 344.4 %while.21 = (s32[]{:T(128)}, bf16[32,4096]{1,0:T(8,128)(2,1)S(1)}, bf16[10,32,4096]{2,1,0:T(8,128)(2,1)S(1)}, bf16[10,32,384]{2,1,0:T(8,128)(2,1)S(1)}, f32[4096...) while((s32[]{:T(128)}, bf16[32,4096]{1,0:T(8,128)(2,1)S(1)}, ...), condition=%wide.region_4.5_spmd, body=%wide.region_3.4_spmd.sunk | while | flops 268435488 | bytes 6291852 | solution.py:231
  128.7 8.3 %collective-permute-done = bf16[32,4096]{1,0:T(8,128)(2,1)S(1)} collective-permute-done((bf16[32,4096]{1,0:T(8,128)(2,1)S(1)}, bf16[32,4096]{1,0:T(8,128)(2,1)S(1)}, u32[]{:S(2)}, u32[]{:S(2)}) %collective-permute-start) | collective-permute-done | bytes 262176 | tf_op jit(solution)/shard_map/while/body/eval_jaxpr/ppermute | solution.py:16
  143.8 7.4 %collective-permute-done = bf16[32,4096]{1,0:T(8,128)(2,1)S(1)} collective-permute-done((bf16[32,4096]{1,0:T(8,128)(2,1)S(1)}, bf16[32,4096]{1,0:T(8,128)(2,1)S(1)}, u32[]{:S(2)}, u32[]{:S(2)}) %collective-permute-start) | collective-permute-done | bytes 262176 | tf_op jit(solution)/shard_map/while/body/eval_jaxpr/ppermute | solution.py:16
  224.8 7.0 %collective-permute-done = bf16[32,4096]{1,0:T(8,128)(2,1)S(1)} collective-permute-done((bf16[32,4096]{1,0:T(8,128)(2,1)S(1)}, bf16[32,4096]{1,0:T(8,128)(2,1)S(1)}, u32[]{:S(2)}, u32[]{:S(2)}) %collective-permute-start) | collective-permute-done | bytes 262176 | tf_op jit(solution)/shard_map/while/body/eval_jaxpr/ppermute | solution.py:16
  266.3 9.3 %collective-permute-done = bf16[32,4096]{1,0:T(8,128)(2,1)S(1)} collective-permute-done((bf16[32,4096]{1,0:T(8,128)(2,1)S(1)}, bf16[32,4096]{1,0:T(8,128)(2,1)S(1)}, u32[]{:S(2)}, u32[]{:S(2)}) %collective-permute-start) | collective-permute-done | bytes 262176 | tf_op jit(solution)/shard_map/while/body/eval_jaxpr/ppermute | solution.py:16
  282.4 9.4 %collective-permute-done = bf16[32,4096]{1,0:T(8,128)(2,1)S(1)} collective-permute-done((bf16[32,4096]{1,0:T(8,128)(2,1)S(1)}, bf16[32,4096]{1,0:T(8,128)(2,1)S(1)}, u32[]{:S(2)}, u32[]{:S(2)}) %collective-permute-start) | collective-permute-done | bytes 262176 | tf_op jit(solution)/shard_map/while/body/eval_jaxpr/ppermute | solution.py:16
  298.7 9.4 %collective-permute-done = bf16[32,4096]{1,0:T(8,128)(2,1)S(1)} collective-permute-done((bf16[32,4096]{1,0:T(8,128)(2,1)S(1)}, bf16[32,4096]{1,0:T(8,128)(2,1)S(1)}, u32[]{:S(2)}, u32[]{:S(2)}) %collective-permute-start) | collective-permute-done | bytes 262176 | tf_op jit(solution)/shard_map/while/body/eval_jaxpr/ppermute | solution.py:16
  314.9 9.4 %collective-permute-done = bf16[32,4096]{1,0:T(8,128)(2,1)S(1)} collective-permute-done((bf16[32,4096]{1,0:T(8,128)(2,1)S(1)}, bf16[32,4096]{1,0:T(8,128)(2,1)S(1)}, u32[]{:S(2)}, u32[]{:S(2)}) %collective-permute-start) | collective-permute-done | bytes 262176 | tf_op jit(solution)/shard_map/while/body/eval_jaxpr/ppermute | solution.py:16
  331.1 9.4 %collective-permute-done = bf16[32,4096]{1,0:T(8,128)(2,1)S(1)} collective-permute-done((bf16[32,4096]{1,0:T(8,128)(2,1)S(1)}, bf16[32,4096]{1,0:T(8,128)(2,1)S(1)}, u32[]{:S(2)}, u32[]{:S(2)}) %collective-permute-start) | collective-permute-done | bytes 262176 | tf_op jit(solution)/shard_map/while/body/eval_jaxpr/ppermute | solution.py:16
  347.4 10.0 %collective-permute-done = bf16[32,4096]{1,0:T(8,128)(2,1)S(1)} collective-permute-done((bf16[32,4096]{1,0:T(8,128)(2,1)S(1)}, bf16[32,4096]{1,0:T(8,128)(2,1)S(1)}, u32[]{:S(2)}, u32[]{:S(2)}) %collective-permute-start) | collective-permute-done | bytes 262176 | tf_op jit(solution)/shard_map/while/body/eval_jaxpr/ppermute | solution.py:16
  364.2 11.4 %collective-permute-done = bf16[32,4096]{1,0:T(8,128)(2,1)S(1)} collective-permute-done((bf16[32,4096]{1,0:T(8,128)(2,1)S(1)}, bf16[32,4096]{1,0:T(8,128)(2,1)S(1)}, u32[]{:S(2)}, u32[]{:S(2)}) %collective-permute-start) | collective-permute-done | bytes 262176 | tf_op jit(solution)/shard_map/while/body/eval_jaxpr/ppermute | solution.py:16
  382.4 13.2 %collective-permute-done = bf16[32,4096]{1,0:T(8,128)(2,1)S(1)} collective-permute-done((bf16[32,4096]{1,0:T(8,128)(2,1)S(1)}, bf16[32,4096]{1,0:T(8,128)(2,1)S(1)}, u32[]{:S(2)}, u32[]{:S(2)}) %collective-permute-start) | collective-permute-done | bytes 262176 | tf_op jit(solution)/shard_map/while/body/eval_jaxpr/ppermute | solution.py:16
  402.4 12.3 %collective-permute-done = bf16[32,4096]{1,0:T(8,128)(2,1)S(1)} collective-permute-done((bf16[32,4096]{1,0:T(8,128)(2,1)S(1)}, bf16[32,4096]{1,0:T(8,128)(2,1)S(1)}, u32[]{:S(2)}, u32[]{:S(2)}) %collective-permute-start) | collective-permute-done | bytes 262176 | tf_op jit(solution)/shard_map/while/body/eval_jaxpr/ppermute | solution.py:16
  421.5 11.3 %collective-permute-done = bf16[32,4096]{1,0:T(8,128)(2,1)S(1)} collective-permute-done((bf16[32,4096]{1,0:T(8,128)(2,1)S(1)}, bf16[32,4096]{1,0:T(8,128)(2,1)S(1)}, u32[]{:S(2)}, u32[]{:S(2)}) %collective-permute-start) | collective-permute-done | bytes 262176 | tf_op jit(solution)/shard_map/while/body/eval_jaxpr/ppermute | solution.py:16
  439.6 11.2 %collective-permute-done = bf16[32,4096]{1,0:T(8,128)(2,1)S(1)} collective-permute-done((bf16[32,4096]{1,0:T(8,128)(2,1)S(1)}, bf16[32,4096]{1,0:T(8,128)(2,1)S(1)}, u32[]{:S(2)}, u32[]{:S(2)}) %collective-permute-start) | collective-permute-done | bytes 262176 | tf_op jit(solution)/shard_map/while/body/eval_jaxpr/ppermute | solution.py:16
  457.6 8.6 %collective-permute-done = bf16[32,4096]{1,0:T(8,128)(2,1)S(1)} collective-permute-done((bf16[32,4096]{1,0:T(8,128)(2,1)S(1)}, bf16[32,4096]{1,0:T(8,128)(2,1)S(1)}, u32[]{:S(2)}, u32[]{:S(2)}) %collective-permute-start) | collective-permute-done | bytes 262176 | tf_op jit(solution)/shard_map/while/body/eval_jaxpr/ppermute | solution.py:16
  489.5 66.6 %reduce-scatter.4.cloned.1.call-done = bf16[1,2048,512]{1,2,0:T(8,128)(2,1)} async-done(((bf16[2,2048,512]{1,2,0:T(8,128)(2,1)}), bf16[1,2048,512]{1,2,0:T(8,128)(2,1)}) %reduce-scatter.4.cloned.1.call-update) | async-done | bytes 2097168 | tf_op jit(solution)/shard_map/reduce_scatter | solution.py:255
  560.1 41.4 %reduce-scatter.6.cloned.1.call-done = bf16[1,256,512]{2,1,0:T(8,128)(2,1)} async-done(((bf16[8,256,512]{2,1,0:T(8,128)(2,1)}), bf16[1,256,512]{2,1,0:T(8,128)(2,1)}) %reduce-scatter.6.cloned.1.call-update) | async-done | bytes 262160 | tf_op jit(solution)/shard_map/reduce_scatter | solution.py:256
  601.6 38.9 %all-gather = f32[32,1,4096]{2,1,0:T(1,128)S(1)} all-gather(f32[1,1,4096]{2,1,0:T(1,128)} %bitcast.35), channel_id=1, replica_groups=mesh['sh'=2,'sy'=8,'fx'=2,'fz'=8,'fc'=2] {'fx','fz','fc'}, dimensions={0}, use_global_device_ids=true | all-gather | bytes 540672 | tf_op jit(solution)/shard_map/all_gather | solution.py:259
  (139 shorter events, 256.5 us)
Async XLA Ops:
  7.2 55.1 %all-gather.4.cloned.1.call-start = ((), (), s32[]{:S(2)}) async-start(), calls=%async_computation.3 | async-start | bytes 2654208 | tf_op jit(solution)/shard_map/all_gather | solution.py:163
  13.7 76.2 %all-gather.6.cloned.1.call-start = ((), (), s32[]{:S(2)}) async-start(), calls=%async_computation.4 | async-start | bytes 7077888 | tf_op jit(solution)/shard_map/all_gather | solution.py:164
  62.3 493.9 %reduce-scatter.4.cloned.1.call-start = ((), (), s32[]{:S(2)}) async-start(), calls=%async_computation.5 | async-start | bytes 6291456 | tf_op jit(solution)/shard_map/reduce_scatter | solution.py:255
  127.4 9.6 %collective-permute-start = (bf16[32,4096]{1,0:T(8,128)(2,1)S(1)}, bf16[32,4096]{1,0:T(8,128)(2,1)S(1)}, u32[]{:S(2)}, u32[]{:S(2)}) collective-permute-start(bf16[32,4096]{1,0:T(8,128)(2,1)S(1)} %get-tuple-element.643), channel_id=1, source_target_pairs={{32,0},{64,32},{96,64},{128,96},{160,128},{192,160},{224,192},{256... | collective-permute-start | bytes 786440 | tf_op jit(solution)/shard_map/while/body/eval_jaxpr/ppermute | solution.py:16
  142.5 8.7 %collective-permute-start = (bf16[32,4096]{1,0:T(8,128)(2,1)S(1)}, bf16[32,4096]{1,0:T(8,128)(2,1)S(1)}, u32[]{:S(2)}, u32[]{:S(2)}) collective-permute-start(bf16[32,4096]{1,0:T(8,128)(2,1)S(1)} %get-tuple-element.643), channel_id=1, source_target_pairs={{32,0},{64,32},{96,64},{128,96},{160,128},{192,160},{224,192},{256... | collective-permute-start | bytes 786440 | tf_op jit(solution)/shard_map/while/body/eval_jaxpr/ppermute | solution.py:16
  196.1 8.0 %collective-permute-start = (bf16[32,4096]{1,0:T(8,128)(2,1)S(1)}, bf16[32,4096]{1,0:T(8,128)(2,1)S(1)}, u32[]{:S(2)}, u32[]{:S(2)}) collective-permute-start(bf16[32,4096]{1,0:T(8,128)(2,1)S(1)} %get-tuple-element.643), channel_id=1, source_target_pairs={{32,0},{64,32},{96,64},{128,96},{160,128},{192,160},{224,192},{256... | collective-permute-start | bytes 786440 | tf_op jit(solution)/shard_map/while/body/eval_jaxpr/ppermute | solution.py:16
  209.7 8.3 %collective-permute-start = (bf16[32,4096]{1,0:T(8,128)(2,1)S(1)}, bf16[32,4096]{1,0:T(8,128)(2,1)S(1)}, u32[]{:S(2)}, u32[]{:S(2)}) collective-permute-start(bf16[32,4096]{1,0:T(8,128)(2,1)S(1)} %get-tuple-element.643), channel_id=1, source_target_pairs={{32,0},{64,32},{96,64},{128,96},{160,128},{192,160},{224,192},{256... | collective-permute-start | bytes 786440 | tf_op jit(solution)/shard_map/while/body/eval_jaxpr/ppermute | solution.py:16
  223.5 8.3 %collective-permute-start = (bf16[32,4096]{1,0:T(8,128)(2,1)S(1)}, bf16[32,4096]{1,0:T(8,128)(2,1)S(1)}, u32[]{:S(2)}, u32[]{:S(2)}) collective-permute-start(bf16[32,4096]{1,0:T(8,128)(2,1)S(1)} %get-tuple-element.643), channel_id=1, source_target_pairs={{32,0},{64,32},{96,64},{128,96},{160,128},{192,160},{224,192},{256... | collective-permute-start | bytes 786440 | tf_op jit(solution)/shard_map/while/body/eval_jaxpr/ppermute | solution.py:16
  237.4 8.3 %collective-permute-start = (bf16[32,4096]{1,0:T(8,128)(2,1)S(1)}, bf16[32,4096]{1,0:T(8,128)(2,1)S(1)}, u32[]{:S(2)}, u32[]{:S(2)}) collective-permute-start(bf16[32,4096]{1,0:T(8,128)(2,1)S(1)} %get-tuple-element.643), channel_id=1, source_target_pairs={{32,0},{64,32},{96,64},{128,96},{160,128},{192,160},{224,192},{256... | collective-permute-start | bytes 786440 | tf_op jit(solution)/shard_map/while/body/eval_jaxpr/ppermute | solution.py:16
  251.2 8.3 %collective-permute-start = (bf16[32,4096]{1,0:T(8,128)(2,1)S(1)}, bf16[32,4096]{1,0:T(8,128)(2,1)S(1)}, u32[]{:S(2)}, u32[]{:S(2)}) collective-permute-start(bf16[32,4096]{1,0:T(8,128)(2,1)S(1)} %get-tuple-element.643), channel_id=1, source_target_pairs={{32,0},{64,32},{96,64},{128,96},{160,128},{192,160},{224,192},{256... | collective-permute-start | bytes 786440 | tf_op jit(solution)/shard_map/while/body/eval_jaxpr/ppermute | solution.py:16
  265.0 10.6 %collective-permute-start = (bf16[32,4096]{1,0:T(8,128)(2,1)S(1)}, bf16[32,4096]{1,0:T(8,128)(2,1)S(1)}, u32[]{:S(2)}, u32[]{:S(2)}) collective-permute-start(bf16[32,4096]{1,0:T(8,128)(2,1)S(1)} %get-tuple-element.643), channel_id=1, source_target_pairs={{32,0},{64,32},{96,64},{128,96},{160,128},{192,160},{224,192},{256... | collective-permute-start | bytes 786440 | tf_op jit(solution)/shard_map/while/body/eval_jaxpr/ppermute | solution.py:16
  281.1 10.7 %collective-permute-start = (bf16[32,4096]{1,0:T(8,128)(2,1)S(1)}, bf16[32,4096]{1,0:T(8,128)(2,1)S(1)}, u32[]{:S(2)}, u32[]{:S(2)}) collective-permute-start(bf16[32,4096]{1,0:T(8,128)(2,1)S(1)} %get-tuple-element.643), channel_id=1, source_target_pairs={{32,0},{64,32},{96,64},{128,96},{160,128},{192,160},{224,192},{256... | collective-permute-start | bytes 786440 | tf_op jit(solution)/shard_map/while/body/eval_jaxpr/ppermute | solution.py:16
  297.4 10.7 %collective-permute-start = (bf16[32,4096]{1,0:T(8,128)(2,1)S(1)}, bf16[32,4096]{1,0:T(8,128)(2,1)S(1)}, u32[]{:S(2)}, u32[]{:S(2)}) collective-permute-start(bf16[32,4096]{1,0:T(8,128)(2,1)S(1)} %get-tuple-element.643), channel_id=1, source_target_pairs={{32,0},{64,32},{96,64},{128,96},{160,128},{192,160},{224,192},{256... | collective-permute-start | bytes 786440 | tf_op jit(solution)/shard_map/while/body/eval_jaxpr/ppermute | solution.py:16
  313.6 10.7 %collective-permute-start = (bf16[32,4096]{1,0:T(8,128)(2,1)S(1)}, bf16[32,4096]{1,0:T(8,128)(2,1)S(1)}, u32[]{:S(2)}, u32[]{:S(2)}) collective-permute-start(bf16[32,4096]{1,0:T(8,128)(2,1)S(1)} %get-tuple-element.643), channel_id=1, source_target_pairs={{32,0},{64,32},{96,64},{128,96},{160,128},{192,160},{224,192},{256... | collective-permute-start | bytes 786440 | tf_op jit(solution)/shard_map/while/body/eval_jaxpr/ppermute | solution.py:16
  329.8 10.7 %collective-permute-start = (bf16[32,4096]{1,0:T(8,128)(2,1)S(1)}, bf16[32,4096]{1,0:T(8,128)(2,1)S(1)}, u32[]{:S(2)}, u32[]{:S(2)}) collective-permute-start(bf16[32,4096]{1,0:T(8,128)(2,1)S(1)} %get-tuple-element.643), channel_id=1, source_target_pairs={{32,0},{64,32},{96,64},{128,96},{160,128},{192,160},{224,192},{256... | collective-permute-start | bytes 786440 | tf_op jit(solution)/shard_map/while/body/eval_jaxpr/ppermute | solution.py:16
  346.1 11.3 %collective-permute-start = (bf16[32,4096]{1,0:T(8,128)(2,1)S(1)}, bf16[32,4096]{1,0:T(8,128)(2,1)S(1)}, u32[]{:S(2)}, u32[]{:S(2)}) collective-permute-start(bf16[32,4096]{1,0:T(8,128)(2,1)S(1)} %get-tuple-element.643), channel_id=1, source_target_pairs={{32,0},{64,32},{96,64},{128,96},{160,128},{192,160},{224,192},{256... | collective-permute-start | bytes 786440 | tf_op jit(solution)/shard_map/while/body/eval_jaxpr/ppermute | solution.py:16
  362.9 12.7 %collective-permute-start = (bf16[32,4096]{1,0:T(8,128)(2,1)S(1)}, bf16[32,4096]{1,0:T(8,128)(2,1)S(1)}, u32[]{:S(2)}, u32[]{:S(2)}) collective-permute-start(bf16[32,4096]{1,0:T(8,128)(2,1)S(1)} %get-tuple-element.643), channel_id=1, source_target_pairs={{32,0},{64,32},{96,64},{128,96},{160,128},{192,160},{224,192},{256... | collective-permute-start | bytes 786440 | tf_op jit(solution)/shard_map/while/body/eval_jaxpr/ppermute | solution.py:16
  381.1 14.5 %collective-permute-start = (bf16[32,4096]{1,0:T(8,128)(2,1)S(1)}, bf16[32,4096]{1,0:T(8,128)(2,1)S(1)}, u32[]{:S(2)}, u32[]{:S(2)}) collective-permute-start(bf16[32,4096]{1,0:T(8,128)(2,1)S(1)} %get-tuple-element.643), channel_id=1, source_target_pairs={{32,0},{64,32},{96,64},{128,96},{160,128},{192,160},{224,192},{256... | collective-permute-start | bytes 786440 | tf_op jit(solution)/shard_map/while/body/eval_jaxpr/ppermute | solution.py:16
  401.1 13.6 %collective-permute-start = (bf16[32,4096]{1,0:T(8,128)(2,1)S(1)}, bf16[32,4096]{1,0:T(8,128)(2,1)S(1)}, u32[]{:S(2)}, u32[]{:S(2)}) collective-permute-start(bf16[32,4096]{1,0:T(8,128)(2,1)S(1)} %get-tuple-element.643), channel_id=1, source_target_pairs={{32,0},{64,32},{96,64},{128,96},{160,128},{192,160},{224,192},{256... | collective-permute-start | bytes 786440 | tf_op jit(solution)/shard_map/while/body/eval_jaxpr/ppermute | solution.py:16
  420.2 12.6 %collective-permute-start = (bf16[32,4096]{1,0:T(8,128)(2,1)S(1)}, bf16[32,4096]{1,0:T(8,128)(2,1)S(1)}, u32[]{:S(2)}, u32[]{:S(2)}) collective-permute-start(bf16[32,4096]{1,0:T(8,128)(2,1)S(1)} %get-tuple-element.643), channel_id=1, source_target_pairs={{32,0},{64,32},{96,64},{128,96},{160,128},{192,160},{224,192},{256... | collective-permute-start | bytes 786440 | tf_op jit(solution)/shard_map/while/body/eval_jaxpr/ppermute | solution.py:16
  438.3 12.5 %collective-permute-start = (bf16[32,4096]{1,0:T(8,128)(2,1)S(1)}, bf16[32,4096]{1,0:T(8,128)(2,1)S(1)}, u32[]{:S(2)}, u32[]{:S(2)}) collective-permute-start(bf16[32,4096]{1,0:T(8,128)(2,1)S(1)} %get-tuple-element.643), channel_id=1, source_target_pairs={{32,0},{64,32},{96,64},{128,96},{160,128},{192,160},{224,192},{256... | collective-permute-start | bytes 786440 | tf_op jit(solution)/shard_map/while/body/eval_jaxpr/ppermute | solution.py:16
  456.3 9.9 %collective-permute-start = (bf16[32,4096]{1,0:T(8,128)(2,1)S(1)}, bf16[32,4096]{1,0:T(8,128)(2,1)S(1)}, u32[]{:S(2)}, u32[]{:S(2)}) collective-permute-start(bf16[32,4096]{1,0:T(8,128)(2,1)S(1)} %get-tuple-element.643), channel_id=1, source_target_pairs={{32,0},{64,32},{96,64},{128,96},{160,128},{192,160},{224,192},{256... | collective-permute-start | bytes 786440 | tf_op jit(solution)/shard_map/while/body/eval_jaxpr/ppermute | solution.py:16
  489.4 112.1 %reduce-scatter.6.cloned.1.call-start = ((), (), s32[]{:S(2)}) async-start(), calls=%async_computation.6 | async-start | bytes 2359296 | tf_op jit(solution)/shard_map/reduce_scatter | solution.py:256
  560.1 81.4 %reduce-scatter.8.cloned.1.call-start = ((), (), s32[]{:S(2)}) async-start(), calls=%async_computation.7 | async-start | bytes 393216 | tf_op jit(solution)/shard_map/reduce_scatter | solution.py:257
  (10 other events, 95.3 us)
Sparse Core Ops, SparseCore 0:
  13.8 48.4 all-gather.3
  64.3 25.5 all-gather.5
  489.6 66.5 reduce-scatter.3
  560.2 41.2 reduce-scatter.5
  604.4 22.3 reduce-scatter.7

commit v4 on v3

--- a/solution.py
+++ b/solution.py
@@ -253,10 +253,11 @@
     ).astype(jnp.bfloat16)
     cols = terms.shape[1]
     terms = lax.psum_scatter(terms.reshape(FC, -1, cols), "fc", scatter_dimension=0, tiled=True)
+    gain_sum = jnp.sum(lax.all_gather(gain_acc, FSDP, axis=0), axis=0)
+    terms, gain_sum = lax.optimization_barrier((terms, gain_sum))
     terms = lax.psum_scatter(terms.reshape(FZ, -1, cols), "fz", scatter_dimension=0, tiled=True)
     terms = lax.psum_scatter(terms.reshape(FX, -1, cols), "fx", scatter_dimension=0, tiled=True)
     shard = terms.reshape(rows_here, cols).astype(jnp.float32)
-    gain_sum = jnp.sum(lax.all_gather(gain_acc, FSDP, axis=0), axis=0)
     return (shard[None], gain_sum[None])
 
 

time: 651 us -> 646 us (level)
  waiting for transfers between devices: 362 us -> 339 us
  blocking collectives: 44.2 us -> 62.4 us
    reduce_scatter x1, waiting for transfers between devices: 66.6 us -> 8.6 us  [on_device(): lax.psum_scatter(terms.reshape(FC, -1, cols), 'fc', scatter_dimension=0,...]
    reduce_scatter x1, waiting for transfers between devices: 0.01 us -> 24.8 us  [on_device(): lax.psum_scatter(terms.reshape(FX, -1, cols), 'fx', scatter_dimension=0,...]
    all_gather x1, blocking collectives: 38.9 us -> 57 us  [on_device(): gain_sum = jnp.sum(lax.all_gather(gain_acc, FSDP, axis=0), axis=0)]
    reduce_scatter x1, waiting for transfers between devices: 41.4 us -> 51.6 us  [on_device(): lax.psum_scatter(terms.reshape(FZ, -1, cols), 'fz', scatter_dimension=0,...]
  transfers between devices with their start and end apart: 27 -> 27, of which waited for: 26 -> 27; matrix products, arithmetic and copies ran while one was open for 3% -> 3% of each run, Pallas kernels for 0% -> 0%
where the time goes in v4:
time: 646 us; the launch traced here: 645 us
  waiting for transfers between devices  339 us (52%)
  Pallas kernels  125 us (19%)
  blocking collectives  62.4 us (10%)
  local copies, waits for them, and re-layouts  55 us (9%)
  starting transfers between devices  28.4 us (4%)
  other arithmetic  15.9 us (2%)
  between operations  14 us (2%)
    ppermute x22, waiting for transfers between devices, passed_along(): lax.ppermute(value, axis, [(source, source + steps) for source in range(l...  195 us
    pallas_call x23, Pallas kernels, tick_call(): pl.pallas_call(tick_kernel, out_shape=(jax.ShapeDtypeStruct((length, widt...  125 us
    all_gather x1, blocking collectives, on_device(): gain_sum = jnp.sum(lax.all_gather(gain_acc, FSDP, axis=0), axis=0)  57 us
    reduce_scatter x1, waiting for transfers between devices, on_device(): lax.psum_scatter(terms.reshape(FZ, -1, cols), 'fz', scatter_dimension=0,...  51.6 us
    all_gather x1, waiting for transfers between devices, on_device(): staged = lax.all_gather(staged, 'fz', axis=0, tiled=True)  48.5 us
    ppermute x22, starting transfers between devices, passed_along(): lax.ppermute(value, axis, [(source, source + steps) for source in range(l...  28.2 us
    reduce_scatter x1, waiting for transfers between devices, on_device(): lax.psum_scatter(terms.reshape(FX, -1, cols), 'fx', scatter_dimension=0,...  24.8 us
  transfers between devices with their start and end apart: 27, of which 27 were waited for; matrix products, arithmetic and copies ran while one was open for 3% of the time, Pallas kernels for 0%

profile of v4, /device:TPU:1, one launch (start us, length us, event | category | flops | bytes accessed | tf_op | source)
XLA Modules:
  0.0 644.7 jit_solution(9064387064302259701)
XLA Ops:
  13.7 48.5 %all-gather.4.cloned.1.call-done = bf16[2304,512]{1,0:T(8,128)(2,1)} async-done(((bf16[288,512]{1,0:T(8,128)(2,1)}), bf16[2304,512]{1,0:T(8,128)(2,1)}) %all-gather.4.cloned.1.call-update) | async-done | bytes 2359312 | tf_op jit(solution)/shard_map/all_gather | solution.py:163
  68.3 7.2 %copy.29 = f32[256,2,8,2,128]{0,4,1,2,3:T(8,128)} copy(f32[256,2,8,2,128]{4,3,2,1,0:T(2,128)} %reshape.194) | data formatting | bytes 8388608 | tf_op jit(solution)/shard_map/convert_element_type | solution.py:176
  78.9 11.0 %all-gather.6.cloned.1.call-done = bf16[4608,512]{1,0:T(8,128)(2,1)} async-done(((bf16[2304,512]{1,0:T(8,128)(2,1)}), bf16[4608,512]{1,0:T(8,128)(2,1)}) %all-gather.6.cloned.1.call-update) | async-done | bytes 4718608 | tf_op jit(solution)/shard_map/all_gather | solution.py:164
  89.9 9.4 %copy.30 = bf16[2,8,2,144,512]{4,2,1,0,3:T(2,128)(2,1)} copy(bf16[2,8,2,144,512]{4,3,0,1,2:T(8,128)(2,1)} %bitcast.86) | data formatting | bytes 9437184 | tf_op jit(solution)/shard_map/transpose | solution.py:167
  99.3 8.1 %reshape.183 = bf16[32,144,512]{2,0,1:T(8,128)(2,1)} reshape(bf16[2,8,2,144,512]{4,2,1,0,3:T(2,128)(2,1)} %copy.30) | data formatting | bytes 9437184 | tf_op jit(solution)/shard_map/reshape | solution.py:168
  121.8 344.4 %while.21 = (s32[]{:T(128)}, bf16[32,4096]{1,0:T(8,128)(2,1)S(1)}, bf16[10,32,4096]{2,1,0:T(8,128)(2,1)S(1)}, bf16[10,32,384]{2,1,0:T(8,128)(2,1)S(1)}, f32[4096...) while((s32[]{:T(128)}, bf16[32,4096]{1,0:T(8,128)(2,1)S(1)}, ...), condition=%wide.region_4.5_spmd, body=%wide.region_3.4_spmd.sunk | while | flops 268435488 | bytes 6291852 | solution.py:231
  128.7 8.3 %collective-permute-done = bf16[32,4096]{1,0:T(8,128)(2,1)S(1)} collective-permute-done((bf16[32,4096]{1,0:T(8,128)(2,1)S(1)}, bf16[32,4096]{1,0:T(8,128)(2,1)S(1)}, u32[]{:S(2)}, u32[]{:S(2)}) %collective-permute-start) | collective-permute-done | bytes 262176 | tf_op jit(solution)/shard_map/while/body/eval_jaxpr/ppermute | solution.py:16
  143.8 7.4 %collective-permute-done = bf16[32,4096]{1,0:T(8,128)(2,1)S(1)} collective-permute-done((bf16[32,4096]{1,0:T(8,128)(2,1)S(1)}, bf16[32,4096]{1,0:T(8,128)(2,1)S(1)}, u32[]{:S(2)}, u32[]{:S(2)}) %collective-permute-start) | collective-permute-done | bytes 262176 | tf_op jit(solution)/shard_map/while/body/eval_jaxpr/ppermute | solution.py:16
  266.3 9.3 %collective-permute-done = bf16[32,4096]{1,0:T(8,128)(2,1)S(1)} collective-permute-done((bf16[32,4096]{1,0:T(8,128)(2,1)S(1)}, bf16[32,4096]{1,0:T(8,128)(2,1)S(1)}, u32[]{:S(2)}, u32[]{:S(2)}) %collective-permute-start) | collective-permute-done | bytes 262176 | tf_op jit(solution)/shard_map/while/body/eval_jaxpr/ppermute | solution.py:16
  282.4 9.4 %collective-permute-done = bf16[32,4096]{1,0:T(8,128)(2,1)S(1)} collective-permute-done((bf16[32,4096]{1,0:T(8,128)(2,1)S(1)}, bf16[32,4096]{1,0:T(8,128)(2,1)S(1)}, u32[]{:S(2)}, u32[]{:S(2)}) %collective-permute-start) | collective-permute-done | bytes 262176 | tf_op jit(solution)/shard_map/while/body/eval_jaxpr/ppermute | solution.py:16
  298.7 9.4 %collective-permute-done = bf16[32,4096]{1,0:T(8,128)(2,1)S(1)} collective-permute-done((bf16[32,4096]{1,0:T(8,128)(2,1)S(1)}, bf16[32,4096]{1,0:T(8,128)(2,1)S(1)}, u32[]{:S(2)}, u32[]{:S(2)}) %collective-permute-start) | collective-permute-done | bytes 262176 | tf_op jit(solution)/shard_map/while/body/eval_jaxpr/ppermute | solution.py:16
  314.9 9.4 %collective-permute-done = bf16[32,4096]{1,0:T(8,128)(2,1)S(1)} collective-permute-done((bf16[32,4096]{1,0:T(8,128)(2,1)S(1)}, bf16[32,4096]{1,0:T(8,128)(2,1)S(1)}, u32[]{:S(2)}, u32[]{:S(2)}) %collective-permute-start) | collective-permute-done | bytes 262176 | tf_op jit(solution)/shard_map/while/body/eval_jaxpr/ppermute | solution.py:16
  331.1 9.4 %collective-permute-done = bf16[32,4096]{1,0:T(8,128)(2,1)S(1)} collective-permute-done((bf16[32,4096]{1,0:T(8,128)(2,1)S(1)}, bf16[32,4096]{1,0:T(8,128)(2,1)S(1)}, u32[]{:S(2)}, u32[]{:S(2)}) %collective-permute-start) | collective-permute-done | bytes 262176 | tf_op jit(solution)/shard_map/while/body/eval_jaxpr/ppermute | solution.py:16
  347.4 10.0 %collective-permute-done = bf16[32,4096]{1,0:T(8,128)(2,1)S(1)} collective-permute-done((bf16[32,4096]{1,0:T(8,128)(2,1)S(1)}, bf16[32,4096]{1,0:T(8,128)(2,1)S(1)}, u32[]{:S(2)}, u32[]{:S(2)}) %collective-permute-start) | collective-permute-done | bytes 262176 | tf_op jit(solution)/shard_map/while/body/eval_jaxpr/ppermute | solution.py:16
  364.2 11.4 %collective-permute-done = bf16[32,4096]{1,0:T(8,128)(2,1)S(1)} collective-permute-done((bf16[32,4096]{1,0:T(8,128)(2,1)S(1)}, bf16[32,4096]{1,0:T(8,128)(2,1)S(1)}, u32[]{:S(2)}, u32[]{:S(2)}) %collective-permute-start) | collective-permute-done | bytes 262176 | tf_op jit(solution)/shard_map/while/body/eval_jaxpr/ppermute | solution.py:16
  382.4 13.2 %collective-permute-done = bf16[32,4096]{1,0:T(8,128)(2,1)S(1)} collective-permute-done((bf16[32,4096]{1,0:T(8,128)(2,1)S(1)}, bf16[32,4096]{1,0:T(8,128)(2,1)S(1)}, u32[]{:S(2)}, u32[]{:S(2)}) %collective-permute-start) | collective-permute-done | bytes 262176 | tf_op jit(solution)/shard_map/while/body/eval_jaxpr/ppermute | solution.py:16
  402.4 12.3 %collective-permute-done = bf16[32,4096]{1,0:T(8,128)(2,1)S(1)} collective-permute-done((bf16[32,4096]{1,0:T(8,128)(2,1)S(1)}, bf16[32,4096]{1,0:T(8,128)(2,1)S(1)}, u32[]{:S(2)}, u32[]{:S(2)}) %collective-permute-start) | collective-permute-done | bytes 262176 | tf_op jit(solution)/shard_map/while/body/eval_jaxpr/ppermute | solution.py:16
  421.5 11.3 %collective-permute-done = bf16[32,4096]{1,0:T(8,128)(2,1)S(1)} collective-permute-done((bf16[32,4096]{1,0:T(8,128)(2,1)S(1)}, bf16[32,4096]{1,0:T(8,128)(2,1)S(1)}, u32[]{:S(2)}, u32[]{:S(2)}) %collective-permute-start) | collective-permute-done | bytes 262176 | tf_op jit(solution)/shard_map/while/body/eval_jaxpr/ppermute | solution.py:16
  439.6 11.2 %collective-permute-done = bf16[32,4096]{1,0:T(8,128)(2,1)S(1)} collective-permute-done((bf16[32,4096]{1,0:T(8,128)(2,1)S(1)}, bf16[32,4096]{1,0:T(8,128)(2,1)S(1)}, u32[]{:S(2)}, u32[]{:S(2)}) %collective-permute-start) | collective-permute-done | bytes 262176 | tf_op jit(solution)/shard_map/while/body/eval_jaxpr/ppermute | solution.py:16
  457.6 8.6 %collective-permute-done = bf16[32,4096]{1,0:T(8,128)(2,1)S(1)} collective-permute-done((bf16[32,4096]{1,0:T(8,128)(2,1)S(1)}, bf16[32,4096]{1,0:T(8,128)(2,1)S(1)}, u32[]{:S(2)}, u32[]{:S(2)}) %collective-permute-start) | collective-permute-done | bytes 262176 | tf_op jit(solution)/shard_map/while/body/eval_jaxpr/ppermute | solution.py:16
  489.5 57.0 %all-gather = f32[32,1,4096]{2,1,0:T(1,128)S(1)} all-gather(f32[1,1,4096]{2,1,0:T(1,128)} %bitcast.33), channel_id=1, replica_groups=mesh['sh'=2,'sy'=8,'fx'=2,'fz'=8,'fc'=2] {'fx','fz','fc'}, dimensions={0}, use_global_device_ids=true | all-gather | bytes 540672 | tf_op jit(solution)/shard_map/all_gather | solution.py:256
  547.5 8.6 %reduce-scatter.4.cloned.1.call-done = bf16[1,2048,512]{1,2,0:T(8,128)(2,1)} async-done(((bf16[2,2048,512]{1,2,0:T(8,128)(2,1)}), bf16[1,2048,512]{1,2,0:T(8,128)(2,1)}) %reduce-scatter.4.cloned.1.call-update) | async-done | bytes 2097168 | tf_op jit(solution)/shard_map/reduce_scatter | solution.py:255
  560.1 51.6 %reduce-scatter.6.cloned.1.call-done = bf16[1,256,512]{2,1,0:T(8,128)(2,1)} async-done(((bf16[8,256,512]{2,1,0:T(8,128)(2,1)}), bf16[1,256,512]{2,1,0:T(8,128)(2,1)}) %reduce-scatter.6.cloned.1.call-update) | async-done | bytes 262160 | tf_op jit(solution)/shard_map/reduce_scatter | solution.py:258
  611.7 24.8 %reduce-scatter.8.cloned.1.call-done = bf16[1,128,512]{2,1,0:T(8,128)(2,1)} async-done(((bf16[2,128,512]{2,1,0:T(8,128)(2,1)}), bf16[1,128,512]{2,1,0:T(8,128)(2,1)}) %reduce-scatter.8.cloned.1.call-update) | async-done | bytes 131088 | tf_op jit(solution)/shard_map/reduce_scatter | solution.py:259
  (139 shorter events, 263.6 us)
Async XLA Ops:
  7.2 55.1 %all-gather.4.cloned.1.call-start = ((), (), s32[]{:S(2)}) async-start(), calls=%async_computation.3 | async-start | bytes 2654208 | tf_op jit(solution)/shard_map/all_gather | solution.py:163
  13.7 76.2 %all-gather.6.cloned.1.call-start = ((), (), s32[]{:S(2)}) async-start(), calls=%async_computation.4 | async-start | bytes 7077888 | tf_op jit(solution)/shard_map/all_gather | solution.py:164
  62.3 493.9 %reduce-scatter.4.cloned.1.call-start = ((), (), s32[]{:S(2)}) async-start(), calls=%async_computation.5 | async-start | bytes 6291456 | tf_op jit(solution)/shard_map/reduce_scatter | solution.py:255
  127.4 9.6 %collective-permute-start = (bf16[32,4096]{1,0:T(8,128)(2,1)S(1)}, bf16[32,4096]{1,0:T(8,128)(2,1)S(1)}, u32[]{:S(2)}, u32[]{:S(2)}) collective-permute-start(bf16[32,4096]{1,0:T(8,128)(2,1)S(1)} %get-tuple-element.647), channel_id=1, source_target_pairs={{32,0},{64,32},{96,64},{128,96},{160,128},{192,160},{224,192},{256... | collective-permute-start | bytes 786440 | tf_op jit(solution)/shard_map/while/body/eval_jaxpr/ppermute | solution.py:16
  142.5 8.7 %collective-permute-start = (bf16[32,4096]{1,0:T(8,128)(2,1)S(1)}, bf16[32,4096]{1,0:T(8,128)(2,1)S(1)}, u32[]{:S(2)}, u32[]{:S(2)}) collective-permute-start(bf16[32,4096]{1,0:T(8,128)(2,1)S(1)} %get-tuple-element.647), channel_id=1, source_target_pairs={{32,0},{64,32},{96,64},{128,96},{160,128},{192,160},{224,192},{256... | collective-permute-start | bytes 786440 | tf_op jit(solution)/shard_map/while/body/eval_jaxpr/ppermute | solution.py:16
  196.1 8.0 %collective-permute-start = (bf16[32,4096]{1,0:T(8,128)(2,1)S(1)}, bf16[32,4096]{1,0:T(8,128)(2,1)S(1)}, u32[]{:S(2)}, u32[]{:S(2)}) collective-permute-start(bf16[32,4096]{1,0:T(8,128)(2,1)S(1)} %get-tuple-element.647), channel_id=1, source_target_pairs={{32,0},{64,32},{96,64},{128,96},{160,128},{192,160},{224,192},{256... | collective-permute-start | bytes 786440 | tf_op jit(solution)/shard_map/while/body/eval_jaxpr/ppermute | solution.py:16
  209.7 8.3 %collective-permute-start = (bf16[32,4096]{1,0:T(8,128)(2,1)S(1)}, bf16[32,4096]{1,0:T(8,128)(2,1)S(1)}, u32[]{:S(2)}, u32[]{:S(2)}) collective-permute-start(bf16[32,4096]{1,0:T(8,128)(2,1)S(1)} %get-tuple-element.647), channel_id=1, source_target_pairs={{32,0},{64,32},{96,64},{128,96},{160,128},{192,160},{224,192},{256... | collective-permute-start | bytes 786440 | tf_op jit(solution)/shard_map/while/body/eval_jaxpr/ppermute | solution.py:16
  223.5 8.3 %collective-permute-start = (bf16[32,4096]{1,0:T(8,128)(2,1)S(1)}, bf16[32,4096]{1,0:T(8,128)(2,1)S(1)}, u32[]{:S(2)}, u32[]{:S(2)}) collective-permute-start(bf16[32,4096]{1,0:T(8,128)(2,1)S(1)} %get-tuple-element.647), channel_id=1, source_target_pairs={{32,0},{64,32},{96,64},{128,96},{160,128},{192,160},{224,192},{256... | collective-permute-start | bytes 786440 | tf_op jit(solution)/shard_map/while/body/eval_jaxpr/ppermute | solution.py:16
  237.4 8.3 %collective-permute-start = (bf16[32,4096]{1,0:T(8,128)(2,1)S(1)}, bf16[32,4096]{1,0:T(8,128)(2,1)S(1)}, u32[]{:S(2)}, u32[]{:S(2)}) collective-permute-start(bf16[32,4096]{1,0:T(8,128)(2,1)S(1)} %get-tuple-element.647), channel_id=1, source_target_pairs={{32,0},{64,32},{96,64},{128,96},{160,128},{192,160},{224,192},{256... | collective-permute-start | bytes 786440 | tf_op jit(solution)/shard_map/while/body/eval_jaxpr/ppermute | solution.py:16
  251.2 8.3 %collective-permute-start = (bf16[32,4096]{1,0:T(8,128)(2,1)S(1)}, bf16[32,4096]{1,0:T(8,128)(2,1)S(1)}, u32[]{:S(2)}, u32[]{:S(2)}) collective-permute-start(bf16[32,4096]{1,0:T(8,128)(2,1)S(1)} %get-tuple-element.647), channel_id=1, source_target_pairs={{32,0},{64,32},{96,64},{128,96},{160,128},{192,160},{224,192},{256... | collective-permute-start | bytes 786440 | tf_op jit(solution)/shard_map/while/body/eval_jaxpr/ppermute | solution.py:16
  265.0 10.6 %collective-permute-start = (bf16[32,4096]{1,0:T(8,128)(2,1)S(1)}, bf16[32,4096]{1,0:T(8,128)(2,1)S(1)}, u32[]{:S(2)}, u32[]{:S(2)}) collective-permute-start(bf16[32,4096]{1,0:T(8,128)(2,1)S(1)} %get-tuple-element.647), channel_id=1, source_target_pairs={{32,0},{64,32},{96,64},{128,96},{160,128},{192,160},{224,192},{256... | collective-permute-start | bytes 786440 | tf_op jit(solution)/shard_map/while/body/eval_jaxpr/ppermute | solution.py:16
  281.1 10.7 %collective-permute-start = (bf16[32,4096]{1,0:T(8,128)(2,1)S(1)}, bf16[32,4096]{1,0:T(8,128)(2,1)S(1)}, u32[]{:S(2)}, u32[]{:S(2)}) collective-permute-start(bf16[32,4096]{1,0:T(8,128)(2,1)S(1)} %get-tuple-element.647), channel_id=1, source_target_pairs={{32,0},{64,32},{96,64},{128,96},{160,128},{192,160},{224,192},{256... | collective-permute-start | bytes 786440 | tf_op jit(solution)/shard_map/while/body/eval_jaxpr/ppermute | solution.py:16
  297.4 10.7 %collective-permute-start = (bf16[32,4096]{1,0:T(8,128)(2,1)S(1)}, bf16[32,4096]{1,0:T(8,128)(2,1)S(1)}, u32[]{:S(2)}, u32[]{:S(2)}) collective-permute-start(bf16[32,4096]{1,0:T(8,128)(2,1)S(1)} %get-tuple-element.647), channel_id=1, source_target_pairs={{32,0},{64,32},{96,64},{128,96},{160,128},{192,160},{224,192},{256... | collective-permute-start | bytes 786440 | tf_op jit(solution)/shard_map/while/body/eval_jaxpr/ppermute | solution.py:16
  313.6 10.7 %collective-permute-start = (bf16[32,4096]{1,0:T(8,128)(2,1)S(1)}, bf16[32,4096]{1,0:T(8,128)(2,1)S(1)}, u32[]{:S(2)}, u32[]{:S(2)}) collective-permute-start(bf16[32,4096]{1,0:T(8,128)(2,1)S(1)} %get-tuple-element.647), channel_id=1, source_target_pairs={{32,0},{64,32},{96,64},{128,96},{160,128},{192,160},{224,192},{256... | collective-permute-start | bytes 786440 | tf_op jit(solution)/shard_map/while/body/eval_jaxpr/ppermute | solution.py:16
  329.8 10.7 %collective-permute-start = (bf16[32,4096]{1,0:T(8,128)(2,1)S(1)}, bf16[32,4096]{1,0:T(8,128)(2,1)S(1)}, u32[]{:S(2)}, u32[]{:S(2)}) collective-permute-start(bf16[32,4096]{1,0:T(8,128)(2,1)S(1)} %get-tuple-element.647), channel_id=1, source_target_pairs={{32,0},{64,32},{96,64},{128,96},{160,128},{192,160},{224,192},{256... | collective-permute-start | bytes 786440 | tf_op jit(solution)/shard_map/while/body/eval_jaxpr/ppermute | solution.py:16
  346.1 11.3 %collective-permute-start = (bf16[32,4096]{1,0:T(8,128)(2,1)S(1)}, bf16[32,4096]{1,0:T(8,128)(2,1)S(1)}, u32[]{:S(2)}, u32[]{:S(2)}) collective-permute-start(bf16[32,4096]{1,0:T(8,128)(2,1)S(1)} %get-tuple-element.647), channel_id=1, source_target_pairs={{32,0},{64,32},{96,64},{128,96},{160,128},{192,160},{224,192},{256... | collective-permute-start | bytes 786440 | tf_op jit(solution)/shard_map/while/body/eval_jaxpr/ppermute | solution.py:16
  362.9 12.7 %collective-permute-start = (bf16[32,4096]{1,0:T(8,128)(2,1)S(1)}, bf16[32,4096]{1,0:T(8,128)(2,1)S(1)}, u32[]{:S(2)}, u32[]{:S(2)}) collective-permute-start(bf16[32,4096]{1,0:T(8,128)(2,1)S(1)} %get-tuple-element.647), channel_id=1, source_target_pairs={{32,0},{64,32},{96,64},{128,96},{160,128},{192,160},{224,192},{256... | collective-permute-start | bytes 786440 | tf_op jit(solution)/shard_map/while/body/eval_jaxpr/ppermute | solution.py:16
  381.1 14.5 %collective-permute-start = (bf16[32,4096]{1,0:T(8,128)(2,1)S(1)}, bf16[32,4096]{1,0:T(8,128)(2,1)S(1)}, u32[]{:S(2)}, u32[]{:S(2)}) collective-permute-start(bf16[32,4096]{1,0:T(8,128)(2,1)S(1)} %get-tuple-element.647), channel_id=1, source_target_pairs={{32,0},{64,32},{96,64},{128,96},{160,128},{192,160},{224,192},{256... | collective-permute-start | bytes 786440 | tf_op jit(solution)/shard_map/while/body/eval_jaxpr/ppermute | solution.py:16
  401.1 13.6 %collective-permute-start = (bf16[32,4096]{1,0:T(8,128)(2,1)S(1)}, bf16[32,4096]{1,0:T(8,128)(2,1)S(1)}, u32[]{:S(2)}, u32[]{:S(2)}) collective-permute-start(bf16[32,4096]{1,0:T(8,128)(2,1)S(1)} %get-tuple-element.647), channel_id=1, source_target_pairs={{32,0},{64,32},{96,64},{128,96},{160,128},{192,160},{224,192},{256... | collective-permute-start | bytes 786440 | tf_op jit(solution)/shard_map/while/body/eval_jaxpr/ppermute | solution.py:16
  420.2 12.6 %collective-permute-start = (bf16[32,4096]{1,0:T(8,128)(2,1)S(1)}, bf16[32,4096]{1,0:T(8,128)(2,1)S(1)}, u32[]{:S(2)}, u32[]{:S(2)}) collective-permute-start(bf16[32,4096]{1,0:T(8,128)(2,1)S(1)} %get-tuple-element.647), channel_id=1, source_target_pairs={{32,0},{64,32},{96,64},{128,96},{160,128},{192,160},{224,192},{256... | collective-permute-start | bytes 786440 | tf_op jit(solution)/shard_map/while/body/eval_jaxpr/ppermute | solution.py:16
  438.3 12.5 %collective-permute-start = (bf16[32,4096]{1,0:T(8,128)(2,1)S(1)}, bf16[32,4096]{1,0:T(8,128)(2,1)S(1)}, u32[]{:S(2)}, u32[]{:S(2)}) collective-permute-start(bf16[32,4096]{1,0:T(8,128)(2,1)S(1)} %get-tuple-element.647), channel_id=1, source_target_pairs={{32,0},{64,32},{96,64},{128,96},{160,128},{192,160},{224,192},{256... | collective-permute-start | bytes 786440 | tf_op jit(solution)/shard_map/while/body/eval_jaxpr/ppermute | solution.py:16
  456.3 9.9 %collective-permute-start = (bf16[32,4096]{1,0:T(8,128)(2,1)S(1)}, bf16[32,4096]{1,0:T(8,128)(2,1)S(1)}, u32[]{:S(2)}, u32[]{:S(2)}) collective-permute-start(bf16[32,4096]{1,0:T(8,128)(2,1)S(1)} %get-tuple-element.647), channel_id=1, source_target_pairs={{32,0},{64,32},{96,64},{128,96},{160,128},{192,160},{224,192},{256... | collective-permute-start | bytes 786440 | tf_op jit(solution)/shard_map/while/body/eval_jaxpr/ppermute | solution.py:16
  489.4 122.2 %reduce-scatter.6.cloned.1.call-start = ((), (), s32[]{:S(2)}) async-start(), calls=%async_computation.6 | async-start | bytes 2359296 | tf_op jit(solution)/shard_map/reduce_scatter | solution.py:258
  560.1 76.5 %reduce-scatter.8.cloned.1.call-start = ((), (), s32[]{:S(2)}) async-start(), calls=%async_computation.7 | async-start | bytes 393216 | tf_op jit(solution)/shard_map/reduce_scatter | solution.py:259
  (10 other events, 95.3 us)
Sparse Core Ops, SparseCore 0:
  13.8 48.4 all-gather.3
  64.3 25.5 all-gather.5
  489.6 66.5 reduce-scatter.3
  560.2 51.4 reduce-scatter.5
  614.5 21.9 reduce-scatter.7

commit v5 on v4

--- a/solution.py
+++ b/solution.py
@@ -201,12 +201,15 @@
     sin2 = jnp.concatenate([sine_table, -sine_table], axis=-1)
     gain_row = wide_gain.reshape(1, width)
 
-    def tick(tick_no, received, state):
+    pairs = micro_count // 2
+
+    def half_tick(period, stream, received, state):
         grad_store, proj_store, gain_acc = state
-        micro = tick_no - (sections - 1 - here)
-        active = jnp.logical_and(micro >= 0, micro < micro_count)
+        pair = period - (sections - 1 - here)
+        active = jnp.logical_and(pair >= 0, pair < pairs)
+        micro = 2 * pair + stream
         clipped = jnp.clip(micro, 0, micro_count - 1)
-        slot = jnp.clip(micro, -1, micro_count) + 1
+        slot = jnp.where(active, micro + 1, jnp.where(pair < 0, 0, micro_count + 1))
         scal = jnp.stack(
             [clipped, slot, active.astype(jnp.int32), (here == sections - 1).astype(jnp.int32)]
         ).astype(jnp.int32)
@@ -216,22 +219,26 @@
         )
         return grad_out, (grad_store, proj_store, gain_acc.reshape(width))
 
-    def step_loop(tick_no, carry):
-        received, state = carry
-        sent, state = tick(tick_no, received, state)
-        received = passed_along(sent, SECTION, -1)
-        return (received, state)
+    def step_loop(period, carry):
+        received_a, received_b, state = carry
+        sent_a, state = half_tick(period, 0, received_a, state)
+        received_a = passed_along(sent_a, SECTION, -1)
+        sent_b, state = half_tick(period, 1, received_b, state)
+        received_b = passed_along(sent_b, SECTION, -1)
+        return (received_a, received_b, state)
 
     state_start = (
         jnp.zeros((micro_count + 2, length, width), jnp.bfloat16),
         jnp.zeros((micro_count + 2, length, 3 * head), jnp.bfloat16),
         jnp.zeros((width,), jnp.float32),
     )
-    total_ticks = sections + micro_count - 1
-    received, state = lax.fori_loop(
-        0, total_ticks - 1, step_loop, (jnp.zeros((length, width), jnp.bfloat16), state_start)
-    )
-    leftover, state = tick(total_ticks - 1, received, state)
+    total_periods = sections + pairs - 1
+    zero_grad = jnp.zeros((length, width), jnp.bfloat16)
+    received_a, received_b, state = lax.fori_loop(
+        0, total_periods - 1, step_loop, (zero_grad, zero_grad, state_start)
+    )
+    leftover, state = half_tick(total_periods - 1, 0, received_a, state)
+    leftover, state = half_tick(total_periods - 1, 1, received_b, state)
     grad_store, proj_store, gain_acc = state
     tokens_all = micro_count * length
     grad_flat = grad_store[1 : micro_count + 1].reshape(tokens_all, width)

time: 646 us -> 709 us (1.098)
  Pallas kernels: 125 us -> 202 us
  waiting for transfers between devices: 339 us -> 319 us
  starting transfers between devices: 28.4 us -> 46.3 us
  blocking collectives: 62.4 us -> 46.8 us
    pallas_call x23 -> x38, Pallas kernels: 125 us -> 202 us  [tick_call(): pl.pallas_call(tick_kernel, out_shape=(jax.ShapeDtypeStruct((length, widt...]
    ppermute x22 -> x36, waiting for transfers between devices: 195 us -> 172 us  [passed_along(): lax.ppermute(value, axis, [(source, source + steps) for source in range(l...]
    ppermute x22 -> x36, starting transfers between devices: 28.2 us -> 46.1 us  [passed_along(): lax.ppermute(value, axis, [(source, source + steps) for source in range(l...]
    all_gather x1, blocking collectives: 57 us -> 41.5 us  [on_device(): gain_sum = jnp.sum(lax.all_gather(gain_acc, FSDP, axis=0), axis=0)]
  transfers between devices with their start and end apart: 27 -> 41, of which waited for: 27 -> 39; matrix products, arithmetic and copies ran while one was open for 3% -> 2% of each run, Pallas kernels for 0% -> 12%
where the time goes in v5:
time: 709 us; the launch traced here: 707 us
  waiting for transfers between devices  319 us (45%)
  Pallas kernels  202 us (28%)
  local copies, waits for them, and re-layouts  56.3 us (8%)
  blocking collectives  46.8 us (7%)
  starting transfers between devices  46.3 us (7%)
  other arithmetic  16.3 us (2%)
  between operations  13.9 us (2%)
    pallas_call x38, Pallas kernels, tick_call(): pl.pallas_call(tick_kernel, out_shape=(jax.ShapeDtypeStruct((length, widt...  202 us
    ppermute x36, waiting for transfers between devices, passed_along(): lax.ppermute(value, axis, [(source, source + steps) for source in range(l...  172 us
    reduce_scatter x1, waiting for transfers between devices, on_device(): lax.psum_scatter(terms.reshape(FZ, -1, cols), 'fz', scatter_dimension=0,...  51.2 us
    all_gather x1, waiting for transfers between devices, on_device(): staged = lax.all_gather(staged, 'fz', axis=0, tiled=True)  48.5 us
    ppermute x36, starting transfers between devices, passed_along(): lax.ppermute(value, axis, [(source, source + steps) for source in range(l...  46.1 us
    all_gather x1, blocking collectives, on_device(): gain_sum = jnp.sum(lax.all_gather(gain_acc, FSDP, axis=0), axis=0)  41.5 us
    reduce_scatter x1, waiting for transfers between devices, on_device(): lax.psum_scatter(terms.reshape(FX, -1, cols), 'fx', scatter_dimension=0,...  24.9 us
  transfers between devices with their start and end apart: 41, of which 39 were waited for; matrix products, arithmetic and copies ran while one was open for 2% of the time, Pallas kernels for 12%

profile of v5, /device:TPU:1, one launch (start us, length us, event | category | flops | bytes accessed | tf_op | source)
XLA Modules:
  0.0 707.5 jit_solution(7683102168647636413)
XLA Ops:
  13.7 48.5 %all-gather.4.cloned.1.call-done = bf16[2304,512]{1,0:T(8,128)(2,1)} async-done(((bf16[288,512]{1,0:T(8,128)(2,1)}), bf16[2304,512]{1,0:T(8,128)(2,1)}) %all-gather.4.cloned.1.call-update) | async-done | bytes 2359312 | tf_op jit(solution)/shard_map/all_gather | solution.py:163
  68.3 7.2 %copy.36 = f32[256,2,8,2,128]{0,4,1,2,3:T(8,128)} copy(f32[256,2,8,2,128]{4,3,2,1,0:T(2,128)} %reshape.195) | data formatting | bytes 8388608 | tf_op jit(solution)/shard_map/convert_element_type | solution.py:176
  78.9 11.0 %all-gather.6.cloned.1.call-done = bf16[4608,512]{1,0:T(8,128)(2,1)} async-done(((bf16[2304,512]{1,0:T(8,128)(2,1)}), bf16[4608,512]{1,0:T(8,128)(2,1)}) %all-gather.6.cloned.1.call-update) | async-done | bytes 4718608 | tf_op jit(solution)/shard_map/all_gather | solution.py:164
  89.9 9.4 %copy.37 = bf16[2,8,2,144,512]{4,2,1,0,3:T(2,128)(2,1)} copy(bf16[2,8,2,144,512]{4,3,0,1,2:T(8,128)(2,1)} %bitcast.94) | data formatting | bytes 9437184 | tf_op jit(solution)/shard_map/transpose | solution.py:167
  99.3 8.1 %reshape.184 = bf16[32,144,512]{2,0,1:T(8,128)(2,1)} reshape(bf16[2,8,2,144,512]{4,2,1,0,3:T(2,128)(2,1)} %copy.37) | data formatting | bytes 9437184 | tf_op jit(solution)/shard_map/reshape | solution.py:168
  125.2 412.0 %while.23 = (s32[]{:T(128)}, bf16[32,4096]{1,0:T(8,128)(2,1)}, bf16[32,4096]{1,0:T(8,128)(2,1)}, bf16[10,32,4096]{2,1,0:T(8,128)(2,1)S(1)}, bf16[10,32,384]{2,1,...) while((s32[]{:T(128)}, bf16[32,4096]{1,0:T(8,128)(2,1)}, ...), condition=%wide.region_4.5_spmd, body=%wide.region_3.4_spmd.sunk | while | flops 536870912 | bytes 41943672 | solution.py:237
  222.8 7.0 collective-permute-done.1
  243.7 7.7 %collective-permute-done.1 = bf16[32,4096]{1,0:T(8,128)(2,1)} collective-permute-done((bf16[32,4096]{1,0:T(8,128)(2,1)S(1)}, bf16[32,4096]{1,0:T(8,128)(2,1)}, u32[]{:S(2)}, u32[]{:S(2)}) %collective-permute-start.1) | collective-permute-done | bytes 262176 | tf_op jit(solution)/shard_map/while/body/eval_jaxpr/ppermute | solution.py:16
  266.0 7.7 %collective-permute-done.1 = bf16[32,4096]{1,0:T(8,128)(2,1)} collective-permute-done((bf16[32,4096]{1,0:T(8,128)(2,1)S(1)}, bf16[32,4096]{1,0:T(8,128)(2,1)}, u32[]{:S(2)}, u32[]{:S(2)}) %collective-permute-start.1) | collective-permute-done | bytes 262176 | tf_op jit(solution)/shard_map/while/body/eval_jaxpr/ppermute | solution.py:16
  288.2 7.7 %collective-permute-done.1 = bf16[32,4096]{1,0:T(8,128)(2,1)} collective-permute-done((bf16[32,4096]{1,0:T(8,128)(2,1)S(1)}, bf16[32,4096]{1,0:T(8,128)(2,1)}, u32[]{:S(2)}, u32[]{:S(2)}) %collective-permute-start.1) | collective-permute-done | bytes 262176 | tf_op jit(solution)/shard_map/while/body/eval_jaxpr/ppermute | solution.py:16
  310.4 7.7 %collective-permute-done.1 = bf16[32,4096]{1,0:T(8,128)(2,1)} collective-permute-done((bf16[32,4096]{1,0:T(8,128)(2,1)S(1)}, bf16[32,4096]{1,0:T(8,128)(2,1)}, u32[]{:S(2)}, u32[]{:S(2)}) %collective-permute-start.1) | collective-permute-done | bytes 262176 | tf_op jit(solution)/shard_map/while/body/eval_jaxpr/ppermute | solution.py:16
  332.7 7.7 %collective-permute-done.1 = bf16[32,4096]{1,0:T(8,128)(2,1)} collective-permute-done((bf16[32,4096]{1,0:T(8,128)(2,1)S(1)}, bf16[32,4096]{1,0:T(8,128)(2,1)}, u32[]{:S(2)}, u32[]{:S(2)}) %collective-permute-start.1) | collective-permute-done | bytes 262176 | tf_op jit(solution)/shard_map/while/body/eval_jaxpr/ppermute | solution.py:16
  357.0 7.7 %collective-permute-done.1 = bf16[32,4096]{1,0:T(8,128)(2,1)} collective-permute-done((bf16[32,4096]{1,0:T(8,128)(2,1)S(1)}, bf16[32,4096]{1,0:T(8,128)(2,1)}, u32[]{:S(2)}, u32[]{:S(2)}) %collective-permute-start.1) | collective-permute-done | bytes 262176 | tf_op jit(solution)/shard_map/while/body/eval_jaxpr/ppermute | solution.py:16
  381.6 7.7 %collective-permute-done.1 = bf16[32,4096]{1,0:T(8,128)(2,1)} collective-permute-done((bf16[32,4096]{1,0:T(8,128)(2,1)S(1)}, bf16[32,4096]{1,0:T(8,128)(2,1)}, u32[]{:S(2)}, u32[]{:S(2)}) %collective-permute-start.1) | collective-permute-done | bytes 262176 | tf_op jit(solution)/shard_map/while/body/eval_jaxpr/ppermute | solution.py:16
  406.3 7.7 %collective-permute-done.1 = bf16[32,4096]{1,0:T(8,128)(2,1)} collective-permute-done((bf16[32,4096]{1,0:T(8,128)(2,1)S(1)}, bf16[32,4096]{1,0:T(8,128)(2,1)}, u32[]{:S(2)}, u32[]{:S(2)}) %collective-permute-start.1) | collective-permute-done | bytes 262176 | tf_op jit(solution)/shard_map/while/body/eval_jaxpr/ppermute | solution.py:16
  430.9 7.7 %collective-permute-done.1 = bf16[32,4096]{1,0:T(8,128)(2,1)} collective-permute-done((bf16[32,4096]{1,0:T(8,128)(2,1)S(1)}, bf16[32,4096]{1,0:T(8,128)(2,1)}, u32[]{:S(2)}, u32[]{:S(2)}) %collective-permute-start.1) | collective-permute-done | bytes 262176 | tf_op jit(solution)/shard_map/while/body/eval_jaxpr/ppermute | solution.py:16
  455.5 7.7 %collective-permute-done.1 = bf16[32,4096]{1,0:T(8,128)(2,1)} collective-permute-done((bf16[32,4096]{1,0:T(8,128)(2,1)S(1)}, bf16[32,4096]{1,0:T(8,128)(2,1)}, u32[]{:S(2)}, u32[]{:S(2)}) %collective-permute-start.1) | collective-permute-done | bytes 262176 | tf_op jit(solution)/shard_map/while/body/eval_jaxpr/ppermute | solution.py:16
  480.2 7.7 %collective-permute-done.1 = bf16[32,4096]{1,0:T(8,128)(2,1)} collective-permute-done((bf16[32,4096]{1,0:T(8,128)(2,1)S(1)}, bf16[32,4096]{1,0:T(8,128)(2,1)}, u32[]{:S(2)}, u32[]{:S(2)}) %collective-permute-start.1) | collective-permute-done | bytes 262176 | tf_op jit(solution)/shard_map/while/body/eval_jaxpr/ppermute | solution.py:16
  504.8 7.7 %collective-permute-done.1 = bf16[32,4096]{1,0:T(8,128)(2,1)} collective-permute-done((bf16[32,4096]{1,0:T(8,128)(2,1)S(1)}, bf16[32,4096]{1,0:T(8,128)(2,1)}, u32[]{:S(2)}, u32[]{:S(2)}) %collective-permute-start.1) | collective-permute-done | bytes 262176 | tf_op jit(solution)/shard_map/while/body/eval_jaxpr/ppermute | solution.py:16
  529.5 7.7 %collective-permute-done.1 = bf16[32,4096]{1,0:T(8,128)(2,1)} collective-permute-done((bf16[32,4096]{1,0:T(8,128)(2,1)S(1)}, bf16[32,4096]{1,0:T(8,128)(2,1)}, u32[]{:S(2)}, u32[]{:S(2)}) %collective-permute-start.1) | collective-permute-done | bytes 262176 | tf_op jit(solution)/shard_map/while/body/eval_jaxpr/ppermute | solution.py:16
  565.9 41.5 %all-gather = f32[32,1,4096]{2,1,0:T(1,128)S(1)} all-gather(f32[1,1,4096]{2,1,0:T(1,128)} %bitcast.37), channel_id=1, replica_groups=mesh['sh'=2,'sy'=8,'fx'=2,'fz'=8,'fc'=2] {'fx','fz','fc'}, dimensions={0}, use_global_device_ids=true | all-gather | bytes 540672 | tf_op jit(solution)/shard_map/all_gather | solution.py:263
  608.4 10.9 %reduce-scatter.4.cloned.1.call-done = bf16[1,2048,512]{1,2,0:T(8,128)(2,1)} async-done(((bf16[2,2048,512]{1,2,0:T(8,128)(2,1)}), bf16[1,2048,512]{1,2,0:T(8,128)(2,1)}) %reduce-scatter.4.cloned.1.call-update) | async-done | bytes 2097168 | tf_op jit(solution)/shard_map/reduce_scatter | solution.py:262
  623.3 51.2 %reduce-scatter.6.cloned.1.call-done = bf16[1,256,512]{2,1,0:T(8,128)(2,1)} async-done(((bf16[8,256,512]{2,1,0:T(8,128)(2,1)}), bf16[1,256,512]{2,1,0:T(8,128)(2,1)}) %reduce-scatter.6.cloned.1.call-update) | async-done | bytes 262160 | tf_op jit(solution)/shard_map/reduce_scatter | solution.py:265
  674.5 24.9 %reduce-scatter.8.cloned.1.call-done = bf16[1,128,512]{2,1,0:T(8,128)(2,1)} async-done(((bf16[2,128,512]{2,1,0:T(8,128)(2,1)}), bf16[1,128,512]{2,1,0:T(8,128)(2,1)}) %reduce-scatter.8.cloned.1.call-update) | async-done | bytes 131088 | tf_op jit(solution)/shard_map/reduce_scatter | solution.py:266
  (287 shorter events, 372.9 us)
Async XLA Ops:
  7.2 55.1 %all-gather.4.cloned.1.call-start = ((), (), s32[]{:S(2)}) async-start(), calls=%async_computation.3 | async-start | bytes 2654208 | tf_op jit(solution)/shard_map/all_gather | solution.py:163
  13.7 76.2 %all-gather.6.cloned.1.call-start = ((), (), s32[]{:S(2)}) async-start(), calls=%async_computation.4 | async-start | bytes 7077888 | tf_op jit(solution)/shard_map/all_gather | solution.py:164
  62.3 557.0 %reduce-scatter.4.cloned.1.call-start = ((), (), s32[]{:S(2)}) async-start(), calls=%async_computation.5 | async-start | bytes 6291456 | tf_op jit(solution)/shard_map/reduce_scatter | solution.py:262
  137.3 10.3 %collective-permute-start.1 = (bf16[32,4096]{1,0:T(8,128)(2,1)S(1)}, bf16[32,4096]{1,0:T(8,128)(2,1)}, u32[]{:S(2)}, u32[]{:S(2)}) collective-permute-start(bf16[32,4096]{1,0:T(8,128)(2,1)S(1)} %get-tuple-element.726), channel_id=1, source_target_pairs={{32,0},{64,32},{96,64},{128,96},{160,128},{192,160},{224,192},{256... | collective-permute-start | bytes 786440 | tf_op jit(solution)/shard_map/while/body/eval_jaxpr/ppermute | solution.py:16
  263.5 10.2 %collective-permute-start.1 = (bf16[32,4096]{1,0:T(8,128)(2,1)S(1)}, bf16[32,4096]{1,0:T(8,128)(2,1)}, u32[]{:S(2)}, u32[]{:S(2)}) collective-permute-start(bf16[32,4096]{1,0:T(8,128)(2,1)S(1)} %get-tuple-element.726), channel_id=1, source_target_pairs={{32,0},{64,32},{96,64},{128,96},{160,128},{192,160},{224,192},{256... | collective-permute-start | bytes 786440 | tf_op jit(solution)/shard_map/while/body/eval_jaxpr/ppermute | solution.py:16
  285.7 10.2 %collective-permute-start.1 = (bf16[32,4096]{1,0:T(8,128)(2,1)S(1)}, bf16[32,4096]{1,0:T(8,128)(2,1)}, u32[]{:S(2)}, u32[]{:S(2)}) collective-permute-start(bf16[32,4096]{1,0:T(8,128)(2,1)S(1)} %get-tuple-element.726), channel_id=1, source_target_pairs={{32,0},{64,32},{96,64},{128,96},{160,128},{192,160},{224,192},{256... | collective-permute-start | bytes 786440 | tf_op jit(solution)/shard_map/while/body/eval_jaxpr/ppermute | solution.py:16
  346.2 10.8 %collective-permute-start = (bf16[32,4096]{1,0:T(8,128)(2,1)S(1)}, bf16[32,4096]{1,0:T(8,128)(2,1)}, u32[]{:S(2)}, u32[]{:S(2)}) collective-permute-start(bf16[32,4096]{1,0:T(8,128)(2,1)S(1)} %get-tuple-element.721), channel_id=1, source_target_pairs={{32,0},{64,32},{96,64},{128,96},{160,128},{192,160},{224,192},{256... | collective-permute-start | bytes 786440 | tf_op jit(solution)/shard_map/while/body/eval_jaxpr/ppermute | solution.py:16
  352.4 12.3 %collective-permute-start.1 = (bf16[32,4096]{1,0:T(8,128)(2,1)S(1)}, bf16[32,4096]{1,0:T(8,128)(2,1)}, u32[]{:S(2)}, u32[]{:S(2)}) collective-permute-start(bf16[32,4096]{1,0:T(8,128)(2,1)S(1)} %get-tuple-element.726), channel_id=1, source_target_pairs={{32,0},{64,32},{96,64},{128,96},{160,128},{192,160},{224,192},{256... | collective-permute-start | bytes 786440 | tf_op jit(solution)/shard_map/while/body/eval_jaxpr/ppermute | solution.py:16
  370.5 11.1 %collective-permute-start = (bf16[32,4096]{1,0:T(8,128)(2,1)S(1)}, bf16[32,4096]{1,0:T(8,128)(2,1)}, u32[]{:S(2)}, u32[]{:S(2)}) collective-permute-start(bf16[32,4096]{1,0:T(8,128)(2,1)S(1)} %get-tuple-element.721), channel_id=1, source_target_pairs={{32,0},{64,32},{96,64},{128,96},{160,128},{192,160},{224,192},{256... | collective-permute-start | bytes 786440 | tf_op jit(solution)/shard_map/while/body/eval_jaxpr/ppermute | solution.py:16
  376.7 12.6 %collective-permute-start.1 = (bf16[32,4096]{1,0:T(8,128)(2,1)S(1)}, bf16[32,4096]{1,0:T(8,128)(2,1)}, u32[]{:S(2)}, u32[]{:S(2)}) collective-permute-start(bf16[32,4096]{1,0:T(8,128)(2,1)S(1)} %get-tuple-element.726), channel_id=1, source_target_pairs={{32,0},{64,32},{96,64},{128,96},{160,128},{192,160},{224,192},{256... | collective-permute-start | bytes 786440 | tf_op jit(solution)/shard_map/while/body/eval_jaxpr/ppermute | solution.py:16
  395.2 11.1 %collective-permute-start = (bf16[32,4096]{1,0:T(8,128)(2,1)S(1)}, bf16[32,4096]{1,0:T(8,128)(2,1)}, u32[]{:S(2)}, u32[]{:S(2)}) collective-permute-start(bf16[32,4096]{1,0:T(8,128)(2,1)S(1)} %get-tuple-element.721), channel_id=1, source_target_pairs={{32,0},{64,32},{96,64},{128,96},{160,128},{192,160},{224,192},{256... | collective-permute-start | bytes 786440 | tf_op jit(solution)/shard_map/while/body/eval_jaxpr/ppermute | solution.py:16
  401.4 12.6 %collective-permute-start.1 = (bf16[32,4096]{1,0:T(8,128)(2,1)S(1)}, bf16[32,4096]{1,0:T(8,128)(2,1)}, u32[]{:S(2)}, u32[]{:S(2)}) collective-permute-start(bf16[32,4096]{1,0:T(8,128)(2,1)S(1)} %get-tuple-element.726), channel_id=1, source_target_pairs={{32,0},{64,32},{96,64},{128,96},{160,128},{192,160},{224,192},{256... | collective-permute-start | bytes 786440 | tf_op jit(solution)/shard_map/while/body/eval_jaxpr/ppermute | solution.py:16
  419.8 11.1 %collective-permute-start = (bf16[32,4096]{1,0:T(8,128)(2,1)S(1)}, bf16[32,4096]{1,0:T(8,128)(2,1)}, u32[]{:S(2)}, u32[]{:S(2)}) collective-permute-start(bf16[32,4096]{1,0:T(8,128)(2,1)S(1)} %get-tuple-element.721), channel_id=1, source_target_pairs={{32,0},{64,32},{96,64},{128,96},{160,128},{192,160},{224,192},{256... | collective-permute-start | bytes 786440 | tf_op jit(solution)/shard_map/while/body/eval_jaxpr/ppermute | solution.py:16
  426.0 12.6 %collective-permute-start.1 = (bf16[32,4096]{1,0:T(8,128)(2,1)S(1)}, bf16[32,4096]{1,0:T(8,128)(2,1)}, u32[]{:S(2)}, u32[]{:S(2)}) collective-permute-start(bf16[32,4096]{1,0:T(8,128)(2,1)S(1)} %get-tuple-element.726), channel_id=1, source_target_pairs={{32,0},{64,32},{96,64},{128,96},{160,128},{192,160},{224,192},{256... | collective-permute-start | bytes 786440 | tf_op jit(solution)/shard_map/while/body/eval_jaxpr/ppermute | solution.py:16
  444.4 11.1 %collective-permute-start = (bf16[32,4096]{1,0:T(8,128)(2,1)S(1)}, bf16[32,4096]{1,0:T(8,128)(2,1)}, u32[]{:S(2)}, u32[]{:S(2)}) collective-permute-start(bf16[32,4096]{1,0:T(8,128)(2,1)S(1)} %get-tuple-element.721), channel_id=1, source_target_pairs={{32,0},{64,32},{96,64},{128,96},{160,128},{192,160},{224,192},{256... | collective-permute-start | bytes 786440 | tf_op jit(solution)/shard_map/while/body/eval_jaxpr/ppermute | solution.py:16
  450.6 12.6 %collective-permute-start.1 = (bf16[32,4096]{1,0:T(8,128)(2,1)S(1)}, bf16[32,4096]{1,0:T(8,128)(2,1)}, u32[]{:S(2)}, u32[]{:S(2)}) collective-permute-start(bf16[32,4096]{1,0:T(8,128)(2,1)S(1)} %get-tuple-element.726), channel_id=1, source_target_pairs={{32,0},{64,32},{96,64},{128,96},{160,128},{192,160},{224,192},{256... | collective-permute-start | bytes 786440 | tf_op jit(solution)/shard_map/while/body/eval_jaxpr/ppermute | solution.py:16
  469.1 11.1 %collective-permute-start = (bf16[32,4096]{1,0:T(8,128)(2,1)S(1)}, bf16[32,4096]{1,0:T(8,128)(2,1)}, u32[]{:S(2)}, u32[]{:S(2)}) collective-permute-start(bf16[32,4096]{1,0:T(8,128)(2,1)S(1)} %get-tuple-element.721), channel_id=1, source_target_pairs={{32,0},{64,32},{96,64},{128,96},{160,128},{192,160},{224,192},{256... | collective-permute-start | bytes 786440 | tf_op jit(solution)/shard_map/while/body/eval_jaxpr/ppermute | solution.py:16
  475.3 12.6 %collective-permute-start.1 = (bf16[32,4096]{1,0:T(8,128)(2,1)S(1)}, bf16[32,4096]{1,0:T(8,128)(2,1)}, u32[]{:S(2)}, u32[]{:S(2)}) collective-permute-start(bf16[32,4096]{1,0:T(8,128)(2,1)S(1)} %get-tuple-element.726), channel_id=1, source_target_pairs={{32,0},{64,32},{96,64},{128,96},{160,128},{192,160},{224,192},{256... | collective-permute-start | bytes 786440 | tf_op jit(solution)/shard_map/while/body/eval_jaxpr/ppermute | solution.py:16
  493.7 11.1 %collective-permute-start = (bf16[32,4096]{1,0:T(8,128)(2,1)S(1)}, bf16[32,4096]{1,0:T(8,128)(2,1)}, u32[]{:S(2)}, u32[]{:S(2)}) collective-permute-start(bf16[32,4096]{1,0:T(8,128)(2,1)S(1)} %get-tuple-element.721), channel_id=1, source_target_pairs={{32,0},{64,32},{96,64},{128,96},{160,128},{192,160},{224,192},{256... | collective-permute-start | bytes 786440 | tf_op jit(solution)/shard_map/while/body/eval_jaxpr/ppermute | solution.py:16
  499.9 12.6 %collective-permute-start.1 = (bf16[32,4096]{1,0:T(8,128)(2,1)S(1)}, bf16[32,4096]{1,0:T(8,128)(2,1)}, u32[]{:S(2)}, u32[]{:S(2)}) collective-permute-start(bf16[32,4096]{1,0:T(8,128)(2,1)S(1)} %get-tuple-element.726), channel_id=1, source_target_pairs={{32,0},{64,32},{96,64},{128,96},{160,128},{192,160},{224,192},{256... | collective-permute-start | bytes 786440 | tf_op jit(solution)/shard_map/while/body/eval_jaxpr/ppermute | solution.py:16
  518.4 11.1 %collective-permute-start = (bf16[32,4096]{1,0:T(8,128)(2,1)S(1)}, bf16[32,4096]{1,0:T(8,128)(2,1)}, u32[]{:S(2)}, u32[]{:S(2)}) collective-permute-start(bf16[32,4096]{1,0:T(8,128)(2,1)S(1)} %get-tuple-element.721), channel_id=1, source_target_pairs={{32,0},{64,32},{96,64},{128,96},{160,128},{192,160},{224,192},{256... | collective-permute-start | bytes 786440 | tf_op jit(solution)/shard_map/while/body/eval_jaxpr/ppermute | solution.py:16
  524.6 12.6 %collective-permute-start.1 = (bf16[32,4096]{1,0:T(8,128)(2,1)S(1)}, bf16[32,4096]{1,0:T(8,128)(2,1)}, u32[]{:S(2)}, u32[]{:S(2)}) collective-permute-start(bf16[32,4096]{1,0:T(8,128)(2,1)S(1)} %get-tuple-element.726), channel_id=1, source_target_pairs={{32,0},{64,32},{96,64},{128,96},{160,128},{192,160},{224,192},{256... | collective-permute-start | bytes 786440 | tf_op jit(solution)/shard_map/while/body/eval_jaxpr/ppermute | solution.py:16
  565.9 108.6 %reduce-scatter.6.cloned.1.call-start = ((), (), s32[]{:S(2)}) async-start(), calls=%async_computation.6 | async-start | bytes 2359296 | tf_op jit(solution)/shard_map/reduce_scatter | solution.py:265
  623.2 76.1 %reduce-scatter.8.cloned.1.call-start = ((), (), s32[]{:S(2)}) async-start(), calls=%async_computation.7 | async-start | bytes 393216 | tf_op jit(solution)/shard_map/reduce_scatter | solution.py:266
  (78 other events, 614.6 us)
Sparse Core Ops, SparseCore 0:
  13.8 48.4 all-gather.3
  64.3 25.5 all-gather.5
  566.0 53.2 reduce-scatter.3
  623.3 51.0 reduce-scatter.5
  677.3 21.9 reduce-scatter.7

commit v6 on v4

--- a/solution.py
+++ b/solution.py
@@ -80,7 +80,7 @@
     gq = gq * cosine + pltpu.roll(gq, head // 2, 1) * sine
     gk = gk * cosine + pltpu.roll(gk, head // 2, 1) * sine
     gp = jnp.concatenate([gq, gk, gv], axis=-1).astype(jnp.bfloat16)
-    gh = lax.dot_general(gp, wp_ref[...], (((1,), (1,)), ((), ())), preferred_element_type=jnp.float32)
+    gh = jnp.dot(gp, wp_ref[...], preferred_element_type=jnp.float32)
     normed = normed_ref[...]
     gain_term = jnp.sum(gh * normed, axis=0, keepdims=True)
     gn = gh * gain_ref[...]
@@ -115,7 +115,7 @@
                 full((length, width)),
                 per_micro((length, width)),
                 full((width, head)),
-                full((width, 3 * head)),
+                full((3 * head, width)),
                 full((1, width)),
                 per_micro((length, width)),
                 per_micro((length, 1)),
@@ -200,6 +200,7 @@
     cos2 = jnp.concatenate([cosine, cosine], axis=-1)
     sin2 = jnp.concatenate([sine_table, -sine_table], axis=-1)
     gain_row = wide_gain.reshape(1, width)
+    w_proj_t = w_proj.T
 
     def tick(tick_no, received, state):
         grad_store, proj_store, gain_acc = state
@@ -211,7 +212,7 @@
             [clipped, slot, active.astype(jnp.int32), (here == sections - 1).astype(jnp.int32)]
         ).astype(jnp.int32)
         grad_out, grad_store, proj_store, gain_acc = tick_call(
-            scal, received, upstream, w_back, w_proj, gain_row, normed, inv_rms, probs, probs_b,
+            scal, received, upstream, w_back, w_proj_t, gain_row, normed, inv_rms, probs, probs_b,
             query_rows, key_rows, value_rows, cos2, sin2, grad_store, proj_store, gain_acc.reshape(1, width),
         )
         return grad_out, (grad_store, proj_store, gain_acc.reshape(width))

time: 646 us -> 654 us (1.012)
  local copies, waits for them, and re-layouts: 55 us -> 70.8 us
  Pallas kernels: 125 us -> 117 us
    slice x3 -> x2, local copies, waits for them, and re-layouts: 4.58 us -> 13.8 us  [on_device(): gathered[:, :rows_here, :].reshape(groups * rows_here, weights.shape[2])]
    pallas_call x23, Pallas kernels: 125 us -> 117 us  [tick_call(): pl.pallas_call(tick_kernel, out_shape=(jax.ShapeDtypeStruct((length, widt...]
where the time goes in v6:
time: 654 us; the launch traced here: 653 us
  waiting for transfers between devices  339 us (52%)
  Pallas kernels  117 us (18%)
  local copies, waits for them, and re-layouts  70.8 us (11%)
  blocking collectives  63.8 us (10%)
  starting transfers between devices  28.4 us (4%)
  other arithmetic  15.9 us (2%)
  between operations  14 us (2%)
    ppermute x22, waiting for transfers between devices, passed_along(): lax.ppermute(value, axis, [(source, source + steps) for source in range(l...  194 us
    pallas_call x23, Pallas kernels, tick_call(): pl.pallas_call(tick_kernel, out_shape=(jax.ShapeDtypeStruct((length, widt...  117 us
    all_gather x1, blocking collectives, on_device(): gain_sum = jnp.sum(lax.all_gather(gain_acc, FSDP, axis=0), axis=0)  58.5 us
    reduce_scatter x1, waiting for transfers between devices, on_device(): lax.psum_scatter(terms.reshape(FZ, -1, cols), 'fz', scatter_dimension=0,...  51.5 us
    all_gather x1, waiting for transfers between devices, on_device(): staged = lax.all_gather(staged, 'fz', axis=0, tiled=True)  48.5 us
    ppermute x22, starting transfers between devices, passed_along(): lax.ppermute(value, axis, [(source, source + steps) for source in range(l...  28.2 us
    reduce_scatter x1, waiting for transfers between devices, on_device(): lax.psum_scatter(terms.reshape(FX, -1, cols), 'fx', scatter_dimension=0,...  24.9 us
    slice x2, local copies, waits for them, and re-layouts, on_device(): gathered[:, :rows_here, :].reshape(groups * rows_here, weights.shape[2])  13.8 us
  transfers between devices with their start and end apart: 27, of which 27 were waited for; matrix products, arithmetic and copies ran while one was open for 3% of the time, Pallas kernels for 0%

profile of v6, /device:TPU:1, one launch (start us, length us, event | category | flops | bytes accessed | tf_op | source)
XLA Modules:
  0.0 652.8 jit_solution(3809871413385824621)
XLA Ops:
  13.7 48.5 %all-gather.4.cloned.1.call-done = bf16[2304,512]{1,0:T(8,128)(2,1)} async-done(((bf16[288,512]{1,0:T(8,128)(2,1)}), bf16[2304,512]{1,0:T(8,128)(2,1)}) %all-gather.4.cloned.1.call-update) | async-done | bytes 2359312 | tf_op jit(solution)/shard_map/all_gather | solution.py:163
  78.9 11.0 %all-gather.6.cloned.1.call-done = bf16[4608,512]{1,0:T(8,128)(2,1)} async-done(((bf16[2304,512]{1,0:T(8,128)(2,1)}), bf16[4608,512]{1,0:T(8,128)(2,1)}) %all-gather.6.cloned.1.call-update) | async-done | bytes 4718608 | tf_op jit(solution)/shard_map/all_gather | solution.py:164
  89.9 9.4 %copy.36 = bf16[2,8,2,144,512]{4,2,1,0,3:T(2,128)(2,1)} copy(bf16[2,8,2,144,512]{4,3,0,1,2:T(8,128)(2,1)} %bitcast.94) | data formatting | bytes 9437184 | tf_op jit(solution)/shard_map/transpose | solution.py:167
  99.3 8.1 %reshape.183 = bf16[32,144,512]{2,0,1:T(8,128)(2,1)} reshape(bf16[2,8,2,144,512]{4,2,1,0,3:T(2,128)(2,1)} %copy.36) | data formatting | bytes 9437184 | tf_op jit(solution)/shard_map/reshape | solution.py:168
  112.8 9.1 %copy.38 = bf16[32,128,512]{1,0,2:T(8,128)(2,1)} copy(bf16[32,128,512]{2,0,1:T(8,128)(2,1)} %slice.52) | data formatting | bytes 8388608 | tf_op jit(solution)/shard_map/slice | solution.py:170
  137.5 335.7 %while.21 = (s32[]{:T(128)}, bf16[32,4096]{1,0:T(8,128)(2,1)S(1)}, bf16[10,32,4096]{2,1,0:T(8,128)(2,1)S(1)}, bf16[10,32,384]{2,1,0:T(8,128)(2,1)S(1)}, f32[4096...) while((s32[]{:T(128)}, bf16[32,4096]{1,0:T(8,128)(2,1)S(1)}, ...), condition=%wide.region_4.5_spmd, body=%wide.region_3.4_spmd.sunk | while | flops 268435488 | bytes 6291852 | solution.py:232
  144.0 8.3 %collective-permute-done = bf16[32,4096]{1,0:T(8,128)(2,1)S(1)} collective-permute-done((bf16[32,4096]{1,0:T(8,128)(2,1)S(1)}, bf16[32,4096]{1,0:T(8,128)(2,1)S(1)}, u32[]{:S(2)}, u32[]{:S(2)}) %collective-permute-start) | collective-permute-done | bytes 262176 | tf_op jit(solution)/shard_map/while/body/eval_jaxpr/ppermute | solution.py:16
  158.7 7.4 %collective-permute-done = bf16[32,4096]{1,0:T(8,128)(2,1)S(1)} collective-permute-done((bf16[32,4096]{1,0:T(8,128)(2,1)S(1)}, bf16[32,4096]{1,0:T(8,128)(2,1)S(1)}, u32[]{:S(2)}, u32[]{:S(2)}) %collective-permute-start) | collective-permute-done | bytes 262176 | tf_op jit(solution)/shard_map/while/body/eval_jaxpr/ppermute | solution.py:16
  277.9 9.3 %collective-permute-done = bf16[32,4096]{1,0:T(8,128)(2,1)S(1)} collective-permute-done((bf16[32,4096]{1,0:T(8,128)(2,1)S(1)}, bf16[32,4096]{1,0:T(8,128)(2,1)S(1)}, u32[]{:S(2)}, u32[]{:S(2)}) %collective-permute-start) | collective-permute-done | bytes 262176 | tf_op jit(solution)/shard_map/while/body/eval_jaxpr/ppermute | solution.py:16
  293.7 9.4 %collective-permute-done = bf16[32,4096]{1,0:T(8,128)(2,1)S(1)} collective-permute-done((bf16[32,4096]{1,0:T(8,128)(2,1)S(1)}, bf16[32,4096]{1,0:T(8,128)(2,1)S(1)}, u32[]{:S(2)}, u32[]{:S(2)}) %collective-permute-start) | collective-permute-done | bytes 262176 | tf_op jit(solution)/shard_map/while/body/eval_jaxpr/ppermute | solution.py:16
  309.5 9.4 %collective-permute-done = bf16[32,4096]{1,0:T(8,128)(2,1)S(1)} collective-permute-done((bf16[32,4096]{1,0:T(8,128)(2,1)S(1)}, bf16[32,4096]{1,0:T(8,128)(2,1)S(1)}, u32[]{:S(2)}, u32[]{:S(2)}) %collective-permute-start) | collective-permute-done | bytes 262176 | tf_op jit(solution)/shard_map/while/body/eval_jaxpr/ppermute | solution.py:16
  325.4 9.4 %collective-permute-done = bf16[32,4096]{1,0:T(8,128)(2,1)S(1)} collective-permute-done((bf16[32,4096]{1,0:T(8,128)(2,1)S(1)}, bf16[32,4096]{1,0:T(8,128)(2,1)S(1)}, u32[]{:S(2)}, u32[]{:S(2)}) %collective-permute-start) | collective-permute-done | bytes 262176 | tf_op jit(solution)/shard_map/while/body/eval_jaxpr/ppermute | solution.py:16
  341.3 9.4 %collective-permute-done = bf16[32,4096]{1,0:T(8,128)(2,1)S(1)} collective-permute-done((bf16[32,4096]{1,0:T(8,128)(2,1)S(1)}, bf16[32,4096]{1,0:T(8,128)(2,1)S(1)}, u32[]{:S(2)}, u32[]{:S(2)}) %collective-permute-start) | collective-permute-done | bytes 262176 | tf_op jit(solution)/shard_map/while/body/eval_jaxpr/ppermute | solution.py:16
  357.1 10.4 %collective-permute-done = bf16[32,4096]{1,0:T(8,128)(2,1)S(1)} collective-permute-done((bf16[32,4096]{1,0:T(8,128)(2,1)S(1)}, bf16[32,4096]{1,0:T(8,128)(2,1)S(1)}, u32[]{:S(2)}, u32[]{:S(2)}) %collective-permute-start) | collective-permute-done | bytes 262176 | tf_op jit(solution)/shard_map/while/body/eval_jaxpr/ppermute | solution.py:16
  373.9 11.9 %collective-permute-done = bf16[32,4096]{1,0:T(8,128)(2,1)S(1)} collective-permute-done((bf16[32,4096]{1,0:T(8,128)(2,1)S(1)}, bf16[32,4096]{1,0:T(8,128)(2,1)S(1)}, u32[]{:S(2)}, u32[]{:S(2)}) %collective-permute-start) | collective-permute-done | bytes 262176 | tf_op jit(solution)/shard_map/while/body/eval_jaxpr/ppermute | solution.py:16
  392.3 13.0 %collective-permute-done = bf16[32,4096]{1,0:T(8,128)(2,1)S(1)} collective-permute-done((bf16[32,4096]{1,0:T(8,128)(2,1)S(1)}, bf16[32,4096]{1,0:T(8,128)(2,1)S(1)}, u32[]{:S(2)}, u32[]{:S(2)}) %collective-permute-start) | collective-permute-done | bytes 262176 | tf_op jit(solution)/shard_map/while/body/eval_jaxpr/ppermute | solution.py:16
  411.7 12.1 %collective-permute-done = bf16[32,4096]{1,0:T(8,128)(2,1)S(1)} collective-permute-done((bf16[32,4096]{1,0:T(8,128)(2,1)S(1)}, bf16[32,4096]{1,0:T(8,128)(2,1)S(1)}, u32[]{:S(2)}, u32[]{:S(2)}) %collective-permute-start) | collective-permute-done | bytes 262176 | tf_op jit(solution)/shard_map/while/body/eval_jaxpr/ppermute | solution.py:16
  430.3 12.0 %collective-permute-done = bf16[32,4096]{1,0:T(8,128)(2,1)S(1)} collective-permute-done((bf16[32,4096]{1,0:T(8,128)(2,1)S(1)}, bf16[32,4096]{1,0:T(8,128)(2,1)S(1)}, u32[]{:S(2)}, u32[]{:S(2)}) %collective-permute-start) | collective-permute-done | bytes 262176 | tf_op jit(solution)/shard_map/while/body/eval_jaxpr/ppermute | solution.py:16
  448.8 9.2 %collective-permute-done = bf16[32,4096]{1,0:T(8,128)(2,1)S(1)} collective-permute-done((bf16[32,4096]{1,0:T(8,128)(2,1)S(1)}, bf16[32,4096]{1,0:T(8,128)(2,1)S(1)}, u32[]{:S(2)}, u32[]{:S(2)}) %collective-permute-start) | collective-permute-done | bytes 262176 | tf_op jit(solution)/shard_map/while/body/eval_jaxpr/ppermute | solution.py:16
  464.4 8.8 %collective-permute-done = bf16[32,4096]{1,0:T(8,128)(2,1)S(1)} collective-permute-done((bf16[32,4096]{1,0:T(8,128)(2,1)S(1)}, bf16[32,4096]{1,0:T(8,128)(2,1)S(1)}, u32[]{:S(2)}, u32[]{:S(2)}) %collective-permute-start) | collective-permute-done | bytes 262176 | tf_op jit(solution)/shard_map/while/body/eval_jaxpr/ppermute | solution.py:16
  496.1 58.5 %all-gather = f32[32,1,4096]{2,1,0:T(1,128)S(1)} all-gather(f32[1,1,4096]{2,1,0:T(1,128)} %bitcast.33), channel_id=1, replica_groups=mesh['sh'=2,'sy'=8,'fx'=2,'fz'=8,'fc'=2] {'fx','fz','fc'}, dimensions={0}, use_global_device_ids=true | all-gather | bytes 540672 | tf_op jit(solution)/shard_map/all_gather | solution.py:257
  555.6 8.6 %reduce-scatter.4.cloned.1.call-done = bf16[1,2048,512]{1,2,0:T(8,128)(2,1)} async-done(((bf16[2,2048,512]{1,2,0:T(8,128)(2,1)}), bf16[1,2048,512]{1,2,0:T(8,128)(2,1)}) %reduce-scatter.4.cloned.1.call-update) | async-done | bytes 2097168 | tf_op jit(solution)/shard_map/reduce_scatter | solution.py:256
  568.2 51.5 %reduce-scatter.6.cloned.1.call-done = bf16[1,256,512]{2,1,0:T(8,128)(2,1)} async-done(((bf16[8,256,512]{2,1,0:T(8,128)(2,1)}), bf16[1,256,512]{2,1,0:T(8,128)(2,1)}) %reduce-scatter.6.cloned.1.call-update) | async-done | bytes 262160 | tf_op jit(solution)/shard_map/reduce_scatter | solution.py:259
  619.7 24.9 %reduce-scatter.8.cloned.1.call-done = bf16[1,128,512]{2,1,0:T(8,128)(2,1)} async-done(((bf16[2,128,512]{2,1,0:T(8,128)(2,1)}), bf16[1,128,512]{2,1,0:T(8,128)(2,1)}) %reduce-scatter.8.cloned.1.call-update) | async-done | bytes 131088 | tf_op jit(solution)/shard_map/reduce_scatter | solution.py:260
  (140 shorter events, 268.8 us)
Async XLA Ops:
  7.2 55.1 %all-gather.4.cloned.1.call-start = ((), (), s32[]{:S(2)}) async-start(), calls=%async_computation.3 | async-start | bytes 2654208 | tf_op jit(solution)/shard_map/all_gather | solution.py:163
  13.7 76.2 %all-gather.6.cloned.1.call-start = ((), (), s32[]{:S(2)}) async-start(), calls=%async_computation.4 | async-start | bytes 7077888 | tf_op jit(solution)/shard_map/all_gather | solution.py:164
  62.3 501.9 %reduce-scatter.4.cloned.1.call-start = ((), (), s32[]{:S(2)}) async-start(), calls=%async_computation.5 | async-start | bytes 6291456 | tf_op jit(solution)/shard_map/reduce_scatter | solution.py:256
  142.7 9.6 %collective-permute-start = (bf16[32,4096]{1,0:T(8,128)(2,1)S(1)}, bf16[32,4096]{1,0:T(8,128)(2,1)S(1)}, u32[]{:S(2)}, u32[]{:S(2)}) collective-permute-start(bf16[32,4096]{1,0:T(8,128)(2,1)S(1)} %get-tuple-element.667), channel_id=1, source_target_pairs={{32,0},{64,32},{96,64},{128,96},{160,128},{192,160},{224,192},{256... | collective-permute-start | bytes 786440 | tf_op jit(solution)/shard_map/while/body/eval_jaxpr/ppermute | solution.py:16
  157.4 8.7 %collective-permute-start = (bf16[32,4096]{1,0:T(8,128)(2,1)S(1)}, bf16[32,4096]{1,0:T(8,128)(2,1)S(1)}, u32[]{:S(2)}, u32[]{:S(2)}) collective-permute-start(bf16[32,4096]{1,0:T(8,128)(2,1)S(1)} %get-tuple-element.667), channel_id=1, source_target_pairs={{32,0},{64,32},{96,64},{128,96},{160,128},{192,160},{224,192},{256... | collective-permute-start | bytes 786440 | tf_op jit(solution)/shard_map/while/body/eval_jaxpr/ppermute | solution.py:16
  209.6 8.0 %collective-permute-start = (bf16[32,4096]{1,0:T(8,128)(2,1)S(1)}, bf16[32,4096]{1,0:T(8,128)(2,1)S(1)}, u32[]{:S(2)}, u32[]{:S(2)}) collective-permute-start(bf16[32,4096]{1,0:T(8,128)(2,1)S(1)} %get-tuple-element.667), channel_id=1, source_target_pairs={{32,0},{64,32},{96,64},{128,96},{160,128},{192,160},{224,192},{256... | collective-permute-start | bytes 786440 | tf_op jit(solution)/shard_map/while/body/eval_jaxpr/ppermute | solution.py:16
  222.8 8.3 %collective-permute-start = (bf16[32,4096]{1,0:T(8,128)(2,1)S(1)}, bf16[32,4096]{1,0:T(8,128)(2,1)S(1)}, u32[]{:S(2)}, u32[]{:S(2)}) collective-permute-start(bf16[32,4096]{1,0:T(8,128)(2,1)S(1)} %get-tuple-element.667), channel_id=1, source_target_pairs={{32,0},{64,32},{96,64},{128,96},{160,128},{192,160},{224,192},{256... | collective-permute-start | bytes 786440 | tf_op jit(solution)/shard_map/while/body/eval_jaxpr/ppermute | solution.py:16
  236.2 8.3 %collective-permute-start = (bf16[32,4096]{1,0:T(8,128)(2,1)S(1)}, bf16[32,4096]{1,0:T(8,128)(2,1)S(1)}, u32[]{:S(2)}, u32[]{:S(2)}) collective-permute-start(bf16[32,4096]{1,0:T(8,128)(2,1)S(1)} %get-tuple-element.667), channel_id=1, source_target_pairs={{32,0},{64,32},{96,64},{128,96},{160,128},{192,160},{224,192},{256... | collective-permute-start | bytes 786440 | tf_op jit(solution)/shard_map/while/body/eval_jaxpr/ppermute | solution.py:16
  249.7 8.3 %collective-permute-start = (bf16[32,4096]{1,0:T(8,128)(2,1)S(1)}, bf16[32,4096]{1,0:T(8,128)(2,1)S(1)}, u32[]{:S(2)}, u32[]{:S(2)}) collective-permute-start(bf16[32,4096]{1,0:T(8,128)(2,1)S(1)} %get-tuple-element.667), channel_id=1, source_target_pairs={{32,0},{64,32},{96,64},{128,96},{160,128},{192,160},{224,192},{256... | collective-permute-start | bytes 786440 | tf_op jit(solution)/shard_map/while/body/eval_jaxpr/ppermute | solution.py:16
  263.2 8.3 %collective-permute-start = (bf16[32,4096]{1,0:T(8,128)(2,1)S(1)}, bf16[32,4096]{1,0:T(8,128)(2,1)S(1)}, u32[]{:S(2)}, u32[]{:S(2)}) collective-permute-start(bf16[32,4096]{1,0:T(8,128)(2,1)S(1)} %get-tuple-element.667), channel_id=1, source_target_pairs={{32,0},{64,32},{96,64},{128,96},{160,128},{192,160},{224,192},{256... | collective-permute-start | bytes 786440 | tf_op jit(solution)/shard_map/while/body/eval_jaxpr/ppermute | solution.py:16
  276.6 10.6 %collective-permute-start = (bf16[32,4096]{1,0:T(8,128)(2,1)S(1)}, bf16[32,4096]{1,0:T(8,128)(2,1)S(1)}, u32[]{:S(2)}, u32[]{:S(2)}) collective-permute-start(bf16[32,4096]{1,0:T(8,128)(2,1)S(1)} %get-tuple-element.667), channel_id=1, source_target_pairs={{32,0},{64,32},{96,64},{128,96},{160,128},{192,160},{224,192},{256... | collective-permute-start | bytes 786440 | tf_op jit(solution)/shard_map/while/body/eval_jaxpr/ppermute | solution.py:16
  292.4 10.7 %collective-permute-start = (bf16[32,4096]{1,0:T(8,128)(2,1)S(1)}, bf16[32,4096]{1,0:T(8,128)(2,1)S(1)}, u32[]{:S(2)}, u32[]{:S(2)}) collective-permute-start(bf16[32,4096]{1,0:T(8,128)(2,1)S(1)} %get-tuple-element.667), channel_id=1, source_target_pairs={{32,0},{64,32},{96,64},{128,96},{160,128},{192,160},{224,192},{256... | collective-permute-start | bytes 786440 | tf_op jit(solution)/shard_map/while/body/eval_jaxpr/ppermute | solution.py:16
  308.2 10.7 %collective-permute-start = (bf16[32,4096]{1,0:T(8,128)(2,1)S(1)}, bf16[32,4096]{1,0:T(8,128)(2,1)S(1)}, u32[]{:S(2)}, u32[]{:S(2)}) collective-permute-start(bf16[32,4096]{1,0:T(8,128)(2,1)S(1)} %get-tuple-element.667), channel_id=1, source_target_pairs={{32,0},{64,32},{96,64},{128,96},{160,128},{192,160},{224,192},{256... | collective-permute-start | bytes 786440 | tf_op jit(solution)/shard_map/while/body/eval_jaxpr/ppermute | solution.py:16
  324.1 10.7 %collective-permute-start = (bf16[32,4096]{1,0:T(8,128)(2,1)S(1)}, bf16[32,4096]{1,0:T(8,128)(2,1)S(1)}, u32[]{:S(2)}, u32[]{:S(2)}) collective-permute-start(bf16[32,4096]{1,0:T(8,128)(2,1)S(1)} %get-tuple-element.667), channel_id=1, source_target_pairs={{32,0},{64,32},{96,64},{128,96},{160,128},{192,160},{224,192},{256... | collective-permute-start | bytes 786440 | tf_op jit(solution)/shard_map/while/body/eval_jaxpr/ppermute | solution.py:16
  340.0 10.7 %collective-permute-start = (bf16[32,4096]{1,0:T(8,128)(2,1)S(1)}, bf16[32,4096]{1,0:T(8,128)(2,1)S(1)}, u32[]{:S(2)}, u32[]{:S(2)}) collective-permute-start(bf16[32,4096]{1,0:T(8,128)(2,1)S(1)} %get-tuple-element.667), channel_id=1, source_target_pairs={{32,0},{64,32},{96,64},{128,96},{160,128},{192,160},{224,192},{256... | collective-permute-start | bytes 786440 | tf_op jit(solution)/shard_map/while/body/eval_jaxpr/ppermute | solution.py:16
  355.8 11.6 %collective-permute-start = (bf16[32,4096]{1,0:T(8,128)(2,1)S(1)}, bf16[32,4096]{1,0:T(8,128)(2,1)S(1)}, u32[]{:S(2)}, u32[]{:S(2)}) collective-permute-start(bf16[32,4096]{1,0:T(8,128)(2,1)S(1)} %get-tuple-element.667), channel_id=1, source_target_pairs={{32,0},{64,32},{96,64},{128,96},{160,128},{192,160},{224,192},{256... | collective-permute-start | bytes 786440 | tf_op jit(solution)/shard_map/while/body/eval_jaxpr/ppermute | solution.py:16
  372.6 13.2 %collective-permute-start = (bf16[32,4096]{1,0:T(8,128)(2,1)S(1)}, bf16[32,4096]{1,0:T(8,128)(2,1)S(1)}, u32[]{:S(2)}, u32[]{:S(2)}) collective-permute-start(bf16[32,4096]{1,0:T(8,128)(2,1)S(1)} %get-tuple-element.667), channel_id=1, source_target_pairs={{32,0},{64,32},{96,64},{128,96},{160,128},{192,160},{224,192},{256... | collective-permute-start | bytes 786440 | tf_op jit(solution)/shard_map/while/body/eval_jaxpr/ppermute | solution.py:16
  391.0 14.3 %collective-permute-start = (bf16[32,4096]{1,0:T(8,128)(2,1)S(1)}, bf16[32,4096]{1,0:T(8,128)(2,1)S(1)}, u32[]{:S(2)}, u32[]{:S(2)}) collective-permute-start(bf16[32,4096]{1,0:T(8,128)(2,1)S(1)} %get-tuple-element.667), channel_id=1, source_target_pairs={{32,0},{64,32},{96,64},{128,96},{160,128},{192,160},{224,192},{256... | collective-permute-start | bytes 786440 | tf_op jit(solution)/shard_map/while/body/eval_jaxpr/ppermute | solution.py:16
  410.4 13.4 %collective-permute-start = (bf16[32,4096]{1,0:T(8,128)(2,1)S(1)}, bf16[32,4096]{1,0:T(8,128)(2,1)S(1)}, u32[]{:S(2)}, u32[]{:S(2)}) collective-permute-start(bf16[32,4096]{1,0:T(8,128)(2,1)S(1)} %get-tuple-element.667), channel_id=1, source_target_pairs={{32,0},{64,32},{96,64},{128,96},{160,128},{192,160},{224,192},{256... | collective-permute-start | bytes 786440 | tf_op jit(solution)/shard_map/while/body/eval_jaxpr/ppermute | solution.py:16
  429.0 13.3 %collective-permute-start = (bf16[32,4096]{1,0:T(8,128)(2,1)S(1)}, bf16[32,4096]{1,0:T(8,128)(2,1)S(1)}, u32[]{:S(2)}, u32[]{:S(2)}) collective-permute-start(bf16[32,4096]{1,0:T(8,128)(2,1)S(1)} %get-tuple-element.667), channel_id=1, source_target_pairs={{32,0},{64,32},{96,64},{128,96},{160,128},{192,160},{224,192},{256... | collective-permute-start | bytes 786440 | tf_op jit(solution)/shard_map/while/body/eval_jaxpr/ppermute | solution.py:16
  447.5 10.5 %collective-permute-start = (bf16[32,4096]{1,0:T(8,128)(2,1)S(1)}, bf16[32,4096]{1,0:T(8,128)(2,1)S(1)}, u32[]{:S(2)}, u32[]{:S(2)}) collective-permute-start(bf16[32,4096]{1,0:T(8,128)(2,1)S(1)} %get-tuple-element.667), channel_id=1, source_target_pairs={{32,0},{64,32},{96,64},{128,96},{160,128},{192,160},{224,192},{256... | collective-permute-start | bytes 786440 | tf_op jit(solution)/shard_map/while/body/eval_jaxpr/ppermute | solution.py:16
  463.1 10.1 %collective-permute-start = (bf16[32,4096]{1,0:T(8,128)(2,1)S(1)}, bf16[32,4096]{1,0:T(8,128)(2,1)S(1)}, u32[]{:S(2)}, u32[]{:S(2)}) collective-permute-start(bf16[32,4096]{1,0:T(8,128)(2,1)S(1)} %get-tuple-element.667), channel_id=1, source_target_pairs={{32,0},{64,32},{96,64},{128,96},{160,128},{192,160},{224,192},{256... | collective-permute-start | bytes 786440 | tf_op jit(solution)/shard_map/while/body/eval_jaxpr/ppermute | solution.py:16
  496.1 123.6 %reduce-scatter.6.cloned.1.call-start = ((), (), s32[]{:S(2)}) async-start(), calls=%async_computation.6 | async-start | bytes 2359296 | tf_op jit(solution)/shard_map/reduce_scatter | solution.py:259
  568.1 76.5 %reduce-scatter.8.cloned.1.call-start = ((), (), s32[]{:S(2)}) async-start(), calls=%async_computation.7 | async-start | bytes 393216 | tf_op jit(solution)/shard_map/reduce_scatter | solution.py:260
  (9 other events, 100.3 us)
Sparse Core Ops, SparseCore 0:
  13.8 48.4 all-gather.3
  64.3 25.5 all-gather.5
  496.2 67.9 reduce-scatter.3
  568.2 51.3 reduce-scatter.5
  622.5 22.0 reduce-scatter.7

commit v7 on v4

--- a/solution.py
+++ b/solution.py
@@ -146,6 +146,38 @@
       query_rows, key_rows, value_rows, cos2, sin2, grad_store, proj_store, gain_acc)
 
 
+def unpack_kernel(rows_ref, gain_ref, wp_ref, wb_ref, gain_out):
+    proj_cols = wp_ref.shape[-1]
+    block = rows_ref[...]
+    wp_ref[...] = block[:, :proj_cols]
+    wb_ref[...] = block[:, proj_cols:]
+    gain_out[...] = gain_ref[0:1, : gain_out.shape[-1]].astype(jnp.float32)
+
+
+def unpack_weights(staged, rows_here, head):
+    cols = staged.shape[-1]
+    groups = FC * FZ * FX
+    natural = lambda c, z, x: x * (FZ * FC) + z * FC + c
+    return pl.pallas_call(
+        unpack_kernel,
+        out_shape=(
+            jax.ShapeDtypeStruct((groups * rows_here, 3 * head), staged.dtype),
+            jax.ShapeDtypeStruct((groups * rows_here, cols - 3 * head), staged.dtype),
+            jax.ShapeDtypeStruct((1, groups * rows_here), jnp.float32),
+        ),
+        grid=(FC, FZ, FX),
+        in_specs=[
+            pl.BlockSpec((None, None, None, rows_here, cols), lambda c, z, x: (c, z, x, 0, 0)),
+            pl.BlockSpec((None, None, None, 16, cols), lambda c, z, x: (c, z, x, rows_here // 16, 0)),
+        ],
+        out_specs=[
+            pl.BlockSpec((rows_here, 3 * head), lambda c, z, x: (natural(c, z, x), 0)),
+            pl.BlockSpec((rows_here, cols - 3 * head), lambda c, z, x: (natural(c, z, x), 0)),
+            pl.BlockSpec((1, rows_here), lambda c, z, x: (0, natural(c, z, x))),
+        ],
+    )(staged, staged)
+
+
 def on_device(inputs, upstream, weights, gain):
     sections = SH * SY
     here = lax.axis_index("sh") * SY + lax.axis_index("sy")
@@ -162,16 +194,10 @@
     staged = lax.all_gather(packed, "fx", axis=0, tiled=True)
     staged = lax.all_gather(staged, "fz", axis=0, tiled=True)
     staged = lax.all_gather(staged, "fc", axis=0, tiled=True)
-    gathered = (
-        staged.reshape(FC, FZ, FX, rows_here + 16, weights.shape[2])
-        .transpose(2, 1, 0, 3, 4)
-        .reshape(groups, rows_here + 16, weights.shape[2])
-    )
-    w_full = gathered[:, :rows_here, :].reshape(groups * rows_here, weights.shape[2])
-    gain_full = gathered[:, rows_here, :rows_here].reshape(groups * rows_here)
-    wide_gain = gain_full.astype(jnp.float32)
-    w_proj = w_full[:, : 3 * head]
-    w_back = w_full[:, 3 * head :]
+    w_proj, w_back, gain_row = unpack_weights(
+        staged.reshape(FC, FZ, FX, rows_here + 16, weights.shape[2]), rows_here, head
+    )
+    wide_gain = gain_row.reshape(groups * rows_here)
 
     xfloat = inputs[0].astype(jnp.float32)
     inv_rms = lax.rsqrt(jnp.mean(xfloat * xfloat, axis=-1, keepdims=True) + 1e-05)
@@ -199,7 +225,6 @@
 
     cos2 = jnp.concatenate([cosine, cosine], axis=-1)
     sin2 = jnp.concatenate([sine_table, -sine_table], axis=-1)
-    gain_row = wide_gain.reshape(1, width)
 
     def tick(tick_no, received, state):
         grad_store, proj_store, gain_acc = state

time: 646 us -> 630 us (0.975)
  local copies, waits for them, and re-layouts: 55 us -> 29.3 us
    pallas_call x0 -> x1, Pallas kernels: none -> 17.4 us  [unpack_weights(): pl.pallas_call(unpack_kernel, out_shape=(jax.ShapeDtypeStruct((groups * r...]
    pallas_call x23, Pallas kernels: 125 us -> 114 us  [tick_call(): pl.pallas_call(tick_kernel, out_shape=(jax.ShapeDtypeStruct((length, widt...]
    transpose x1 -> x0, local copies, waits for them, and re-layouts: 9.36 us -> none  [on_device(): gathered = staged.reshape(FC, FZ, FX, rows_here + 16, weights.shape[2]).t...]
    reshape x1 -> x0, local copies, waits for them, and re-layouts: 8.1 us -> none  [on_device(): gathered = staged.reshape(FC, FZ, FX, rows_here + 16, weights.shape[2]).t...]
    slice x5 -> x0, local copies, waits for them, and re-layouts: 7.73 us -> none  [the longest x3 4.58 us: on_device(): gathered[:, :rows_here, :].reshape(groups * rows_here, weights.shape[2])]
where the time goes in v7:
time: 630 us; the launch traced here: 629 us
  waiting for transfers between devices  339 us (54%)
  Pallas kernels  131 us (21%)
  blocking collectives  62.4 us (10%)
  local copies, waits for them, and re-layouts  29.3 us (5%)
  starting transfers between devices  28.6 us (5%)
  other arithmetic  15.2 us (2%)
  between operations  14 us (2%)
  matrix products  7.95 us (1%)
    ppermute x22, waiting for transfers between devices, passed_along(): lax.ppermute(value, axis, [(source, source + steps) for source in range(l...  195 us
    pallas_call x23, Pallas kernels, tick_call(): pl.pallas_call(tick_kernel, out_shape=(jax.ShapeDtypeStruct((length, widt...  114 us
    all_gather x1, blocking collectives, on_device(): gain_sum = jnp.sum(lax.all_gather(gain_acc, FSDP, axis=0), axis=0)  57 us
    reduce_scatter x1, waiting for transfers between devices, on_device(): lax.psum_scatter(terms.reshape(FZ, -1, cols), 'fz', scatter_dimension=0,...  51.3 us
    all_gather x1, waiting for transfers between devices, on_device(): staged = lax.all_gather(staged, 'fz', axis=0, tiled=True)  48.5 us
    ppermute x22, starting transfers between devices, passed_along(): lax.ppermute(value, axis, [(source, source + steps) for source in range(l...  28.4 us
    reduce_scatter x1, waiting for transfers between devices, on_device(): lax.psum_scatter(terms.reshape(FX, -1, cols), 'fx', scatter_dimension=0,...  24.9 us
    pallas_call x1, Pallas kernels, unpack_weights(): pl.pallas_call(unpack_kernel, out_shape=(jax.ShapeDtypeStruct((groups * r...  17.4 us
  transfers between devices with their start and end apart: 27, of which 27 were waited for; matrix products, arithmetic and copies ran while one was open for 3% of the time, Pallas kernels for 0%

profile of v7, /device:TPU:1, one launch (start us, length us, event | category | flops | bytes accessed | tf_op | source)
XLA Modules:
  0.0 628.5 jit_solution(8423391262650621565)
XLA Ops:
  13.7 48.5 %all-gather.4.cloned.1.call-done = bf16[2304,512]{1,0:T(8,128)(2,1)} async-done(((bf16[288,512]{1,0:T(8,128)(2,1)}), bf16[2304,512]{1,0:T(8,128)(2,1)}) %all-gather.4.cloned.1.call-update) | async-done | bytes 2359312 | tf_op jit(solution)/shard_map/all_gather | solution.py:195
  68.3 7.3 %copy.25 = f32[256,2,8,2,128]{0,4,1,2,3:T(8,128)} copy(f32[256,2,8,2,128]{4,3,2,1,0:T(2,128)} %reshape.164) | data formatting | bytes 8388608 | tf_op jit(solution)/shard_map/convert_element_type | solution.py:202
  79.1 10.8 %all-gather.6.cloned.1.call-done = bf16[4608,512]{1,0:T(8,128)(2,1)} async-done(((bf16[2304,512]{1,0:T(8,128)(2,1)}), bf16[4608,512]{1,0:T(8,128)(2,1)}) %all-gather.6.cloned.1.call-update) | async-done | bytes 4718608 | tf_op jit(solution)/shard_map/all_gather | solution.py:196
  89.9 17.4 %shard_map.59 = (bf16[4096,384]{1,0:T(8,128)(2,1)S(1)}, bf16[4096,128]{1,0:T(8,128)(2,1)}, f32[1,4096]{1,0:T(1,128)S(1)}) custom-call(bf16[2,8,2,144,512]{4,3,2,1,0:T(8,128)(2,1)} %bitcast.74, bf16[2,8,2,144,512]{4,3,2,1,0:T(8,128)(2,1)} %bitcast.75), custom_call_target="tpu_custom_call" | custom-call | tf_op jit(solution)/shard_map/pallas_call | solution.py:161
  116.4 333.6 %while.21 = (s32[]{:T(128)}, bf16[32,4096]{1,0:T(8,128)(2,1)S(1)}, bf16[10,32,4096]{2,1,0:T(8,128)(2,1)S(1)}, bf16[10,32,384]{2,1,0:T(8,128)(2,1)S(1)}, f32[4096...) while((s32[]{:T(128)}, bf16[32,4096]{1,0:T(8,128)(2,1)S(1)}, ...), condition=%wide.region_4.5_spmd, body=%wide.region_3.4_spmd.sunk | while | flops 268435488 | bytes 6291852 | solution.py:256
  122.7 8.3 %collective-permute-done = bf16[32,4096]{1,0:T(8,128)(2,1)S(1)} collective-permute-done((bf16[32,4096]{1,0:T(8,128)(2,1)S(1)}, bf16[32,4096]{1,0:T(8,128)(2,1)S(1)}, u32[]{:S(2)}, u32[]{:S(2)}) %collective-permute-start) | collective-permute-done | bytes 262176 | tf_op jit(solution)/shard_map/while/body/eval_jaxpr/ppermute | solution.py:16
  137.3 7.4 %collective-permute-done = bf16[32,4096]{1,0:T(8,128)(2,1)S(1)} collective-permute-done((bf16[32,4096]{1,0:T(8,128)(2,1)S(1)}, bf16[32,4096]{1,0:T(8,128)(2,1)S(1)}, u32[]{:S(2)}, u32[]{:S(2)}) %collective-permute-start) | collective-permute-done | bytes 262176 | tf_op jit(solution)/shard_map/while/body/eval_jaxpr/ppermute | solution.py:16
  228.8 7.0 %collective-permute-done = bf16[32,4096]{1,0:T(8,128)(2,1)S(1)} collective-permute-done((bf16[32,4096]{1,0:T(8,128)(2,1)S(1)}, bf16[32,4096]{1,0:T(8,128)(2,1)S(1)}, u32[]{:S(2)}, u32[]{:S(2)}) %collective-permute-start) | collective-permute-done | bytes 262176 | tf_op jit(solution)/shard_map/while/body/eval_jaxpr/ppermute | solution.py:16
  255.4 9.3 %collective-permute-done = bf16[32,4096]{1,0:T(8,128)(2,1)S(1)} collective-permute-done((bf16[32,4096]{1,0:T(8,128)(2,1)S(1)}, bf16[32,4096]{1,0:T(8,128)(2,1)S(1)}, u32[]{:S(2)}, u32[]{:S(2)}) %collective-permute-start) | collective-permute-done | bytes 262176 | tf_op jit(solution)/shard_map/while/body/eval_jaxpr/ppermute | solution.py:16
  271.1 9.4 %collective-permute-done = bf16[32,4096]{1,0:T(8,128)(2,1)S(1)} collective-permute-done((bf16[32,4096]{1,0:T(8,128)(2,1)S(1)}, bf16[32,4096]{1,0:T(8,128)(2,1)S(1)}, u32[]{:S(2)}, u32[]{:S(2)}) %collective-permute-start) | collective-permute-done | bytes 262176 | tf_op jit(solution)/shard_map/while/body/eval_jaxpr/ppermute | solution.py:16
  286.8 9.4 %collective-permute-done = bf16[32,4096]{1,0:T(8,128)(2,1)S(1)} collective-permute-done((bf16[32,4096]{1,0:T(8,128)(2,1)S(1)}, bf16[32,4096]{1,0:T(8,128)(2,1)S(1)}, u32[]{:S(2)}, u32[]{:S(2)}) %collective-permute-start) | collective-permute-done | bytes 262176 | tf_op jit(solution)/shard_map/while/body/eval_jaxpr/ppermute | solution.py:16
  302.6 9.4 %collective-permute-done = bf16[32,4096]{1,0:T(8,128)(2,1)S(1)} collective-permute-done((bf16[32,4096]{1,0:T(8,128)(2,1)S(1)}, bf16[32,4096]{1,0:T(8,128)(2,1)S(1)}, u32[]{:S(2)}, u32[]{:S(2)}) %collective-permute-start) | collective-permute-done | bytes 262176 | tf_op jit(solution)/shard_map/while/body/eval_jaxpr/ppermute | solution.py:16
  318.3 9.4 %collective-permute-done = bf16[32,4096]{1,0:T(8,128)(2,1)S(1)} collective-permute-done((bf16[32,4096]{1,0:T(8,128)(2,1)S(1)}, bf16[32,4096]{1,0:T(8,128)(2,1)S(1)}, u32[]{:S(2)}, u32[]{:S(2)}) %collective-permute-start) | collective-permute-done | bytes 262176 | tf_op jit(solution)/shard_map/while/body/eval_jaxpr/ppermute | solution.py:16
  334.0 10.6 %collective-permute-done = bf16[32,4096]{1,0:T(8,128)(2,1)S(1)} collective-permute-done((bf16[32,4096]{1,0:T(8,128)(2,1)S(1)}, bf16[32,4096]{1,0:T(8,128)(2,1)S(1)}, u32[]{:S(2)}, u32[]{:S(2)}) %collective-permute-start) | collective-permute-done | bytes 262176 | tf_op jit(solution)/shard_map/while/body/eval_jaxpr/ppermute | solution.py:16
  351.0 12.1 %collective-permute-done = bf16[32,4096]{1,0:T(8,128)(2,1)S(1)} collective-permute-done((bf16[32,4096]{1,0:T(8,128)(2,1)S(1)}, bf16[32,4096]{1,0:T(8,128)(2,1)S(1)}, u32[]{:S(2)}, u32[]{:S(2)}) %collective-permute-start) | collective-permute-done | bytes 262176 | tf_op jit(solution)/shard_map/while/body/eval_jaxpr/ppermute | solution.py:16
  369.4 12.9 %collective-permute-done = bf16[32,4096]{1,0:T(8,128)(2,1)S(1)} collective-permute-done((bf16[32,4096]{1,0:T(8,128)(2,1)S(1)}, bf16[32,4096]{1,0:T(8,128)(2,1)S(1)}, u32[]{:S(2)}, u32[]{:S(2)}) %collective-permute-start) | collective-permute-done | bytes 262176 | tf_op jit(solution)/shard_map/while/body/eval_jaxpr/ppermute | solution.py:16
  388.6 12.3 %collective-permute-done = bf16[32,4096]{1,0:T(8,128)(2,1)S(1)} collective-permute-done((bf16[32,4096]{1,0:T(8,128)(2,1)S(1)}, bf16[32,4096]{1,0:T(8,128)(2,1)S(1)}, u32[]{:S(2)}, u32[]{:S(2)}) %collective-permute-start) | collective-permute-done | bytes 262176 | tf_op jit(solution)/shard_map/while/body/eval_jaxpr/ppermute | solution.py:16
  407.3 11.2 %collective-permute-done = bf16[32,4096]{1,0:T(8,128)(2,1)S(1)} collective-permute-done((bf16[32,4096]{1,0:T(8,128)(2,1)S(1)}, bf16[32,4096]{1,0:T(8,128)(2,1)S(1)}, u32[]{:S(2)}, u32[]{:S(2)}) %collective-permute-start) | collective-permute-done | bytes 262176 | tf_op jit(solution)/shard_map/while/body/eval_jaxpr/ppermute | solution.py:16
  424.8 9.0 %collective-permute-done = bf16[32,4096]{1,0:T(8,128)(2,1)S(1)} collective-permute-done((bf16[32,4096]{1,0:T(8,128)(2,1)S(1)}, bf16[32,4096]{1,0:T(8,128)(2,1)S(1)}, u32[]{:S(2)}, u32[]{:S(2)}) %collective-permute-start) | collective-permute-done | bytes 262176 | tf_op jit(solution)/shard_map/while/body/eval_jaxpr/ppermute | solution.py:16
  440.1 9.9 %collective-permute-done = bf16[32,4096]{1,0:T(8,128)(2,1)S(1)} collective-permute-done((bf16[32,4096]{1,0:T(8,128)(2,1)S(1)}, bf16[32,4096]{1,0:T(8,128)(2,1)S(1)}, u32[]{:S(2)}, u32[]{:S(2)}) %collective-permute-start) | collective-permute-done | bytes 262176 | tf_op jit(solution)/shard_map/while/body/eval_jaxpr/ppermute | solution.py:16
  473.1 57.0 %all-gather = f32[32,1,4096]{2,1,0:T(1,128)S(1)} all-gather(f32[1,1,4096]{2,1,0:T(1,128)S(1)} %bitcast.81), channel_id=1, replica_groups=mesh['sh'=2,'sy'=8,'fx'=2,'fz'=8,'fc'=2] {'fx','fz','fc'}, dimensions={0}, use_global_device_ids=true | all-gather | bytes 540672 | tf_op jit(solution)/shard_map/all_gather | solution.py:281
  531.1 9.1 %reduce-scatter.4.cloned.1.call-done = bf16[1,2048,512]{1,2,0:T(8,128)(2,1)} async-done(((bf16[2,2048,512]{1,2,0:T(8,128)(2,1)}), bf16[1,2048,512]{1,2,0:T(8,128)(2,1)}) %reduce-scatter.4.cloned.1.call-update) | async-done | bytes 2097168 | tf_op jit(solution)/shard_map/reduce_scatter | solution.py:280
  544.2 51.3 %reduce-scatter.6.cloned.1.call-done = bf16[1,256,512]{2,1,0:T(8,128)(2,1)} async-done(((bf16[8,256,512]{2,1,0:T(8,128)(2,1)}), bf16[1,256,512]{2,1,0:T(8,128)(2,1)}) %reduce-scatter.6.cloned.1.call-update) | async-done | bytes 262160 | tf_op jit(solution)/shard_map/reduce_scatter | solution.py:283
  595.5 24.9 %reduce-scatter.8.cloned.1.call-done = bf16[1,128,512]{2,1,0:T(8,128)(2,1)} async-done(((bf16[2,128,512]{2,1,0:T(8,128)(2,1)}), bf16[1,128,512]{2,1,0:T(8,128)(2,1)}) %reduce-scatter.8.cloned.1.call-update) | async-done | bytes 131088 | tf_op jit(solution)/shard_map/reduce_scatter | solution.py:284
  (138 shorter events, 240.0 us)
Async XLA Ops:
  7.2 55.1 %all-gather.4.cloned.1.call-start = ((), (), s32[]{:S(2)}) async-start(), calls=%async_computation.3 | async-start | bytes 2654208 | tf_op jit(solution)/shard_map/all_gather | solution.py:195
  13.7 76.2 %all-gather.6.cloned.1.call-start = ((), (), s32[]{:S(2)}) async-start(), calls=%async_computation.4 | async-start | bytes 7077888 | tf_op jit(solution)/shard_map/all_gather | solution.py:196
  62.3 477.9 %reduce-scatter.4.cloned.1.call-start = ((), (), s32[]{:S(2)}) async-start(), calls=%async_computation.5 | async-start | bytes 6291456 | tf_op jit(solution)/shard_map/reduce_scatter | solution.py:280
  121.4 9.6 %collective-permute-start = (bf16[32,4096]{1,0:T(8,128)(2,1)S(1)}, bf16[32,4096]{1,0:T(8,128)(2,1)S(1)}, u32[]{:S(2)}, u32[]{:S(2)}) collective-permute-start(bf16[32,4096]{1,0:T(8,128)(2,1)S(1)} %get-tuple-element.651), channel_id=1, source_target_pairs={{32,0},{64,32},{96,64},{128,96},{160,128},{192,160},{224,192},{256... | collective-permute-start | bytes 786440 | tf_op jit(solution)/shard_map/while/body/eval_jaxpr/ppermute | solution.py:16
  136.0 8.7 %collective-permute-start = (bf16[32,4096]{1,0:T(8,128)(2,1)S(1)}, bf16[32,4096]{1,0:T(8,128)(2,1)S(1)}, u32[]{:S(2)}, u32[]{:S(2)}) collective-permute-start(bf16[32,4096]{1,0:T(8,128)(2,1)S(1)} %get-tuple-element.651), channel_id=1, source_target_pairs={{32,0},{64,32},{96,64},{128,96},{160,128},{192,160},{224,192},{256... | collective-permute-start | bytes 786440 | tf_op jit(solution)/shard_map/while/body/eval_jaxpr/ppermute | solution.py:16
  187.7 8.0 %collective-permute-start = (bf16[32,4096]{1,0:T(8,128)(2,1)S(1)}, bf16[32,4096]{1,0:T(8,128)(2,1)S(1)}, u32[]{:S(2)}, u32[]{:S(2)}) collective-permute-start(bf16[32,4096]{1,0:T(8,128)(2,1)S(1)} %get-tuple-element.651), channel_id=1, source_target_pairs={{32,0},{64,32},{96,64},{128,96},{160,128},{192,160},{224,192},{256... | collective-permute-start | bytes 786440 | tf_op jit(solution)/shard_map/while/body/eval_jaxpr/ppermute | solution.py:16
  200.8 8.3 %collective-permute-start = (bf16[32,4096]{1,0:T(8,128)(2,1)S(1)}, bf16[32,4096]{1,0:T(8,128)(2,1)S(1)}, u32[]{:S(2)}, u32[]{:S(2)}) collective-permute-start(bf16[32,4096]{1,0:T(8,128)(2,1)S(1)} %get-tuple-element.651), channel_id=1, source_target_pairs={{32,0},{64,32},{96,64},{128,96},{160,128},{192,160},{224,192},{256... | collective-permute-start | bytes 786440 | tf_op jit(solution)/shard_map/while/body/eval_jaxpr/ppermute | solution.py:16
  214.1 8.3 %collective-permute-start = (bf16[32,4096]{1,0:T(8,128)(2,1)S(1)}, bf16[32,4096]{1,0:T(8,128)(2,1)S(1)}, u32[]{:S(2)}, u32[]{:S(2)}) collective-permute-start(bf16[32,4096]{1,0:T(8,128)(2,1)S(1)} %get-tuple-element.651), channel_id=1, source_target_pairs={{32,0},{64,32},{96,64},{128,96},{160,128},{192,160},{224,192},{256... | collective-permute-start | bytes 786440 | tf_op jit(solution)/shard_map/while/body/eval_jaxpr/ppermute | solution.py:16
  227.5 8.3 %collective-permute-start = (bf16[32,4096]{1,0:T(8,128)(2,1)S(1)}, bf16[32,4096]{1,0:T(8,128)(2,1)S(1)}, u32[]{:S(2)}, u32[]{:S(2)}) collective-permute-start(bf16[32,4096]{1,0:T(8,128)(2,1)S(1)} %get-tuple-element.651), channel_id=1, source_target_pairs={{32,0},{64,32},{96,64},{128,96},{160,128},{192,160},{224,192},{256... | collective-permute-start | bytes 786440 | tf_op jit(solution)/shard_map/while/body/eval_jaxpr/ppermute | solution.py:16
  240.8 8.3 %collective-permute-start = (bf16[32,4096]{1,0:T(8,128)(2,1)S(1)}, bf16[32,4096]{1,0:T(8,128)(2,1)S(1)}, u32[]{:S(2)}, u32[]{:S(2)}) collective-permute-start(bf16[32,4096]{1,0:T(8,128)(2,1)S(1)} %get-tuple-element.651), channel_id=1, source_target_pairs={{32,0},{64,32},{96,64},{128,96},{160,128},{192,160},{224,192},{256... | collective-permute-start | bytes 786440 | tf_op jit(solution)/shard_map/while/body/eval_jaxpr/ppermute | solution.py:16
  254.1 10.6 %collective-permute-start = (bf16[32,4096]{1,0:T(8,128)(2,1)S(1)}, bf16[32,4096]{1,0:T(8,128)(2,1)S(1)}, u32[]{:S(2)}, u32[]{:S(2)}) collective-permute-start(bf16[32,4096]{1,0:T(8,128)(2,1)S(1)} %get-tuple-element.651), channel_id=1, source_target_pairs={{32,0},{64,32},{96,64},{128,96},{160,128},{192,160},{224,192},{256... | collective-permute-start | bytes 786440 | tf_op jit(solution)/shard_map/while/body/eval_jaxpr/ppermute | solution.py:16
  269.8 10.7 %collective-permute-start = (bf16[32,4096]{1,0:T(8,128)(2,1)S(1)}, bf16[32,4096]{1,0:T(8,128)(2,1)S(1)}, u32[]{:S(2)}, u32[]{:S(2)}) collective-permute-start(bf16[32,4096]{1,0:T(8,128)(2,1)S(1)} %get-tuple-element.651), channel_id=1, source_target_pairs={{32,0},{64,32},{96,64},{128,96},{160,128},{192,160},{224,192},{256... | collective-permute-start | bytes 786440 | tf_op jit(solution)/shard_map/while/body/eval_jaxpr/ppermute | solution.py:16
  285.5 10.7 %collective-permute-start = (bf16[32,4096]{1,0:T(8,128)(2,1)S(1)}, bf16[32,4096]{1,0:T(8,128)(2,1)S(1)}, u32[]{:S(2)}, u32[]{:S(2)}) collective-permute-start(bf16[32,4096]{1,0:T(8,128)(2,1)S(1)} %get-tuple-element.651), channel_id=1, source_target_pairs={{32,0},{64,32},{96,64},{128,96},{160,128},{192,160},{224,192},{256... | collective-permute-start | bytes 786440 | tf_op jit(solution)/shard_map/while/body/eval_jaxpr/ppermute | solution.py:16
  301.2 10.7 %collective-permute-start = (bf16[32,4096]{1,0:T(8,128)(2,1)S(1)}, bf16[32,4096]{1,0:T(8,128)(2,1)S(1)}, u32[]{:S(2)}, u32[]{:S(2)}) collective-permute-start(bf16[32,4096]{1,0:T(8,128)(2,1)S(1)} %get-tuple-element.651), channel_id=1, source_target_pairs={{32,0},{64,32},{96,64},{128,96},{160,128},{192,160},{224,192},{256... | collective-permute-start | bytes 786440 | tf_op jit(solution)/shard_map/while/body/eval_jaxpr/ppermute | solution.py:16
  317.0 10.7 %collective-permute-start = (bf16[32,4096]{1,0:T(8,128)(2,1)S(1)}, bf16[32,4096]{1,0:T(8,128)(2,1)S(1)}, u32[]{:S(2)}, u32[]{:S(2)}) collective-permute-start(bf16[32,4096]{1,0:T(8,128)(2,1)S(1)} %get-tuple-element.651), channel_id=1, source_target_pairs={{32,0},{64,32},{96,64},{128,96},{160,128},{192,160},{224,192},{256... | collective-permute-start | bytes 786440 | tf_op jit(solution)/shard_map/while/body/eval_jaxpr/ppermute | solution.py:16
  332.7 11.9 %collective-permute-start = (bf16[32,4096]{1,0:T(8,128)(2,1)S(1)}, bf16[32,4096]{1,0:T(8,128)(2,1)S(1)}, u32[]{:S(2)}, u32[]{:S(2)}) collective-permute-start(bf16[32,4096]{1,0:T(8,128)(2,1)S(1)} %get-tuple-element.651), channel_id=1, source_target_pairs={{32,0},{64,32},{96,64},{128,96},{160,128},{192,160},{224,192},{256... | collective-permute-start | bytes 786440 | tf_op jit(solution)/shard_map/while/body/eval_jaxpr/ppermute | solution.py:16
  349.7 13.4 %collective-permute-start = (bf16[32,4096]{1,0:T(8,128)(2,1)S(1)}, bf16[32,4096]{1,0:T(8,128)(2,1)S(1)}, u32[]{:S(2)}, u32[]{:S(2)}) collective-permute-start(bf16[32,4096]{1,0:T(8,128)(2,1)S(1)} %get-tuple-element.651), channel_id=1, source_target_pairs={{32,0},{64,32},{96,64},{128,96},{160,128},{192,160},{224,192},{256... | collective-permute-start | bytes 786440 | tf_op jit(solution)/shard_map/while/body/eval_jaxpr/ppermute | solution.py:16
  368.0 14.2 %collective-permute-start = (bf16[32,4096]{1,0:T(8,128)(2,1)S(1)}, bf16[32,4096]{1,0:T(8,128)(2,1)S(1)}, u32[]{:S(2)}, u32[]{:S(2)}) collective-permute-start(bf16[32,4096]{1,0:T(8,128)(2,1)S(1)} %get-tuple-element.651), channel_id=1, source_target_pairs={{32,0},{64,32},{96,64},{128,96},{160,128},{192,160},{224,192},{256... | collective-permute-start | bytes 786440 | tf_op jit(solution)/shard_map/while/body/eval_jaxpr/ppermute | solution.py:16
  387.3 13.7 %collective-permute-start = (bf16[32,4096]{1,0:T(8,128)(2,1)S(1)}, bf16[32,4096]{1,0:T(8,128)(2,1)S(1)}, u32[]{:S(2)}, u32[]{:S(2)}) collective-permute-start(bf16[32,4096]{1,0:T(8,128)(2,1)S(1)} %get-tuple-element.651), channel_id=1, source_target_pairs={{32,0},{64,32},{96,64},{128,96},{160,128},{192,160},{224,192},{256... | collective-permute-start | bytes 786440 | tf_op jit(solution)/shard_map/while/body/eval_jaxpr/ppermute | solution.py:16
  406.0 12.5 %collective-permute-start = (bf16[32,4096]{1,0:T(8,128)(2,1)S(1)}, bf16[32,4096]{1,0:T(8,128)(2,1)S(1)}, u32[]{:S(2)}, u32[]{:S(2)}) collective-permute-start(bf16[32,4096]{1,0:T(8,128)(2,1)S(1)} %get-tuple-element.651), channel_id=1, source_target_pairs={{32,0},{64,32},{96,64},{128,96},{160,128},{192,160},{224,192},{256... | collective-permute-start | bytes 786440 | tf_op jit(solution)/shard_map/while/body/eval_jaxpr/ppermute | solution.py:16
  423.5 10.3 %collective-permute-start = (bf16[32,4096]{1,0:T(8,128)(2,1)S(1)}, bf16[32,4096]{1,0:T(8,128)(2,1)S(1)}, u32[]{:S(2)}, u32[]{:S(2)}) collective-permute-start(bf16[32,4096]{1,0:T(8,128)(2,1)S(1)} %get-tuple-element.651), channel_id=1, source_target_pairs={{32,0},{64,32},{96,64},{128,96},{160,128},{192,160},{224,192},{256... | collective-permute-start | bytes 786440 | tf_op jit(solution)/shard_map/while/body/eval_jaxpr/ppermute | solution.py:16
  438.8 11.2 %collective-permute-start = (bf16[32,4096]{1,0:T(8,128)(2,1)S(1)}, bf16[32,4096]{1,0:T(8,128)(2,1)S(1)}, u32[]{:S(2)}, u32[]{:S(2)}) collective-permute-start(bf16[32,4096]{1,0:T(8,128)(2,1)S(1)} %get-tuple-element.651), channel_id=1, source_target_pairs={{32,0},{64,32},{96,64},{128,96},{160,128},{192,160},{224,192},{256... | collective-permute-start | bytes 786440 | tf_op jit(solution)/shard_map/while/body/eval_jaxpr/ppermute | solution.py:16
  473.0 122.4 %reduce-scatter.6.cloned.1.call-start = ((), (), s32[]{:S(2)}) async-start(), calls=%async_computation.6 | async-start | bytes 2359296 | tf_op jit(solution)/shard_map/reduce_scatter | solution.py:283
  544.1 76.3 %reduce-scatter.8.cloned.1.call-start = ((), (), s32[]{:S(2)}) async-start(), calls=%async_computation.7 | async-start | bytes 393216 | tf_op jit(solution)/shard_map/reduce_scatter | solution.py:284
  (12 other events, 104.4 us)
Sparse Core Ops, SparseCore 0:
  13.8 48.4 all-gather.3
  64.3 25.5 all-gather.5
  473.1 66.9 reduce-scatter.3
  544.2 51.1 reduce-scatter.5
  598.3 22.0 reduce-scatter.7

commit v8 on v7

--- a/solution.py
+++ b/solution.py
@@ -178,6 +178,34 @@
     )(staged, staged)
 
 
+def terms_kernel(hid_ref, g_ref, gp_ref, att_ref, out_ref):
+    tokens = hid_ref.shape[0]
+    gp = gp_ref[...].reshape(tokens, gp_ref.shape[-1])
+    grads = g_ref[...].reshape(tokens, g_ref.shape[-1])
+    first = lax.dot_general(hid_ref[...], gp, (((0,), (0,)), ((), ())), preferred_element_type=jnp.float32)
+    second = lax.dot_general(grads, att_ref[...], (((0,), (0,)), ((), ())), preferred_element_type=jnp.float32)
+    out_ref[...] = jnp.concatenate([first, second], axis=-1).astype(out_ref.dtype)
+
+
+def weight_terms(hidden_flat, grad_store, proj_store, att_flat, rows_here):
+    tokens, width = hidden_flat.shape
+    micro_count, length = grad_store.shape[0] - 2, grad_store.shape[1]
+    cols = proj_store.shape[-1] + att_flat.shape[-1]
+    staged = lambda j: (j % FC) * (FZ * FX) + ((j // FC) % FZ) * FX + j // (FC * FZ)
+    return pl.pallas_call(
+        terms_kernel,
+        out_shape=jax.ShapeDtypeStruct((width, cols), jnp.bfloat16),
+        grid=(width // rows_here,),
+        in_specs=[
+            pl.BlockSpec((tokens, rows_here), lambda j: (0, j)),
+            pl.BlockSpec((micro_count, length, rows_here), lambda j: (0, 0, j)),
+            pl.BlockSpec((micro_count, length, proj_store.shape[-1]), lambda j: (0, 0, 0)),
+            pl.BlockSpec((tokens, att_flat.shape[-1]), lambda j: (0, 0)),
+        ],
+        out_specs=pl.BlockSpec((rows_here, cols), lambda j: (staged(j), 0)),
+    )(hidden_flat, grad_store, proj_store, att_flat)
+
+
 def on_device(inputs, upstream, weights, gain):
     sections = SH * SY
     here = lax.axis_index("sh") * SY + lax.axis_index("sy")
@@ -231,7 +259,7 @@
         micro = tick_no - (sections - 1 - here)
         active = jnp.logical_and(micro >= 0, micro < micro_count)
         clipped = jnp.clip(micro, 0, micro_count - 1)
-        slot = jnp.clip(micro, -1, micro_count) + 1
+        slot = jnp.where(active, micro, jnp.where(micro < 0, micro_count, micro_count + 1))
         scal = jnp.stack(
             [clipped, slot, active.astype(jnp.int32), (here == sections - 1).astype(jnp.int32)]
         ).astype(jnp.int32)
@@ -259,23 +287,10 @@
     leftover, state = tick(total_ticks - 1, received, state)
     grad_store, proj_store, gain_acc = state
     tokens_all = micro_count * length
-    grad_flat = grad_store[1 : micro_count + 1].reshape(tokens_all, width)
-    proj_flat = proj_store[1 : micro_count + 1].reshape(tokens_all, 3 * head)
-    att_flat = attended.reshape(tokens_all, head)
-    def stage_order(rows):
-        return (
-            rows.reshape(tokens_all, FX, FZ, FC, rows_here)
-            .transpose(0, 3, 2, 1, 4)
-            .reshape(tokens_all, width)
-        )
-
-    terms = jnp.concatenate(
-        [
-            contract_rows(stage_order(hidden.reshape(tokens_all, width)), proj_flat),
-            contract_rows(stage_order(grad_flat), att_flat),
-        ],
-        axis=1,
-    ).astype(jnp.bfloat16)
+    terms = weight_terms(
+        hidden.reshape(tokens_all, width), grad_store, proj_store,
+        attended.reshape(tokens_all, head), rows_here,
+    )
     cols = terms.shape[1]
     terms = lax.psum_scatter(terms.reshape(FC, -1, cols), "fc", scatter_dimension=0, tiled=True)
     gain_sum = jnp.sum(lax.all_gather(gain_acc, FSDP, axis=0), axis=0)

time: 630 us -> 632 us (level)
  local copies, waits for them, and re-layouts: 29.3 us -> 1.48 us
  Pallas kernels: 131 us -> 151 us
  waiting for transfers between devices: 339 us -> 352 us
    pallas_call x0 -> x1, Pallas kernels: none -> 19.9 us  [weight_terms(): pl.pallas_call(terms_kernel, out_shape=jax.ShapeDtypeStruct((width, cols)...]
    all_gather x1, waiting for transfers between devices: 10.8 us -> 23.4 us  [on_device(): staged = lax.all_gather(staged, 'fc', axis=0, tiled=True)]
    convert_element_type x2 -> x0, local copies, waits for them, and re-layouts: 12.6 us -> none  [on_device(): xfloat = inputs[0].astype(jnp.float32)]
    another operation x2 -> x0, local copies, waits for them, and re-layouts: 9.14 us -> none  [stage_order(): rows.reshape(tokens_all, FX, FZ, FC, rows_here).transpose(0, 3, 2, 1, 4)]
  transfers between devices with their start and end apart: 27 -> 27, of which waited for: 27 -> 27; matrix products, arithmetic and copies ran while one was open for 3% -> 1% of each run, Pallas kernels for 0% -> 0%
where the time goes in v8:
time: 632 us; the launch traced here: 630 us
  waiting for transfers between devices  352 us (56%)
  Pallas kernels  151 us (24%)
  blocking collectives  62.4 us (10%)
  starting transfers between devices  28.6 us (5%)
  other arithmetic  13.9 us (2%)
  between operations  13.9 us (2%)
    ppermute x22, waiting for transfers between devices, passed_along(): lax.ppermute(value, axis, [(source, source + steps) for source in range(l...  195 us
    pallas_call x23, Pallas kernels, tick_call(): pl.pallas_call(tick_kernel, out_shape=(jax.ShapeDtypeStruct((length, widt...  114 us
    all_gather x1, blocking collectives, on_device(): gain_sum = jnp.sum(lax.all_gather(gain_acc, FSDP, axis=0), axis=0)  57.1 us
    reduce_scatter x1, waiting for transfers between devices, on_device(): lax.psum_scatter(terms.reshape(FZ, -1, cols), 'fz', scatter_dimension=0,...  51.2 us
    all_gather x1, waiting for transfers between devices, on_device(): staged = lax.all_gather(staged, 'fz', axis=0, tiled=True)  48.5 us
    ppermute x22, starting transfers between devices, passed_along(): lax.ppermute(value, axis, [(source, source + steps) for source in range(l...  28.4 us
    reduce_scatter x1, waiting for transfers between devices, on_device(): lax.psum_scatter(terms.reshape(FX, -1, cols), 'fx', scatter_dimension=0,...  24.9 us
    all_gather x1, waiting for transfers between devices, on_device(): staged = lax.all_gather(staged, 'fc', axis=0, tiled=True)  23.4 us
  transfers between devices with their start and end apart: 27, of which 27 were waited for; matrix products, arithmetic and copies ran while one was open for 1% of the time, Pallas kernels for 0%

profile of v8, /device:TPU:1, one launch (start us, length us, event | category | flops | bytes accessed | tf_op | source)
XLA Modules:
  0.0 629.9 jit_solution(15454522012787763192)
XLA Ops:
  13.7 48.5 %all-gather.4.cloned.1.call-done = bf16[2304,512]{1,0:T(8,128)(2,1)} async-done(((bf16[288,512]{1,0:T(8,128)(2,1)}), bf16[2304,512]{1,0:T(8,128)(2,1)}) %all-gather.4.cloned.1.call-update) | async-done | bytes 2359312 | tf_op jit(solution)/shard_map/all_gather | solution.py:223
  66.5 23.4 %all-gather.6.cloned.1.call-done = bf16[4608,512]{1,0:T(8,128)(2,1)} async-done(((bf16[2304,512]{1,0:T(8,128)(2,1)}), bf16[4608,512]{1,0:T(8,128)(2,1)}) %all-gather.6.cloned.1.call-update) | async-done | bytes 4718608 | tf_op jit(solution)/shard_map/all_gather | solution.py:224
  89.9 17.3 %shard_map.59 = (bf16[4096,384]{1,0:T(8,128)(2,1)S(1)}, bf16[4096,128]{1,0:T(8,128)(2,1)}, f32[1,4096]{1,0:T(1,128)S(1)}) custom-call(bf16[2,8,2,144,512]{4,3,2,1,0:T(8,128)(2,1)} %bitcast.54, bf16[2,8,2,144,512]{4,3,2,1,0:T(8,128)(2,1)} %bitcast.55), custom_call_target="tpu_custom_call" | custom-call | tf_op jit(solution)/shard_map/pallas_call | solution.py:161
  119.2 333.5 %while.21 = (s32[]{:T(128)}, bf16[32,4096]{1,0:T(8,128)(2,1)S(1)}, bf16[10,32,4096]{2,1,0:T(8,128)(2,1)S(1)}, bf16[10,32,384]{2,1,0:T(8,128)(2,1)S(1)}, f32[4096...) while((s32[]{:T(128)}, bf16[32,4096]{1,0:T(8,128)(2,1)S(1)}, ...), condition=%wide.region_4.5_spmd, body=%wide.region_3.4_spmd.sunk | while | flops 268435488 | bytes 6291851 | solution.py:284
  125.6 8.3 %collective-permute-done = bf16[32,4096]{1,0:T(8,128)(2,1)S(1)} collective-permute-done((bf16[32,4096]{1,0:T(8,128)(2,1)S(1)}, bf16[32,4096]{1,0:T(8,128)(2,1)S(1)}, u32[]{:S(2)}, u32[]{:S(2)}) %collective-permute-start) | collective-permute-done | bytes 262176 | tf_op jit(solution)/shard_map/while/body/eval_jaxpr/ppermute | solution.py:16
  140.2 7.4 %collective-permute-done = bf16[32,4096]{1,0:T(8,128)(2,1)S(1)} collective-permute-done((bf16[32,4096]{1,0:T(8,128)(2,1)S(1)}, bf16[32,4096]{1,0:T(8,128)(2,1)S(1)}, u32[]{:S(2)}, u32[]{:S(2)}) %collective-permute-start) | collective-permute-done | bytes 262176 | tf_op jit(solution)/shard_map/while/body/eval_jaxpr/ppermute | solution.py:16
  231.5 7.0 %collective-permute-done = bf16[32,4096]{1,0:T(8,128)(2,1)S(1)} collective-permute-done((bf16[32,4096]{1,0:T(8,128)(2,1)S(1)}, bf16[32,4096]{1,0:T(8,128)(2,1)S(1)}, u32[]{:S(2)}, u32[]{:S(2)}) %collective-permute-start) | collective-permute-done | bytes 262176 | tf_op jit(solution)/shard_map/while/body/eval_jaxpr/ppermute | solution.py:16
  258.2 9.4 %collective-permute-done = bf16[32,4096]{1,0:T(8,128)(2,1)S(1)} collective-permute-done((bf16[32,4096]{1,0:T(8,128)(2,1)S(1)}, bf16[32,4096]{1,0:T(8,128)(2,1)S(1)}, u32[]{:S(2)}, u32[]{:S(2)}) %collective-permute-start) | collective-permute-done | bytes 262176 | tf_op jit(solution)/shard_map/while/body/eval_jaxpr/ppermute | solution.py:16
  273.9 9.4 %collective-permute-done = bf16[32,4096]{1,0:T(8,128)(2,1)S(1)} collective-permute-done((bf16[32,4096]{1,0:T(8,128)(2,1)S(1)}, bf16[32,4096]{1,0:T(8,128)(2,1)S(1)}, u32[]{:S(2)}, u32[]{:S(2)}) %collective-permute-start) | collective-permute-done | bytes 262176 | tf_op jit(solution)/shard_map/while/body/eval_jaxpr/ppermute | solution.py:16
  289.6 9.4 %collective-permute-done = bf16[32,4096]{1,0:T(8,128)(2,1)S(1)} collective-permute-done((bf16[32,4096]{1,0:T(8,128)(2,1)S(1)}, bf16[32,4096]{1,0:T(8,128)(2,1)S(1)}, u32[]{:S(2)}, u32[]{:S(2)}) %collective-permute-start) | collective-permute-done | bytes 262176 | tf_op jit(solution)/shard_map/while/body/eval_jaxpr/ppermute | solution.py:16
  305.4 9.4 %collective-permute-done = bf16[32,4096]{1,0:T(8,128)(2,1)S(1)} collective-permute-done((bf16[32,4096]{1,0:T(8,128)(2,1)S(1)}, bf16[32,4096]{1,0:T(8,128)(2,1)S(1)}, u32[]{:S(2)}, u32[]{:S(2)}) %collective-permute-start) | collective-permute-done | bytes 262176 | tf_op jit(solution)/shard_map/while/body/eval_jaxpr/ppermute | solution.py:16
  321.1 9.4 %collective-permute-done = bf16[32,4096]{1,0:T(8,128)(2,1)S(1)} collective-permute-done((bf16[32,4096]{1,0:T(8,128)(2,1)S(1)}, bf16[32,4096]{1,0:T(8,128)(2,1)S(1)}, u32[]{:S(2)}, u32[]{:S(2)}) %collective-permute-start) | collective-permute-done | bytes 262176 | tf_op jit(solution)/shard_map/while/body/eval_jaxpr/ppermute | solution.py:16
  336.8 10.6 %collective-permute-done = bf16[32,4096]{1,0:T(8,128)(2,1)S(1)} collective-permute-done((bf16[32,4096]{1,0:T(8,128)(2,1)S(1)}, bf16[32,4096]{1,0:T(8,128)(2,1)S(1)}, u32[]{:S(2)}, u32[]{:S(2)}) %collective-permute-start) | collective-permute-done | bytes 262176 | tf_op jit(solution)/shard_map/while/body/eval_jaxpr/ppermute | solution.py:16
  353.8 12.1 %collective-permute-done = bf16[32,4096]{1,0:T(8,128)(2,1)S(1)} collective-permute-done((bf16[32,4096]{1,0:T(8,128)(2,1)S(1)}, bf16[32,4096]{1,0:T(8,128)(2,1)S(1)}, u32[]{:S(2)}, u32[]{:S(2)}) %collective-permute-start) | collective-permute-done | bytes 262176 | tf_op jit(solution)/shard_map/while/body/eval_jaxpr/ppermute | solution.py:16
  372.2 12.9 %collective-permute-done = bf16[32,4096]{1,0:T(8,128)(2,1)S(1)} collective-permute-done((bf16[32,4096]{1,0:T(8,128)(2,1)S(1)}, bf16[32,4096]{1,0:T(8,128)(2,1)S(1)}, u32[]{:S(2)}, u32[]{:S(2)}) %collective-permute-start) | collective-permute-done | bytes 262176 | tf_op jit(solution)/shard_map/while/body/eval_jaxpr/ppermute | solution.py:16
  391.4 12.4 %collective-permute-done = bf16[32,4096]{1,0:T(8,128)(2,1)S(1)} collective-permute-done((bf16[32,4096]{1,0:T(8,128)(2,1)S(1)}, bf16[32,4096]{1,0:T(8,128)(2,1)S(1)}, u32[]{:S(2)}, u32[]{:S(2)}) %collective-permute-start) | collective-permute-done | bytes 262176 | tf_op jit(solution)/shard_map/while/body/eval_jaxpr/ppermute | solution.py:16
  410.1 11.2 %collective-permute-done = bf16[32,4096]{1,0:T(8,128)(2,1)S(1)} collective-permute-done((bf16[32,4096]{1,0:T(8,128)(2,1)S(1)}, bf16[32,4096]{1,0:T(8,128)(2,1)S(1)}, u32[]{:S(2)}, u32[]{:S(2)}) %collective-permute-start) | collective-permute-done | bytes 262176 | tf_op jit(solution)/shard_map/while/body/eval_jaxpr/ppermute | solution.py:16
  427.6 9.0 %collective-permute-done = bf16[32,4096]{1,0:T(8,128)(2,1)S(1)} collective-permute-done((bf16[32,4096]{1,0:T(8,128)(2,1)S(1)}, bf16[32,4096]{1,0:T(8,128)(2,1)S(1)}, u32[]{:S(2)}, u32[]{:S(2)}) %collective-permute-start) | collective-permute-done | bytes 262176 | tf_op jit(solution)/shard_map/while/body/eval_jaxpr/ppermute | solution.py:16
  442.9 9.9 %collective-permute-done = bf16[32,4096]{1,0:T(8,128)(2,1)S(1)} collective-permute-done((bf16[32,4096]{1,0:T(8,128)(2,1)S(1)}, bf16[32,4096]{1,0:T(8,128)(2,1)S(1)}, u32[]{:S(2)}, u32[]{:S(2)}) %collective-permute-start) | collective-permute-done | bytes 262176 | tf_op jit(solution)/shard_map/while/body/eval_jaxpr/ppermute | solution.py:16
  458.4 19.9 %shard_map.61 = bf16[4096,512]{1,0:T(8,128)(2,1)} custom-call(bf16[256,4096]{1,0:T(8,128)(2,1)} %fusion.3.hid_ref, bf16[10,32,4096]{2,1,0:T(8,128)(2,1)S(1)} %get-tuple-element.424.g_ref, bf16[10,32,384]{2,1,0:T(8,128)(2,1)S(1)} %get-tuple-element.425.gp_ref, bf16[256,128]{1,0:T(8,128)(2,1)} %bitcast.64), custom_call_target="tpu_custom_call" | custom-call | tf_op jit(solution)/shard_map/pallas_call | solution.py:195
  478.3 57.1 %all-gather = f32[32,1,4096]{2,1,0:T(1,128)S(1)} all-gather(f32[1,1,4096]{2,1,0:T(1,128)S(1)} %bitcast.61), channel_id=1, replica_groups=mesh['sh'=2,'sy'=8,'fx'=2,'fz'=8,'fc'=2] {'fx','fz','fc'}, dimensions={0}, use_global_device_ids=true | all-gather | bytes 540672 | tf_op jit(solution)/shard_map/all_gather | solution.py:296
  536.4 9.1 %reduce-scatter.4.cloned.1.call-done = bf16[1,2048,512]{2,1,0:T(8,128)(2,1)} async-done(((bf16[2,2048,512]{2,1,0:T(8,128)(2,1)}), bf16[1,2048,512]{2,1,0:T(8,128)(2,1)}) %reduce-scatter.4.cloned.1.call-update) | async-done | bytes 2097168 | tf_op jit(solution)/shard_map/reduce_scatter | solution.py:295
  545.6 51.2 %reduce-scatter.6.cloned.1.call-done = bf16[1,256,512]{2,1,0:T(8,128)(2,1)} async-done(((bf16[8,256,512]{2,1,0:T(8,128)(2,1)}), bf16[1,256,512]{2,1,0:T(8,128)(2,1)}) %reduce-scatter.6.cloned.1.call-update) | async-done | bytes 262160 | tf_op jit(solution)/shard_map/reduce_scatter | solution.py:298
  596.8 24.9 %reduce-scatter.8.cloned.1.call-done = bf16[1,128,512]{2,1,0:T(8,128)(2,1)} async-done(((bf16[2,128,512]{2,1,0:T(8,128)(2,1)}), bf16[1,128,512]{2,1,0:T(8,128)(2,1)}) %reduce-scatter.8.cloned.1.call-update) | async-done | bytes 131088 | tf_op jit(solution)/shard_map/reduce_scatter | solution.py:299
  (124 shorter events, 216.2 us)
Async XLA Ops:
  7.2 55.1 %all-gather.4.cloned.1.call-start = ((), (), s32[]{:S(2)}) async-start(), calls=%async_computation.3 | async-start | bytes 2654208 | tf_op jit(solution)/shard_map/all_gather | solution.py:223
  13.7 76.2 %all-gather.6.cloned.1.call-start = ((), (), s32[]{:S(2)}) async-start(), calls=%async_computation.4 | async-start | bytes 7077888 | tf_op jit(solution)/shard_map/all_gather | solution.py:224
  62.3 483.2 %reduce-scatter.4.cloned.1.call-start = ((), (), s32[]{:S(2)}) async-start(), calls=%async_computation.5 | async-start | bytes 6291456 | tf_op jit(solution)/shard_map/reduce_scatter | solution.py:295
  124.3 9.6 %collective-permute-start = (bf16[32,4096]{1,0:T(8,128)(2,1)S(1)}, bf16[32,4096]{1,0:T(8,128)(2,1)S(1)}, u32[]{:S(2)}, u32[]{:S(2)}) collective-permute-start(bf16[32,4096]{1,0:T(8,128)(2,1)S(1)} %get-tuple-element.651), channel_id=1, source_target_pairs={{32,0},{64,32},{96,64},{128,96},{160,128},{192,160},{224,192},{256... | collective-permute-start | bytes 786440 | tf_op jit(solution)/shard_map/while/body/eval_jaxpr/ppermute | solution.py:16
  138.9 8.7 %collective-permute-start = (bf16[32,4096]{1,0:T(8,128)(2,1)S(1)}, bf16[32,4096]{1,0:T(8,128)(2,1)S(1)}, u32[]{:S(2)}, u32[]{:S(2)}) collective-permute-start(bf16[32,4096]{1,0:T(8,128)(2,1)S(1)} %get-tuple-element.651), channel_id=1, source_target_pairs={{32,0},{64,32},{96,64},{128,96},{160,128},{192,160},{224,192},{256... | collective-permute-start | bytes 786440 | tf_op jit(solution)/shard_map/while/body/eval_jaxpr/ppermute | solution.py:16
  190.5 8.0 %collective-permute-start = (bf16[32,4096]{1,0:T(8,128)(2,1)S(1)}, bf16[32,4096]{1,0:T(8,128)(2,1)S(1)}, u32[]{:S(2)}, u32[]{:S(2)}) collective-permute-start(bf16[32,4096]{1,0:T(8,128)(2,1)S(1)} %get-tuple-element.651), channel_id=1, source_target_pairs={{32,0},{64,32},{96,64},{128,96},{160,128},{192,160},{224,192},{256... | collective-permute-start | bytes 786440 | tf_op jit(solution)/shard_map/while/body/eval_jaxpr/ppermute | solution.py:16
  203.5 8.3 %collective-permute-start = (bf16[32,4096]{1,0:T(8,128)(2,1)S(1)}, bf16[32,4096]{1,0:T(8,128)(2,1)S(1)}, u32[]{:S(2)}, u32[]{:S(2)}) collective-permute-start(bf16[32,4096]{1,0:T(8,128)(2,1)S(1)} %get-tuple-element.651), channel_id=1, source_target_pairs={{32,0},{64,32},{96,64},{128,96},{160,128},{192,160},{224,192},{256... | collective-permute-start | bytes 786440 | tf_op jit(solution)/shard_map/while/body/eval_jaxpr/ppermute | solution.py:16
  216.9 8.3 %collective-permute-start = (bf16[32,4096]{1,0:T(8,128)(2,1)S(1)}, bf16[32,4096]{1,0:T(8,128)(2,1)S(1)}, u32[]{:S(2)}, u32[]{:S(2)}) collective-permute-start(bf16[32,4096]{1,0:T(8,128)(2,1)S(1)} %get-tuple-element.651), channel_id=1, source_target_pairs={{32,0},{64,32},{96,64},{128,96},{160,128},{192,160},{224,192},{256... | collective-permute-start | bytes 786440 | tf_op jit(solution)/shard_map/while/body/eval_jaxpr/ppermute | solution.py:16
  230.2 8.3 %collective-permute-start = (bf16[32,4096]{1,0:T(8,128)(2,1)S(1)}, bf16[32,4096]{1,0:T(8,128)(2,1)S(1)}, u32[]{:S(2)}, u32[]{:S(2)}) collective-permute-start(bf16[32,4096]{1,0:T(8,128)(2,1)S(1)} %get-tuple-element.651), channel_id=1, source_target_pairs={{32,0},{64,32},{96,64},{128,96},{160,128},{192,160},{224,192},{256... | collective-permute-start | bytes 786440 | tf_op jit(solution)/shard_map/while/body/eval_jaxpr/ppermute | solution.py:16
  243.6 8.3 %collective-permute-start = (bf16[32,4096]{1,0:T(8,128)(2,1)S(1)}, bf16[32,4096]{1,0:T(8,128)(2,1)S(1)}, u32[]{:S(2)}, u32[]{:S(2)}) collective-permute-start(bf16[32,4096]{1,0:T(8,128)(2,1)S(1)} %get-tuple-element.651), channel_id=1, source_target_pairs={{32,0},{64,32},{96,64},{128,96},{160,128},{192,160},{224,192},{256... | collective-permute-start | bytes 786440 | tf_op jit(solution)/shard_map/while/body/eval_jaxpr/ppermute | solution.py:16
  256.9 10.7 %collective-permute-start = (bf16[32,4096]{1,0:T(8,128)(2,1)S(1)}, bf16[32,4096]{1,0:T(8,128)(2,1)S(1)}, u32[]{:S(2)}, u32[]{:S(2)}) collective-permute-start(bf16[32,4096]{1,0:T(8,128)(2,1)S(1)} %get-tuple-element.651), channel_id=1, source_target_pairs={{32,0},{64,32},{96,64},{128,96},{160,128},{192,160},{224,192},{256... | collective-permute-start | bytes 786440 | tf_op jit(solution)/shard_map/while/body/eval_jaxpr/ppermute | solution.py:16
  272.6 10.7 %collective-permute-start = (bf16[32,4096]{1,0:T(8,128)(2,1)S(1)}, bf16[32,4096]{1,0:T(8,128)(2,1)S(1)}, u32[]{:S(2)}, u32[]{:S(2)}) collective-permute-start(bf16[32,4096]{1,0:T(8,128)(2,1)S(1)} %get-tuple-element.651), channel_id=1, source_target_pairs={{32,0},{64,32},{96,64},{128,96},{160,128},{192,160},{224,192},{256... | collective-permute-start | bytes 786440 | tf_op jit(solution)/shard_map/while/body/eval_jaxpr/ppermute | solution.py:16
  288.3 10.7 %collective-permute-start = (bf16[32,4096]{1,0:T(8,128)(2,1)S(1)}, bf16[32,4096]{1,0:T(8,128)(2,1)S(1)}, u32[]{:S(2)}, u32[]{:S(2)}) collective-permute-start(bf16[32,4096]{1,0:T(8,128)(2,1)S(1)} %get-tuple-element.651), channel_id=1, source_target_pairs={{32,0},{64,32},{96,64},{128,96},{160,128},{192,160},{224,192},{256... | collective-permute-start | bytes 786440 | tf_op jit(solution)/shard_map/while/body/eval_jaxpr/ppermute | solution.py:16
  304.1 10.7 %collective-permute-start = (bf16[32,4096]{1,0:T(8,128)(2,1)S(1)}, bf16[32,4096]{1,0:T(8,128)(2,1)S(1)}, u32[]{:S(2)}, u32[]{:S(2)}) collective-permute-start(bf16[32,4096]{1,0:T(8,128)(2,1)S(1)} %get-tuple-element.651), channel_id=1, source_target_pairs={{32,0},{64,32},{96,64},{128,96},{160,128},{192,160},{224,192},{256... | collective-permute-start | bytes 786440 | tf_op jit(solution)/shard_map/while/body/eval_jaxpr/ppermute | solution.py:16
  319.8 10.7 %collective-permute-start = (bf16[32,4096]{1,0:T(8,128)(2,1)S(1)}, bf16[32,4096]{1,0:T(8,128)(2,1)S(1)}, u32[]{:S(2)}, u32[]{:S(2)}) collective-permute-start(bf16[32,4096]{1,0:T(8,128)(2,1)S(1)} %get-tuple-element.651), channel_id=1, source_target_pairs={{32,0},{64,32},{96,64},{128,96},{160,128},{192,160},{224,192},{256... | collective-permute-start | bytes 786440 | tf_op jit(solution)/shard_map/while/body/eval_jaxpr/ppermute | solution.py:16
  335.5 11.9 %collective-permute-start = (bf16[32,4096]{1,0:T(8,128)(2,1)S(1)}, bf16[32,4096]{1,0:T(8,128)(2,1)S(1)}, u32[]{:S(2)}, u32[]{:S(2)}) collective-permute-start(bf16[32,4096]{1,0:T(8,128)(2,1)S(1)} %get-tuple-element.651), channel_id=1, source_target_pairs={{32,0},{64,32},{96,64},{128,96},{160,128},{192,160},{224,192},{256... | collective-permute-start | bytes 786440 | tf_op jit(solution)/shard_map/while/body/eval_jaxpr/ppermute | solution.py:16
  352.5 13.4 %collective-permute-start = (bf16[32,4096]{1,0:T(8,128)(2,1)S(1)}, bf16[32,4096]{1,0:T(8,128)(2,1)S(1)}, u32[]{:S(2)}, u32[]{:S(2)}) collective-permute-start(bf16[32,4096]{1,0:T(8,128)(2,1)S(1)} %get-tuple-element.651), channel_id=1, source_target_pairs={{32,0},{64,32},{96,64},{128,96},{160,128},{192,160},{224,192},{256... | collective-permute-start | bytes 786440 | tf_op jit(solution)/shard_map/while/body/eval_jaxpr/ppermute | solution.py:16
  370.9 14.2 %collective-permute-start = (bf16[32,4096]{1,0:T(8,128)(2,1)S(1)}, bf16[32,4096]{1,0:T(8,128)(2,1)S(1)}, u32[]{:S(2)}, u32[]{:S(2)}) collective-permute-start(bf16[32,4096]{1,0:T(8,128)(2,1)S(1)} %get-tuple-element.651), channel_id=1, source_target_pairs={{32,0},{64,32},{96,64},{128,96},{160,128},{192,160},{224,192},{256... | collective-permute-start | bytes 786440 | tf_op jit(solution)/shard_map/while/body/eval_jaxpr/ppermute | solution.py:16
  390.1 13.7 %collective-permute-start = (bf16[32,4096]{1,0:T(8,128)(2,1)S(1)}, bf16[32,4096]{1,0:T(8,128)(2,1)S(1)}, u32[]{:S(2)}, u32[]{:S(2)}) collective-permute-start(bf16[32,4096]{1,0:T(8,128)(2,1)S(1)} %get-tuple-element.651), channel_id=1, source_target_pairs={{32,0},{64,32},{96,64},{128,96},{160,128},{192,160},{224,192},{256... | collective-permute-start | bytes 786440 | tf_op jit(solution)/shard_map/while/body/eval_jaxpr/ppermute | solution.py:16
  408.8 12.5 %collective-permute-start = (bf16[32,4096]{1,0:T(8,128)(2,1)S(1)}, bf16[32,4096]{1,0:T(8,128)(2,1)S(1)}, u32[]{:S(2)}, u32[]{:S(2)}) collective-permute-start(bf16[32,4096]{1,0:T(8,128)(2,1)S(1)} %get-tuple-element.651), channel_id=1, source_target_pairs={{32,0},{64,32},{96,64},{128,96},{160,128},{192,160},{224,192},{256... | collective-permute-start | bytes 786440 | tf_op jit(solution)/shard_map/while/body/eval_jaxpr/ppermute | solution.py:16
  426.3 10.3 %collective-permute-start = (bf16[32,4096]{1,0:T(8,128)(2,1)S(1)}, bf16[32,4096]{1,0:T(8,128)(2,1)S(1)}, u32[]{:S(2)}, u32[]{:S(2)}) collective-permute-start(bf16[32,4096]{1,0:T(8,128)(2,1)S(1)} %get-tuple-element.651), channel_id=1, source_target_pairs={{32,0},{64,32},{96,64},{128,96},{160,128},{192,160},{224,192},{256... | collective-permute-start | bytes 786440 | tf_op jit(solution)/shard_map/while/body/eval_jaxpr/ppermute | solution.py:16
  441.6 11.2 %collective-permute-start = (bf16[32,4096]{1,0:T(8,128)(2,1)S(1)}, bf16[32,4096]{1,0:T(8,128)(2,1)S(1)}, u32[]{:S(2)}, u32[]{:S(2)}) collective-permute-start(bf16[32,4096]{1,0:T(8,128)(2,1)S(1)} %get-tuple-element.651), channel_id=1, source_target_pairs={{32,0},{64,32},{96,64},{128,96},{160,128},{192,160},{224,192},{256... | collective-permute-start | bytes 786440 | tf_op jit(solution)/shard_map/while/body/eval_jaxpr/ppermute | solution.py:16
  478.3 118.5 %reduce-scatter.6.cloned.1.call-start = ((), (), s32[]{:S(2)}) async-start(), calls=%async_computation.6 | async-start | bytes 2359296 | tf_op jit(solution)/shard_map/reduce_scatter | solution.py:298
  545.5 76.2 %reduce-scatter.8.cloned.1.call-start = ((), (), s32[]{:S(2)}) async-start(), calls=%async_computation.7 | async-start | bytes 393216 | tf_op jit(solution)/shard_map/reduce_scatter | solution.py:299
  (10 other events, 103.5 us)
Sparse Core Ops, SparseCore 0:
  13.8 48.4 all-gather.3
  64.3 25.5 all-gather.5
  478.4 67.0 reduce-scatter.3
  548.4 48.2 reduce-scatter.5
  599.6 22.0 reduce-scatter.7

commit v9 on v8

--- a/solution.py
+++ b/solution.py
@@ -293,9 +293,9 @@
     )
     cols = terms.shape[1]
     terms = lax.psum_scatter(terms.reshape(FC, -1, cols), "fc", scatter_dimension=0, tiled=True)
+    terms = lax.psum_scatter(terms.reshape(FZ, -1, cols), "fz", scatter_dimension=0, tiled=True)
     gain_sum = jnp.sum(lax.all_gather(gain_acc, FSDP, axis=0), axis=0)
     terms, gain_sum = lax.optimization_barrier((terms, gain_sum))
-    terms = lax.psum_scatter(terms.reshape(FZ, -1, cols), "fz", scatter_dimension=0, tiled=True)
     terms = lax.psum_scatter(terms.reshape(FX, -1, cols), "fx", scatter_dimension=0, tiled=True)
     shard = terms.reshape(rows_here, cols).astype(jnp.float32)
     return (shard[None], gain_sum[None])

time: 632 us -> 626 us (level)
  blocking collectives: 62.4 us -> 41.8 us
  waiting for transfers between devices: 352 us -> 366 us
    reduce_scatter x1, waiting for transfers between devices: 9.11 us -> 67.2 us  [on_device(): lax.psum_scatter(terms.reshape(FC, -1, cols), 'fc', scatter_dimension=0,...]
    reduce_scatter x1, waiting for transfers between devices: 51.2 us -> 7.75 us  [on_device(): lax.psum_scatter(terms.reshape(FZ, -1, cols), 'fz', scatter_dimension=0,...]
    all_gather x1, blocking collectives: 57.1 us -> 36.5 us  [on_device(): gain_sum = jnp.sum(lax.all_gather(gain_acc, FSDP, axis=0), axis=0)]
where the time goes in v9:
time: 626 us; the launch traced here: 623 us
  waiting for transfers between devices  366 us (58%)
  Pallas kernels  151 us (24%)
  blocking collectives  41.8 us (7%)
  starting transfers between devices  28.6 us (5%)
  other arithmetic  13.9 us (2%)
  between operations  13.9 us (2%)
    ppermute x22, waiting for transfers between devices, passed_along(): lax.ppermute(value, axis, [(source, source + steps) for source in range(l...  195 us
    pallas_call x23, Pallas kernels, tick_call(): pl.pallas_call(tick_kernel, out_shape=(jax.ShapeDtypeStruct((length, widt...  114 us
    reduce_scatter x1, waiting for transfers between devices, on_device(): lax.psum_scatter(terms.reshape(FC, -1, cols), 'fc', scatter_dimension=0,...  67.2 us
    all_gather x1, waiting for transfers between devices, on_device(): staged = lax.all_gather(staged, 'fz', axis=0, tiled=True)  48.5 us
    all_gather x1, blocking collectives, on_device(): gain_sum = jnp.sum(lax.all_gather(gain_acc, FSDP, axis=0), axis=0)  36.5 us
    ppermute x22, starting transfers between devices, passed_along(): lax.ppermute(value, axis, [(source, source + steps) for source in range(l...  28.4 us
    reduce_scatter x1, waiting for transfers between devices, on_device(): lax.psum_scatter(terms.reshape(FX, -1, cols), 'fx', scatter_dimension=0,...  24.3 us
    all_gather x1, waiting for transfers between devices, on_device(): staged = lax.all_gather(staged, 'fc', axis=0, tiled=True)  23.4 us
  transfers between devices with their start and end apart: 27, of which 27 were waited for; matrix products, arithmetic and copies ran while one was open for 1% of the time, Pallas kernels for 0%

profile of v9, /device:TPU:1, one launch (start us, length us, event | category | flops | bytes accessed | tf_op | source)
XLA Modules:
  0.0 623.3 jit_solution(8585245021472994075)
XLA Ops:
  13.7 48.5 %all-gather.4.cloned.1.call-done = bf16[2304,512]{1,0:T(8,128)(2,1)} async-done(((bf16[288,512]{1,0:T(8,128)(2,1)}), bf16[2304,512]{1,0:T(8,128)(2,1)}) %all-gather.4.cloned.1.call-update) | async-done | bytes 2359312 | tf_op jit(solution)/shard_map/all_gather | solution.py:223
  66.5 23.4 %all-gather.6.cloned.1.call-done = bf16[4608,512]{1,0:T(8,128)(2,1)} async-done(((bf16[2304,512]{1,0:T(8,128)(2,1)}), bf16[4608,512]{1,0:T(8,128)(2,1)}) %all-gather.6.cloned.1.call-update) | async-done | bytes 4718608 | tf_op jit(solution)/shard_map/all_gather | solution.py:224
  89.9 17.3 %shard_map.59 = (bf16[4096,384]{1,0:T(8,128)(2,1)S(1)}, bf16[4096,128]{1,0:T(8,128)(2,1)}, f32[1,4096]{1,0:T(1,128)S(1)}) custom-call(bf16[2,8,2,144,512]{4,3,2,1,0:T(8,128)(2,1)} %bitcast.54, bf16[2,8,2,144,512]{4,3,2,1,0:T(8,128)(2,1)} %bitcast.55), custom_call_target="tpu_custom_call" | custom-call | tf_op jit(solution)/shard_map/pallas_call | solution.py:161
  119.2 333.5 %while.21 = (s32[]{:T(128)}, bf16[32,4096]{1,0:T(8,128)(2,1)S(1)}, bf16[10,32,4096]{2,1,0:T(8,128)(2,1)S(1)}, bf16[10,32,384]{2,1,0:T(8,128)(2,1)S(1)}, f32[4096...) while((s32[]{:T(128)}, bf16[32,4096]{1,0:T(8,128)(2,1)S(1)}, ...), condition=%wide.region_4.5_spmd, body=%wide.region_3.4_spmd.sunk | while | flops 268435488 | bytes 6291851 | solution.py:284
  125.6 8.3 %collective-permute-done = bf16[32,4096]{1,0:T(8,128)(2,1)S(1)} collective-permute-done((bf16[32,4096]{1,0:T(8,128)(2,1)S(1)}, bf16[32,4096]{1,0:T(8,128)(2,1)S(1)}, u32[]{:S(2)}, u32[]{:S(2)}) %collective-permute-start) | collective-permute-done | bytes 262176 | tf_op jit(solution)/shard_map/while/body/eval_jaxpr/ppermute | solution.py:16
  140.2 7.4 %collective-permute-done = bf16[32,4096]{1,0:T(8,128)(2,1)S(1)} collective-permute-done((bf16[32,4096]{1,0:T(8,128)(2,1)S(1)}, bf16[32,4096]{1,0:T(8,128)(2,1)S(1)}, u32[]{:S(2)}, u32[]{:S(2)}) %collective-permute-start) | collective-permute-done | bytes 262176 | tf_op jit(solution)/shard_map/while/body/eval_jaxpr/ppermute | solution.py:16
  231.5 7.0 %collective-permute-done = bf16[32,4096]{1,0:T(8,128)(2,1)S(1)} collective-permute-done((bf16[32,4096]{1,0:T(8,128)(2,1)S(1)}, bf16[32,4096]{1,0:T(8,128)(2,1)S(1)}, u32[]{:S(2)}, u32[]{:S(2)}) %collective-permute-start) | collective-permute-done | bytes 262176 | tf_op jit(solution)/shard_map/while/body/eval_jaxpr/ppermute | solution.py:16
  258.2 9.4 %collective-permute-done = bf16[32,4096]{1,0:T(8,128)(2,1)S(1)} collective-permute-done((bf16[32,4096]{1,0:T(8,128)(2,1)S(1)}, bf16[32,4096]{1,0:T(8,128)(2,1)S(1)}, u32[]{:S(2)}, u32[]{:S(2)}) %collective-permute-start) | collective-permute-done | bytes 262176 | tf_op jit(solution)/shard_map/while/body/eval_jaxpr/ppermute | solution.py:16
  273.9 9.4 %collective-permute-done = bf16[32,4096]{1,0:T(8,128)(2,1)S(1)} collective-permute-done((bf16[32,4096]{1,0:T(8,128)(2,1)S(1)}, bf16[32,4096]{1,0:T(8,128)(2,1)S(1)}, u32[]{:S(2)}, u32[]{:S(2)}) %collective-permute-start) | collective-permute-done | bytes 262176 | tf_op jit(solution)/shard_map/while/body/eval_jaxpr/ppermute | solution.py:16
  289.6 9.4 %collective-permute-done = bf16[32,4096]{1,0:T(8,128)(2,1)S(1)} collective-permute-done((bf16[32,4096]{1,0:T(8,128)(2,1)S(1)}, bf16[32,4096]{1,0:T(8,128)(2,1)S(1)}, u32[]{:S(2)}, u32[]{:S(2)}) %collective-permute-start) | collective-permute-done | bytes 262176 | tf_op jit(solution)/shard_map/while/body/eval_jaxpr/ppermute | solution.py:16
  305.4 9.4 %collective-permute-done = bf16[32,4096]{1,0:T(8,128)(2,1)S(1)} collective-permute-done((bf16[32,4096]{1,0:T(8,128)(2,1)S(1)}, bf16[32,4096]{1,0:T(8,128)(2,1)S(1)}, u32[]{:S(2)}, u32[]{:S(2)}) %collective-permute-start) | collective-permute-done | bytes 262176 | tf_op jit(solution)/shard_map/while/body/eval_jaxpr/ppermute | solution.py:16
  321.1 9.4 %collective-permute-done = bf16[32,4096]{1,0:T(8,128)(2,1)S(1)} collective-permute-done((bf16[32,4096]{1,0:T(8,128)(2,1)S(1)}, bf16[32,4096]{1,0:T(8,128)(2,1)S(1)}, u32[]{:S(2)}, u32[]{:S(2)}) %collective-permute-start) | collective-permute-done | bytes 262176 | tf_op jit(solution)/shard_map/while/body/eval_jaxpr/ppermute | solution.py:16
  336.8 10.6 %collective-permute-done = bf16[32,4096]{1,0:T(8,128)(2,1)S(1)} collective-permute-done((bf16[32,4096]{1,0:T(8,128)(2,1)S(1)}, bf16[32,4096]{1,0:T(8,128)(2,1)S(1)}, u32[]{:S(2)}, u32[]{:S(2)}) %collective-permute-start) | collective-permute-done | bytes 262176 | tf_op jit(solution)/shard_map/while/body/eval_jaxpr/ppermute | solution.py:16
  353.8 12.1 %collective-permute-done = bf16[32,4096]{1,0:T(8,128)(2,1)S(1)} collective-permute-done((bf16[32,4096]{1,0:T(8,128)(2,1)S(1)}, bf16[32,4096]{1,0:T(8,128)(2,1)S(1)}, u32[]{:S(2)}, u32[]{:S(2)}) %collective-permute-start) | collective-permute-done | bytes 262176 | tf_op jit(solution)/shard_map/while/body/eval_jaxpr/ppermute | solution.py:16
  372.2 12.9 %collective-permute-done = bf16[32,4096]{1,0:T(8,128)(2,1)S(1)} collective-permute-done((bf16[32,4096]{1,0:T(8,128)(2,1)S(1)}, bf16[32,4096]{1,0:T(8,128)(2,1)S(1)}, u32[]{:S(2)}, u32[]{:S(2)}) %collective-permute-start) | collective-permute-done | bytes 262176 | tf_op jit(solution)/shard_map/while/body/eval_jaxpr/ppermute | solution.py:16
  391.4 12.4 %collective-permute-done = bf16[32,4096]{1,0:T(8,128)(2,1)S(1)} collective-permute-done((bf16[32,4096]{1,0:T(8,128)(2,1)S(1)}, bf16[32,4096]{1,0:T(8,128)(2,1)S(1)}, u32[]{:S(2)}, u32[]{:S(2)}) %collective-permute-start) | collective-permute-done | bytes 262176 | tf_op jit(solution)/shard_map/while/body/eval_jaxpr/ppermute | solution.py:16
  410.1 11.2 %collective-permute-done = bf16[32,4096]{1,0:T(8,128)(2,1)S(1)} collective-permute-done((bf16[32,4096]{1,0:T(8,128)(2,1)S(1)}, bf16[32,4096]{1,0:T(8,128)(2,1)S(1)}, u32[]{:S(2)}, u32[]{:S(2)}) %collective-permute-start) | collective-permute-done | bytes 262176 | tf_op jit(solution)/shard_map/while/body/eval_jaxpr/ppermute | solution.py:16
  427.6 9.0 %collective-permute-done = bf16[32,4096]{1,0:T(8,128)(2,1)S(1)} collective-permute-done((bf16[32,4096]{1,0:T(8,128)(2,1)S(1)}, bf16[32,4096]{1,0:T(8,128)(2,1)S(1)}, u32[]{:S(2)}, u32[]{:S(2)}) %collective-permute-start) | collective-permute-done | bytes 262176 | tf_op jit(solution)/shard_map/while/body/eval_jaxpr/ppermute | solution.py:16
  442.9 9.9 %collective-permute-done = bf16[32,4096]{1,0:T(8,128)(2,1)S(1)} collective-permute-done((bf16[32,4096]{1,0:T(8,128)(2,1)S(1)}, bf16[32,4096]{1,0:T(8,128)(2,1)S(1)}, u32[]{:S(2)}, u32[]{:S(2)}) %collective-permute-start) | collective-permute-done | bytes 262176 | tf_op jit(solution)/shard_map/while/body/eval_jaxpr/ppermute | solution.py:16
  458.4 19.9 %shard_map.61 = bf16[4096,512]{1,0:T(8,128)(2,1)} custom-call(bf16[256,4096]{1,0:T(8,128)(2,1)} %fusion.3.hid_ref, bf16[10,32,4096]{2,1,0:T(8,128)(2,1)S(1)} %get-tuple-element.424.g_ref, bf16[10,32,384]{2,1,0:T(8,128)(2,1)S(1)} %get-tuple-element.425.gp_ref, bf16[256,128]{1,0:T(8,128)(2,1)} %bitcast.64), custom_call_target="tpu_custom_call" | custom-call | tf_op jit(solution)/shard_map/pallas_call | solution.py:195
  478.3 67.2 %reduce-scatter.4.cloned.1.call-done = bf16[1,2048,512]{2,1,0:T(8,128)(2,1)} async-done(((bf16[2,2048,512]{2,1,0:T(8,128)(2,1)}), bf16[1,2048,512]{2,1,0:T(8,128)(2,1)}) %reduce-scatter.4.cloned.1.call-update) | async-done | bytes 2097168 | tf_op jit(solution)/shard_map/reduce_scatter | solution.py:295
  545.6 36.5 %all-gather = f32[32,1,4096]{2,1,0:T(1,128)S(1)} all-gather(f32[1,1,4096]{2,1,0:T(1,128)S(1)} %bitcast.61), channel_id=1, replica_groups=mesh['sh'=2,'sy'=8,'fx'=2,'fz'=8,'fc'=2] {'fx','fz','fc'}, dimensions={0}, use_global_device_ids=true | all-gather | bytes 540672 | tf_op jit(solution)/shard_map/all_gather | solution.py:297
  583.1 7.7 %reduce-scatter.6.cloned.1.call-done = bf16[1,256,512]{2,1,0:T(8,128)(2,1)} async-done(((bf16[8,256,512]{2,1,0:T(8,128)(2,1)}), bf16[1,256,512]{2,1,0:T(8,128)(2,1)}) %reduce-scatter.6.cloned.1.call-update) | async-done | bytes 262160 | tf_op jit(solution)/shard_map/reduce_scatter | solution.py:296
  590.8 24.3 %reduce-scatter.8.cloned.1.call-done = bf16[1,128,512]{2,1,0:T(8,128)(2,1)} async-done(((bf16[2,128,512]{2,1,0:T(8,128)(2,1)}), bf16[1,128,512]{2,1,0:T(8,128)(2,1)}) %reduce-scatter.8.cloned.1.call-update) | async-done | bytes 131088 | tf_op jit(solution)/shard_map/reduce_scatter | solution.py:299
  (124 shorter events, 216.2 us)
Async XLA Ops:
  7.2 55.1 %all-gather.4.cloned.1.call-start = ((), (), s32[]{:S(2)}) async-start(), calls=%async_computation.3 | async-start | bytes 2654208 | tf_op jit(solution)/shard_map/all_gather | solution.py:223
  13.7 76.2 %all-gather.6.cloned.1.call-start = ((), (), s32[]{:S(2)}) async-start(), calls=%async_computation.4 | async-start | bytes 7077888 | tf_op jit(solution)/shard_map/all_gather | solution.py:224
  62.3 483.2 %reduce-scatter.4.cloned.1.call-start = ((), (), s32[]{:S(2)}) async-start(), calls=%async_computation.5 | async-start | bytes 6291456 | tf_op jit(solution)/shard_map/reduce_scatter | solution.py:295
  124.3 9.6 %collective-permute-start = (bf16[32,4096]{1,0:T(8,128)(2,1)S(1)}, bf16[32,4096]{1,0:T(8,128)(2,1)S(1)}, u32[]{:S(2)}, u32[]{:S(2)}) collective-permute-start(bf16[32,4096]{1,0:T(8,128)(2,1)S(1)} %get-tuple-element.651), channel_id=1, source_target_pairs={{32,0},{64,32},{96,64},{128,96},{160,128},{192,160},{224,192},{256... | collective-permute-start | bytes 786440 | tf_op jit(solution)/shard_map/while/body/eval_jaxpr/ppermute | solution.py:16
  138.9 8.7 %collective-permute-start = (bf16[32,4096]{1,0:T(8,128)(2,1)S(1)}, bf16[32,4096]{1,0:T(8,128)(2,1)S(1)}, u32[]{:S(2)}, u32[]{:S(2)}) collective-permute-start(bf16[32,4096]{1,0:T(8,128)(2,1)S(1)} %get-tuple-element.651), channel_id=1, source_target_pairs={{32,0},{64,32},{96,64},{128,96},{160,128},{192,160},{224,192},{256... | collective-permute-start | bytes 786440 | tf_op jit(solution)/shard_map/while/body/eval_jaxpr/ppermute | solution.py:16
  190.5 8.0 %collective-permute-start = (bf16[32,4096]{1,0:T(8,128)(2,1)S(1)}, bf16[32,4096]{1,0:T(8,128)(2,1)S(1)}, u32[]{:S(2)}, u32[]{:S(2)}) collective-permute-start(bf16[32,4096]{1,0:T(8,128)(2,1)S(1)} %get-tuple-element.651), channel_id=1, source_target_pairs={{32,0},{64,32},{96,64},{128,96},{160,128},{192,160},{224,192},{256... | collective-permute-start | bytes 786440 | tf_op jit(solution)/shard_map/while/body/eval_jaxpr/ppermute | solution.py:16
  203.5 8.3 %collective-permute-start = (bf16[32,4096]{1,0:T(8,128)(2,1)S(1)}, bf16[32,4096]{1,0:T(8,128)(2,1)S(1)}, u32[]{:S(2)}, u32[]{:S(2)}) collective-permute-start(bf16[32,4096]{1,0:T(8,128)(2,1)S(1)} %get-tuple-element.651), channel_id=1, source_target_pairs={{32,0},{64,32},{96,64},{128,96},{160,128},{192,160},{224,192},{256... | collective-permute-start | bytes 786440 | tf_op jit(solution)/shard_map/while/body/eval_jaxpr/ppermute | solution.py:16
  216.9 8.3 %collective-permute-start = (bf16[32,4096]{1,0:T(8,128)(2,1)S(1)}, bf16[32,4096]{1,0:T(8,128)(2,1)S(1)}, u32[]{:S(2)}, u32[]{:S(2)}) collective-permute-start(bf16[32,4096]{1,0:T(8,128)(2,1)S(1)} %get-tuple-element.651), channel_id=1, source_target_pairs={{32,0},{64,32},{96,64},{128,96},{160,128},{192,160},{224,192},{256... | collective-permute-start | bytes 786440 | tf_op jit(solution)/shard_map/while/body/eval_jaxpr/ppermute | solution.py:16
  230.2 8.3 %collective-permute-start = (bf16[32,4096]{1,0:T(8,128)(2,1)S(1)}, bf16[32,4096]{1,0:T(8,128)(2,1)S(1)}, u32[]{:S(2)}, u32[]{:S(2)}) collective-permute-start(bf16[32,4096]{1,0:T(8,128)(2,1)S(1)} %get-tuple-element.651), channel_id=1, source_target_pairs={{32,0},{64,32},{96,64},{128,96},{160,128},{192,160},{224,192},{256... | collective-permute-start | bytes 786440 | tf_op jit(solution)/shard_map/while/body/eval_jaxpr/ppermute | solution.py:16
  243.6 8.3 %collective-permute-start = (bf16[32,4096]{1,0:T(8,128)(2,1)S(1)}, bf16[32,4096]{1,0:T(8,128)(2,1)S(1)}, u32[]{:S(2)}, u32[]{:S(2)}) collective-permute-start(bf16[32,4096]{1,0:T(8,128)(2,1)S(1)} %get-tuple-element.651), channel_id=1, source_target_pairs={{32,0},{64,32},{96,64},{128,96},{160,128},{192,160},{224,192},{256... | collective-permute-start | bytes 786440 | tf_op jit(solution)/shard_map/while/body/eval_jaxpr/ppermute | solution.py:16
  256.9 10.7 %collective-permute-start = (bf16[32,4096]{1,0:T(8,128)(2,1)S(1)}, bf16[32,4096]{1,0:T(8,128)(2,1)S(1)}, u32[]{:S(2)}, u32[]{:S(2)}) collective-permute-start(bf16[32,4096]{1,0:T(8,128)(2,1)S(1)} %get-tuple-element.651), channel_id=1, source_target_pairs={{32,0},{64,32},{96,64},{128,96},{160,128},{192,160},{224,192},{256... | collective-permute-start | bytes 786440 | tf_op jit(solution)/shard_map/while/body/eval_jaxpr/ppermute | solution.py:16
  272.6 10.7 %collective-permute-start = (bf16[32,4096]{1,0:T(8,128)(2,1)S(1)}, bf16[32,4096]{1,0:T(8,128)(2,1)S(1)}, u32[]{:S(2)}, u32[]{:S(2)}) collective-permute-start(bf16[32,4096]{1,0:T(8,128)(2,1)S(1)} %get-tuple-element.651), channel_id=1, source_target_pairs={{32,0},{64,32},{96,64},{128,96},{160,128},{192,160},{224,192},{256... | collective-permute-start | bytes 786440 | tf_op jit(solution)/shard_map/while/body/eval_jaxpr/ppermute | solution.py:16
  288.3 10.7 %collective-permute-start = (bf16[32,4096]{1,0:T(8,128)(2,1)S(1)}, bf16[32,4096]{1,0:T(8,128)(2,1)S(1)}, u32[]{:S(2)}, u32[]{:S(2)}) collective-permute-start(bf16[32,4096]{1,0:T(8,128)(2,1)S(1)} %get-tuple-element.651), channel_id=1, source_target_pairs={{32,0},{64,32},{96,64},{128,96},{160,128},{192,160},{224,192},{256... | collective-permute-start | bytes 786440 | tf_op jit(solution)/shard_map/while/body/eval_jaxpr/ppermute | solution.py:16
  304.1 10.7 %collective-permute-start = (bf16[32,4096]{1,0:T(8,128)(2,1)S(1)}, bf16[32,4096]{1,0:T(8,128)(2,1)S(1)}, u32[]{:S(2)}, u32[]{:S(2)}) collective-permute-start(bf16[32,4096]{1,0:T(8,128)(2,1)S(1)} %get-tuple-element.651), channel_id=1, source_target_pairs={{32,0},{64,32},{96,64},{128,96},{160,128},{192,160},{224,192},{256... | collective-permute-start | bytes 786440 | tf_op jit(solution)/shard_map/while/body/eval_jaxpr/ppermute | solution.py:16
  319.8 10.7 %collective-permute-start = (bf16[32,4096]{1,0:T(8,128)(2,1)S(1)}, bf16[32,4096]{1,0:T(8,128)(2,1)S(1)}, u32[]{:S(2)}, u32[]{:S(2)}) collective-permute-start(bf16[32,4096]{1,0:T(8,128)(2,1)S(1)} %get-tuple-element.651), channel_id=1, source_target_pairs={{32,0},{64,32},{96,64},{128,96},{160,128},{192,160},{224,192},{256... | collective-permute-start | bytes 786440 | tf_op jit(solution)/shard_map/while/body/eval_jaxpr/ppermute | solution.py:16
  335.5 11.9 %collective-permute-start = (bf16[32,4096]{1,0:T(8,128)(2,1)S(1)}, bf16[32,4096]{1,0:T(8,128)(2,1)S(1)}, u32[]{:S(2)}, u32[]{:S(2)}) collective-permute-start(bf16[32,4096]{1,0:T(8,128)(2,1)S(1)} %get-tuple-element.651), channel_id=1, source_target_pairs={{32,0},{64,32},{96,64},{128,96},{160,128},{192,160},{224,192},{256... | collective-permute-start | bytes 786440 | tf_op jit(solution)/shard_map/while/body/eval_jaxpr/ppermute | solution.py:16
  352.5 13.4 %collective-permute-start = (bf16[32,4096]{1,0:T(8,128)(2,1)S(1)}, bf16[32,4096]{1,0:T(8,128)(2,1)S(1)}, u32[]{:S(2)}, u32[]{:S(2)}) collective-permute-start(bf16[32,4096]{1,0:T(8,128)(2,1)S(1)} %get-tuple-element.651), channel_id=1, source_target_pairs={{32,0},{64,32},{96,64},{128,96},{160,128},{192,160},{224,192},{256... | collective-permute-start | bytes 786440 | tf_op jit(solution)/shard_map/while/body/eval_jaxpr/ppermute | solution.py:16
  370.9 14.2 %collective-permute-start = (bf16[32,4096]{1,0:T(8,128)(2,1)S(1)}, bf16[32,4096]{1,0:T(8,128)(2,1)S(1)}, u32[]{:S(2)}, u32[]{:S(2)}) collective-permute-start(bf16[32,4096]{1,0:T(8,128)(2,1)S(1)} %get-tuple-element.651), channel_id=1, source_target_pairs={{32,0},{64,32},{96,64},{128,96},{160,128},{192,160},{224,192},{256... | collective-permute-start | bytes 786440 | tf_op jit(solution)/shard_map/while/body/eval_jaxpr/ppermute | solution.py:16
  390.1 13.7 %collective-permute-start = (bf16[32,4096]{1,0:T(8,128)(2,1)S(1)}, bf16[32,4096]{1,0:T(8,128)(2,1)S(1)}, u32[]{:S(2)}, u32[]{:S(2)}) collective-permute-start(bf16[32,4096]{1,0:T(8,128)(2,1)S(1)} %get-tuple-element.651), channel_id=1, source_target_pairs={{32,0},{64,32},{96,64},{128,96},{160,128},{192,160},{224,192},{256... | collective-permute-start | bytes 786440 | tf_op jit(solution)/shard_map/while/body/eval_jaxpr/ppermute | solution.py:16
  408.8 12.5 %collective-permute-start = (bf16[32,4096]{1,0:T(8,128)(2,1)S(1)}, bf16[32,4096]{1,0:T(8,128)(2,1)S(1)}, u32[]{:S(2)}, u32[]{:S(2)}) collective-permute-start(bf16[32,4096]{1,0:T(8,128)(2,1)S(1)} %get-tuple-element.651), channel_id=1, source_target_pairs={{32,0},{64,32},{96,64},{128,96},{160,128},{192,160},{224,192},{256... | collective-permute-start | bytes 786440 | tf_op jit(solution)/shard_map/while/body/eval_jaxpr/ppermute | solution.py:16
  426.3 10.3 %collective-permute-start = (bf16[32,4096]{1,0:T(8,128)(2,1)S(1)}, bf16[32,4096]{1,0:T(8,128)(2,1)S(1)}, u32[]{:S(2)}, u32[]{:S(2)}) collective-permute-start(bf16[32,4096]{1,0:T(8,128)(2,1)S(1)} %get-tuple-element.651), channel_id=1, source_target_pairs={{32,0},{64,32},{96,64},{128,96},{160,128},{192,160},{224,192},{256... | collective-permute-start | bytes 786440 | tf_op jit(solution)/shard_map/while/body/eval_jaxpr/ppermute | solution.py:16
  441.6 11.2 %collective-permute-start = (bf16[32,4096]{1,0:T(8,128)(2,1)S(1)}, bf16[32,4096]{1,0:T(8,128)(2,1)S(1)}, u32[]{:S(2)}, u32[]{:S(2)}) collective-permute-start(bf16[32,4096]{1,0:T(8,128)(2,1)S(1)} %get-tuple-element.651), channel_id=1, source_target_pairs={{32,0},{64,32},{96,64},{128,96},{160,128},{192,160},{224,192},{256... | collective-permute-start | bytes 786440 | tf_op jit(solution)/shard_map/while/body/eval_jaxpr/ppermute | solution.py:16
  478.3 112.5 %reduce-scatter.6.cloned.1.call-start = ((), (), s32[]{:S(2)}) async-start(), calls=%async_computation.6 | async-start | bytes 2359296 | tf_op jit(solution)/shard_map/reduce_scatter | solution.py:296
  545.5 69.6 %reduce-scatter.8.cloned.1.call-start = ((), (), s32[]{:S(2)}) async-start(), calls=%async_computation.7 | async-start | bytes 393216 | tf_op jit(solution)/shard_map/reduce_scatter | solution.py:299
  (10 other events, 103.5 us)
Sparse Core Ops, SparseCore 0:
  13.8 48.4 all-gather.3
  64.3 25.5 all-gather.5
  478.4 67.0 reduce-scatter.3
  548.4 42.3 reduce-scatter.5
  593.7 21.4 reduce-scatter.7

commit v10 on v9

--- a/solution.py
+++ b/solution.py
@@ -148,35 +148,35 @@
 
 def unpack_kernel(rows_ref, gain_ref, wp_ref, wb_ref, gain_out):
     proj_cols = wp_ref.shape[-1]
-    block = rows_ref[...]
-    wp_ref[...] = block[:, :proj_cols]
-    wb_ref[...] = block[:, proj_cols:]
-    gain_out[...] = gain_ref[0:1, : gain_out.shape[-1]].astype(jnp.float32)
+    rows = rows_ref.shape[1]
+    for core in range(rows_ref.shape[0]):
+        block = rows_ref[core]
+        wp_ref[core * rows : (core + 1) * rows, :] = block[:, :proj_cols]
+        wb_ref[core * rows : (core + 1) * rows, :] = block[:, proj_cols:]
+        gain_out[core : core + 1, :] = gain_ref[core, 0:1, : gain_out.shape[-1]].astype(jnp.float32)
 
 
 def unpack_weights(staged, rows_here, head):
     cols = staged.shape[-1]
     groups = FC * FZ * FX
-    natural = lambda c, z, x: x * (FZ * FC) + z * FC + c
     return pl.pallas_call(
         unpack_kernel,
         out_shape=(
             jax.ShapeDtypeStruct((groups * rows_here, 3 * head), staged.dtype),
             jax.ShapeDtypeStruct((groups * rows_here, cols - 3 * head), staged.dtype),
-            jax.ShapeDtypeStruct((1, groups * rows_here), jnp.float32),
-        ),
-        grid=(FC, FZ, FX),
+            jax.ShapeDtypeStruct((FX * FZ, FC, rows_here), jnp.float32),
+        ),
+        grid=(FX, FZ),
         in_specs=[
-            pl.BlockSpec((None, None, None, rows_here, cols), lambda c, z, x: (c, z, x, 0, 0)),
-            pl.BlockSpec((None, None, None, 16, cols), lambda c, z, x: (c, z, x, rows_here // 16, 0)),
+            pl.BlockSpec((FC, None, None, rows_here, cols), lambda x, z: (0, z, x, 0, 0)),
+            pl.BlockSpec((FC, None, None, 16, cols), lambda x, z: (0, z, x, rows_here // 16, 0)),
         ],
         out_specs=[
-            pl.BlockSpec((rows_here, 3 * head), lambda c, z, x: (natural(c, z, x), 0)),
-            pl.BlockSpec((rows_here, cols - 3 * head), lambda c, z, x: (natural(c, z, x), 0)),
-            pl.BlockSpec((1, rows_here), lambda c, z, x: (0, natural(c, z, x))),
+            pl.BlockSpec((FC * rows_here, 3 * head), lambda x, z: (x * FZ + z, 0)),
+            pl.BlockSpec((FC * rows_here, cols - 3 * head), lambda x, z: (x * FZ + z, 0)),
+            pl.BlockSpec((None, FC, rows_here), lambda x, z: (x * FZ + z, 0, 0)),
         ],
     )(staged, staged)
-
 
 def terms_kernel(hid_ref, g_ref, gp_ref, att_ref, out_ref):
     tokens = hid_ref.shape[0]
@@ -225,6 +225,7 @@
     w_proj, w_back, gain_row = unpack_weights(
         staged.reshape(FC, FZ, FX, rows_here + 16, weights.shape[2]), rows_here, head
     )
+    gain_row = gain_row.reshape(1, groups * rows_here)
     wide_gain = gain_row.reshape(groups * rows_here)
 
     xfloat = inputs[0].astype(jnp.float32)

time: 626 us -> 618 us (0.987)
  Pallas kernels: 151 us -> 144 us
    pallas_call x1, Pallas kernels: 17.3 us -> 9.7 us  [unpack_weights(): pl.pallas_call(unpack_kernel, out_shape=(jax.ShapeDtypeStruct((groups * r...]
where the time goes in v10:
time: 618 us; the launch traced here: 616 us
  waiting for transfers between devices  366 us (59%)
  Pallas kernels  144 us (23%)
  blocking collectives  41.8 us (7%)
  starting transfers between devices  28.6 us (5%)
  other arithmetic  13.9 us (2%)
  between operations  13.9 us (2%)
    ppermute x22, waiting for transfers between devices, passed_along(): lax.ppermute(value, axis, [(source, source + steps) for source in range(l...  195 us
    pallas_call x23, Pallas kernels, tick_call(): pl.pallas_call(tick_kernel, out_shape=(jax.ShapeDtypeStruct((length, widt...  114 us
    reduce_scatter x1, waiting for transfers between devices, on_device(): lax.psum_scatter(terms.reshape(FC, -1, cols), 'fc', scatter_dimension=0,...  67.1 us
    all_gather x1, waiting for transfers between devices, on_device(): staged = lax.all_gather(staged, 'fz', axis=0, tiled=True)  48.5 us
    all_gather x1, blocking collectives, on_device(): gain_sum = jnp.sum(lax.all_gather(gain_acc, FSDP, axis=0), axis=0)  36.5 us
    ppermute x22, starting transfers between devices, passed_along(): lax.ppermute(value, axis, [(source, source + steps) for source in range(l...  28.4 us
    reduce_scatter x1, waiting for transfers between devices, on_device(): lax.psum_scatter(terms.reshape(FX, -1, cols), 'fx', scatter_dimension=0,...  24.6 us
    all_gather x1, waiting for transfers between devices, on_device(): staged = lax.all_gather(staged, 'fc', axis=0, tiled=True)  23.4 us
  transfers between devices with their start and end apart: 27, of which 27 were waited for; matrix products, arithmetic and copies ran while one was open for 1% of the time, Pallas kernels for 0%

profile of v10, /device:TPU:1, one launch (start us, length us, event | category | flops | bytes accessed | tf_op | source)
XLA Modules:
  0.0 615.8 jit_solution(9647964881441362238)
XLA Ops:
  13.7 48.5 %all-gather.4.cloned.1.call-done = bf16[2304,512]{1,0:T(8,128)(2,1)} async-done(((bf16[288,512]{1,0:T(8,128)(2,1)}), bf16[2304,512]{1,0:T(8,128)(2,1)}) %all-gather.4.cloned.1.call-update) | async-done | bytes 2359312 | tf_op jit(solution)/shard_map/all_gather | solution.py:223
  66.5 23.4 %all-gather.6.cloned.1.call-done = bf16[4608,512]{1,0:T(8,128)(2,1)} async-done(((bf16[2304,512]{1,0:T(8,128)(2,1)}), bf16[4608,512]{1,0:T(8,128)(2,1)}) %all-gather.6.cloned.1.call-update) | async-done | bytes 4718608 | tf_op jit(solution)/shard_map/all_gather | solution.py:224
  89.9 9.7 %shard_map.59 = (bf16[4096,384]{1,0:T(8,128)(2,1)S(1)}, bf16[4096,128]{1,0:T(8,128)(2,1)}, f32[16,2,128]{2,1,0:T(2,128)S(1)}) custom-call(bf16[2,8,2,144,512]{4,3,2,1,0:T(8,128)(2,1)} %bitcast.55, bf16[2,8,2,144,512]{4,3,2,1,0:T(8,128)(2,1)} %bitcast.56), custom_call_target="tpu_custom_call" | custom-call | tf_op jit(solution)/shard_map/pallas_call | solution.py:162
  111.6 333.6 %while.21 = (s32[]{:T(128)}, bf16[32,4096]{1,0:T(8,128)(2,1)S(1)}, bf16[10,32,4096]{2,1,0:T(8,128)(2,1)S(1)}, bf16[10,32,384]{2,1,0:T(8,128)(2,1)S(1)}, f32[4096...) while((s32[]{:T(128)}, bf16[32,4096]{1,0:T(8,128)(2,1)S(1)}, ...), condition=%wide.region_4.5_spmd, body=%wide.region_3.4_spmd.sunk | while | flops 268435488 | bytes 6291851 | solution.py:285
  118.0 8.3 %collective-permute-done = bf16[32,4096]{1,0:T(8,128)(2,1)S(1)} collective-permute-done((bf16[32,4096]{1,0:T(8,128)(2,1)S(1)}, bf16[32,4096]{1,0:T(8,128)(2,1)S(1)}, u32[]{:S(2)}, u32[]{:S(2)}) %collective-permute-start) | collective-permute-done | bytes 262176 | tf_op jit(solution)/shard_map/while/body/eval_jaxpr/ppermute | solution.py:16
  132.6 7.4 %collective-permute-done = bf16[32,4096]{1,0:T(8,128)(2,1)S(1)} collective-permute-done((bf16[32,4096]{1,0:T(8,128)(2,1)S(1)}, bf16[32,4096]{1,0:T(8,128)(2,1)S(1)}, u32[]{:S(2)}, u32[]{:S(2)}) %collective-permute-start) | collective-permute-done | bytes 262176 | tf_op jit(solution)/shard_map/while/body/eval_jaxpr/ppermute | solution.py:16
  224.0 7.0 %collective-permute-done = bf16[32,4096]{1,0:T(8,128)(2,1)S(1)} collective-permute-done((bf16[32,4096]{1,0:T(8,128)(2,1)S(1)}, bf16[32,4096]{1,0:T(8,128)(2,1)S(1)}, u32[]{:S(2)}, u32[]{:S(2)}) %collective-permute-start) | collective-permute-done | bytes 262176 | tf_op jit(solution)/shard_map/while/body/eval_jaxpr/ppermute | solution.py:16
  250.7 9.2 %collective-permute-done = bf16[32,4096]{1,0:T(8,128)(2,1)S(1)} collective-permute-done((bf16[32,4096]{1,0:T(8,128)(2,1)S(1)}, bf16[32,4096]{1,0:T(8,128)(2,1)S(1)}, u32[]{:S(2)}, u32[]{:S(2)}) %collective-permute-start) | collective-permute-done | bytes 262176 | tf_op jit(solution)/shard_map/while/body/eval_jaxpr/ppermute | solution.py:16
  266.2 9.4 %collective-permute-done = bf16[32,4096]{1,0:T(8,128)(2,1)S(1)} collective-permute-done((bf16[32,4096]{1,0:T(8,128)(2,1)S(1)}, bf16[32,4096]{1,0:T(8,128)(2,1)S(1)}, u32[]{:S(2)}, u32[]{:S(2)}) %collective-permute-start) | collective-permute-done | bytes 262176 | tf_op jit(solution)/shard_map/while/body/eval_jaxpr/ppermute | solution.py:16
  281.9 9.4 %collective-permute-done = bf16[32,4096]{1,0:T(8,128)(2,1)S(1)} collective-permute-done((bf16[32,4096]{1,0:T(8,128)(2,1)S(1)}, bf16[32,4096]{1,0:T(8,128)(2,1)S(1)}, u32[]{:S(2)}, u32[]{:S(2)}) %collective-permute-start) | collective-permute-done | bytes 262176 | tf_op jit(solution)/shard_map/while/body/eval_jaxpr/ppermute | solution.py:16
  297.7 9.4 %collective-permute-done = bf16[32,4096]{1,0:T(8,128)(2,1)S(1)} collective-permute-done((bf16[32,4096]{1,0:T(8,128)(2,1)S(1)}, bf16[32,4096]{1,0:T(8,128)(2,1)S(1)}, u32[]{:S(2)}, u32[]{:S(2)}) %collective-permute-start) | collective-permute-done | bytes 262176 | tf_op jit(solution)/shard_map/while/body/eval_jaxpr/ppermute | solution.py:16
  313.4 9.4 %collective-permute-done = bf16[32,4096]{1,0:T(8,128)(2,1)S(1)} collective-permute-done((bf16[32,4096]{1,0:T(8,128)(2,1)S(1)}, bf16[32,4096]{1,0:T(8,128)(2,1)S(1)}, u32[]{:S(2)}, u32[]{:S(2)}) %collective-permute-start) | collective-permute-done | bytes 262176 | tf_op jit(solution)/shard_map/while/body/eval_jaxpr/ppermute | solution.py:16
  329.1 10.7 %collective-permute-done = bf16[32,4096]{1,0:T(8,128)(2,1)S(1)} collective-permute-done((bf16[32,4096]{1,0:T(8,128)(2,1)S(1)}, bf16[32,4096]{1,0:T(8,128)(2,1)S(1)}, u32[]{:S(2)}, u32[]{:S(2)}) %collective-permute-start) | collective-permute-done | bytes 262176 | tf_op jit(solution)/shard_map/while/body/eval_jaxpr/ppermute | solution.py:16
  346.1 12.1 %collective-permute-done = bf16[32,4096]{1,0:T(8,128)(2,1)S(1)} collective-permute-done((bf16[32,4096]{1,0:T(8,128)(2,1)S(1)}, bf16[32,4096]{1,0:T(8,128)(2,1)S(1)}, u32[]{:S(2)}, u32[]{:S(2)}) %collective-permute-start) | collective-permute-done | bytes 262176 | tf_op jit(solution)/shard_map/while/body/eval_jaxpr/ppermute | solution.py:16
  364.5 12.9 %collective-permute-done = bf16[32,4096]{1,0:T(8,128)(2,1)S(1)} collective-permute-done((bf16[32,4096]{1,0:T(8,128)(2,1)S(1)}, bf16[32,4096]{1,0:T(8,128)(2,1)S(1)}, u32[]{:S(2)}, u32[]{:S(2)}) %collective-permute-start) | collective-permute-done | bytes 262176 | tf_op jit(solution)/shard_map/while/body/eval_jaxpr/ppermute | solution.py:16
  383.8 12.5 %collective-permute-done = bf16[32,4096]{1,0:T(8,128)(2,1)S(1)} collective-permute-done((bf16[32,4096]{1,0:T(8,128)(2,1)S(1)}, bf16[32,4096]{1,0:T(8,128)(2,1)S(1)}, u32[]{:S(2)}, u32[]{:S(2)}) %collective-permute-start) | collective-permute-done | bytes 262176 | tf_op jit(solution)/shard_map/while/body/eval_jaxpr/ppermute | solution.py:16
  402.5 11.0 %collective-permute-done = bf16[32,4096]{1,0:T(8,128)(2,1)S(1)} collective-permute-done((bf16[32,4096]{1,0:T(8,128)(2,1)S(1)}, bf16[32,4096]{1,0:T(8,128)(2,1)S(1)}, u32[]{:S(2)}, u32[]{:S(2)}) %collective-permute-start) | collective-permute-done | bytes 262176 | tf_op jit(solution)/shard_map/while/body/eval_jaxpr/ppermute | solution.py:16
  419.9 8.9 %collective-permute-done = bf16[32,4096]{1,0:T(8,128)(2,1)S(1)} collective-permute-done((bf16[32,4096]{1,0:T(8,128)(2,1)S(1)}, bf16[32,4096]{1,0:T(8,128)(2,1)S(1)}, u32[]{:S(2)}, u32[]{:S(2)}) %collective-permute-start) | collective-permute-done | bytes 262176 | tf_op jit(solution)/shard_map/while/body/eval_jaxpr/ppermute | solution.py:16
  435.1 10.1 %collective-permute-done = bf16[32,4096]{1,0:T(8,128)(2,1)S(1)} collective-permute-done((bf16[32,4096]{1,0:T(8,128)(2,1)S(1)}, bf16[32,4096]{1,0:T(8,128)(2,1)S(1)}, u32[]{:S(2)}, u32[]{:S(2)}) %collective-permute-start) | collective-permute-done | bytes 262176 | tf_op jit(solution)/shard_map/while/body/eval_jaxpr/ppermute | solution.py:16
  450.8 19.9 %shard_map.61 = bf16[4096,512]{1,0:T(8,128)(2,1)} custom-call(bf16[256,4096]{1,0:T(8,128)(2,1)} %fusion.3.hid_ref, bf16[10,32,4096]{2,1,0:T(8,128)(2,1)S(1)} %get-tuple-element.424.g_ref, bf16[10,32,384]{2,1,0:T(8,128)(2,1)S(1)} %get-tuple-element.425.gp_ref, bf16[256,128]{1,0:T(8,128)(2,1)} %bitcast.66), custom_call_target="tpu_custom_call" | custom-call | tf_op jit(solution)/shard_map/pallas_call | solution.py:195
  470.8 67.1 %reduce-scatter.4.cloned.1.call-done = bf16[1,2048,512]{2,1,0:T(8,128)(2,1)} async-done(((bf16[2,2048,512]{2,1,0:T(8,128)(2,1)}), bf16[1,2048,512]{2,1,0:T(8,128)(2,1)}) %reduce-scatter.4.cloned.1.call-update) | async-done | bytes 2097168 | tf_op jit(solution)/shard_map/reduce_scatter | solution.py:296
  537.9 36.5 %all-gather = f32[32,1,4096]{2,1,0:T(1,128)S(1)} all-gather(f32[1,1,4096]{2,1,0:T(1,128)S(1)} %bitcast.62), channel_id=1, replica_groups=mesh['sh'=2,'sy'=8,'fx'=2,'fz'=8,'fc'=2] {'fx','fz','fc'}, dimensions={0}, use_global_device_ids=true | all-gather | bytes 540672 | tf_op jit(solution)/shard_map/all_gather | solution.py:298
  575.4 7.6 %reduce-scatter.6.cloned.1.call-done = bf16[1,256,512]{2,1,0:T(8,128)(2,1)} async-done(((bf16[8,256,512]{2,1,0:T(8,128)(2,1)}), bf16[1,256,512]{2,1,0:T(8,128)(2,1)}) %reduce-scatter.6.cloned.1.call-update) | async-done | bytes 262160 | tf_op jit(solution)/shard_map/reduce_scatter | solution.py:297
  583.0 24.6 %reduce-scatter.8.cloned.1.call-done = bf16[1,128,512]{2,1,0:T(8,128)(2,1)} async-done(((bf16[2,128,512]{2,1,0:T(8,128)(2,1)}), bf16[1,128,512]{2,1,0:T(8,128)(2,1)}) %reduce-scatter.8.cloned.1.call-update) | async-done | bytes 131088 | tf_op jit(solution)/shard_map/reduce_scatter | solution.py:300
  (124 shorter events, 216.4 us)
Async XLA Ops:
  7.2 55.1 %all-gather.4.cloned.1.call-start = ((), (), s32[]{:S(2)}) async-start(), calls=%async_computation.3 | async-start | bytes 2654208 | tf_op jit(solution)/shard_map/all_gather | solution.py:223
  13.7 76.2 %all-gather.6.cloned.1.call-start = ((), (), s32[]{:S(2)}) async-start(), calls=%async_computation.4 | async-start | bytes 7077888 | tf_op jit(solution)/shard_map/all_gather | solution.py:224
  62.3 475.6 %reduce-scatter.4.cloned.1.call-start = ((), (), s32[]{:S(2)}) async-start(), calls=%async_computation.5 | async-start | bytes 6291456 | tf_op jit(solution)/shard_map/reduce_scatter | solution.py:296
  116.7 9.6 %collective-permute-start = (bf16[32,4096]{1,0:T(8,128)(2,1)S(1)}, bf16[32,4096]{1,0:T(8,128)(2,1)S(1)}, u32[]{:S(2)}, u32[]{:S(2)}) collective-permute-start(bf16[32,4096]{1,0:T(8,128)(2,1)S(1)} %get-tuple-element.651), channel_id=1, source_target_pairs={{32,0},{64,32},{96,64},{128,96},{160,128},{192,160},{224,192},{256... | collective-permute-start | bytes 786440 | tf_op jit(solution)/shard_map/while/body/eval_jaxpr/ppermute | solution.py:16
  131.3 8.7 %collective-permute-start = (bf16[32,4096]{1,0:T(8,128)(2,1)S(1)}, bf16[32,4096]{1,0:T(8,128)(2,1)S(1)}, u32[]{:S(2)}, u32[]{:S(2)}) collective-permute-start(bf16[32,4096]{1,0:T(8,128)(2,1)S(1)} %get-tuple-element.651), channel_id=1, source_target_pairs={{32,0},{64,32},{96,64},{128,96},{160,128},{192,160},{224,192},{256... | collective-permute-start | bytes 786440 | tf_op jit(solution)/shard_map/while/body/eval_jaxpr/ppermute | solution.py:16
  183.0 8.0 %collective-permute-start = (bf16[32,4096]{1,0:T(8,128)(2,1)S(1)}, bf16[32,4096]{1,0:T(8,128)(2,1)S(1)}, u32[]{:S(2)}, u32[]{:S(2)}) collective-permute-start(bf16[32,4096]{1,0:T(8,128)(2,1)S(1)} %get-tuple-element.651), channel_id=1, source_target_pairs={{32,0},{64,32},{96,64},{128,96},{160,128},{192,160},{224,192},{256... | collective-permute-start | bytes 786440 | tf_op jit(solution)/shard_map/while/body/eval_jaxpr/ppermute | solution.py:16
  196.1 8.3 %collective-permute-start = (bf16[32,4096]{1,0:T(8,128)(2,1)S(1)}, bf16[32,4096]{1,0:T(8,128)(2,1)S(1)}, u32[]{:S(2)}, u32[]{:S(2)}) collective-permute-start(bf16[32,4096]{1,0:T(8,128)(2,1)S(1)} %get-tuple-element.651), channel_id=1, source_target_pairs={{32,0},{64,32},{96,64},{128,96},{160,128},{192,160},{224,192},{256... | collective-permute-start | bytes 786440 | tf_op jit(solution)/shard_map/while/body/eval_jaxpr/ppermute | solution.py:16
  209.4 8.3 %collective-permute-start = (bf16[32,4096]{1,0:T(8,128)(2,1)S(1)}, bf16[32,4096]{1,0:T(8,128)(2,1)S(1)}, u32[]{:S(2)}, u32[]{:S(2)}) collective-permute-start(bf16[32,4096]{1,0:T(8,128)(2,1)S(1)} %get-tuple-element.651), channel_id=1, source_target_pairs={{32,0},{64,32},{96,64},{128,96},{160,128},{192,160},{224,192},{256... | collective-permute-start | bytes 786440 | tf_op jit(solution)/shard_map/while/body/eval_jaxpr/ppermute | solution.py:16
  222.7 8.3 %collective-permute-start = (bf16[32,4096]{1,0:T(8,128)(2,1)S(1)}, bf16[32,4096]{1,0:T(8,128)(2,1)S(1)}, u32[]{:S(2)}, u32[]{:S(2)}) collective-permute-start(bf16[32,4096]{1,0:T(8,128)(2,1)S(1)} %get-tuple-element.651), channel_id=1, source_target_pairs={{32,0},{64,32},{96,64},{128,96},{160,128},{192,160},{224,192},{256... | collective-permute-start | bytes 786440 | tf_op jit(solution)/shard_map/while/body/eval_jaxpr/ppermute | solution.py:16
  236.1 8.3 %collective-permute-start = (bf16[32,4096]{1,0:T(8,128)(2,1)S(1)}, bf16[32,4096]{1,0:T(8,128)(2,1)S(1)}, u32[]{:S(2)}, u32[]{:S(2)}) collective-permute-start(bf16[32,4096]{1,0:T(8,128)(2,1)S(1)} %get-tuple-element.651), channel_id=1, source_target_pairs={{32,0},{64,32},{96,64},{128,96},{160,128},{192,160},{224,192},{256... | collective-permute-start | bytes 786440 | tf_op jit(solution)/shard_map/while/body/eval_jaxpr/ppermute | solution.py:16
  249.4 10.5 %collective-permute-start = (bf16[32,4096]{1,0:T(8,128)(2,1)S(1)}, bf16[32,4096]{1,0:T(8,128)(2,1)S(1)}, u32[]{:S(2)}, u32[]{:S(2)}) collective-permute-start(bf16[32,4096]{1,0:T(8,128)(2,1)S(1)} %get-tuple-element.651), channel_id=1, source_target_pairs={{32,0},{64,32},{96,64},{128,96},{160,128},{192,160},{224,192},{256... | collective-permute-start | bytes 786440 | tf_op jit(solution)/shard_map/while/body/eval_jaxpr/ppermute | solution.py:16
  264.9 10.7 %collective-permute-start = (bf16[32,4096]{1,0:T(8,128)(2,1)S(1)}, bf16[32,4096]{1,0:T(8,128)(2,1)S(1)}, u32[]{:S(2)}, u32[]{:S(2)}) collective-permute-start(bf16[32,4096]{1,0:T(8,128)(2,1)S(1)} %get-tuple-element.651), channel_id=1, source_target_pairs={{32,0},{64,32},{96,64},{128,96},{160,128},{192,160},{224,192},{256... | collective-permute-start | bytes 786440 | tf_op jit(solution)/shard_map/while/body/eval_jaxpr/ppermute | solution.py:16
  280.6 10.7 %collective-permute-start = (bf16[32,4096]{1,0:T(8,128)(2,1)S(1)}, bf16[32,4096]{1,0:T(8,128)(2,1)S(1)}, u32[]{:S(2)}, u32[]{:S(2)}) collective-permute-start(bf16[32,4096]{1,0:T(8,128)(2,1)S(1)} %get-tuple-element.651), channel_id=1, source_target_pairs={{32,0},{64,32},{96,64},{128,96},{160,128},{192,160},{224,192},{256... | collective-permute-start | bytes 786440 | tf_op jit(solution)/shard_map/while/body/eval_jaxpr/ppermute | solution.py:16
  296.4 10.7 %collective-permute-start = (bf16[32,4096]{1,0:T(8,128)(2,1)S(1)}, bf16[32,4096]{1,0:T(8,128)(2,1)S(1)}, u32[]{:S(2)}, u32[]{:S(2)}) collective-permute-start(bf16[32,4096]{1,0:T(8,128)(2,1)S(1)} %get-tuple-element.651), channel_id=1, source_target_pairs={{32,0},{64,32},{96,64},{128,96},{160,128},{192,160},{224,192},{256... | collective-permute-start | bytes 786440 | tf_op jit(solution)/shard_map/while/body/eval_jaxpr/ppermute | solution.py:16
  312.1 10.7 %collective-permute-start = (bf16[32,4096]{1,0:T(8,128)(2,1)S(1)}, bf16[32,4096]{1,0:T(8,128)(2,1)S(1)}, u32[]{:S(2)}, u32[]{:S(2)}) collective-permute-start(bf16[32,4096]{1,0:T(8,128)(2,1)S(1)} %get-tuple-element.651), channel_id=1, source_target_pairs={{32,0},{64,32},{96,64},{128,96},{160,128},{192,160},{224,192},{256... | collective-permute-start | bytes 786440 | tf_op jit(solution)/shard_map/while/body/eval_jaxpr/ppermute | solution.py:16
  327.8 12.0 %collective-permute-start = (bf16[32,4096]{1,0:T(8,128)(2,1)S(1)}, bf16[32,4096]{1,0:T(8,128)(2,1)S(1)}, u32[]{:S(2)}, u32[]{:S(2)}) collective-permute-start(bf16[32,4096]{1,0:T(8,128)(2,1)S(1)} %get-tuple-element.651), channel_id=1, source_target_pairs={{32,0},{64,32},{96,64},{128,96},{160,128},{192,160},{224,192},{256... | collective-permute-start | bytes 786440 | tf_op jit(solution)/shard_map/while/body/eval_jaxpr/ppermute | solution.py:16
  344.8 13.4 %collective-permute-start = (bf16[32,4096]{1,0:T(8,128)(2,1)S(1)}, bf16[32,4096]{1,0:T(8,128)(2,1)S(1)}, u32[]{:S(2)}, u32[]{:S(2)}) collective-permute-start(bf16[32,4096]{1,0:T(8,128)(2,1)S(1)} %get-tuple-element.651), channel_id=1, source_target_pairs={{32,0},{64,32},{96,64},{128,96},{160,128},{192,160},{224,192},{256... | collective-permute-start | bytes 786440 | tf_op jit(solution)/shard_map/while/body/eval_jaxpr/ppermute | solution.py:16
  363.2 14.2 %collective-permute-start = (bf16[32,4096]{1,0:T(8,128)(2,1)S(1)}, bf16[32,4096]{1,0:T(8,128)(2,1)S(1)}, u32[]{:S(2)}, u32[]{:S(2)}) collective-permute-start(bf16[32,4096]{1,0:T(8,128)(2,1)S(1)} %get-tuple-element.651), channel_id=1, source_target_pairs={{32,0},{64,32},{96,64},{128,96},{160,128},{192,160},{224,192},{256... | collective-permute-start | bytes 786440 | tf_op jit(solution)/shard_map/while/body/eval_jaxpr/ppermute | solution.py:16
  382.5 13.8 %collective-permute-start = (bf16[32,4096]{1,0:T(8,128)(2,1)S(1)}, bf16[32,4096]{1,0:T(8,128)(2,1)S(1)}, u32[]{:S(2)}, u32[]{:S(2)}) collective-permute-start(bf16[32,4096]{1,0:T(8,128)(2,1)S(1)} %get-tuple-element.651), channel_id=1, source_target_pairs={{32,0},{64,32},{96,64},{128,96},{160,128},{192,160},{224,192},{256... | collective-permute-start | bytes 786440 | tf_op jit(solution)/shard_map/while/body/eval_jaxpr/ppermute | solution.py:16
  401.2 12.3 %collective-permute-start = (bf16[32,4096]{1,0:T(8,128)(2,1)S(1)}, bf16[32,4096]{1,0:T(8,128)(2,1)S(1)}, u32[]{:S(2)}, u32[]{:S(2)}) collective-permute-start(bf16[32,4096]{1,0:T(8,128)(2,1)S(1)} %get-tuple-element.651), channel_id=1, source_target_pairs={{32,0},{64,32},{96,64},{128,96},{160,128},{192,160},{224,192},{256... | collective-permute-start | bytes 786440 | tf_op jit(solution)/shard_map/while/body/eval_jaxpr/ppermute | solution.py:16
  418.6 10.2 %collective-permute-start = (bf16[32,4096]{1,0:T(8,128)(2,1)S(1)}, bf16[32,4096]{1,0:T(8,128)(2,1)S(1)}, u32[]{:S(2)}, u32[]{:S(2)}) collective-permute-start(bf16[32,4096]{1,0:T(8,128)(2,1)S(1)} %get-tuple-element.651), channel_id=1, source_target_pairs={{32,0},{64,32},{96,64},{128,96},{160,128},{192,160},{224,192},{256... | collective-permute-start | bytes 786440 | tf_op jit(solution)/shard_map/while/body/eval_jaxpr/ppermute | solution.py:16
  433.8 11.4 %collective-permute-start = (bf16[32,4096]{1,0:T(8,128)(2,1)S(1)}, bf16[32,4096]{1,0:T(8,128)(2,1)S(1)}, u32[]{:S(2)}, u32[]{:S(2)}) collective-permute-start(bf16[32,4096]{1,0:T(8,128)(2,1)S(1)} %get-tuple-element.651), channel_id=1, source_target_pairs={{32,0},{64,32},{96,64},{128,96},{160,128},{192,160},{224,192},{256... | collective-permute-start | bytes 786440 | tf_op jit(solution)/shard_map/while/body/eval_jaxpr/ppermute | solution.py:16
  470.7 112.3 %reduce-scatter.6.cloned.1.call-start = ((), (), s32[]{:S(2)}) async-start(), calls=%async_computation.6 | async-start | bytes 2359296 | tf_op jit(solution)/shard_map/reduce_scatter | solution.py:297
  537.9 69.7 %reduce-scatter.8.cloned.1.call-start = ((), (), s32[]{:S(2)}) async-start(), calls=%async_computation.7 | async-start | bytes 393216 | tf_op jit(solution)/shard_map/reduce_scatter | solution.py:300
  (10 other events, 103.7 us)
Sparse Core Ops, SparseCore 0:
  13.8 48.4 all-gather.3
  64.3 25.5 all-gather.5
  470.8 66.9 reduce-scatter.3
  540.8 42.1 reduce-scatter.5
  585.8 21.7 reduce-scatter.7

commit v11 on v10

--- a/solution.py
+++ b/solution.py
@@ -180,31 +180,39 @@
 
 def terms_kernel(hid_ref, g_ref, gp_ref, att_ref, out_ref):
     tokens = hid_ref.shape[0]
+    rows = out_ref.shape[1]
     gp = gp_ref[...].reshape(tokens, gp_ref.shape[-1])
     grads = g_ref[...].reshape(tokens, g_ref.shape[-1])
-    first = lax.dot_general(hid_ref[...], gp, (((0,), (0,)), ((), ())), preferred_element_type=jnp.float32)
-    second = lax.dot_general(grads, att_ref[...], (((0,), (0,)), ((), ())), preferred_element_type=jnp.float32)
-    out_ref[...] = jnp.concatenate([first, second], axis=-1).astype(out_ref.dtype)
+    att = att_ref[...]
+    for core in range(out_ref.shape[0]):
+        cut = slice(core * rows, (core + 1) * rows)
+        first = lax.dot_general(
+            hid_ref[:, cut], gp, (((0,), (0,)), ((), ())), preferred_element_type=jnp.float32
+        )
+        second = lax.dot_general(
+            grads[:, cut], att, (((0,), (0,)), ((), ())), preferred_element_type=jnp.float32
+        )
+        out_ref[core] = jnp.concatenate([first, second], axis=-1).astype(out_ref.dtype)
 
 
 def weight_terms(hidden_flat, grad_store, proj_store, att_flat, rows_here):
     tokens, width = hidden_flat.shape
     micro_count, length = grad_store.shape[0] - 2, grad_store.shape[1]
     cols = proj_store.shape[-1] + att_flat.shape[-1]
-    staged = lambda j: (j % FC) * (FZ * FX) + ((j // FC) % FZ) * FX + j // (FC * FZ)
-    return pl.pallas_call(
+    both = FC * rows_here
+    out = pl.pallas_call(
         terms_kernel,
-        out_shape=jax.ShapeDtypeStruct((width, cols), jnp.bfloat16),
-        grid=(width // rows_here,),
+        out_shape=jax.ShapeDtypeStruct((FC, FZ * FX, rows_here, cols), jnp.bfloat16),
+        grid=(FX, FZ),
         in_specs=[
-            pl.BlockSpec((tokens, rows_here), lambda j: (0, j)),
-            pl.BlockSpec((micro_count, length, rows_here), lambda j: (0, 0, j)),
-            pl.BlockSpec((micro_count, length, proj_store.shape[-1]), lambda j: (0, 0, 0)),
-            pl.BlockSpec((tokens, att_flat.shape[-1]), lambda j: (0, 0)),
+            pl.BlockSpec((tokens, both), lambda x, z: (0, x * FZ + z)),
+            pl.BlockSpec((micro_count, length, both), lambda x, z: (0, 0, x * FZ + z)),
+            pl.BlockSpec((micro_count, length, proj_store.shape[-1]), lambda x, z: (0, 0, 0)),
+            pl.BlockSpec((tokens, att_flat.shape[-1]), lambda x, z: (0, 0)),
         ],
-        out_specs=pl.BlockSpec((rows_here, cols), lambda j: (staged(j), 0)),
+        out_specs=pl.BlockSpec((FC, None, rows_here, cols), lambda x, z: (0, z * FX + x, 0, 0)),
     )(hidden_flat, grad_store, proj_store, att_flat)
-
+    return out.reshape(width, cols)
 
 def on_device(inputs, upstream, weights, gain):
     sections = SH * SY

time: 618 us -> 609 us (0.985)
  Pallas kernels: 144 us -> 136 us
    pallas_call x1, Pallas kernels: 19.9 us -> 11.9 us  [weight_terms(): pl.pallas_call(terms_kernel, out_shape=jax.ShapeDtypeStruct((FC, FZ * FX,...]
where the time goes in v11:
time: 609 us; the launch traced here: 608 us
  waiting for transfers between devices  366 us (60%)
  Pallas kernels  136 us (22%)
  blocking collectives  41.9 us (7%)
  starting transfers between devices  28.6 us (5%)
  other arithmetic  13.9 us (2%)
  between operations  13.9 us (2%)
  matrix products  6.12 us (1%)
    ppermute x22, waiting for transfers between devices, passed_along(): lax.ppermute(value, axis, [(source, source + steps) for source in range(l...  195 us
    pallas_call x23, Pallas kernels, tick_call(): pl.pallas_call(tick_kernel, out_shape=(jax.ShapeDtypeStruct((length, widt...  114 us
    reduce_scatter x1, waiting for transfers between devices, on_device(): lax.psum_scatter(terms.reshape(FC, -1, cols), 'fc', scatter_dimension=0,...  67.1 us
    all_gather x1, waiting for transfers between devices, on_device(): staged = lax.all_gather(staged, 'fz', axis=0, tiled=True)  48.5 us
    all_gather x1, blocking collectives, on_device(): gain_sum = jnp.sum(lax.all_gather(gain_acc, FSDP, axis=0), axis=0)  36.5 us
    ppermute x22, starting transfers between devices, passed_along(): lax.ppermute(value, axis, [(source, source + steps) for source in range(l...  28.4 us
    reduce_scatter x1, waiting for transfers between devices, on_device(): lax.psum_scatter(terms.reshape(FX, -1, cols), 'fx', scatter_dimension=0,...  24.5 us
    all_gather x1, waiting for transfers between devices, on_device(): staged = lax.all_gather(staged, 'fc', axis=0, tiled=True)  23.4 us
  transfers between devices with their start and end apart: 27, of which 27 were waited for; matrix products, arithmetic and copies ran while one was open for 1% of the time, Pallas kernels for 0%

profile of v11, /device:TPU:1, one launch (start us, length us, event | category | flops | bytes accessed | tf_op | source)
XLA Modules:
  0.0 607.7 jit_solution(6301519536342556110)
XLA Ops:
  13.7 48.5 %all-gather.4.cloned.1.call-done = bf16[2304,512]{1,0:T(8,128)(2,1)} async-done(((bf16[288,512]{1,0:T(8,128)(2,1)}), bf16[2304,512]{1,0:T(8,128)(2,1)}) %all-gather.4.cloned.1.call-update) | async-done | bytes 2359312 | tf_op jit(solution)/shard_map/all_gather | solution.py:231
  66.5 23.4 %all-gather.6.cloned.1.call-done = bf16[4608,512]{1,0:T(8,128)(2,1)} async-done(((bf16[2304,512]{1,0:T(8,128)(2,1)}), bf16[4608,512]{1,0:T(8,128)(2,1)}) %all-gather.6.cloned.1.call-update) | async-done | bytes 4718608 | tf_op jit(solution)/shard_map/all_gather | solution.py:232
  89.9 9.7 %shard_map.59 = (bf16[4096,384]{1,0:T(8,128)(2,1)S(1)}, bf16[4096,128]{1,0:T(8,128)(2,1)}, f32[16,2,128]{2,1,0:T(2,128)S(1)}) custom-call(bf16[2,8,2,144,512]{4,3,2,1,0:T(8,128)(2,1)} %bitcast.55, bf16[2,8,2,144,512]{4,3,2,1,0:T(8,128)(2,1)} %bitcast.56), custom_call_target="tpu_custom_call" | custom-call | tf_op jit(solution)/shard_map/pallas_call | solution.py:162
  111.6 333.6 %while.21 = (s32[]{:T(128)}, bf16[32,4096]{1,0:T(8,128)(2,1)S(1)}, bf16[10,32,4096]{2,1,0:T(8,128)(2,1)S(1)}, bf16[10,32,384]{2,1,0:T(8,128)(2,1)S(1)}, f32[4096...) while((s32[]{:T(128)}, bf16[32,4096]{1,0:T(8,128)(2,1)S(1)}, ...), condition=%wide.region_4.5_spmd, body=%wide.region_3.4_spmd.sunk | while | flops 268435488 | bytes 6291851 | solution.py:293
  118.0 8.3 %collective-permute-done = bf16[32,4096]{1,0:T(8,128)(2,1)S(1)} collective-permute-done((bf16[32,4096]{1,0:T(8,128)(2,1)S(1)}, bf16[32,4096]{1,0:T(8,128)(2,1)S(1)}, u32[]{:S(2)}, u32[]{:S(2)}) %collective-permute-start) | collective-permute-done | bytes 262176 | tf_op jit(solution)/shard_map/while/body/eval_jaxpr/ppermute | solution.py:16
  132.6 7.4 %collective-permute-done = bf16[32,4096]{1,0:T(8,128)(2,1)S(1)} collective-permute-done((bf16[32,4096]{1,0:T(8,128)(2,1)S(1)}, bf16[32,4096]{1,0:T(8,128)(2,1)S(1)}, u32[]{:S(2)}, u32[]{:S(2)}) %collective-permute-start) | collective-permute-done | bytes 262176 | tf_op jit(solution)/shard_map/while/body/eval_jaxpr/ppermute | solution.py:16
  224.0 7.0 %collective-permute-done = bf16[32,4096]{1,0:T(8,128)(2,1)S(1)} collective-permute-done((bf16[32,4096]{1,0:T(8,128)(2,1)S(1)}, bf16[32,4096]{1,0:T(8,128)(2,1)S(1)}, u32[]{:S(2)}, u32[]{:S(2)}) %collective-permute-start) | collective-permute-done | bytes 262176 | tf_op jit(solution)/shard_map/while/body/eval_jaxpr/ppermute | solution.py:16
  250.7 9.2 %collective-permute-done = bf16[32,4096]{1,0:T(8,128)(2,1)S(1)} collective-permute-done((bf16[32,4096]{1,0:T(8,128)(2,1)S(1)}, bf16[32,4096]{1,0:T(8,128)(2,1)S(1)}, u32[]{:S(2)}, u32[]{:S(2)}) %collective-permute-start) | collective-permute-done | bytes 262176 | tf_op jit(solution)/shard_map/while/body/eval_jaxpr/ppermute | solution.py:16
  266.2 9.4 %collective-permute-done = bf16[32,4096]{1,0:T(8,128)(2,1)S(1)} collective-permute-done((bf16[32,4096]{1,0:T(8,128)(2,1)S(1)}, bf16[32,4096]{1,0:T(8,128)(2,1)S(1)}, u32[]{:S(2)}, u32[]{:S(2)}) %collective-permute-start) | collective-permute-done | bytes 262176 | tf_op jit(solution)/shard_map/while/body/eval_jaxpr/ppermute | solution.py:16
  281.9 9.4 %collective-permute-done = bf16[32,4096]{1,0:T(8,128)(2,1)S(1)} collective-permute-done((bf16[32,4096]{1,0:T(8,128)(2,1)S(1)}, bf16[32,4096]{1,0:T(8,128)(2,1)S(1)}, u32[]{:S(2)}, u32[]{:S(2)}) %collective-permute-start) | collective-permute-done | bytes 262176 | tf_op jit(solution)/shard_map/while/body/eval_jaxpr/ppermute | solution.py:16
  297.7 9.4 %collective-permute-done = bf16[32,4096]{1,0:T(8,128)(2,1)S(1)} collective-permute-done((bf16[32,4096]{1,0:T(8,128)(2,1)S(1)}, bf16[32,4096]{1,0:T(8,128)(2,1)S(1)}, u32[]{:S(2)}, u32[]{:S(2)}) %collective-permute-start) | collective-permute-done | bytes 262176 | tf_op jit(solution)/shard_map/while/body/eval_jaxpr/ppermute | solution.py:16
  313.4 9.4 %collective-permute-done = bf16[32,4096]{1,0:T(8,128)(2,1)S(1)} collective-permute-done((bf16[32,4096]{1,0:T(8,128)(2,1)S(1)}, bf16[32,4096]{1,0:T(8,128)(2,1)S(1)}, u32[]{:S(2)}, u32[]{:S(2)}) %collective-permute-start) | collective-permute-done | bytes 262176 | tf_op jit(solution)/shard_map/while/body/eval_jaxpr/ppermute | solution.py:16
  329.1 10.7 %collective-permute-done = bf16[32,4096]{1,0:T(8,128)(2,1)S(1)} collective-permute-done((bf16[32,4096]{1,0:T(8,128)(2,1)S(1)}, bf16[32,4096]{1,0:T(8,128)(2,1)S(1)}, u32[]{:S(2)}, u32[]{:S(2)}) %collective-permute-start) | collective-permute-done | bytes 262176 | tf_op jit(solution)/shard_map/while/body/eval_jaxpr/ppermute | solution.py:16
  346.1 12.1 %collective-permute-done = bf16[32,4096]{1,0:T(8,128)(2,1)S(1)} collective-permute-done((bf16[32,4096]{1,0:T(8,128)(2,1)S(1)}, bf16[32,4096]{1,0:T(8,128)(2,1)S(1)}, u32[]{:S(2)}, u32[]{:S(2)}) %collective-permute-start) | collective-permute-done | bytes 262176 | tf_op jit(solution)/shard_map/while/body/eval_jaxpr/ppermute | solution.py:16
  364.5 12.9 %collective-permute-done = bf16[32,4096]{1,0:T(8,128)(2,1)S(1)} collective-permute-done((bf16[32,4096]{1,0:T(8,128)(2,1)S(1)}, bf16[32,4096]{1,0:T(8,128)(2,1)S(1)}, u32[]{:S(2)}, u32[]{:S(2)}) %collective-permute-start) | collective-permute-done | bytes 262176 | tf_op jit(solution)/shard_map/while/body/eval_jaxpr/ppermute | solution.py:16
  383.8 12.5 %collective-permute-done = bf16[32,4096]{1,0:T(8,128)(2,1)S(1)} collective-permute-done((bf16[32,4096]{1,0:T(8,128)(2,1)S(1)}, bf16[32,4096]{1,0:T(8,128)(2,1)S(1)}, u32[]{:S(2)}, u32[]{:S(2)}) %collective-permute-start) | collective-permute-done | bytes 262176 | tf_op jit(solution)/shard_map/while/body/eval_jaxpr/ppermute | solution.py:16
  402.5 11.0 %collective-permute-done = bf16[32,4096]{1,0:T(8,128)(2,1)S(1)} collective-permute-done((bf16[32,4096]{1,0:T(8,128)(2,1)S(1)}, bf16[32,4096]{1,0:T(8,128)(2,1)S(1)}, u32[]{:S(2)}, u32[]{:S(2)}) %collective-permute-start) | collective-permute-done | bytes 262176 | tf_op jit(solution)/shard_map/while/body/eval_jaxpr/ppermute | solution.py:16
  419.9 8.9 %collective-permute-done = bf16[32,4096]{1,0:T(8,128)(2,1)S(1)} collective-permute-done((bf16[32,4096]{1,0:T(8,128)(2,1)S(1)}, bf16[32,4096]{1,0:T(8,128)(2,1)S(1)}, u32[]{:S(2)}, u32[]{:S(2)}) %collective-permute-start) | collective-permute-done | bytes 262176 | tf_op jit(solution)/shard_map/while/body/eval_jaxpr/ppermute | solution.py:16
  435.1 10.1 %collective-permute-done = bf16[32,4096]{1,0:T(8,128)(2,1)S(1)} collective-permute-done((bf16[32,4096]{1,0:T(8,128)(2,1)S(1)}, bf16[32,4096]{1,0:T(8,128)(2,1)S(1)}, u32[]{:S(2)}, u32[]{:S(2)}) %collective-permute-start) | collective-permute-done | bytes 262176 | tf_op jit(solution)/shard_map/while/body/eval_jaxpr/ppermute | solution.py:16
  450.8 11.9 %shard_map.61 = bf16[2,16,128,512]{3,2,1,0:T(8,128)(2,1)} custom-call(bf16[256,4096]{1,0:T(8,128)(2,1)} %fusion.3.hid_ref, bf16[10,32,4096]{2,1,0:T(8,128)(2,1)S(1)} %get-tuple-element.424.g_ref, bf16[10,32,384]{2,1,0:T(8,128)(2,1)S(1)} %get-tuple-element.425.gp_ref, bf16[256,128]{1,0:T(8,128)(2,1)} %bitcast.66), custom_call_target="tpu_custom_call" | custom-call | tf_op jit(solution)/shard_map/pallas_call | solution.py:203
  462.8 67.1 %reduce-scatter.4.cloned.1.call-done = bf16[1,2048,512]{2,1,0:T(8,128)(2,1)} async-done(((bf16[2,2048,512]{2,1,0:T(8,128)(2,1)}), bf16[1,2048,512]{2,1,0:T(8,128)(2,1)}) %reduce-scatter.4.cloned.1.call-update) | async-done | bytes 2097168 | tf_op jit(solution)/shard_map/reduce_scatter | solution.py:304
  529.9 36.5 %all-gather = f32[32,1,4096]{2,1,0:T(1,128)S(1)} all-gather(f32[1,1,4096]{2,1,0:T(1,128)S(1)} %bitcast.62), channel_id=1, replica_groups=mesh['sh'=2,'sy'=8,'fx'=2,'fz'=8,'fc'=2] {'fx','fz','fc'}, dimensions={0}, use_global_device_ids=true | all-gather | bytes 540672 | tf_op jit(solution)/shard_map/all_gather | solution.py:306
  567.5 7.6 %reduce-scatter.6.cloned.1.call-done = bf16[1,256,512]{2,1,0:T(8,128)(2,1)} async-done(((bf16[8,256,512]{2,1,0:T(8,128)(2,1)}), bf16[1,256,512]{2,1,0:T(8,128)(2,1)}) %reduce-scatter.6.cloned.1.call-update) | async-done | bytes 262160 | tf_op jit(solution)/shard_map/reduce_scatter | solution.py:305
  575.0 24.5 %reduce-scatter.8.cloned.1.call-done = bf16[1,128,512]{2,1,0:T(8,128)(2,1)} async-done(((bf16[2,128,512]{2,1,0:T(8,128)(2,1)}), bf16[1,128,512]{2,1,0:T(8,128)(2,1)}) %reduce-scatter.8.cloned.1.call-update) | async-done | bytes 131088 | tf_op jit(solution)/shard_map/reduce_scatter | solution.py:308
  (124 shorter events, 216.4 us)
Async XLA Ops:
  7.2 55.1 %all-gather.4.cloned.1.call-start = ((), (), s32[]{:S(2)}) async-start(), calls=%async_computation.3 | async-start | bytes 2654208 | tf_op jit(solution)/shard_map/all_gather | solution.py:231
  13.7 76.2 %all-gather.6.cloned.1.call-start = ((), (), s32[]{:S(2)}) async-start(), calls=%async_computation.4 | async-start | bytes 7077888 | tf_op jit(solution)/shard_map/all_gather | solution.py:232
  62.3 467.6 %reduce-scatter.4.cloned.1.call-start = ((), (), s32[]{:S(2)}) async-start(), calls=%async_computation.5 | async-start | bytes 6291456 | tf_op jit(solution)/shard_map/reduce_scatter | solution.py:304
  116.7 9.6 %collective-permute-start = (bf16[32,4096]{1,0:T(8,128)(2,1)S(1)}, bf16[32,4096]{1,0:T(8,128)(2,1)S(1)}, u32[]{:S(2)}, u32[]{:S(2)}) collective-permute-start(bf16[32,4096]{1,0:T(8,128)(2,1)S(1)} %get-tuple-element.651), channel_id=1, source_target_pairs={{32,0},{64,32},{96,64},{128,96},{160,128},{192,160},{224,192},{256... | collective-permute-start | bytes 786440 | tf_op jit(solution)/shard_map/while/body/eval_jaxpr/ppermute | solution.py:16
  131.3 8.7 %collective-permute-start = (bf16[32,4096]{1,0:T(8,128)(2,1)S(1)}, bf16[32,4096]{1,0:T(8,128)(2,1)S(1)}, u32[]{:S(2)}, u32[]{:S(2)}) collective-permute-start(bf16[32,4096]{1,0:T(8,128)(2,1)S(1)} %get-tuple-element.651), channel_id=1, source_target_pairs={{32,0},{64,32},{96,64},{128,96},{160,128},{192,160},{224,192},{256... | collective-permute-start | bytes 786440 | tf_op jit(solution)/shard_map/while/body/eval_jaxpr/ppermute | solution.py:16
  183.0 8.0 %collective-permute-start = (bf16[32,4096]{1,0:T(8,128)(2,1)S(1)}, bf16[32,4096]{1,0:T(8,128)(2,1)S(1)}, u32[]{:S(2)}, u32[]{:S(2)}) collective-permute-start(bf16[32,4096]{1,0:T(8,128)(2,1)S(1)} %get-tuple-element.651), channel_id=1, source_target_pairs={{32,0},{64,32},{96,64},{128,96},{160,128},{192,160},{224,192},{256... | collective-permute-start | bytes 786440 | tf_op jit(solution)/shard_map/while/body/eval_jaxpr/ppermute | solution.py:16
  196.1 8.3 %collective-permute-start = (bf16[32,4096]{1,0:T(8,128)(2,1)S(1)}, bf16[32,4096]{1,0:T(8,128)(2,1)S(1)}, u32[]{:S(2)}, u32[]{:S(2)}) collective-permute-start(bf16[32,4096]{1,0:T(8,128)(2,1)S(1)} %get-tuple-element.651), channel_id=1, source_target_pairs={{32,0},{64,32},{96,64},{128,96},{160,128},{192,160},{224,192},{256... | collective-permute-start | bytes 786440 | tf_op jit(solution)/shard_map/while/body/eval_jaxpr/ppermute | solution.py:16
  209.4 8.3 %collective-permute-start = (bf16[32,4096]{1,0:T(8,128)(2,1)S(1)}, bf16[32,4096]{1,0:T(8,128)(2,1)S(1)}, u32[]{:S(2)}, u32[]{:S(2)}) collective-permute-start(bf16[32,4096]{1,0:T(8,128)(2,1)S(1)} %get-tuple-element.651), channel_id=1, source_target_pairs={{32,0},{64,32},{96,64},{128,96},{160,128},{192,160},{224,192},{256... | collective-permute-start | bytes 786440 | tf_op jit(solution)/shard_map/while/body/eval_jaxpr/ppermute | solution.py:16
  222.7 8.3 %collective-permute-start = (bf16[32,4096]{1,0:T(8,128)(2,1)S(1)}, bf16[32,4096]{1,0:T(8,128)(2,1)S(1)}, u32[]{:S(2)}, u32[]{:S(2)}) collective-permute-start(bf16[32,4096]{1,0:T(8,128)(2,1)S(1)} %get-tuple-element.651), channel_id=1, source_target_pairs={{32,0},{64,32},{96,64},{128,96},{160,128},{192,160},{224,192},{256... | collective-permute-start | bytes 786440 | tf_op jit(solution)/shard_map/while/body/eval_jaxpr/ppermute | solution.py:16
  236.1 8.3 %collective-permute-start = (bf16[32,4096]{1,0:T(8,128)(2,1)S(1)}, bf16[32,4096]{1,0:T(8,128)(2,1)S(1)}, u32[]{:S(2)}, u32[]{:S(2)}) collective-permute-start(bf16[32,4096]{1,0:T(8,128)(2,1)S(1)} %get-tuple-element.651), channel_id=1, source_target_pairs={{32,0},{64,32},{96,64},{128,96},{160,128},{192,160},{224,192},{256... | collective-permute-start | bytes 786440 | tf_op jit(solution)/shard_map/while/body/eval_jaxpr/ppermute | solution.py:16
  249.4 10.5 %collective-permute-start = (bf16[32,4096]{1,0:T(8,128)(2,1)S(1)}, bf16[32,4096]{1,0:T(8,128)(2,1)S(1)}, u32[]{:S(2)}, u32[]{:S(2)}) collective-permute-start(bf16[32,4096]{1,0:T(8,128)(2,1)S(1)} %get-tuple-element.651), channel_id=1, source_target_pairs={{32,0},{64,32},{96,64},{128,96},{160,128},{192,160},{224,192},{256... | collective-permute-start | bytes 786440 | tf_op jit(solution)/shard_map/while/body/eval_jaxpr/ppermute | solution.py:16
  264.9 10.7 %collective-permute-start = (bf16[32,4096]{1,0:T(8,128)(2,1)S(1)}, bf16[32,4096]{1,0:T(8,128)(2,1)S(1)}, u32[]{:S(2)}, u32[]{:S(2)}) collective-permute-start(bf16[32,4096]{1,0:T(8,128)(2,1)S(1)} %get-tuple-element.651), channel_id=1, source_target_pairs={{32,0},{64,32},{96,64},{128,96},{160,128},{192,160},{224,192},{256... | collective-permute-start | bytes 786440 | tf_op jit(solution)/shard_map/while/body/eval_jaxpr/ppermute | solution.py:16
  280.6 10.7 %collective-permute-start = (bf16[32,4096]{1,0:T(8,128)(2,1)S(1)}, bf16[32,4096]{1,0:T(8,128)(2,1)S(1)}, u32[]{:S(2)}, u32[]{:S(2)}) collective-permute-start(bf16[32,4096]{1,0:T(8,128)(2,1)S(1)} %get-tuple-element.651), channel_id=1, source_target_pairs={{32,0},{64,32},{96,64},{128,96},{160,128},{192,160},{224,192},{256... | collective-permute-start | bytes 786440 | tf_op jit(solution)/shard_map/while/body/eval_jaxpr/ppermute | solution.py:16
  296.4 10.7 %collective-permute-start = (bf16[32,4096]{1,0:T(8,128)(2,1)S(1)}, bf16[32,4096]{1,0:T(8,128)(2,1)S(1)}, u32[]{:S(2)}, u32[]{:S(2)}) collective-permute-start(bf16[32,4096]{1,0:T(8,128)(2,1)S(1)} %get-tuple-element.651), channel_id=1, source_target_pairs={{32,0},{64,32},{96,64},{128,96},{160,128},{192,160},{224,192},{256... | collective-permute-start | bytes 786440 | tf_op jit(solution)/shard_map/while/body/eval_jaxpr/ppermute | solution.py:16
  312.1 10.7 %collective-permute-start = (bf16[32,4096]{1,0:T(8,128)(2,1)S(1)}, bf16[32,4096]{1,0:T(8,128)(2,1)S(1)}, u32[]{:S(2)}, u32[]{:S(2)}) collective-permute-start(bf16[32,4096]{1,0:T(8,128)(2,1)S(1)} %get-tuple-element.651), channel_id=1, source_target_pairs={{32,0},{64,32},{96,64},{128,96},{160,128},{192,160},{224,192},{256... | collective-permute-start | bytes 786440 | tf_op jit(solution)/shard_map/while/body/eval_jaxpr/ppermute | solution.py:16
  327.8 12.0 %collective-permute-start = (bf16[32,4096]{1,0:T(8,128)(2,1)S(1)}, bf16[32,4096]{1,0:T(8,128)(2,1)S(1)}, u32[]{:S(2)}, u32[]{:S(2)}) collective-permute-start(bf16[32,4096]{1,0:T(8,128)(2,1)S(1)} %get-tuple-element.651), channel_id=1, source_target_pairs={{32,0},{64,32},{96,64},{128,96},{160,128},{192,160},{224,192},{256... | collective-permute-start | bytes 786440 | tf_op jit(solution)/shard_map/while/body/eval_jaxpr/ppermute | solution.py:16
  344.8 13.4 %collective-permute-start = (bf16[32,4096]{1,0:T(8,128)(2,1)S(1)}, bf16[32,4096]{1,0:T(8,128)(2,1)S(1)}, u32[]{:S(2)}, u32[]{:S(2)}) collective-permute-start(bf16[32,4096]{1,0:T(8,128)(2,1)S(1)} %get-tuple-element.651), channel_id=1, source_target_pairs={{32,0},{64,32},{96,64},{128,96},{160,128},{192,160},{224,192},{256... | collective-permute-start | bytes 786440 | tf_op jit(solution)/shard_map/while/body/eval_jaxpr/ppermute | solution.py:16
  363.2 14.2 %collective-permute-start = (bf16[32,4096]{1,0:T(8,128)(2,1)S(1)}, bf16[32,4096]{1,0:T(8,128)(2,1)S(1)}, u32[]{:S(2)}, u32[]{:S(2)}) collective-permute-start(bf16[32,4096]{1,0:T(8,128)(2,1)S(1)} %get-tuple-element.651), channel_id=1, source_target_pairs={{32,0},{64,32},{96,64},{128,96},{160,128},{192,160},{224,192},{256... | collective-permute-start | bytes 786440 | tf_op jit(solution)/shard_map/while/body/eval_jaxpr/ppermute | solution.py:16
  382.5 13.8 %collective-permute-start = (bf16[32,4096]{1,0:T(8,128)(2,1)S(1)}, bf16[32,4096]{1,0:T(8,128)(2,1)S(1)}, u32[]{:S(2)}, u32[]{:S(2)}) collective-permute-start(bf16[32,4096]{1,0:T(8,128)(2,1)S(1)} %get-tuple-element.651), channel_id=1, source_target_pairs={{32,0},{64,32},{96,64},{128,96},{160,128},{192,160},{224,192},{256... | collective-permute-start | bytes 786440 | tf_op jit(solution)/shard_map/while/body/eval_jaxpr/ppermute | solution.py:16
  401.2 12.3 %collective-permute-start = (bf16[32,4096]{1,0:T(8,128)(2,1)S(1)}, bf16[32,4096]{1,0:T(8,128)(2,1)S(1)}, u32[]{:S(2)}, u32[]{:S(2)}) collective-permute-start(bf16[32,4096]{1,0:T(8,128)(2,1)S(1)} %get-tuple-element.651), channel_id=1, source_target_pairs={{32,0},{64,32},{96,64},{128,96},{160,128},{192,160},{224,192},{256... | collective-permute-start | bytes 786440 | tf_op jit(solution)/shard_map/while/body/eval_jaxpr/ppermute | solution.py:16
  418.6 10.2 %collective-permute-start = (bf16[32,4096]{1,0:T(8,128)(2,1)S(1)}, bf16[32,4096]{1,0:T(8,128)(2,1)S(1)}, u32[]{:S(2)}, u32[]{:S(2)}) collective-permute-start(bf16[32,4096]{1,0:T(8,128)(2,1)S(1)} %get-tuple-element.651), channel_id=1, source_target_pairs={{32,0},{64,32},{96,64},{128,96},{160,128},{192,160},{224,192},{256... | collective-permute-start | bytes 786440 | tf_op jit(solution)/shard_map/while/body/eval_jaxpr/ppermute | solution.py:16
  433.8 11.4 %collective-permute-start = (bf16[32,4096]{1,0:T(8,128)(2,1)S(1)}, bf16[32,4096]{1,0:T(8,128)(2,1)S(1)}, u32[]{:S(2)}, u32[]{:S(2)}) collective-permute-start(bf16[32,4096]{1,0:T(8,128)(2,1)S(1)} %get-tuple-element.651), channel_id=1, source_target_pairs={{32,0},{64,32},{96,64},{128,96},{160,128},{192,160},{224,192},{256... | collective-permute-start | bytes 786440 | tf_op jit(solution)/shard_map/while/body/eval_jaxpr/ppermute | solution.py:16
  462.7 112.3 %reduce-scatter.6.cloned.1.call-start = ((), (), s32[]{:S(2)}) async-start(), calls=%async_computation.6 | async-start | bytes 2359296 | tf_op jit(solution)/shard_map/reduce_scatter | solution.py:305
  529.9 69.6 %reduce-scatter.8.cloned.1.call-start = ((), (), s32[]{:S(2)}) async-start(), calls=%async_computation.7 | async-start | bytes 393216 | tf_op jit(solution)/shard_map/reduce_scatter | solution.py:308
  (10 other events, 103.7 us)
Sparse Core Ops, SparseCore 0:
  13.8 48.4 all-gather.3
  64.3 25.5 all-gather.5
  462.9 66.9 reduce-scatter.3
  532.8 42.1 reduce-scatter.5
  577.9 21.6 reduce-scatter.7

commit v12 on v11

--- a/solution.py
+++ b/solution.py
@@ -148,33 +148,37 @@
 
 def unpack_kernel(rows_ref, gain_ref, wp_ref, wb_ref, gain_out):
     proj_cols = wp_ref.shape[-1]
-    rows = rows_ref.shape[1]
-    for core in range(rows_ref.shape[0]):
-        block = rows_ref[core]
-        wp_ref[core * rows : (core + 1) * rows, :] = block[:, :proj_cols]
-        wb_ref[core * rows : (core + 1) * rows, :] = block[:, proj_cols:]
-        gain_out[core : core + 1, :] = gain_ref[core, 0:1, : gain_out.shape[-1]].astype(jnp.float32)
+    rows = rows_ref.shape[2]
+    fc, fz = rows_ref.shape[0], rows_ref.shape[1]
+    for z in range(fz):
+        for core in range(fc):
+            at = z * fc + core
+            block = rows_ref[core, z]
+            wp_ref[at * rows : (at + 1) * rows, :] = block[:, :proj_cols]
+            wb_ref[at * rows : (at + 1) * rows, :] = block[:, proj_cols:]
+            gain_out[at : at + 1, :] = gain_ref[core, z, 0:1, : gain_out.shape[-1]].astype(jnp.float32)
 
 
 def unpack_weights(staged, rows_here, head):
     cols = staged.shape[-1]
     groups = FC * FZ * FX
+    span = FC * FZ
     return pl.pallas_call(
         unpack_kernel,
         out_shape=(
             jax.ShapeDtypeStruct((groups * rows_here, 3 * head), staged.dtype),
             jax.ShapeDtypeStruct((groups * rows_here, cols - 3 * head), staged.dtype),
-            jax.ShapeDtypeStruct((FX * FZ, FC, rows_here), jnp.float32),
-        ),
-        grid=(FX, FZ),
+            jax.ShapeDtypeStruct((FX, span, rows_here), jnp.float32),
+        ),
+        grid=(FX,),
         in_specs=[
-            pl.BlockSpec((FC, None, None, rows_here, cols), lambda x, z: (0, z, x, 0, 0)),
-            pl.BlockSpec((FC, None, None, 16, cols), lambda x, z: (0, z, x, rows_here // 16, 0)),
+            pl.BlockSpec((FC, FZ, None, rows_here, cols), lambda x: (0, 0, x, 0, 0)),
+            pl.BlockSpec((FC, FZ, None, 16, cols), lambda x: (0, 0, x, rows_here // 16, 0)),
         ],
         out_specs=[
-            pl.BlockSpec((FC * rows_here, 3 * head), lambda x, z: (x * FZ + z, 0)),
-            pl.BlockSpec((FC * rows_here, cols - 3 * head), lambda x, z: (x * FZ + z, 0)),
-            pl.BlockSpec((None, FC, rows_here), lambda x, z: (x * FZ + z, 0, 0)),
+            pl.BlockSpec((span * rows_here, 3 * head), lambda x: (x, 0)),
+            pl.BlockSpec((span * rows_here, cols - 3 * head), lambda x: (x, 0)),
+            pl.BlockSpec((None, span, rows_here), lambda x: (x, 0, 0)),
         ],
     )(staged, staged)
 

time: 609 us -> 602 us (0.989)
  Pallas kernels: 136 us -> 129 us
    pallas_call x1, Pallas kernels: 9.7 us -> 3.33 us  [unpack_weights(): pl.pallas_call(unpack_kernel, out_shape=(jax.ShapeDtypeStruct((groups * r...]
where the time goes in v12:
time: 602 us; the launch traced here: 601 us
  waiting for transfers between devices  366 us (61%)
  Pallas kernels  129 us (21%)
  blocking collectives  41.8 us (7%)
  starting transfers between devices  28.6 us (5%)
  other arithmetic  13.9 us (2%)
  between operations  13.9 us (2%)
  matrix products  6.11 us (1%)
    ppermute x22, waiting for transfers between devices, passed_along(): lax.ppermute(value, axis, [(source, source + steps) for source in range(l...  195 us
    pallas_call x23, Pallas kernels, tick_call(): pl.pallas_call(tick_kernel, out_shape=(jax.ShapeDtypeStruct((length, widt...  114 us
    reduce_scatter x1, waiting for transfers between devices, on_device(): lax.psum_scatter(terms.reshape(FC, -1, cols), 'fc', scatter_dimension=0,...  67.2 us
    all_gather x1, waiting for transfers between devices, on_device(): staged = lax.all_gather(staged, 'fz', axis=0, tiled=True)  48.5 us
    all_gather x1, blocking collectives, on_device(): gain_sum = jnp.sum(lax.all_gather(gain_acc, FSDP, axis=0), axis=0)  36.5 us
    ppermute x22, starting transfers between devices, passed_along(): lax.ppermute(value, axis, [(source, source + steps) for source in range(l...  28.4 us
    reduce_scatter x1, waiting for transfers between devices, on_device(): lax.psum_scatter(terms.reshape(FX, -1, cols), 'fx', scatter_dimension=0,...  24.4 us
    all_gather x1, waiting for transfers between devices, on_device(): staged = lax.all_gather(staged, 'fc', axis=0, tiled=True)  23.4 us
  transfers between devices with their start and end apart: 27, of which 27 were waited for; matrix products, arithmetic and copies ran while one was open for 1% of the time, Pallas kernels for 0%

profile of v12, /device:TPU:1, one launch (start us, length us, event | category | flops | bytes accessed | tf_op | source)
XLA Modules:
  0.0 601.3 jit_solution(14524509881904112524)
XLA Ops:
  13.7 48.5 %all-gather.4.cloned.1.call-done = bf16[2304,512]{1,0:T(8,128)(2,1)} async-done(((bf16[288,512]{1,0:T(8,128)(2,1)}), bf16[2304,512]{1,0:T(8,128)(2,1)}) %all-gather.4.cloned.1.call-update) | async-done | bytes 2359312 | tf_op jit(solution)/shard_map/all_gather | solution.py:235
  66.5 23.4 %all-gather.6.cloned.1.call-done = bf16[4608,512]{1,0:T(8,128)(2,1)} async-done(((bf16[2304,512]{1,0:T(8,128)(2,1)}), bf16[4608,512]{1,0:T(8,128)(2,1)}) %all-gather.6.cloned.1.call-update) | async-done | bytes 4718608 | tf_op jit(solution)/shard_map/all_gather | solution.py:236
  105.3 333.5 %while.21 = (s32[]{:T(128)}, bf16[32,4096]{1,0:T(8,128)(2,1)S(1)}, bf16[10,32,4096]{2,1,0:T(8,128)(2,1)S(1)}, bf16[10,32,384]{2,1,0:T(8,128)(2,1)S(1)}, f32[4096...) while((s32[]{:T(128)}, bf16[32,4096]{1,0:T(8,128)(2,1)S(1)}, ...), condition=%wide.region_4.5_spmd, body=%wide.region_3.4_spmd.sunk | while | flops 268435488 | bytes 6291851 | solution.py:297
  111.6 8.3 %collective-permute-done = bf16[32,4096]{1,0:T(8,128)(2,1)S(1)} collective-permute-done((bf16[32,4096]{1,0:T(8,128)(2,1)S(1)}, bf16[32,4096]{1,0:T(8,128)(2,1)S(1)}, u32[]{:S(2)}, u32[]{:S(2)}) %collective-permute-start) | collective-permute-done | bytes 262176 | tf_op jit(solution)/shard_map/while/body/eval_jaxpr/ppermute | solution.py:16
  126.2 7.4 %collective-permute-done = bf16[32,4096]{1,0:T(8,128)(2,1)S(1)} collective-permute-done((bf16[32,4096]{1,0:T(8,128)(2,1)S(1)}, bf16[32,4096]{1,0:T(8,128)(2,1)S(1)}, u32[]{:S(2)}, u32[]{:S(2)}) %collective-permute-start) | collective-permute-done | bytes 262176 | tf_op jit(solution)/shard_map/while/body/eval_jaxpr/ppermute | solution.py:16
  190.9 7.0 %collective-permute-done = bf16[32,4096]{1,0:T(8,128)(2,1)S(1)} collective-permute-done((bf16[32,4096]{1,0:T(8,128)(2,1)S(1)}, bf16[32,4096]{1,0:T(8,128)(2,1)S(1)}, u32[]{:S(2)}, u32[]{:S(2)}) %collective-permute-start) | collective-permute-done | bytes 262176 | tf_op jit(solution)/shard_map/while/body/eval_jaxpr/ppermute | solution.py:16
  217.6 7.0 %collective-permute-done = bf16[32,4096]{1,0:T(8,128)(2,1)S(1)} collective-permute-done((bf16[32,4096]{1,0:T(8,128)(2,1)S(1)}, bf16[32,4096]{1,0:T(8,128)(2,1)S(1)}, u32[]{:S(2)}, u32[]{:S(2)}) %collective-permute-start) | collective-permute-done | bytes 262176 | tf_op jit(solution)/shard_map/while/body/eval_jaxpr/ppermute | solution.py:16
  244.3 9.3 %collective-permute-done = bf16[32,4096]{1,0:T(8,128)(2,1)S(1)} collective-permute-done((bf16[32,4096]{1,0:T(8,128)(2,1)S(1)}, bf16[32,4096]{1,0:T(8,128)(2,1)S(1)}, u32[]{:S(2)}, u32[]{:S(2)}) %collective-permute-start) | collective-permute-done | bytes 262176 | tf_op jit(solution)/shard_map/while/body/eval_jaxpr/ppermute | solution.py:16
  259.9 9.4 %collective-permute-done = bf16[32,4096]{1,0:T(8,128)(2,1)S(1)} collective-permute-done((bf16[32,4096]{1,0:T(8,128)(2,1)S(1)}, bf16[32,4096]{1,0:T(8,128)(2,1)S(1)}, u32[]{:S(2)}, u32[]{:S(2)}) %collective-permute-start) | collective-permute-done | bytes 262176 | tf_op jit(solution)/shard_map/while/body/eval_jaxpr/ppermute | solution.py:16
  275.6 9.4 %collective-permute-done = bf16[32,4096]{1,0:T(8,128)(2,1)S(1)} collective-permute-done((bf16[32,4096]{1,0:T(8,128)(2,1)S(1)}, bf16[32,4096]{1,0:T(8,128)(2,1)S(1)}, u32[]{:S(2)}, u32[]{:S(2)}) %collective-permute-start) | collective-permute-done | bytes 262176 | tf_op jit(solution)/shard_map/while/body/eval_jaxpr/ppermute | solution.py:16
  291.4 9.4 %collective-permute-done = bf16[32,4096]{1,0:T(8,128)(2,1)S(1)} collective-permute-done((bf16[32,4096]{1,0:T(8,128)(2,1)S(1)}, bf16[32,4096]{1,0:T(8,128)(2,1)S(1)}, u32[]{:S(2)}, u32[]{:S(2)}) %collective-permute-start) | collective-permute-done | bytes 262176 | tf_op jit(solution)/shard_map/while/body/eval_jaxpr/ppermute | solution.py:16
  307.1 9.4 %collective-permute-done = bf16[32,4096]{1,0:T(8,128)(2,1)S(1)} collective-permute-done((bf16[32,4096]{1,0:T(8,128)(2,1)S(1)}, bf16[32,4096]{1,0:T(8,128)(2,1)S(1)}, u32[]{:S(2)}, u32[]{:S(2)}) %collective-permute-start) | collective-permute-done | bytes 262176 | tf_op jit(solution)/shard_map/while/body/eval_jaxpr/ppermute | solution.py:16
  322.9 10.6 %collective-permute-done = bf16[32,4096]{1,0:T(8,128)(2,1)S(1)} collective-permute-done((bf16[32,4096]{1,0:T(8,128)(2,1)S(1)}, bf16[32,4096]{1,0:T(8,128)(2,1)S(1)}, u32[]{:S(2)}, u32[]{:S(2)}) %collective-permute-start) | collective-permute-done | bytes 262176 | tf_op jit(solution)/shard_map/while/body/eval_jaxpr/ppermute | solution.py:16
  339.8 12.1 %collective-permute-done = bf16[32,4096]{1,0:T(8,128)(2,1)S(1)} collective-permute-done((bf16[32,4096]{1,0:T(8,128)(2,1)S(1)}, bf16[32,4096]{1,0:T(8,128)(2,1)S(1)}, u32[]{:S(2)}, u32[]{:S(2)}) %collective-permute-start) | collective-permute-done | bytes 262176 | tf_op jit(solution)/shard_map/while/body/eval_jaxpr/ppermute | solution.py:16
  358.2 12.9 %collective-permute-done = bf16[32,4096]{1,0:T(8,128)(2,1)S(1)} collective-permute-done((bf16[32,4096]{1,0:T(8,128)(2,1)S(1)}, bf16[32,4096]{1,0:T(8,128)(2,1)S(1)}, u32[]{:S(2)}, u32[]{:S(2)}) %collective-permute-start) | collective-permute-done | bytes 262176 | tf_op jit(solution)/shard_map/while/body/eval_jaxpr/ppermute | solution.py:16
  377.4 12.3 %collective-permute-done = bf16[32,4096]{1,0:T(8,128)(2,1)S(1)} collective-permute-done((bf16[32,4096]{1,0:T(8,128)(2,1)S(1)}, bf16[32,4096]{1,0:T(8,128)(2,1)S(1)}, u32[]{:S(2)}, u32[]{:S(2)}) %collective-permute-start) | collective-permute-done | bytes 262176 | tf_op jit(solution)/shard_map/while/body/eval_jaxpr/ppermute | solution.py:16
  396.1 11.2 %collective-permute-done = bf16[32,4096]{1,0:T(8,128)(2,1)S(1)} collective-permute-done((bf16[32,4096]{1,0:T(8,128)(2,1)S(1)}, bf16[32,4096]{1,0:T(8,128)(2,1)S(1)}, u32[]{:S(2)}, u32[]{:S(2)}) %collective-permute-start) | collective-permute-done | bytes 262176 | tf_op jit(solution)/shard_map/while/body/eval_jaxpr/ppermute | solution.py:16
  413.6 9.0 %collective-permute-done = bf16[32,4096]{1,0:T(8,128)(2,1)S(1)} collective-permute-done((bf16[32,4096]{1,0:T(8,128)(2,1)S(1)}, bf16[32,4096]{1,0:T(8,128)(2,1)S(1)}, u32[]{:S(2)}, u32[]{:S(2)}) %collective-permute-start) | collective-permute-done | bytes 262176 | tf_op jit(solution)/shard_map/while/body/eval_jaxpr/ppermute | solution.py:16
  428.9 9.9 %collective-permute-done = bf16[32,4096]{1,0:T(8,128)(2,1)S(1)} collective-permute-done((bf16[32,4096]{1,0:T(8,128)(2,1)S(1)}, bf16[32,4096]{1,0:T(8,128)(2,1)S(1)}, u32[]{:S(2)}, u32[]{:S(2)}) %collective-permute-start) | collective-permute-done | bytes 262176 | tf_op jit(solution)/shard_map/while/body/eval_jaxpr/ppermute | solution.py:16
  444.4 11.9 %shard_map.61 = bf16[2,16,128,512]{3,2,1,0:T(8,128)(2,1)} custom-call(bf16[256,4096]{1,0:T(8,128)(2,1)} %fusion.3.hid_ref, bf16[10,32,4096]{2,1,0:T(8,128)(2,1)S(1)} %get-tuple-element.424.g_ref, bf16[10,32,384]{2,1,0:T(8,128)(2,1)S(1)} %get-tuple-element.425.gp_ref, bf16[256,128]{1,0:T(8,128)(2,1)} %bitcast.66), custom_call_target="tpu_custom_call" | custom-call | tf_op jit(solution)/shard_map/pallas_call | solution.py:207
  456.4 67.2 %reduce-scatter.4.cloned.1.call-done = bf16[1,2048,512]{2,1,0:T(8,128)(2,1)} async-done(((bf16[2,2048,512]{2,1,0:T(8,128)(2,1)}), bf16[1,2048,512]{2,1,0:T(8,128)(2,1)}) %reduce-scatter.4.cloned.1.call-update) | async-done | bytes 2097168 | tf_op jit(solution)/shard_map/reduce_scatter | solution.py:308
  523.6 36.5 %all-gather = f32[32,1,4096]{2,1,0:T(1,128)S(1)} all-gather(f32[1,1,4096]{2,1,0:T(1,128)S(1)} %bitcast.62), channel_id=1, replica_groups=mesh['sh'=2,'sy'=8,'fx'=2,'fz'=8,'fc'=2] {'fx','fz','fc'}, dimensions={0}, use_global_device_ids=true | all-gather | bytes 540672 | tf_op jit(solution)/shard_map/all_gather | solution.py:310
  561.1 7.7 %reduce-scatter.6.cloned.1.call-done = bf16[1,256,512]{2,1,0:T(8,128)(2,1)} async-done(((bf16[8,256,512]{2,1,0:T(8,128)(2,1)}), bf16[1,256,512]{2,1,0:T(8,128)(2,1)}) %reduce-scatter.6.cloned.1.call-update) | async-done | bytes 262160 | tf_op jit(solution)/shard_map/reduce_scatter | solution.py:309
  568.8 24.4 %reduce-scatter.8.cloned.1.call-done = bf16[1,128,512]{2,1,0:T(8,128)(2,1)} async-done(((bf16[2,128,512]{2,1,0:T(8,128)(2,1)}), bf16[1,128,512]{2,1,0:T(8,128)(2,1)}) %reduce-scatter.8.cloned.1.call-update) | async-done | bytes 131088 | tf_op jit(solution)/shard_map/reduce_scatter | solution.py:312
  (124 shorter events, 212.6 us)
Async XLA Ops:
  7.2 55.1 %all-gather.4.cloned.1.call-start = ((), (), s32[]{:S(2)}) async-start(), calls=%async_computation.3 | async-start | bytes 2654208 | tf_op jit(solution)/shard_map/all_gather | solution.py:235
  13.7 76.2 %all-gather.6.cloned.1.call-start = ((), (), s32[]{:S(2)}) async-start(), calls=%async_computation.4 | async-start | bytes 7077888 | tf_op jit(solution)/shard_map/all_gather | solution.py:236
  62.3 461.3 %reduce-scatter.4.cloned.1.call-start = ((), (), s32[]{:S(2)}) async-start(), calls=%async_computation.5 | async-start | bytes 6291456 | tf_op jit(solution)/shard_map/reduce_scatter | solution.py:308
  110.3 9.6 %collective-permute-start = (bf16[32,4096]{1,0:T(8,128)(2,1)S(1)}, bf16[32,4096]{1,0:T(8,128)(2,1)S(1)}, u32[]{:S(2)}, u32[]{:S(2)}) collective-permute-start(bf16[32,4096]{1,0:T(8,128)(2,1)S(1)} %get-tuple-element.651), channel_id=1, source_target_pairs={{32,0},{64,32},{96,64},{128,96},{160,128},{192,160},{224,192},{256... | collective-permute-start | bytes 786440 | tf_op jit(solution)/shard_map/while/body/eval_jaxpr/ppermute | solution.py:16
  124.9 8.7 %collective-permute-start = (bf16[32,4096]{1,0:T(8,128)(2,1)S(1)}, bf16[32,4096]{1,0:T(8,128)(2,1)S(1)}, u32[]{:S(2)}, u32[]{:S(2)}) collective-permute-start(bf16[32,4096]{1,0:T(8,128)(2,1)S(1)} %get-tuple-element.651), channel_id=1, source_target_pairs={{32,0},{64,32},{96,64},{128,96},{160,128},{192,160},{224,192},{256... | collective-permute-start | bytes 786440 | tf_op jit(solution)/shard_map/while/body/eval_jaxpr/ppermute | solution.py:16
  176.6 8.0 %collective-permute-start = (bf16[32,4096]{1,0:T(8,128)(2,1)S(1)}, bf16[32,4096]{1,0:T(8,128)(2,1)S(1)}, u32[]{:S(2)}, u32[]{:S(2)}) collective-permute-start(bf16[32,4096]{1,0:T(8,128)(2,1)S(1)} %get-tuple-element.651), channel_id=1, source_target_pairs={{32,0},{64,32},{96,64},{128,96},{160,128},{192,160},{224,192},{256... | collective-permute-start | bytes 786440 | tf_op jit(solution)/shard_map/while/body/eval_jaxpr/ppermute | solution.py:16
  189.6 8.3 %collective-permute-start = (bf16[32,4096]{1,0:T(8,128)(2,1)S(1)}, bf16[32,4096]{1,0:T(8,128)(2,1)S(1)}, u32[]{:S(2)}, u32[]{:S(2)}) collective-permute-start(bf16[32,4096]{1,0:T(8,128)(2,1)S(1)} %get-tuple-element.651), channel_id=1, source_target_pairs={{32,0},{64,32},{96,64},{128,96},{160,128},{192,160},{224,192},{256... | collective-permute-start | bytes 786440 | tf_op jit(solution)/shard_map/while/body/eval_jaxpr/ppermute | solution.py:16
  203.0 8.3 %collective-permute-start = (bf16[32,4096]{1,0:T(8,128)(2,1)S(1)}, bf16[32,4096]{1,0:T(8,128)(2,1)S(1)}, u32[]{:S(2)}, u32[]{:S(2)}) collective-permute-start(bf16[32,4096]{1,0:T(8,128)(2,1)S(1)} %get-tuple-element.651), channel_id=1, source_target_pairs={{32,0},{64,32},{96,64},{128,96},{160,128},{192,160},{224,192},{256... | collective-permute-start | bytes 786440 | tf_op jit(solution)/shard_map/while/body/eval_jaxpr/ppermute | solution.py:16
  216.3 8.3 %collective-permute-start = (bf16[32,4096]{1,0:T(8,128)(2,1)S(1)}, bf16[32,4096]{1,0:T(8,128)(2,1)S(1)}, u32[]{:S(2)}, u32[]{:S(2)}) collective-permute-start(bf16[32,4096]{1,0:T(8,128)(2,1)S(1)} %get-tuple-element.651), channel_id=1, source_target_pairs={{32,0},{64,32},{96,64},{128,96},{160,128},{192,160},{224,192},{256... | collective-permute-start | bytes 786440 | tf_op jit(solution)/shard_map/while/body/eval_jaxpr/ppermute | solution.py:16
  229.6 8.3 %collective-permute-start = (bf16[32,4096]{1,0:T(8,128)(2,1)S(1)}, bf16[32,4096]{1,0:T(8,128)(2,1)S(1)}, u32[]{:S(2)}, u32[]{:S(2)}) collective-permute-start(bf16[32,4096]{1,0:T(8,128)(2,1)S(1)} %get-tuple-element.651), channel_id=1, source_target_pairs={{32,0},{64,32},{96,64},{128,96},{160,128},{192,160},{224,192},{256... | collective-permute-start | bytes 786440 | tf_op jit(solution)/shard_map/while/body/eval_jaxpr/ppermute | solution.py:16
  243.0 10.6 %collective-permute-start = (bf16[32,4096]{1,0:T(8,128)(2,1)S(1)}, bf16[32,4096]{1,0:T(8,128)(2,1)S(1)}, u32[]{:S(2)}, u32[]{:S(2)}) collective-permute-start(bf16[32,4096]{1,0:T(8,128)(2,1)S(1)} %get-tuple-element.651), channel_id=1, source_target_pairs={{32,0},{64,32},{96,64},{128,96},{160,128},{192,160},{224,192},{256... | collective-permute-start | bytes 786440 | tf_op jit(solution)/shard_map/while/body/eval_jaxpr/ppermute | solution.py:16
  258.6 10.7 %collective-permute-start = (bf16[32,4096]{1,0:T(8,128)(2,1)S(1)}, bf16[32,4096]{1,0:T(8,128)(2,1)S(1)}, u32[]{:S(2)}, u32[]{:S(2)}) collective-permute-start(bf16[32,4096]{1,0:T(8,128)(2,1)S(1)} %get-tuple-element.651), channel_id=1, source_target_pairs={{32,0},{64,32},{96,64},{128,96},{160,128},{192,160},{224,192},{256... | collective-permute-start | bytes 786440 | tf_op jit(solution)/shard_map/while/body/eval_jaxpr/ppermute | solution.py:16
  274.3 10.7 %collective-permute-start = (bf16[32,4096]{1,0:T(8,128)(2,1)S(1)}, bf16[32,4096]{1,0:T(8,128)(2,1)S(1)}, u32[]{:S(2)}, u32[]{:S(2)}) collective-permute-start(bf16[32,4096]{1,0:T(8,128)(2,1)S(1)} %get-tuple-element.651), channel_id=1, source_target_pairs={{32,0},{64,32},{96,64},{128,96},{160,128},{192,160},{224,192},{256... | collective-permute-start | bytes 786440 | tf_op jit(solution)/shard_map/while/body/eval_jaxpr/ppermute | solution.py:16
  290.1 10.7 %collective-permute-start = (bf16[32,4096]{1,0:T(8,128)(2,1)S(1)}, bf16[32,4096]{1,0:T(8,128)(2,1)S(1)}, u32[]{:S(2)}, u32[]{:S(2)}) collective-permute-start(bf16[32,4096]{1,0:T(8,128)(2,1)S(1)} %get-tuple-element.651), channel_id=1, source_target_pairs={{32,0},{64,32},{96,64},{128,96},{160,128},{192,160},{224,192},{256... | collective-permute-start | bytes 786440 | tf_op jit(solution)/shard_map/while/body/eval_jaxpr/ppermute | solution.py:16
  305.8 10.7 %collective-permute-start = (bf16[32,4096]{1,0:T(8,128)(2,1)S(1)}, bf16[32,4096]{1,0:T(8,128)(2,1)S(1)}, u32[]{:S(2)}, u32[]{:S(2)}) collective-permute-start(bf16[32,4096]{1,0:T(8,128)(2,1)S(1)} %get-tuple-element.651), channel_id=1, source_target_pairs={{32,0},{64,32},{96,64},{128,96},{160,128},{192,160},{224,192},{256... | collective-permute-start | bytes 786440 | tf_op jit(solution)/shard_map/while/body/eval_jaxpr/ppermute | solution.py:16
  321.6 11.9 %collective-permute-start = (bf16[32,4096]{1,0:T(8,128)(2,1)S(1)}, bf16[32,4096]{1,0:T(8,128)(2,1)S(1)}, u32[]{:S(2)}, u32[]{:S(2)}) collective-permute-start(bf16[32,4096]{1,0:T(8,128)(2,1)S(1)} %get-tuple-element.651), channel_id=1, source_target_pairs={{32,0},{64,32},{96,64},{128,96},{160,128},{192,160},{224,192},{256... | collective-permute-start | bytes 786440 | tf_op jit(solution)/shard_map/while/body/eval_jaxpr/ppermute | solution.py:16
  338.5 13.4 %collective-permute-start = (bf16[32,4096]{1,0:T(8,128)(2,1)S(1)}, bf16[32,4096]{1,0:T(8,128)(2,1)S(1)}, u32[]{:S(2)}, u32[]{:S(2)}) collective-permute-start(bf16[32,4096]{1,0:T(8,128)(2,1)S(1)} %get-tuple-element.651), channel_id=1, source_target_pairs={{32,0},{64,32},{96,64},{128,96},{160,128},{192,160},{224,192},{256... | collective-permute-start | bytes 786440 | tf_op jit(solution)/shard_map/while/body/eval_jaxpr/ppermute | solution.py:16
  356.9 14.2 %collective-permute-start = (bf16[32,4096]{1,0:T(8,128)(2,1)S(1)}, bf16[32,4096]{1,0:T(8,128)(2,1)S(1)}, u32[]{:S(2)}, u32[]{:S(2)}) collective-permute-start(bf16[32,4096]{1,0:T(8,128)(2,1)S(1)} %get-tuple-element.651), channel_id=1, source_target_pairs={{32,0},{64,32},{96,64},{128,96},{160,128},{192,160},{224,192},{256... | collective-permute-start | bytes 786440 | tf_op jit(solution)/shard_map/while/body/eval_jaxpr/ppermute | solution.py:16
  376.1 13.7 %collective-permute-start = (bf16[32,4096]{1,0:T(8,128)(2,1)S(1)}, bf16[32,4096]{1,0:T(8,128)(2,1)S(1)}, u32[]{:S(2)}, u32[]{:S(2)}) collective-permute-start(bf16[32,4096]{1,0:T(8,128)(2,1)S(1)} %get-tuple-element.651), channel_id=1, source_target_pairs={{32,0},{64,32},{96,64},{128,96},{160,128},{192,160},{224,192},{256... | collective-permute-start | bytes 786440 | tf_op jit(solution)/shard_map/while/body/eval_jaxpr/ppermute | solution.py:16
  394.8 12.5 %collective-permute-start = (bf16[32,4096]{1,0:T(8,128)(2,1)S(1)}, bf16[32,4096]{1,0:T(8,128)(2,1)S(1)}, u32[]{:S(2)}, u32[]{:S(2)}) collective-permute-start(bf16[32,4096]{1,0:T(8,128)(2,1)S(1)} %get-tuple-element.651), channel_id=1, source_target_pairs={{32,0},{64,32},{96,64},{128,96},{160,128},{192,160},{224,192},{256... | collective-permute-start | bytes 786440 | tf_op jit(solution)/shard_map/while/body/eval_jaxpr/ppermute | solution.py:16
  412.3 10.3 %collective-permute-start = (bf16[32,4096]{1,0:T(8,128)(2,1)S(1)}, bf16[32,4096]{1,0:T(8,128)(2,1)S(1)}, u32[]{:S(2)}, u32[]{:S(2)}) collective-permute-start(bf16[32,4096]{1,0:T(8,128)(2,1)S(1)} %get-tuple-element.651), channel_id=1, source_target_pairs={{32,0},{64,32},{96,64},{128,96},{160,128},{192,160},{224,192},{256... | collective-permute-start | bytes 786440 | tf_op jit(solution)/shard_map/while/body/eval_jaxpr/ppermute | solution.py:16
  427.6 11.2 %collective-permute-start = (bf16[32,4096]{1,0:T(8,128)(2,1)S(1)}, bf16[32,4096]{1,0:T(8,128)(2,1)S(1)}, u32[]{:S(2)}, u32[]{:S(2)}) collective-permute-start(bf16[32,4096]{1,0:T(8,128)(2,1)S(1)} %get-tuple-element.651), channel_id=1, source_target_pairs={{32,0},{64,32},{96,64},{128,96},{160,128},{192,160},{224,192},{256... | collective-permute-start | bytes 786440 | tf_op jit(solution)/shard_map/while/body/eval_jaxpr/ppermute | solution.py:16
  456.3 112.4 %reduce-scatter.6.cloned.1.call-start = ((), (), s32[]{:S(2)}) async-start(), calls=%async_computation.6 | async-start | bytes 2359296 | tf_op jit(solution)/shard_map/reduce_scatter | solution.py:309
  523.6 69.6 %reduce-scatter.8.cloned.1.call-start = ((), (), s32[]{:S(2)}) async-start(), calls=%async_computation.7 | async-start | bytes 393216 | tf_op jit(solution)/shard_map/reduce_scatter | solution.py:312
  (10 other events, 103.6 us)
Sparse Core Ops, SparseCore 0:
  13.8 48.4 all-gather.3
  64.3 25.5 all-gather.5
  456.4 67.0 reduce-scatter.3
  526.5 42.2 reduce-scatter.5
  571.6 21.5 reduce-scatter.7

commit v13 on v12

--- a/solution.py
+++ b/solution.py
@@ -184,37 +184,39 @@
 
 def terms_kernel(hid_ref, g_ref, gp_ref, att_ref, out_ref):
     tokens = hid_ref.shape[0]
-    rows = out_ref.shape[1]
+    fc, fz, rows = out_ref.shape[0], out_ref.shape[1], out_ref.shape[2]
     gp = gp_ref[...].reshape(tokens, gp_ref.shape[-1])
     grads = g_ref[...].reshape(tokens, g_ref.shape[-1])
     att = att_ref[...]
-    for core in range(out_ref.shape[0]):
-        cut = slice(core * rows, (core + 1) * rows)
-        first = lax.dot_general(
-            hid_ref[:, cut], gp, (((0,), (0,)), ((), ())), preferred_element_type=jnp.float32
-        )
-        second = lax.dot_general(
-            grads[:, cut], att, (((0,), (0,)), ((), ())), preferred_element_type=jnp.float32
-        )
-        out_ref[core] = jnp.concatenate([first, second], axis=-1).astype(out_ref.dtype)
+    for z in range(fz):
+        for core in range(fc):
+            at = z * fc + core
+            cut = slice(at * rows, (at + 1) * rows)
+            first = lax.dot_general(
+                hid_ref[:, cut], gp, (((0,), (0,)), ((), ())), preferred_element_type=jnp.float32
+            )
+            second = lax.dot_general(
+                grads[:, cut], att, (((0,), (0,)), ((), ())), preferred_element_type=jnp.float32
+            )
+            out_ref[core, z] = jnp.concatenate([first, second], axis=-1).astype(out_ref.dtype)
 
 
 def weight_terms(hidden_flat, grad_store, proj_store, att_flat, rows_here):
     tokens, width = hidden_flat.shape
     micro_count, length = grad_store.shape[0] - 2, grad_store.shape[1]
     cols = proj_store.shape[-1] + att_flat.shape[-1]
-    both = FC * rows_here
+    span = FC * FZ * rows_here
     out = pl.pallas_call(
         terms_kernel,
-        out_shape=jax.ShapeDtypeStruct((FC, FZ * FX, rows_here, cols), jnp.bfloat16),
-        grid=(FX, FZ),
+        out_shape=jax.ShapeDtypeStruct((FC, FZ, FX, rows_here, cols), jnp.bfloat16),
+        grid=(FX,),
         in_specs=[
-            pl.BlockSpec((tokens, both), lambda x, z: (0, x * FZ + z)),
-            pl.BlockSpec((micro_count, length, both), lambda x, z: (0, 0, x * FZ + z)),
-            pl.BlockSpec((micro_count, length, proj_store.shape[-1]), lambda x, z: (0, 0, 0)),
-            pl.BlockSpec((tokens, att_flat.shape[-1]), lambda x, z: (0, 0)),
+            pl.BlockSpec((tokens, span), lambda x: (0, x)),
+            pl.BlockSpec((micro_count, length, span), lambda x: (0, 0, x)),
+            pl.BlockSpec((micro_count, length, proj_store.shape[-1]), lambda x: (0, 0, 0)),
+            pl.BlockSpec((tokens, att_flat.shape[-1]), lambda x: (0, 0)),
         ],
-        out_specs=pl.BlockSpec((FC, None, rows_here, cols), lambda x, z: (0, z * FX + x, 0, 0)),
+        out_specs=pl.BlockSpec((FC, FZ, None, rows_here, cols), lambda x: (0, 0, x, 0, 0)),
     )(hidden_flat, grad_store, proj_store, att_flat)
     return out.reshape(width, cols)
 

time: 602 us -> 595 us (0.988)
  Pallas kernels: 129 us -> 122 us
    pallas_call x1, Pallas kernels: 11.9 us -> 4.73 us  [weight_terms(): pl.pallas_call(terms_kernel, out_shape=jax.ShapeDtypeStruct((FC, FZ, FX,...]
where the time goes in v13:
time: 595 us; the launch traced here: 594 us
  waiting for transfers between devices  366 us (62%)
  Pallas kernels  122 us (21%)
  blocking collectives  41.9 us (7%)
  starting transfers between devices  28.6 us (5%)
  other arithmetic  13.9 us (2%)
  between operations  13.9 us (2%)
  matrix products  6.11 us (1%)
    ppermute x22, waiting for transfers between devices, passed_along(): lax.ppermute(value, axis, [(source, source + steps) for source in range(l...  195 us
    pallas_call x23, Pallas kernels, tick_call(): pl.pallas_call(tick_kernel, out_shape=(jax.ShapeDtypeStruct((length, widt...  114 us
    reduce_scatter x1, waiting for transfers between devices, on_device(): lax.psum_scatter(terms.reshape(FC, -1, cols), 'fc', scatter_dimension=0,...  67.2 us
    all_gather x1, waiting for transfers between devices, on_device(): staged = lax.all_gather(staged, 'fz', axis=0, tiled=True)  48.5 us
    all_gather x1, blocking collectives, on_device(): gain_sum = jnp.sum(lax.all_gather(gain_acc, FSDP, axis=0), axis=0)  36.5 us
    ppermute x22, starting transfers between devices, passed_along(): lax.ppermute(value, axis, [(source, source + steps) for source in range(l...  28.4 us
    reduce_scatter x1, waiting for transfers between devices, on_device(): lax.psum_scatter(terms.reshape(FX, -1, cols), 'fx', scatter_dimension=0,...  24.5 us
    all_gather x1, waiting for transfers between devices, on_device(): staged = lax.all_gather(staged, 'fc', axis=0, tiled=True)  23.4 us
  transfers between devices with their start and end apart: 27, of which 27 were waited for; matrix products, arithmetic and copies ran while one was open for 1% of the time, Pallas kernels for 0%

profile of v13, /device:TPU:1, one launch (start us, length us, event | category | flops | bytes accessed | tf_op | source)
XLA Modules:
  0.0 594.3 jit_solution(4822379037104327168)
XLA Ops:
  13.7 48.5 %all-gather.4.cloned.1.call-done = bf16[2304,512]{1,0:T(8,128)(2,1)} async-done(((bf16[288,512]{1,0:T(8,128)(2,1)}), bf16[2304,512]{1,0:T(8,128)(2,1)}) %all-gather.4.cloned.1.call-update) | async-done | bytes 2359312 | tf_op jit(solution)/shard_map/all_gather | solution.py:237
  66.5 23.4 %all-gather.6.cloned.1.call-done = bf16[4608,512]{1,0:T(8,128)(2,1)} async-done(((bf16[2304,512]{1,0:T(8,128)(2,1)}), bf16[4608,512]{1,0:T(8,128)(2,1)}) %all-gather.6.cloned.1.call-update) | async-done | bytes 4718608 | tf_op jit(solution)/shard_map/all_gather | solution.py:238
  105.3 333.5 %while.21 = (s32[]{:T(128)}, bf16[32,4096]{1,0:T(8,128)(2,1)S(1)}, bf16[10,32,4096]{2,1,0:T(8,128)(2,1)S(1)}, bf16[10,32,384]{2,1,0:T(8,128)(2,1)S(1)}, f32[4096...) while((s32[]{:T(128)}, bf16[32,4096]{1,0:T(8,128)(2,1)S(1)}, ...), condition=%wide.region_4.5_spmd, body=%wide.region_3.4_spmd.sunk | while | flops 268435488 | bytes 6291851 | solution.py:299
  111.6 8.3 %collective-permute-done = bf16[32,4096]{1,0:T(8,128)(2,1)S(1)} collective-permute-done((bf16[32,4096]{1,0:T(8,128)(2,1)S(1)}, bf16[32,4096]{1,0:T(8,128)(2,1)S(1)}, u32[]{:S(2)}, u32[]{:S(2)}) %collective-permute-start) | collective-permute-done | bytes 262176 | tf_op jit(solution)/shard_map/while/body/eval_jaxpr/ppermute | solution.py:16
  126.2 7.4 %collective-permute-done = bf16[32,4096]{1,0:T(8,128)(2,1)S(1)} collective-permute-done((bf16[32,4096]{1,0:T(8,128)(2,1)S(1)}, bf16[32,4096]{1,0:T(8,128)(2,1)S(1)}, u32[]{:S(2)}, u32[]{:S(2)}) %collective-permute-start) | collective-permute-done | bytes 262176 | tf_op jit(solution)/shard_map/while/body/eval_jaxpr/ppermute | solution.py:16
  190.9 7.0 %collective-permute-done = bf16[32,4096]{1,0:T(8,128)(2,1)S(1)} collective-permute-done((bf16[32,4096]{1,0:T(8,128)(2,1)S(1)}, bf16[32,4096]{1,0:T(8,128)(2,1)S(1)}, u32[]{:S(2)}, u32[]{:S(2)}) %collective-permute-start) | collective-permute-done | bytes 262176 | tf_op jit(solution)/shard_map/while/body/eval_jaxpr/ppermute | solution.py:16
  204.3 7.0 %collective-permute-done = bf16[32,4096]{1,0:T(8,128)(2,1)S(1)} collective-permute-done((bf16[32,4096]{1,0:T(8,128)(2,1)S(1)}, bf16[32,4096]{1,0:T(8,128)(2,1)S(1)}, u32[]{:S(2)}, u32[]{:S(2)}) %collective-permute-start) | collective-permute-done | bytes 262176 | tf_op jit(solution)/shard_map/while/body/eval_jaxpr/ppermute | solution.py:16
  217.6 7.0 %collective-permute-done = bf16[32,4096]{1,0:T(8,128)(2,1)S(1)} collective-permute-done((bf16[32,4096]{1,0:T(8,128)(2,1)S(1)}, bf16[32,4096]{1,0:T(8,128)(2,1)S(1)}, u32[]{:S(2)}, u32[]{:S(2)}) %collective-permute-start) | collective-permute-done | bytes 262176 | tf_op jit(solution)/shard_map/while/body/eval_jaxpr/ppermute | solution.py:16
  244.3 9.3 %collective-permute-done = bf16[32,4096]{1,0:T(8,128)(2,1)S(1)} collective-permute-done((bf16[32,4096]{1,0:T(8,128)(2,1)S(1)}, bf16[32,4096]{1,0:T(8,128)(2,1)S(1)}, u32[]{:S(2)}, u32[]{:S(2)}) %collective-permute-start) | collective-permute-done | bytes 262176 | tf_op jit(solution)/shard_map/while/body/eval_jaxpr/ppermute | solution.py:16
  259.9 9.4 %collective-permute-done = bf16[32,4096]{1,0:T(8,128)(2,1)S(1)} collective-permute-done((bf16[32,4096]{1,0:T(8,128)(2,1)S(1)}, bf16[32,4096]{1,0:T(8,128)(2,1)S(1)}, u32[]{:S(2)}, u32[]{:S(2)}) %collective-permute-start) | collective-permute-done | bytes 262176 | tf_op jit(solution)/shard_map/while/body/eval_jaxpr/ppermute | solution.py:16
  275.6 9.4 %collective-permute-done = bf16[32,4096]{1,0:T(8,128)(2,1)S(1)} collective-permute-done((bf16[32,4096]{1,0:T(8,128)(2,1)S(1)}, bf16[32,4096]{1,0:T(8,128)(2,1)S(1)}, u32[]{:S(2)}, u32[]{:S(2)}) %collective-permute-start) | collective-permute-done | bytes 262176 | tf_op jit(solution)/shard_map/while/body/eval_jaxpr/ppermute | solution.py:16
  291.4 9.4 %collective-permute-done = bf16[32,4096]{1,0:T(8,128)(2,1)S(1)} collective-permute-done((bf16[32,4096]{1,0:T(8,128)(2,1)S(1)}, bf16[32,4096]{1,0:T(8,128)(2,1)S(1)}, u32[]{:S(2)}, u32[]{:S(2)}) %collective-permute-start) | collective-permute-done | bytes 262176 | tf_op jit(solution)/shard_map/while/body/eval_jaxpr/ppermute | solution.py:16
  307.1 9.4 %collective-permute-done = bf16[32,4096]{1,0:T(8,128)(2,1)S(1)} collective-permute-done((bf16[32,4096]{1,0:T(8,128)(2,1)S(1)}, bf16[32,4096]{1,0:T(8,128)(2,1)S(1)}, u32[]{:S(2)}, u32[]{:S(2)}) %collective-permute-start) | collective-permute-done | bytes 262176 | tf_op jit(solution)/shard_map/while/body/eval_jaxpr/ppermute | solution.py:16
  322.9 10.6 %collective-permute-done = bf16[32,4096]{1,0:T(8,128)(2,1)S(1)} collective-permute-done((bf16[32,4096]{1,0:T(8,128)(2,1)S(1)}, bf16[32,4096]{1,0:T(8,128)(2,1)S(1)}, u32[]{:S(2)}, u32[]{:S(2)}) %collective-permute-start) | collective-permute-done | bytes 262176 | tf_op jit(solution)/shard_map/while/body/eval_jaxpr/ppermute | solution.py:16
  339.8 12.1 %collective-permute-done = bf16[32,4096]{1,0:T(8,128)(2,1)S(1)} collective-permute-done((bf16[32,4096]{1,0:T(8,128)(2,1)S(1)}, bf16[32,4096]{1,0:T(8,128)(2,1)S(1)}, u32[]{:S(2)}, u32[]{:S(2)}) %collective-permute-start) | collective-permute-done | bytes 262176 | tf_op jit(solution)/shard_map/while/body/eval_jaxpr/ppermute | solution.py:16
  358.2 12.9 %collective-permute-done = bf16[32,4096]{1,0:T(8,128)(2,1)S(1)} collective-permute-done((bf16[32,4096]{1,0:T(8,128)(2,1)S(1)}, bf16[32,4096]{1,0:T(8,128)(2,1)S(1)}, u32[]{:S(2)}, u32[]{:S(2)}) %collective-permute-start) | collective-permute-done | bytes 262176 | tf_op jit(solution)/shard_map/while/body/eval_jaxpr/ppermute | solution.py:16
  377.4 12.3 %collective-permute-done = bf16[32,4096]{1,0:T(8,128)(2,1)S(1)} collective-permute-done((bf16[32,4096]{1,0:T(8,128)(2,1)S(1)}, bf16[32,4096]{1,0:T(8,128)(2,1)S(1)}, u32[]{:S(2)}, u32[]{:S(2)}) %collective-permute-start) | collective-permute-done | bytes 262176 | tf_op jit(solution)/shard_map/while/body/eval_jaxpr/ppermute | solution.py:16
  396.1 11.2 %collective-permute-done = bf16[32,4096]{1,0:T(8,128)(2,1)S(1)} collective-permute-done((bf16[32,4096]{1,0:T(8,128)(2,1)S(1)}, bf16[32,4096]{1,0:T(8,128)(2,1)S(1)}, u32[]{:S(2)}, u32[]{:S(2)}) %collective-permute-start) | collective-permute-done | bytes 262176 | tf_op jit(solution)/shard_map/while/body/eval_jaxpr/ppermute | solution.py:16
  413.6 9.0 %collective-permute-done = bf16[32,4096]{1,0:T(8,128)(2,1)S(1)} collective-permute-done((bf16[32,4096]{1,0:T(8,128)(2,1)S(1)}, bf16[32,4096]{1,0:T(8,128)(2,1)S(1)}, u32[]{:S(2)}, u32[]{:S(2)}) %collective-permute-start) | collective-permute-done | bytes 262176 | tf_op jit(solution)/shard_map/while/body/eval_jaxpr/ppermute | solution.py:16
  428.9 9.9 %collective-permute-done = bf16[32,4096]{1,0:T(8,128)(2,1)S(1)} collective-permute-done((bf16[32,4096]{1,0:T(8,128)(2,1)S(1)}, bf16[32,4096]{1,0:T(8,128)(2,1)S(1)}, u32[]{:S(2)}, u32[]{:S(2)}) %collective-permute-start) | collective-permute-done | bytes 262176 | tf_op jit(solution)/shard_map/while/body/eval_jaxpr/ppermute | solution.py:16
  449.2 67.2 %reduce-scatter.4.cloned.1.call-done = bf16[1,2048,512]{2,1,0:T(8,128)(2,1)} async-done(((bf16[2,2048,512]{2,1,0:T(8,128)(2,1)}), bf16[1,2048,512]{2,1,0:T(8,128)(2,1)}) %reduce-scatter.4.cloned.1.call-update) | async-done | bytes 2097168 | tf_op jit(solution)/shard_map/reduce_scatter | solution.py:310
  516.5 36.5 %all-gather = f32[32,1,4096]{2,1,0:T(1,128)S(1)} all-gather(f32[1,1,4096]{2,1,0:T(1,128)S(1)} %bitcast.62), channel_id=1, replica_groups=mesh['sh'=2,'sy'=8,'fx'=2,'fz'=8,'fc'=2] {'fx','fz','fc'}, dimensions={0}, use_global_device_ids=true | all-gather | bytes 540672 | tf_op jit(solution)/shard_map/all_gather | solution.py:312
  554.0 7.5 %reduce-scatter.6.cloned.1.call-done = bf16[1,256,512]{2,1,0:T(8,128)(2,1)} async-done(((bf16[8,256,512]{2,1,0:T(8,128)(2,1)}), bf16[1,256,512]{2,1,0:T(8,128)(2,1)}) %reduce-scatter.6.cloned.1.call-update) | async-done | bytes 262160 | tf_op jit(solution)/shard_map/reduce_scatter | solution.py:311
  561.6 24.5 %reduce-scatter.8.cloned.1.call-done = bf16[1,128,512]{2,1,0:T(8,128)(2,1)} async-done(((bf16[2,128,512]{2,1,0:T(8,128)(2,1)}), bf16[1,128,512]{2,1,0:T(8,128)(2,1)}) %reduce-scatter.8.cloned.1.call-update) | async-done | bytes 131088 | tf_op jit(solution)/shard_map/reduce_scatter | solution.py:314
  (124 shorter events, 210.3 us)
Async XLA Ops:
  7.2 55.1 %all-gather.4.cloned.1.call-start = ((), (), s32[]{:S(2)}) async-start(), calls=%async_computation.3 | async-start | bytes 2654208 | tf_op jit(solution)/shard_map/all_gather | solution.py:237
  13.7 76.2 %all-gather.6.cloned.1.call-start = ((), (), s32[]{:S(2)}) async-start(), calls=%async_computation.4 | async-start | bytes 7077888 | tf_op jit(solution)/shard_map/all_gather | solution.py:238
  62.3 454.1 %reduce-scatter.4.cloned.1.call-start = ((), (), s32[]{:S(2)}) async-start(), calls=%async_computation.5 | async-start | bytes 6291456 | tf_op jit(solution)/shard_map/reduce_scatter | solution.py:310
  110.3 9.6 %collective-permute-start = (bf16[32,4096]{1,0:T(8,128)(2,1)S(1)}, bf16[32,4096]{1,0:T(8,128)(2,1)S(1)}, u32[]{:S(2)}, u32[]{:S(2)}) collective-permute-start(bf16[32,4096]{1,0:T(8,128)(2,1)S(1)} %get-tuple-element.651), channel_id=1, source_target_pairs={{32,0},{64,32},{96,64},{128,96},{160,128},{192,160},{224,192},{256... | collective-permute-start | bytes 786440 | tf_op jit(solution)/shard_map/while/body/eval_jaxpr/ppermute | solution.py:16
  124.9 8.7 %collective-permute-start = (bf16[32,4096]{1,0:T(8,128)(2,1)S(1)}, bf16[32,4096]{1,0:T(8,128)(2,1)S(1)}, u32[]{:S(2)}, u32[]{:S(2)}) collective-permute-start(bf16[32,4096]{1,0:T(8,128)(2,1)S(1)} %get-tuple-element.651), channel_id=1, source_target_pairs={{32,0},{64,32},{96,64},{128,96},{160,128},{192,160},{224,192},{256... | collective-permute-start | bytes 786440 | tf_op jit(solution)/shard_map/while/body/eval_jaxpr/ppermute | solution.py:16
  176.6 8.0 %collective-permute-start = (bf16[32,4096]{1,0:T(8,128)(2,1)S(1)}, bf16[32,4096]{1,0:T(8,128)(2,1)S(1)}, u32[]{:S(2)}, u32[]{:S(2)}) collective-permute-start(bf16[32,4096]{1,0:T(8,128)(2,1)S(1)} %get-tuple-element.651), channel_id=1, source_target_pairs={{32,0},{64,32},{96,64},{128,96},{160,128},{192,160},{224,192},{256... | collective-permute-start | bytes 786440 | tf_op jit(solution)/shard_map/while/body/eval_jaxpr/ppermute | solution.py:16
  189.6 8.3 %collective-permute-start = (bf16[32,4096]{1,0:T(8,128)(2,1)S(1)}, bf16[32,4096]{1,0:T(8,128)(2,1)S(1)}, u32[]{:S(2)}, u32[]{:S(2)}) collective-permute-start(bf16[32,4096]{1,0:T(8,128)(2,1)S(1)} %get-tuple-element.651), channel_id=1, source_target_pairs={{32,0},{64,32},{96,64},{128,96},{160,128},{192,160},{224,192},{256... | collective-permute-start | bytes 786440 | tf_op jit(solution)/shard_map/while/body/eval_jaxpr/ppermute | solution.py:16
  203.0 8.3 %collective-permute-start = (bf16[32,4096]{1,0:T(8,128)(2,1)S(1)}, bf16[32,4096]{1,0:T(8,128)(2,1)S(1)}, u32[]{:S(2)}, u32[]{:S(2)}) collective-permute-start(bf16[32,4096]{1,0:T(8,128)(2,1)S(1)} %get-tuple-element.651), channel_id=1, source_target_pairs={{32,0},{64,32},{96,64},{128,96},{160,128},{192,160},{224,192},{256... | collective-permute-start | bytes 786440 | tf_op jit(solution)/shard_map/while/body/eval_jaxpr/ppermute | solution.py:16
  216.3 8.3 %collective-permute-start = (bf16[32,4096]{1,0:T(8,128)(2,1)S(1)}, bf16[32,4096]{1,0:T(8,128)(2,1)S(1)}, u32[]{:S(2)}, u32[]{:S(2)}) collective-permute-start(bf16[32,4096]{1,0:T(8,128)(2,1)S(1)} %get-tuple-element.651), channel_id=1, source_target_pairs={{32,0},{64,32},{96,64},{128,96},{160,128},{192,160},{224,192},{256... | collective-permute-start | bytes 786440 | tf_op jit(solution)/shard_map/while/body/eval_jaxpr/ppermute | solution.py:16
  229.6 8.3 %collective-permute-start = (bf16[32,4096]{1,0:T(8,128)(2,1)S(1)}, bf16[32,4096]{1,0:T(8,128)(2,1)S(1)}, u32[]{:S(2)}, u32[]{:S(2)}) collective-permute-start(bf16[32,4096]{1,0:T(8,128)(2,1)S(1)} %get-tuple-element.651), channel_id=1, source_target_pairs={{32,0},{64,32},{96,64},{128,96},{160,128},{192,160},{224,192},{256... | collective-permute-start | bytes 786440 | tf_op jit(solution)/shard_map/while/body/eval_jaxpr/ppermute | solution.py:16
  243.0 10.6 %collective-permute-start = (bf16[32,4096]{1,0:T(8,128)(2,1)S(1)}, bf16[32,4096]{1,0:T(8,128)(2,1)S(1)}, u32[]{:S(2)}, u32[]{:S(2)}) collective-permute-start(bf16[32,4096]{1,0:T(8,128)(2,1)S(1)} %get-tuple-element.651), channel_id=1, source_target_pairs={{32,0},{64,32},{96,64},{128,96},{160,128},{192,160},{224,192},{256... | collective-permute-start | bytes 786440 | tf_op jit(solution)/shard_map/while/body/eval_jaxpr/ppermute | solution.py:16
  258.6 10.7 %collective-permute-start = (bf16[32,4096]{1,0:T(8,128)(2,1)S(1)}, bf16[32,4096]{1,0:T(8,128)(2,1)S(1)}, u32[]{:S(2)}, u32[]{:S(2)}) collective-permute-start(bf16[32,4096]{1,0:T(8,128)(2,1)S(1)} %get-tuple-element.651), channel_id=1, source_target_pairs={{32,0},{64,32},{96,64},{128,96},{160,128},{192,160},{224,192},{256... | collective-permute-start | bytes 786440 | tf_op jit(solution)/shard_map/while/body/eval_jaxpr/ppermute | solution.py:16
  274.3 10.7 %collective-permute-start = (bf16[32,4096]{1,0:T(8,128)(2,1)S(1)}, bf16[32,4096]{1,0:T(8,128)(2,1)S(1)}, u32[]{:S(2)}, u32[]{:S(2)}) collective-permute-start(bf16[32,4096]{1,0:T(8,128)(2,1)S(1)} %get-tuple-element.651), channel_id=1, source_target_pairs={{32,0},{64,32},{96,64},{128,96},{160,128},{192,160},{224,192},{256... | collective-permute-start | bytes 786440 | tf_op jit(solution)/shard_map/while/body/eval_jaxpr/ppermute | solution.py:16
  290.1 10.7 %collective-permute-start = (bf16[32,4096]{1,0:T(8,128)(2,1)S(1)}, bf16[32,4096]{1,0:T(8,128)(2,1)S(1)}, u32[]{:S(2)}, u32[]{:S(2)}) collective-permute-start(bf16[32,4096]{1,0:T(8,128)(2,1)S(1)} %get-tuple-element.651), channel_id=1, source_target_pairs={{32,0},{64,32},{96,64},{128,96},{160,128},{192,160},{224,192},{256... | collective-permute-start | bytes 786440 | tf_op jit(solution)/shard_map/while/body/eval_jaxpr/ppermute | solution.py:16
  305.8 10.7 %collective-permute-start = (bf16[32,4096]{1,0:T(8,128)(2,1)S(1)}, bf16[32,4096]{1,0:T(8,128)(2,1)S(1)}, u32[]{:S(2)}, u32[]{:S(2)}) collective-permute-start(bf16[32,4096]{1,0:T(8,128)(2,1)S(1)} %get-tuple-element.651), channel_id=1, source_target_pairs={{32,0},{64,32},{96,64},{128,96},{160,128},{192,160},{224,192},{256... | collective-permute-start | bytes 786440 | tf_op jit(solution)/shard_map/while/body/eval_jaxpr/ppermute | solution.py:16
  321.6 11.9 %collective-permute-start = (bf16[32,4096]{1,0:T(8,128)(2,1)S(1)}, bf16[32,4096]{1,0:T(8,128)(2,1)S(1)}, u32[]{:S(2)}, u32[]{:S(2)}) collective-permute-start(bf16[32,4096]{1,0:T(8,128)(2,1)S(1)} %get-tuple-element.651), channel_id=1, source_target_pairs={{32,0},{64,32},{96,64},{128,96},{160,128},{192,160},{224,192},{256... | collective-permute-start | bytes 786440 | tf_op jit(solution)/shard_map/while/body/eval_jaxpr/ppermute | solution.py:16
  338.5 13.4 %collective-permute-start = (bf16[32,4096]{1,0:T(8,128)(2,1)S(1)}, bf16[32,4096]{1,0:T(8,128)(2,1)S(1)}, u32[]{:S(2)}, u32[]{:S(2)}) collective-permute-start(bf16[32,4096]{1,0:T(8,128)(2,1)S(1)} %get-tuple-element.651), channel_id=1, source_target_pairs={{32,0},{64,32},{96,64},{128,96},{160,128},{192,160},{224,192},{256... | collective-permute-start | bytes 786440 | tf_op jit(solution)/shard_map/while/body/eval_jaxpr/ppermute | solution.py:16
  356.9 14.2 %collective-permute-start = (bf16[32,4096]{1,0:T(8,128)(2,1)S(1)}, bf16[32,4096]{1,0:T(8,128)(2,1)S(1)}, u32[]{:S(2)}, u32[]{:S(2)}) collective-permute-start(bf16[32,4096]{1,0:T(8,128)(2,1)S(1)} %get-tuple-element.651), channel_id=1, source_target_pairs={{32,0},{64,32},{96,64},{128,96},{160,128},{192,160},{224,192},{256... | collective-permute-start | bytes 786440 | tf_op jit(solution)/shard_map/while/body/eval_jaxpr/ppermute | solution.py:16
  376.1 13.7 %collective-permute-start = (bf16[32,4096]{1,0:T(8,128)(2,1)S(1)}, bf16[32,4096]{1,0:T(8,128)(2,1)S(1)}, u32[]{:S(2)}, u32[]{:S(2)}) collective-permute-start(bf16[32,4096]{1,0:T(8,128)(2,1)S(1)} %get-tuple-element.651), channel_id=1, source_target_pairs={{32,0},{64,32},{96,64},{128,96},{160,128},{192,160},{224,192},{256... | collective-permute-start | bytes 786440 | tf_op jit(solution)/shard_map/while/body/eval_jaxpr/ppermute | solution.py:16
  394.8 12.5 %collective-permute-start = (bf16[32,4096]{1,0:T(8,128)(2,1)S(1)}, bf16[32,4096]{1,0:T(8,128)(2,1)S(1)}, u32[]{:S(2)}, u32[]{:S(2)}) collective-permute-start(bf16[32,4096]{1,0:T(8,128)(2,1)S(1)} %get-tuple-element.651), channel_id=1, source_target_pairs={{32,0},{64,32},{96,64},{128,96},{160,128},{192,160},{224,192},{256... | collective-permute-start | bytes 786440 | tf_op jit(solution)/shard_map/while/body/eval_jaxpr/ppermute | solution.py:16
  412.3 10.3 %collective-permute-start = (bf16[32,4096]{1,0:T(8,128)(2,1)S(1)}, bf16[32,4096]{1,0:T(8,128)(2,1)S(1)}, u32[]{:S(2)}, u32[]{:S(2)}) collective-permute-start(bf16[32,4096]{1,0:T(8,128)(2,1)S(1)} %get-tuple-element.651), channel_id=1, source_target_pairs={{32,0},{64,32},{96,64},{128,96},{160,128},{192,160},{224,192},{256... | collective-permute-start | bytes 786440 | tf_op jit(solution)/shard_map/while/body/eval_jaxpr/ppermute | solution.py:16
  427.6 11.2 %collective-permute-start = (bf16[32,4096]{1,0:T(8,128)(2,1)S(1)}, bf16[32,4096]{1,0:T(8,128)(2,1)S(1)}, u32[]{:S(2)}, u32[]{:S(2)}) collective-permute-start(bf16[32,4096]{1,0:T(8,128)(2,1)S(1)} %get-tuple-element.651), channel_id=1, source_target_pairs={{32,0},{64,32},{96,64},{128,96},{160,128},{192,160},{224,192},{256... | collective-permute-start | bytes 786440 | tf_op jit(solution)/shard_map/while/body/eval_jaxpr/ppermute | solution.py:16
  449.2 112.4 %reduce-scatter.6.cloned.1.call-start = ((), (), s32[]{:S(2)}) async-start(), calls=%async_computation.6 | async-start | bytes 2359296 | tf_op jit(solution)/shard_map/reduce_scatter | solution.py:311
  516.4 69.7 %reduce-scatter.8.cloned.1.call-start = ((), (), s32[]{:S(2)}) async-start(), calls=%async_computation.7 | async-start | bytes 393216 | tf_op jit(solution)/shard_map/reduce_scatter | solution.py:314
  (10 other events, 103.6 us)
Sparse Core Ops, SparseCore 0:
  13.8 48.4 all-gather.3
  64.3 25.5 all-gather.5
  449.3 67.0 reduce-scatter.3
  519.3 42.1 reduce-scatter.5
  564.4 21.6 reduce-scatter.7

commit v14 on v13

--- a/solution.py
+++ b/solution.py
@@ -309,7 +309,9 @@
     cols = terms.shape[1]
     terms = lax.psum_scatter(terms.reshape(FC, -1, cols), "fc", scatter_dimension=0, tiled=True)
     terms = lax.psum_scatter(terms.reshape(FZ, -1, cols), "fz", scatter_dimension=0, tiled=True)
-    gain_sum = jnp.sum(lax.all_gather(gain_acc, FSDP, axis=0), axis=0)
+    gain_sum = gain_acc
+    for axis in ("fc", "fz", "fx"):
+        gain_sum = jnp.sum(lax.all_gather(gain_sum, axis, axis=0), axis=0)
     terms, gain_sum = lax.optimization_barrier((terms, gain_sum))
     terms = lax.psum_scatter(terms.reshape(FX, -1, cols), "fx", scatter_dimension=0, tiled=True)
     shard = terms.reshape(rows_here, cols).astype(jnp.float32)

time: 595 us -> 595 us (level)
  blocking collectives: 41.9 us -> 30.2 us
  waiting for transfers between devices: 366 us -> 377 us
    all_gather x1 -> x3, blocking collectives: 36.5 us -> 24.8 us  [on_device(): gain_sum = jnp.sum(lax.all_gather(gain_sum, axis, axis=0), axis=0)]
    reduce_scatter x1, waiting for transfers between devices: 7.55 us -> 18.6 us  [on_device(): lax.psum_scatter(terms.reshape(FZ, -1, cols), 'fz', scatter_dimension=0,...]
where the time goes in v14:
time: 595 us; the launch traced here: 594 us
  waiting for transfers between devices  377 us (63%)
  Pallas kernels  122 us (21%)
  blocking collectives  30.2 us (5%)
  starting transfers between devices  28.6 us (5%)
  between operations  13.9 us (2%)
  other arithmetic  13.6 us (2%)
  matrix products  6.11 us (1%)
    ppermute x22, waiting for transfers between devices, passed_along(): lax.ppermute(value, axis, [(source, source + steps) for source in range(l...  195 us
    pallas_call x23, Pallas kernels, tick_call(): pl.pallas_call(tick_kernel, out_shape=(jax.ShapeDtypeStruct((length, widt...  114 us
    reduce_scatter x1, waiting for transfers between devices, on_device(): lax.psum_scatter(terms.reshape(FC, -1, cols), 'fc', scatter_dimension=0,...  67.2 us
    all_gather x1, waiting for transfers between devices, on_device(): staged = lax.all_gather(staged, 'fz', axis=0, tiled=True)  48.5 us
    ppermute x22, starting transfers between devices, passed_along(): lax.ppermute(value, axis, [(source, source + steps) for source in range(l...  28.4 us
    reduce_scatter x1, waiting for transfers between devices, on_device(): lax.psum_scatter(terms.reshape(FX, -1, cols), 'fx', scatter_dimension=0,...  25.1 us
    all_gather x3, blocking collectives, on_device(): gain_sum = jnp.sum(lax.all_gather(gain_sum, axis, axis=0), axis=0)  24.8 us
    all_gather x1, waiting for transfers between devices, on_device(): staged = lax.all_gather(staged, 'fc', axis=0, tiled=True)  23.4 us
  transfers between devices with their start and end apart: 27, of which 27 were waited for; matrix products, arithmetic and copies ran while one was open for 1% of the time, Pallas kernels for 0%

profile of v14, /device:TPU:1, one launch (start us, length us, event | category | flops | bytes accessed | tf_op | source)
XLA Modules:
  0.0 593.9 jit_solution(8428936893893602738)
XLA Ops:
  13.7 48.5 %all-gather.6.cloned.1.call-done = bf16[2304,512]{1,0:T(8,128)(2,1)} async-done(((bf16[288,512]{1,0:T(8,128)(2,1)}), bf16[2304,512]{1,0:T(8,128)(2,1)}) %all-gather.6.cloned.1.call-update) | async-done | bytes 2359312 | tf_op jit(solution)/shard_map/all_gather | solution.py:237
  66.5 23.4 %all-gather.8.cloned.1.call-done = bf16[4608,512]{1,0:T(8,128)(2,1)} async-done(((bf16[2304,512]{1,0:T(8,128)(2,1)}), bf16[4608,512]{1,0:T(8,128)(2,1)}) %all-gather.8.cloned.1.call-update) | async-done | bytes 4718608 | tf_op jit(solution)/shard_map/all_gather | solution.py:238
  105.3 333.5 %while.21 = (s32[]{:T(128)}, bf16[32,4096]{1,0:T(8,128)(2,1)S(1)}, bf16[10,32,4096]{2,1,0:T(8,128)(2,1)S(1)}, bf16[10,32,384]{2,1,0:T(8,128)(2,1)S(1)}, f32[4096...) while((s32[]{:T(128)}, bf16[32,4096]{1,0:T(8,128)(2,1)S(1)}, ...), condition=%wide.region_4.5_spmd, body=%wide.region_3.4_spmd.sunk | while | flops 268435488 | bytes 6291851 | solution.py:299
  111.6 8.3 %collective-permute-done = bf16[32,4096]{1,0:T(8,128)(2,1)S(1)} collective-permute-done((bf16[32,4096]{1,0:T(8,128)(2,1)S(1)}, bf16[32,4096]{1,0:T(8,128)(2,1)S(1)}, u32[]{:S(2)}, u32[]{:S(2)}) %collective-permute-start) | collective-permute-done | bytes 262176 | tf_op jit(solution)/shard_map/while/body/eval_jaxpr/ppermute | solution.py:16
  126.2 7.4 %collective-permute-done = bf16[32,4096]{1,0:T(8,128)(2,1)S(1)} collective-permute-done((bf16[32,4096]{1,0:T(8,128)(2,1)S(1)}, bf16[32,4096]{1,0:T(8,128)(2,1)S(1)}, u32[]{:S(2)}, u32[]{:S(2)}) %collective-permute-start) | collective-permute-done | bytes 262176 | tf_op jit(solution)/shard_map/while/body/eval_jaxpr/ppermute | solution.py:16
  190.9 7.0 %collective-permute-done = bf16[32,4096]{1,0:T(8,128)(2,1)S(1)} collective-permute-done((bf16[32,4096]{1,0:T(8,128)(2,1)S(1)}, bf16[32,4096]{1,0:T(8,128)(2,1)S(1)}, u32[]{:S(2)}, u32[]{:S(2)}) %collective-permute-start) | collective-permute-done | bytes 262176 | tf_op jit(solution)/shard_map/while/body/eval_jaxpr/ppermute | solution.py:16
  204.3 7.0 %collective-permute-done = bf16[32,4096]{1,0:T(8,128)(2,1)S(1)} collective-permute-done((bf16[32,4096]{1,0:T(8,128)(2,1)S(1)}, bf16[32,4096]{1,0:T(8,128)(2,1)S(1)}, u32[]{:S(2)}, u32[]{:S(2)}) %collective-permute-start) | collective-permute-done | bytes 262176 | tf_op jit(solution)/shard_map/while/body/eval_jaxpr/ppermute | solution.py:16
  217.6 7.0 %collective-permute-done = bf16[32,4096]{1,0:T(8,128)(2,1)S(1)} collective-permute-done((bf16[32,4096]{1,0:T(8,128)(2,1)S(1)}, bf16[32,4096]{1,0:T(8,128)(2,1)S(1)}, u32[]{:S(2)}, u32[]{:S(2)}) %collective-permute-start) | collective-permute-done | bytes 262176 | tf_op jit(solution)/shard_map/while/body/eval_jaxpr/ppermute | solution.py:16
  244.3 9.3 %collective-permute-done = bf16[32,4096]{1,0:T(8,128)(2,1)S(1)} collective-permute-done((bf16[32,4096]{1,0:T(8,128)(2,1)S(1)}, bf16[32,4096]{1,0:T(8,128)(2,1)S(1)}, u32[]{:S(2)}, u32[]{:S(2)}) %collective-permute-start) | collective-permute-done | bytes 262176 | tf_op jit(solution)/shard_map/while/body/eval_jaxpr/ppermute | solution.py:16
  259.9 9.4 %collective-permute-done = bf16[32,4096]{1,0:T(8,128)(2,1)S(1)} collective-permute-done((bf16[32,4096]{1,0:T(8,128)(2,1)S(1)}, bf16[32,4096]{1,0:T(8,128)(2,1)S(1)}, u32[]{:S(2)}, u32[]{:S(2)}) %collective-permute-start) | collective-permute-done | bytes 262176 | tf_op jit(solution)/shard_map/while/body/eval_jaxpr/ppermute | solution.py:16
  275.6 9.4 %collective-permute-done = bf16[32,4096]{1,0:T(8,128)(2,1)S(1)} collective-permute-done((bf16[32,4096]{1,0:T(8,128)(2,1)S(1)}, bf16[32,4096]{1,0:T(8,128)(2,1)S(1)}, u32[]{:S(2)}, u32[]{:S(2)}) %collective-permute-start) | collective-permute-done | bytes 262176 | tf_op jit(solution)/shard_map/while/body/eval_jaxpr/ppermute | solution.py:16
  291.4 9.4 %collective-permute-done = bf16[32,4096]{1,0:T(8,128)(2,1)S(1)} collective-permute-done((bf16[32,4096]{1,0:T(8,128)(2,1)S(1)}, bf16[32,4096]{1,0:T(8,128)(2,1)S(1)}, u32[]{:S(2)}, u32[]{:S(2)}) %collective-permute-start) | collective-permute-done | bytes 262176 | tf_op jit(solution)/shard_map/while/body/eval_jaxpr/ppermute | solution.py:16
  307.1 9.4 %collective-permute-done = bf16[32,4096]{1,0:T(8,128)(2,1)S(1)} collective-permute-done((bf16[32,4096]{1,0:T(8,128)(2,1)S(1)}, bf16[32,4096]{1,0:T(8,128)(2,1)S(1)}, u32[]{:S(2)}, u32[]{:S(2)}) %collective-permute-start) | collective-permute-done | bytes 262176 | tf_op jit(solution)/shard_map/while/body/eval_jaxpr/ppermute | solution.py:16
  322.9 10.6 %collective-permute-done = bf16[32,4096]{1,0:T(8,128)(2,1)S(1)} collective-permute-done((bf16[32,4096]{1,0:T(8,128)(2,1)S(1)}, bf16[32,4096]{1,0:T(8,128)(2,1)S(1)}, u32[]{:S(2)}, u32[]{:S(2)}) %collective-permute-start) | collective-permute-done | bytes 262176 | tf_op jit(solution)/shard_map/while/body/eval_jaxpr/ppermute | solution.py:16
  339.8 12.1 %collective-permute-done = bf16[32,4096]{1,0:T(8,128)(2,1)S(1)} collective-permute-done((bf16[32,4096]{1,0:T(8,128)(2,1)S(1)}, bf16[32,4096]{1,0:T(8,128)(2,1)S(1)}, u32[]{:S(2)}, u32[]{:S(2)}) %collective-permute-start) | collective-permute-done | bytes 262176 | tf_op jit(solution)/shard_map/while/body/eval_jaxpr/ppermute | solution.py:16
  358.2 12.9 %collective-permute-done = bf16[32,4096]{1,0:T(8,128)(2,1)S(1)} collective-permute-done((bf16[32,4096]{1,0:T(8,128)(2,1)S(1)}, bf16[32,4096]{1,0:T(8,128)(2,1)S(1)}, u32[]{:S(2)}, u32[]{:S(2)}) %collective-permute-start) | collective-permute-done | bytes 262176 | tf_op jit(solution)/shard_map/while/body/eval_jaxpr/ppermute | solution.py:16
  377.4 12.3 %collective-permute-done = bf16[32,4096]{1,0:T(8,128)(2,1)S(1)} collective-permute-done((bf16[32,4096]{1,0:T(8,128)(2,1)S(1)}, bf16[32,4096]{1,0:T(8,128)(2,1)S(1)}, u32[]{:S(2)}, u32[]{:S(2)}) %collective-permute-start) | collective-permute-done | bytes 262176 | tf_op jit(solution)/shard_map/while/body/eval_jaxpr/ppermute | solution.py:16
  396.1 11.2 %collective-permute-done = bf16[32,4096]{1,0:T(8,128)(2,1)S(1)} collective-permute-done((bf16[32,4096]{1,0:T(8,128)(2,1)S(1)}, bf16[32,4096]{1,0:T(8,128)(2,1)S(1)}, u32[]{:S(2)}, u32[]{:S(2)}) %collective-permute-start) | collective-permute-done | bytes 262176 | tf_op jit(solution)/shard_map/while/body/eval_jaxpr/ppermute | solution.py:16
  413.6 9.0 %collective-permute-done = bf16[32,4096]{1,0:T(8,128)(2,1)S(1)} collective-permute-done((bf16[32,4096]{1,0:T(8,128)(2,1)S(1)}, bf16[32,4096]{1,0:T(8,128)(2,1)S(1)}, u32[]{:S(2)}, u32[]{:S(2)}) %collective-permute-start) | collective-permute-done | bytes 262176 | tf_op jit(solution)/shard_map/while/body/eval_jaxpr/ppermute | solution.py:16
  428.9 9.9 %collective-permute-done = bf16[32,4096]{1,0:T(8,128)(2,1)S(1)} collective-permute-done((bf16[32,4096]{1,0:T(8,128)(2,1)S(1)}, bf16[32,4096]{1,0:T(8,128)(2,1)S(1)}, u32[]{:S(2)}, u32[]{:S(2)}) %collective-permute-start) | collective-permute-done | bytes 262176 | tf_op jit(solution)/shard_map/while/body/eval_jaxpr/ppermute | solution.py:16
  449.2 67.2 %reduce-scatter.4.cloned.1.call-done = bf16[1,2048,512]{2,1,0:T(8,128)(2,1)} async-done(((bf16[2,2048,512]{2,1,0:T(8,128)(2,1)}), bf16[1,2048,512]{2,1,0:T(8,128)(2,1)}) %reduce-scatter.4.cloned.1.call-update) | async-done | bytes 2097168 | tf_op jit(solution)/shard_map/reduce_scatter | solution.py:310
  518.3 19.3 %all-gather = f32[32768]{0:T(1024)S(1)} all-gather(f32[4096]{0:T(1024)S(1)} %reduce_sum.47), channel_id=2, replica_groups=mesh['sh'=2,'sy'=8,'fx'=2,'fz'=8,'fc'=2] {'fz'}, dimensions={0}, use_global_device_ids=true | all-gather | bytes 147456 | tf_op jit(solution)/shard_map/all_gather | solution.py:314
  542.1 18.6 %reduce-scatter.6.cloned.1.call-done = bf16[1,256,512]{2,1,0:T(8,128)(2,1)} async-done(((bf16[8,256,512]{2,1,0:T(8,128)(2,1)}), bf16[1,256,512]{2,1,0:T(8,128)(2,1)}) %reduce-scatter.6.cloned.1.call-update) | async-done | bytes 262160 | tf_op jit(solution)/shard_map/reduce_scatter | solution.py:311
  560.7 25.1 %reduce-scatter.8.cloned.1.call-done = bf16[1,128,512]{2,1,0:T(8,128)(2,1)} async-done(((bf16[2,128,512]{2,1,0:T(8,128)(2,1)}), bf16[1,128,512]{2,1,0:T(8,128)(2,1)}) %reduce-scatter.8.cloned.1.call-update) | async-done | bytes 131088 | tf_op jit(solution)/shard_map/reduce_scatter | solution.py:316
  (130 shorter events, 215.6 us)
Async XLA Ops:
  7.2 55.1 %all-gather.6.cloned.1.call-start = ((), (), s32[]{:S(2)}) async-start(), calls=%async_computation.3 | async-start | bytes 2654208 | tf_op jit(solution)/shard_map/all_gather | solution.py:237
  13.7 76.2 %all-gather.8.cloned.1.call-start = ((), (), s32[]{:S(2)}) async-start(), calls=%async_computation.4 | async-start | bytes 7077888 | tf_op jit(solution)/shard_map/all_gather | solution.py:238
  62.3 454.1 %reduce-scatter.4.cloned.1.call-start = ((), (), s32[]{:S(2)}) async-start(), calls=%async_computation.5 | async-start | bytes 6291456 | tf_op jit(solution)/shard_map/reduce_scatter | solution.py:310
  110.3 9.6 %collective-permute-start = (bf16[32,4096]{1,0:T(8,128)(2,1)S(1)}, bf16[32,4096]{1,0:T(8,128)(2,1)S(1)}, u32[]{:S(2)}, u32[]{:S(2)}) collective-permute-start(bf16[32,4096]{1,0:T(8,128)(2,1)S(1)} %get-tuple-element.671), channel_id=1, source_target_pairs={{32,0},{64,32},{96,64},{128,96},{160,128},{192,160},{224,192},{256... | collective-permute-start | bytes 786440 | tf_op jit(solution)/shard_map/while/body/eval_jaxpr/ppermute | solution.py:16
  124.9 8.7 %collective-permute-start = (bf16[32,4096]{1,0:T(8,128)(2,1)S(1)}, bf16[32,4096]{1,0:T(8,128)(2,1)S(1)}, u32[]{:S(2)}, u32[]{:S(2)}) collective-permute-start(bf16[32,4096]{1,0:T(8,128)(2,1)S(1)} %get-tuple-element.671), channel_id=1, source_target_pairs={{32,0},{64,32},{96,64},{128,96},{160,128},{192,160},{224,192},{256... | collective-permute-start | bytes 786440 | tf_op jit(solution)/shard_map/while/body/eval_jaxpr/ppermute | solution.py:16
  176.6 8.0 %collective-permute-start = (bf16[32,4096]{1,0:T(8,128)(2,1)S(1)}, bf16[32,4096]{1,0:T(8,128)(2,1)S(1)}, u32[]{:S(2)}, u32[]{:S(2)}) collective-permute-start(bf16[32,4096]{1,0:T(8,128)(2,1)S(1)} %get-tuple-element.671), channel_id=1, source_target_pairs={{32,0},{64,32},{96,64},{128,96},{160,128},{192,160},{224,192},{256... | collective-permute-start | bytes 786440 | tf_op jit(solution)/shard_map/while/body/eval_jaxpr/ppermute | solution.py:16
  189.6 8.3 %collective-permute-start = (bf16[32,4096]{1,0:T(8,128)(2,1)S(1)}, bf16[32,4096]{1,0:T(8,128)(2,1)S(1)}, u32[]{:S(2)}, u32[]{:S(2)}) collective-permute-start(bf16[32,4096]{1,0:T(8,128)(2,1)S(1)} %get-tuple-element.671), channel_id=1, source_target_pairs={{32,0},{64,32},{96,64},{128,96},{160,128},{192,160},{224,192},{256... | collective-permute-start | bytes 786440 | tf_op jit(solution)/shard_map/while/body/eval_jaxpr/ppermute | solution.py:16
  203.0 8.3 %collective-permute-start = (bf16[32,4096]{1,0:T(8,128)(2,1)S(1)}, bf16[32,4096]{1,0:T(8,128)(2,1)S(1)}, u32[]{:S(2)}, u32[]{:S(2)}) collective-permute-start(bf16[32,4096]{1,0:T(8,128)(2,1)S(1)} %get-tuple-element.671), channel_id=1, source_target_pairs={{32,0},{64,32},{96,64},{128,96},{160,128},{192,160},{224,192},{256... | collective-permute-start | bytes 786440 | tf_op jit(solution)/shard_map/while/body/eval_jaxpr/ppermute | solution.py:16
  216.3 8.3 %collective-permute-start = (bf16[32,4096]{1,0:T(8,128)(2,1)S(1)}, bf16[32,4096]{1,0:T(8,128)(2,1)S(1)}, u32[]{:S(2)}, u32[]{:S(2)}) collective-permute-start(bf16[32,4096]{1,0:T(8,128)(2,1)S(1)} %get-tuple-element.671), channel_id=1, source_target_pairs={{32,0},{64,32},{96,64},{128,96},{160,128},{192,160},{224,192},{256... | collective-permute-start | bytes 786440 | tf_op jit(solution)/shard_map/while/body/eval_jaxpr/ppermute | solution.py:16
  229.6 8.3 %collective-permute-start = (bf16[32,4096]{1,0:T(8,128)(2,1)S(1)}, bf16[32,4096]{1,0:T(8,128)(2,1)S(1)}, u32[]{:S(2)}, u32[]{:S(2)}) collective-permute-start(bf16[32,4096]{1,0:T(8,128)(2,1)S(1)} %get-tuple-element.671), channel_id=1, source_target_pairs={{32,0},{64,32},{96,64},{128,96},{160,128},{192,160},{224,192},{256... | collective-permute-start | bytes 786440 | tf_op jit(solution)/shard_map/while/body/eval_jaxpr/ppermute | solution.py:16
  243.0 10.6 %collective-permute-start = (bf16[32,4096]{1,0:T(8,128)(2,1)S(1)}, bf16[32,4096]{1,0:T(8,128)(2,1)S(1)}, u32[]{:S(2)}, u32[]{:S(2)}) collective-permute-start(bf16[32,4096]{1,0:T(8,128)(2,1)S(1)} %get-tuple-element.671), channel_id=1, source_target_pairs={{32,0},{64,32},{96,64},{128,96},{160,128},{192,160},{224,192},{256... | collective-permute-start | bytes 786440 | tf_op jit(solution)/shard_map/while/body/eval_jaxpr/ppermute | solution.py:16
  258.6 10.7 %collective-permute-start = (bf16[32,4096]{1,0:T(8,128)(2,1)S(1)}, bf16[32,4096]{1,0:T(8,128)(2,1)S(1)}, u32[]{:S(2)}, u32[]{:S(2)}) collective-permute-start(bf16[32,4096]{1,0:T(8,128)(2,1)S(1)} %get-tuple-element.671), channel_id=1, source_target_pairs={{32,0},{64,32},{96,64},{128,96},{160,128},{192,160},{224,192},{256... | collective-permute-start | bytes 786440 | tf_op jit(solution)/shard_map/while/body/eval_jaxpr/ppermute | solution.py:16
  274.3 10.7 %collective-permute-start = (bf16[32,4096]{1,0:T(8,128)(2,1)S(1)}, bf16[32,4096]{1,0:T(8,128)(2,1)S(1)}, u32[]{:S(2)}, u32[]{:S(2)}) collective-permute-start(bf16[32,4096]{1,0:T(8,128)(2,1)S(1)} %get-tuple-element.671), channel_id=1, source_target_pairs={{32,0},{64,32},{96,64},{128,96},{160,128},{192,160},{224,192},{256... | collective-permute-start | bytes 786440 | tf_op jit(solution)/shard_map/while/body/eval_jaxpr/ppermute | solution.py:16
  290.1 10.7 %collective-permute-start = (bf16[32,4096]{1,0:T(8,128)(2,1)S(1)}, bf16[32,4096]{1,0:T(8,128)(2,1)S(1)}, u32[]{:S(2)}, u32[]{:S(2)}) collective-permute-start(bf16[32,4096]{1,0:T(8,128)(2,1)S(1)} %get-tuple-element.671), channel_id=1, source_target_pairs={{32,0},{64,32},{96,64},{128,96},{160,128},{192,160},{224,192},{256... | collective-permute-start | bytes 786440 | tf_op jit(solution)/shard_map/while/body/eval_jaxpr/ppermute | solution.py:16
  305.8 10.7 %collective-permute-start = (bf16[32,4096]{1,0:T(8,128)(2,1)S(1)}, bf16[32,4096]{1,0:T(8,128)(2,1)S(1)}, u32[]{:S(2)}, u32[]{:S(2)}) collective-permute-start(bf16[32,4096]{1,0:T(8,128)(2,1)S(1)} %get-tuple-element.671), channel_id=1, source_target_pairs={{32,0},{64,32},{96,64},{128,96},{160,128},{192,160},{224,192},{256... | collective-permute-start | bytes 786440 | tf_op jit(solution)/shard_map/while/body/eval_jaxpr/ppermute | solution.py:16
  321.6 11.9 %collective-permute-start = (bf16[32,4096]{1,0:T(8,128)(2,1)S(1)}, bf16[32,4096]{1,0:T(8,128)(2,1)S(1)}, u32[]{:S(2)}, u32[]{:S(2)}) collective-permute-start(bf16[32,4096]{1,0:T(8,128)(2,1)S(1)} %get-tuple-element.671), channel_id=1, source_target_pairs={{32,0},{64,32},{96,64},{128,96},{160,128},{192,160},{224,192},{256... | collective-permute-start | bytes 786440 | tf_op jit(solution)/shard_map/while/body/eval_jaxpr/ppermute | solution.py:16
  338.5 13.4 %collective-permute-start = (bf16[32,4096]{1,0:T(8,128)(2,1)S(1)}, bf16[32,4096]{1,0:T(8,128)(2,1)S(1)}, u32[]{:S(2)}, u32[]{:S(2)}) collective-permute-start(bf16[32,4096]{1,0:T(8,128)(2,1)S(1)} %get-tuple-element.671), channel_id=1, source_target_pairs={{32,0},{64,32},{96,64},{128,96},{160,128},{192,160},{224,192},{256... | collective-permute-start | bytes 786440 | tf_op jit(solution)/shard_map/while/body/eval_jaxpr/ppermute | solution.py:16
  356.9 14.2 %collective-permute-start = (bf16[32,4096]{1,0:T(8,128)(2,1)S(1)}, bf16[32,4096]{1,0:T(8,128)(2,1)S(1)}, u32[]{:S(2)}, u32[]{:S(2)}) collective-permute-start(bf16[32,4096]{1,0:T(8,128)(2,1)S(1)} %get-tuple-element.671), channel_id=1, source_target_pairs={{32,0},{64,32},{96,64},{128,96},{160,128},{192,160},{224,192},{256... | collective-permute-start | bytes 786440 | tf_op jit(solution)/shard_map/while/body/eval_jaxpr/ppermute | solution.py:16
  376.1 13.7 %collective-permute-start = (bf16[32,4096]{1,0:T(8,128)(2,1)S(1)}, bf16[32,4096]{1,0:T(8,128)(2,1)S(1)}, u32[]{:S(2)}, u32[]{:S(2)}) collective-permute-start(bf16[32,4096]{1,0:T(8,128)(2,1)S(1)} %get-tuple-element.671), channel_id=1, source_target_pairs={{32,0},{64,32},{96,64},{128,96},{160,128},{192,160},{224,192},{256... | collective-permute-start | bytes 786440 | tf_op jit(solution)/shard_map/while/body/eval_jaxpr/ppermute | solution.py:16
  394.8 12.5 %collective-permute-start = (bf16[32,4096]{1,0:T(8,128)(2,1)S(1)}, bf16[32,4096]{1,0:T(8,128)(2,1)S(1)}, u32[]{:S(2)}, u32[]{:S(2)}) collective-permute-start(bf16[32,4096]{1,0:T(8,128)(2,1)S(1)} %get-tuple-element.671), channel_id=1, source_target_pairs={{32,0},{64,32},{96,64},{128,96},{160,128},{192,160},{224,192},{256... | collective-permute-start | bytes 786440 | tf_op jit(solution)/shard_map/while/body/eval_jaxpr/ppermute | solution.py:16
  412.3 10.3 %collective-permute-start = (bf16[32,4096]{1,0:T(8,128)(2,1)S(1)}, bf16[32,4096]{1,0:T(8,128)(2,1)S(1)}, u32[]{:S(2)}, u32[]{:S(2)}) collective-permute-start(bf16[32,4096]{1,0:T(8,128)(2,1)S(1)} %get-tuple-element.671), channel_id=1, source_target_pairs={{32,0},{64,32},{96,64},{128,96},{160,128},{192,160},{224,192},{256... | collective-permute-start | bytes 786440 | tf_op jit(solution)/shard_map/while/body/eval_jaxpr/ppermute | solution.py:16
  427.6 11.2 %collective-permute-start = (bf16[32,4096]{1,0:T(8,128)(2,1)S(1)}, bf16[32,4096]{1,0:T(8,128)(2,1)S(1)}, u32[]{:S(2)}, u32[]{:S(2)}) collective-permute-start(bf16[32,4096]{1,0:T(8,128)(2,1)S(1)} %get-tuple-element.671), channel_id=1, source_target_pairs={{32,0},{64,32},{96,64},{128,96},{160,128},{192,160},{224,192},{256... | collective-permute-start | bytes 786440 | tf_op jit(solution)/shard_map/while/body/eval_jaxpr/ppermute | solution.py:16
  449.2 111.5 %reduce-scatter.6.cloned.1.call-start = ((), (), s32[]{:S(2)}) async-start(), calls=%async_computation.6 | async-start | bytes 2359296 | tf_op jit(solution)/shard_map/reduce_scatter | solution.py:311
  516.4 69.4 %reduce-scatter.8.cloned.1.call-start = ((), (), s32[]{:S(2)}) async-start(), calls=%async_computation.7 | async-start | bytes 393216 | tf_op jit(solution)/shard_map/reduce_scatter | solution.py:316
  (10 other events, 103.6 us)
Sparse Core Ops, SparseCore 0:
  13.8 48.4 all-gather.5
  64.3 25.5 all-gather.7
  449.3 67.0 reduce-scatter.3
  519.3 41.2 reduce-scatter.5
  563.5 22.2 reduce-scatter.7

commit v15 on v13

--- a/solution.py
+++ b/solution.py
@@ -57,8 +57,10 @@
 def tick_kernel(
     scal, recv_ref, up_ref, wb_ref, wp_ref, gain_ref, normed_ref, inv_ref, probs_ref, probs_b_ref,
     q_ref, k_ref, v_ref, cos_ref, sin_ref, gstore_in, pstore_in, gacc_ref,
-    out_ref, gstore_ref, pstore_ref, gacc_out,
+    out_ref, gstore_ref, pstore_ref, gacc_out, wp_vmem, wp_sem,
 ):
+    wp_copy = pltpu.make_async_copy(wp_ref, wp_vmem, wp_sem)
+    wp_copy.start()
     head = q_ref.shape[-1]
     score_scale = head ** (-0.5)
     grad_in = jnp.where(scal[3] == 1, up_ref[...], recv_ref[...])
@@ -80,7 +82,8 @@
     gq = gq * cosine + pltpu.roll(gq, head // 2, 1) * sine
     gk = gk * cosine + pltpu.roll(gk, head // 2, 1) * sine
     gp = jnp.concatenate([gq, gk, gv], axis=-1).astype(jnp.bfloat16)
-    gh = lax.dot_general(gp, wp_ref[...], (((1,), (1,)), ((), ())), preferred_element_type=jnp.float32)
+    wp_copy.wait()
+    gh = lax.dot_general(gp, wp_vmem[...], (((1,), (1,)), ((), ())), preferred_element_type=jnp.float32)
     normed = normed_ref[...]
     gain_term = jnp.sum(gh * normed, axis=0, keepdims=True)
     gn = gh * gain_ref[...]
@@ -115,7 +118,7 @@
                 full((length, width)),
                 per_micro((length, width)),
                 full((width, head)),
-                full((width, 3 * head)),
+                pl.BlockSpec(memory_space=pl.ANY),
                 full((1, width)),
                 per_micro((length, width)),
                 per_micro((length, 1)),
@@ -136,6 +139,10 @@
                 per_slot((length, 3 * head)),
                 full((1, width)),
             ],
+            scratch_shapes=[
+                pltpu.VMEM((width, 3 * head), w_proj.dtype),
+                pltpu.SemaphoreType.DMA(()),
+            ],
         ),
         input_output_aliases={15: 1, 16: 2, 17: 3},
         cost_estimate=pl.CostEstimate(

time: 595 us -> 618 us (1.039)
  Pallas kernels: 122 us -> 143 us
    pallas_call x23, Pallas kernels: 114 us -> 135 us  [tick_call(): pl.pallas_call(tick_kernel, out_shape=(jax.ShapeDtypeStruct((length, widt...]
where the time goes in v15:
time: 618 us; the launch traced here: 615 us
  waiting for transfers between devices  366 us (59%)
  Pallas kernels  143 us (23%)
  blocking collectives  41.8 us (7%)
  starting transfers between devices  28.6 us (5%)
  other arithmetic  13.9 us (2%)
  between operations  13.9 us (2%)
    ppermute x22, waiting for transfers between devices, passed_along(): lax.ppermute(value, axis, [(source, source + steps) for source in range(l...  195 us
    pallas_call x23, Pallas kernels, tick_call(): pl.pallas_call(tick_kernel, out_shape=(jax.ShapeDtypeStruct((length, widt...  135 us
    reduce_scatter x1, waiting for transfers between devices, on_device(): lax.psum_scatter(terms.reshape(FC, -1, cols), 'fc', scatter_dimension=0,...  67 us
    all_gather x1, waiting for transfers between devices, on_device(): staged = lax.all_gather(staged, 'fz', axis=0, tiled=True)  48.5 us
    all_gather x1, blocking collectives, on_device(): gain_sum = jnp.sum(lax.all_gather(gain_acc, FSDP, axis=0), axis=0)  36.5 us
    ppermute x22, starting transfers between devices, passed_along(): lax.ppermute(value, axis, [(source, source + steps) for source in range(l...  28.4 us
    reduce_scatter x1, waiting for transfers between devices, on_device(): lax.psum_scatter(terms.reshape(FX, -1, cols), 'fx', scatter_dimension=0,...  24.4 us
    all_gather x1, waiting for transfers between devices, on_device(): staged = lax.all_gather(staged, 'fc', axis=0, tiled=True)  23.4 us
  transfers between devices with their start and end apart: 27, of which 27 were waited for; matrix products, arithmetic and copies ran while one was open for 1% of the time, Pallas kernels for 0%

profile of v15, /device:TPU:1, one launch (start us, length us, event | category | flops | bytes accessed | tf_op | source)
XLA Modules:
  0.0 615.4 jit_solution(16896019951183943595)
XLA Ops:
  13.7 48.5 %all-gather.4.cloned.1.call-done = bf16[2304,512]{1,0:T(8,128)(2,1)} async-done(((bf16[288,512]{1,0:T(8,128)(2,1)}), bf16[2304,512]{1,0:T(8,128)(2,1)}) %all-gather.4.cloned.1.call-update) | async-done | bytes 2359312 | tf_op jit(solution)/shard_map/all_gather | solution.py:244
  66.5 23.4 %all-gather.6.cloned.1.call-done = bf16[4608,512]{1,0:T(8,128)(2,1)} async-done(((bf16[2304,512]{1,0:T(8,128)(2,1)}), bf16[4608,512]{1,0:T(8,128)(2,1)}) %all-gather.6.cloned.1.call-update) | async-done | bytes 4718608 | tf_op jit(solution)/shard_map/all_gather | solution.py:245
  105.3 354.0 %while.21 = (s32[]{:T(128)}, bf16[32,4096]{1,0:T(8,128)(2,1)S(1)}, bf16[10,32,4096]{2,1,0:T(8,128)(2,1)S(1)}, bf16[10,32,384]{2,1,0:T(8,128)(2,1)S(1)}, f32[4096...) while((s32[]{:T(128)}, bf16[32,4096]{1,0:T(8,128)(2,1)S(1)}, ...), condition=%wide.region_4.5_spmd, body=%wide.region_3.4_spmd.sunk | while | flops 268435488 | bytes 6291851 | solution.py:306
  112.5 8.3 %collective-permute-done = bf16[32,4096]{1,0:T(8,128)(2,1)S(1)} collective-permute-done((bf16[32,4096]{1,0:T(8,128)(2,1)S(1)}, bf16[32,4096]{1,0:T(8,128)(2,1)S(1)}, u32[]{:S(2)}, u32[]{:S(2)}) %collective-permute-start) | collective-permute-done | bytes 262176 | tf_op jit(solution)/shard_map/while/body/eval_jaxpr/ppermute | solution.py:16
  128.1 7.4 %collective-permute-done = bf16[32,4096]{1,0:T(8,128)(2,1)S(1)} collective-permute-done((bf16[32,4096]{1,0:T(8,128)(2,1)S(1)}, bf16[32,4096]{1,0:T(8,128)(2,1)S(1)}, u32[]{:S(2)}, u32[]{:S(2)}) %collective-permute-start) | collective-permute-done | bytes 262176 | tf_op jit(solution)/shard_map/while/body/eval_jaxpr/ppermute | solution.py:16
  197.4 7.0 %collective-permute-done = bf16[32,4096]{1,0:T(8,128)(2,1)S(1)} collective-permute-done((bf16[32,4096]{1,0:T(8,128)(2,1)S(1)}, bf16[32,4096]{1,0:T(8,128)(2,1)S(1)}, u32[]{:S(2)}, u32[]{:S(2)}) %collective-permute-start) | collective-permute-done | bytes 262176 | tf_op jit(solution)/shard_map/while/body/eval_jaxpr/ppermute | solution.py:16
  211.7 7.0 %collective-permute-done = bf16[32,4096]{1,0:T(8,128)(2,1)S(1)} collective-permute-done((bf16[32,4096]{1,0:T(8,128)(2,1)S(1)}, bf16[32,4096]{1,0:T(8,128)(2,1)S(1)}, u32[]{:S(2)}, u32[]{:S(2)}) %collective-permute-start) | collective-permute-done | bytes 262176 | tf_op jit(solution)/shard_map/while/body/eval_jaxpr/ppermute | solution.py:16
  226.0 7.0 %collective-permute-done = bf16[32,4096]{1,0:T(8,128)(2,1)S(1)} collective-permute-done((bf16[32,4096]{1,0:T(8,128)(2,1)S(1)}, bf16[32,4096]{1,0:T(8,128)(2,1)S(1)}, u32[]{:S(2)}, u32[]{:S(2)}) %collective-permute-start) | collective-permute-done | bytes 262176 | tf_op jit(solution)/shard_map/while/body/eval_jaxpr/ppermute | solution.py:16
  254.5 9.3 %collective-permute-done = bf16[32,4096]{1,0:T(8,128)(2,1)S(1)} collective-permute-done((bf16[32,4096]{1,0:T(8,128)(2,1)S(1)}, bf16[32,4096]{1,0:T(8,128)(2,1)S(1)}, u32[]{:S(2)}, u32[]{:S(2)}) %collective-permute-start) | collective-permute-done | bytes 262176 | tf_op jit(solution)/shard_map/while/body/eval_jaxpr/ppermute | solution.py:16
  271.0 9.4 %collective-permute-done = bf16[32,4096]{1,0:T(8,128)(2,1)S(1)} collective-permute-done((bf16[32,4096]{1,0:T(8,128)(2,1)S(1)}, bf16[32,4096]{1,0:T(8,128)(2,1)S(1)}, u32[]{:S(2)}, u32[]{:S(2)}) %collective-permute-start) | collective-permute-done | bytes 262176 | tf_op jit(solution)/shard_map/while/body/eval_jaxpr/ppermute | solution.py:16
  287.7 9.4 %collective-permute-done = bf16[32,4096]{1,0:T(8,128)(2,1)S(1)} collective-permute-done((bf16[32,4096]{1,0:T(8,128)(2,1)S(1)}, bf16[32,4096]{1,0:T(8,128)(2,1)S(1)}, u32[]{:S(2)}, u32[]{:S(2)}) %collective-permute-start) | collective-permute-done | bytes 262176 | tf_op jit(solution)/shard_map/while/body/eval_jaxpr/ppermute | solution.py:16
  304.4 9.4 %collective-permute-done = bf16[32,4096]{1,0:T(8,128)(2,1)S(1)} collective-permute-done((bf16[32,4096]{1,0:T(8,128)(2,1)S(1)}, bf16[32,4096]{1,0:T(8,128)(2,1)S(1)}, u32[]{:S(2)}, u32[]{:S(2)}) %collective-permute-start) | collective-permute-done | bytes 262176 | tf_op jit(solution)/shard_map/while/body/eval_jaxpr/ppermute | solution.py:16
  321.0 9.4 %collective-permute-done = bf16[32,4096]{1,0:T(8,128)(2,1)S(1)} collective-permute-done((bf16[32,4096]{1,0:T(8,128)(2,1)S(1)}, bf16[32,4096]{1,0:T(8,128)(2,1)S(1)}, u32[]{:S(2)}, u32[]{:S(2)}) %collective-permute-start) | collective-permute-done | bytes 262176 | tf_op jit(solution)/shard_map/while/body/eval_jaxpr/ppermute | solution.py:16
  337.7 9.6 %collective-permute-done = bf16[32,4096]{1,0:T(8,128)(2,1)S(1)} collective-permute-done((bf16[32,4096]{1,0:T(8,128)(2,1)S(1)}, bf16[32,4096]{1,0:T(8,128)(2,1)S(1)}, u32[]{:S(2)}, u32[]{:S(2)}) %collective-permute-start) | collective-permute-done | bytes 262176 | tf_op jit(solution)/shard_map/while/body/eval_jaxpr/ppermute | solution.py:16
  354.5 10.9 %collective-permute-done = bf16[32,4096]{1,0:T(8,128)(2,1)S(1)} collective-permute-done((bf16[32,4096]{1,0:T(8,128)(2,1)S(1)}, bf16[32,4096]{1,0:T(8,128)(2,1)S(1)}, u32[]{:S(2)}, u32[]{:S(2)}) %collective-permute-start) | collective-permute-done | bytes 262176 | tf_op jit(solution)/shard_map/while/body/eval_jaxpr/ppermute | solution.py:16
  372.7 12.3 %collective-permute-done = bf16[32,4096]{1,0:T(8,128)(2,1)S(1)} collective-permute-done((bf16[32,4096]{1,0:T(8,128)(2,1)S(1)}, bf16[32,4096]{1,0:T(8,128)(2,1)S(1)}, u32[]{:S(2)}, u32[]{:S(2)}) %collective-permute-start) | collective-permute-done | bytes 262176 | tf_op jit(solution)/shard_map/while/body/eval_jaxpr/ppermute | solution.py:16
  392.3 12.9 %collective-permute-done = bf16[32,4096]{1,0:T(8,128)(2,1)S(1)} collective-permute-done((bf16[32,4096]{1,0:T(8,128)(2,1)S(1)}, bf16[32,4096]{1,0:T(8,128)(2,1)S(1)}, u32[]{:S(2)}, u32[]{:S(2)}) %collective-permute-start) | collective-permute-done | bytes 262176 | tf_op jit(solution)/shard_map/while/body/eval_jaxpr/ppermute | solution.py:16
  412.4 12.4 %collective-permute-done = bf16[32,4096]{1,0:T(8,128)(2,1)S(1)} collective-permute-done((bf16[32,4096]{1,0:T(8,128)(2,1)S(1)}, bf16[32,4096]{1,0:T(8,128)(2,1)S(1)}, u32[]{:S(2)}, u32[]{:S(2)}) %collective-permute-start) | collective-permute-done | bytes 262176 | tf_op jit(solution)/shard_map/while/body/eval_jaxpr/ppermute | solution.py:16
  432.0 10.3 %collective-permute-done = bf16[32,4096]{1,0:T(8,128)(2,1)S(1)} collective-permute-done((bf16[32,4096]{1,0:T(8,128)(2,1)S(1)}, bf16[32,4096]{1,0:T(8,128)(2,1)S(1)}, u32[]{:S(2)}, u32[]{:S(2)}) %collective-permute-start) | collective-permute-done | bytes 262176 | tf_op jit(solution)/shard_map/while/body/eval_jaxpr/ppermute | solution.py:16
  449.6 9.7 %collective-permute-done = bf16[32,4096]{1,0:T(8,128)(2,1)S(1)} collective-permute-done((bf16[32,4096]{1,0:T(8,128)(2,1)S(1)}, bf16[32,4096]{1,0:T(8,128)(2,1)S(1)}, u32[]{:S(2)}, u32[]{:S(2)}) %collective-permute-start) | collective-permute-done | bytes 262176 | tf_op jit(solution)/shard_map/while/body/eval_jaxpr/ppermute | solution.py:16
  470.7 67.0 %reduce-scatter.4.cloned.1.call-done = bf16[1,2048,512]{2,1,0:T(8,128)(2,1)} async-done(((bf16[2,2048,512]{2,1,0:T(8,128)(2,1)}), bf16[1,2048,512]{2,1,0:T(8,128)(2,1)}) %reduce-scatter.4.cloned.1.call-update) | async-done | bytes 2097168 | tf_op jit(solution)/shard_map/reduce_scatter | solution.py:317
  537.7 36.5 %all-gather = f32[32,1,4096]{2,1,0:T(1,128)S(1)} all-gather(f32[1,1,4096]{2,1,0:T(1,128)S(1)} %bitcast.62), channel_id=1, replica_groups=mesh['sh'=2,'sy'=8,'fx'=2,'fz'=8,'fc'=2] {'fx','fz','fc'}, dimensions={0}, use_global_device_ids=true | all-gather | bytes 540672 | tf_op jit(solution)/shard_map/all_gather | solution.py:319
  575.2 7.6 %reduce-scatter.6.cloned.1.call-done = bf16[1,256,512]{2,1,0:T(8,128)(2,1)} async-done(((bf16[8,256,512]{2,1,0:T(8,128)(2,1)}), bf16[1,256,512]{2,1,0:T(8,128)(2,1)}) %reduce-scatter.6.cloned.1.call-update) | async-done | bytes 262160 | tf_op jit(solution)/shard_map/reduce_scatter | solution.py:318
  582.8 24.4 %reduce-scatter.8.cloned.1.call-done = bf16[1,128,512]{2,1,0:T(8,128)(2,1)} async-done(((bf16[2,128,512]{2,1,0:T(8,128)(2,1)}), bf16[1,128,512]{2,1,0:T(8,128)(2,1)}) %reduce-scatter.8.cloned.1.call-update) | async-done | bytes 131088 | tf_op jit(solution)/shard_map/reduce_scatter | solution.py:321
  (124 shorter events, 231.7 us)
Async XLA Ops:
  7.2 55.1 %all-gather.4.cloned.1.call-start = ((), (), s32[]{:S(2)}) async-start(), calls=%async_computation.3 | async-start | bytes 2654208 | tf_op jit(solution)/shard_map/all_gather | solution.py:244
  13.7 76.2 %all-gather.6.cloned.1.call-start = ((), (), s32[]{:S(2)}) async-start(), calls=%async_computation.4 | async-start | bytes 7077888 | tf_op jit(solution)/shard_map/all_gather | solution.py:245
  62.3 475.4 %reduce-scatter.4.cloned.1.call-start = ((), (), s32[]{:S(2)}) async-start(), calls=%async_computation.5 | async-start | bytes 6291456 | tf_op jit(solution)/shard_map/reduce_scatter | solution.py:317
  111.2 9.6 %collective-permute-start = (bf16[32,4096]{1,0:T(8,128)(2,1)S(1)}, bf16[32,4096]{1,0:T(8,128)(2,1)S(1)}, u32[]{:S(2)}, u32[]{:S(2)}) collective-permute-start(bf16[32,4096]{1,0:T(8,128)(2,1)S(1)} %get-tuple-element.651), channel_id=1, source_target_pairs={{32,0},{64,32},{96,64},{128,96},{160,128},{192,160},{224,192},{256... | collective-permute-start | bytes 786440 | tf_op jit(solution)/shard_map/while/body/eval_jaxpr/ppermute | solution.py:16
  126.8 8.7 %collective-permute-start = (bf16[32,4096]{1,0:T(8,128)(2,1)S(1)}, bf16[32,4096]{1,0:T(8,128)(2,1)S(1)}, u32[]{:S(2)}, u32[]{:S(2)}) collective-permute-start(bf16[32,4096]{1,0:T(8,128)(2,1)S(1)} %get-tuple-element.651), channel_id=1, source_target_pairs={{32,0},{64,32},{96,64},{128,96},{160,128},{192,160},{224,192},{256... | collective-permute-start | bytes 786440 | tf_op jit(solution)/shard_map/while/body/eval_jaxpr/ppermute | solution.py:16
  182.1 8.0 %collective-permute-start = (bf16[32,4096]{1,0:T(8,128)(2,1)S(1)}, bf16[32,4096]{1,0:T(8,128)(2,1)S(1)}, u32[]{:S(2)}, u32[]{:S(2)}) collective-permute-start(bf16[32,4096]{1,0:T(8,128)(2,1)S(1)} %get-tuple-element.651), channel_id=1, source_target_pairs={{32,0},{64,32},{96,64},{128,96},{160,128},{192,160},{224,192},{256... | collective-permute-start | bytes 786440 | tf_op jit(solution)/shard_map/while/body/eval_jaxpr/ppermute | solution.py:16
  196.1 8.3 %collective-permute-start = (bf16[32,4096]{1,0:T(8,128)(2,1)S(1)}, bf16[32,4096]{1,0:T(8,128)(2,1)S(1)}, u32[]{:S(2)}, u32[]{:S(2)}) collective-permute-start(bf16[32,4096]{1,0:T(8,128)(2,1)S(1)} %get-tuple-element.651), channel_id=1, source_target_pairs={{32,0},{64,32},{96,64},{128,96},{160,128},{192,160},{224,192},{256... | collective-permute-start | bytes 786440 | tf_op jit(solution)/shard_map/while/body/eval_jaxpr/ppermute | solution.py:16
  210.4 8.3 %collective-permute-start = (bf16[32,4096]{1,0:T(8,128)(2,1)S(1)}, bf16[32,4096]{1,0:T(8,128)(2,1)S(1)}, u32[]{:S(2)}, u32[]{:S(2)}) collective-permute-start(bf16[32,4096]{1,0:T(8,128)(2,1)S(1)} %get-tuple-element.651), channel_id=1, source_target_pairs={{32,0},{64,32},{96,64},{128,96},{160,128},{192,160},{224,192},{256... | collective-permute-start | bytes 786440 | tf_op jit(solution)/shard_map/while/body/eval_jaxpr/ppermute | solution.py:16
  224.7 8.3 %collective-permute-start = (bf16[32,4096]{1,0:T(8,128)(2,1)S(1)}, bf16[32,4096]{1,0:T(8,128)(2,1)S(1)}, u32[]{:S(2)}, u32[]{:S(2)}) collective-permute-start(bf16[32,4096]{1,0:T(8,128)(2,1)S(1)} %get-tuple-element.651), channel_id=1, source_target_pairs={{32,0},{64,32},{96,64},{128,96},{160,128},{192,160},{224,192},{256... | collective-permute-start | bytes 786440 | tf_op jit(solution)/shard_map/while/body/eval_jaxpr/ppermute | solution.py:16
  238.9 8.3 %collective-permute-start = (bf16[32,4096]{1,0:T(8,128)(2,1)S(1)}, bf16[32,4096]{1,0:T(8,128)(2,1)S(1)}, u32[]{:S(2)}, u32[]{:S(2)}) collective-permute-start(bf16[32,4096]{1,0:T(8,128)(2,1)S(1)} %get-tuple-element.651), channel_id=1, source_target_pairs={{32,0},{64,32},{96,64},{128,96},{160,128},{192,160},{224,192},{256... | collective-permute-start | bytes 786440 | tf_op jit(solution)/shard_map/while/body/eval_jaxpr/ppermute | solution.py:16
  253.2 10.6 %collective-permute-start = (bf16[32,4096]{1,0:T(8,128)(2,1)S(1)}, bf16[32,4096]{1,0:T(8,128)(2,1)S(1)}, u32[]{:S(2)}, u32[]{:S(2)}) collective-permute-start(bf16[32,4096]{1,0:T(8,128)(2,1)S(1)} %get-tuple-element.651), channel_id=1, source_target_pairs={{32,0},{64,32},{96,64},{128,96},{160,128},{192,160},{224,192},{256... | collective-permute-start | bytes 786440 | tf_op jit(solution)/shard_map/while/body/eval_jaxpr/ppermute | solution.py:16
  269.7 10.7 %collective-permute-start = (bf16[32,4096]{1,0:T(8,128)(2,1)S(1)}, bf16[32,4096]{1,0:T(8,128)(2,1)S(1)}, u32[]{:S(2)}, u32[]{:S(2)}) collective-permute-start(bf16[32,4096]{1,0:T(8,128)(2,1)S(1)} %get-tuple-element.651), channel_id=1, source_target_pairs={{32,0},{64,32},{96,64},{128,96},{160,128},{192,160},{224,192},{256... | collective-permute-start | bytes 786440 | tf_op jit(solution)/shard_map/while/body/eval_jaxpr/ppermute | solution.py:16
  286.4 10.7 %collective-permute-start = (bf16[32,4096]{1,0:T(8,128)(2,1)S(1)}, bf16[32,4096]{1,0:T(8,128)(2,1)S(1)}, u32[]{:S(2)}, u32[]{:S(2)}) collective-permute-start(bf16[32,4096]{1,0:T(8,128)(2,1)S(1)} %get-tuple-element.651), channel_id=1, source_target_pairs={{32,0},{64,32},{96,64},{128,96},{160,128},{192,160},{224,192},{256... | collective-permute-start | bytes 786440 | tf_op jit(solution)/shard_map/while/body/eval_jaxpr/ppermute | solution.py:16
  303.1 10.7 %collective-permute-start = (bf16[32,4096]{1,0:T(8,128)(2,1)S(1)}, bf16[32,4096]{1,0:T(8,128)(2,1)S(1)}, u32[]{:S(2)}, u32[]{:S(2)}) collective-permute-start(bf16[32,4096]{1,0:T(8,128)(2,1)S(1)} %get-tuple-element.651), channel_id=1, source_target_pairs={{32,0},{64,32},{96,64},{128,96},{160,128},{192,160},{224,192},{256... | collective-permute-start | bytes 786440 | tf_op jit(solution)/shard_map/while/body/eval_jaxpr/ppermute | solution.py:16
  319.7 10.7 %collective-permute-start = (bf16[32,4096]{1,0:T(8,128)(2,1)S(1)}, bf16[32,4096]{1,0:T(8,128)(2,1)S(1)}, u32[]{:S(2)}, u32[]{:S(2)}) collective-permute-start(bf16[32,4096]{1,0:T(8,128)(2,1)S(1)} %get-tuple-element.651), channel_id=1, source_target_pairs={{32,0},{64,32},{96,64},{128,96},{160,128},{192,160},{224,192},{256... | collective-permute-start | bytes 786440 | tf_op jit(solution)/shard_map/while/body/eval_jaxpr/ppermute | solution.py:16
  336.4 10.9 %collective-permute-start = (bf16[32,4096]{1,0:T(8,128)(2,1)S(1)}, bf16[32,4096]{1,0:T(8,128)(2,1)S(1)}, u32[]{:S(2)}, u32[]{:S(2)}) collective-permute-start(bf16[32,4096]{1,0:T(8,128)(2,1)S(1)} %get-tuple-element.651), channel_id=1, source_target_pairs={{32,0},{64,32},{96,64},{128,96},{160,128},{192,160},{224,192},{256... | collective-permute-start | bytes 786440 | tf_op jit(solution)/shard_map/while/body/eval_jaxpr/ppermute | solution.py:16
  353.2 12.2 %collective-permute-start = (bf16[32,4096]{1,0:T(8,128)(2,1)S(1)}, bf16[32,4096]{1,0:T(8,128)(2,1)S(1)}, u32[]{:S(2)}, u32[]{:S(2)}) collective-permute-start(bf16[32,4096]{1,0:T(8,128)(2,1)S(1)} %get-tuple-element.651), channel_id=1, source_target_pairs={{32,0},{64,32},{96,64},{128,96},{160,128},{192,160},{224,192},{256... | collective-permute-start | bytes 786440 | tf_op jit(solution)/shard_map/while/body/eval_jaxpr/ppermute | solution.py:16
  371.4 13.6 %collective-permute-start = (bf16[32,4096]{1,0:T(8,128)(2,1)S(1)}, bf16[32,4096]{1,0:T(8,128)(2,1)S(1)}, u32[]{:S(2)}, u32[]{:S(2)}) collective-permute-start(bf16[32,4096]{1,0:T(8,128)(2,1)S(1)} %get-tuple-element.651), channel_id=1, source_target_pairs={{32,0},{64,32},{96,64},{128,96},{160,128},{192,160},{224,192},{256... | collective-permute-start | bytes 786440 | tf_op jit(solution)/shard_map/while/body/eval_jaxpr/ppermute | solution.py:16
  391.0 14.2 %collective-permute-start = (bf16[32,4096]{1,0:T(8,128)(2,1)S(1)}, bf16[32,4096]{1,0:T(8,128)(2,1)S(1)}, u32[]{:S(2)}, u32[]{:S(2)}) collective-permute-start(bf16[32,4096]{1,0:T(8,128)(2,1)S(1)} %get-tuple-element.651), channel_id=1, source_target_pairs={{32,0},{64,32},{96,64},{128,96},{160,128},{192,160},{224,192},{256... | collective-permute-start | bytes 786440 | tf_op jit(solution)/shard_map/while/body/eval_jaxpr/ppermute | solution.py:16
  411.1 13.7 %collective-permute-start = (bf16[32,4096]{1,0:T(8,128)(2,1)S(1)}, bf16[32,4096]{1,0:T(8,128)(2,1)S(1)}, u32[]{:S(2)}, u32[]{:S(2)}) collective-permute-start(bf16[32,4096]{1,0:T(8,128)(2,1)S(1)} %get-tuple-element.651), channel_id=1, source_target_pairs={{32,0},{64,32},{96,64},{128,96},{160,128},{192,160},{224,192},{256... | collective-permute-start | bytes 786440 | tf_op jit(solution)/shard_map/while/body/eval_jaxpr/ppermute | solution.py:16
  430.7 11.6 %collective-permute-start = (bf16[32,4096]{1,0:T(8,128)(2,1)S(1)}, bf16[32,4096]{1,0:T(8,128)(2,1)S(1)}, u32[]{:S(2)}, u32[]{:S(2)}) collective-permute-start(bf16[32,4096]{1,0:T(8,128)(2,1)S(1)} %get-tuple-element.651), channel_id=1, source_target_pairs={{32,0},{64,32},{96,64},{128,96},{160,128},{192,160},{224,192},{256... | collective-permute-start | bytes 786440 | tf_op jit(solution)/shard_map/while/body/eval_jaxpr/ppermute | solution.py:16
  448.3 11.0 %collective-permute-start = (bf16[32,4096]{1,0:T(8,128)(2,1)S(1)}, bf16[32,4096]{1,0:T(8,128)(2,1)S(1)}, u32[]{:S(2)}, u32[]{:S(2)}) collective-permute-start(bf16[32,4096]{1,0:T(8,128)(2,1)S(1)} %get-tuple-element.651), channel_id=1, source_target_pairs={{32,0},{64,32},{96,64},{128,96},{160,128},{192,160},{224,192},{256... | collective-permute-start | bytes 786440 | tf_op jit(solution)/shard_map/while/body/eval_jaxpr/ppermute | solution.py:16
  470.6 112.2 %reduce-scatter.6.cloned.1.call-start = ((), (), s32[]{:S(2)}) async-start(), calls=%async_computation.6 | async-start | bytes 2359296 | tf_op jit(solution)/shard_map/reduce_scatter | solution.py:318
  537.7 69.5 %reduce-scatter.8.cloned.1.call-start = ((), (), s32[]{:S(2)}) async-start(), calls=%async_computation.7 | async-start | bytes 393216 | tf_op jit(solution)/shard_map/reduce_scatter | solution.py:321
  (10 other events, 103.6 us)
Sparse Core Ops, SparseCore 0:
  13.8 48.4 all-gather.3
  64.3 25.5 all-gather.5
  470.8 66.8 reduce-scatter.3
  540.6 42.1 reduce-scatter.5
  585.7 21.5 reduce-scatter.7
